TPU v7x, 128 devices: a whole 4x4x4 slice. The times are simulated.
128 devices in a mesh: row: 16 (over z_hi, x, core), col: 8 (over y, z_lo).
Axes of the slice: x: 4, y: 4, z: 4 (z_hi: 2, z_lo: 2; z = z_hi * 2 + z_lo), core: 2. Of those that a mesh axis runs over, the one named last changes fastest.
Arguments:
- struct_basis: float32 [32768, 1024], P(('row', 'col')), may hold values from -24 to 24
- fluid_basis: float32 [16384, 1024], P(('row', 'col')), may hold values from -24 to 24
- stiff_tiles: float32 [256, 4, 128, 128], P(('row', 'col')), may hold values from -0.0014648438 to 0.0014648438
- mass_tiles: float32 [256, 4, 128, 128], P(('row', 'col')), may hold values from -0.0014648438 to 0.0014648438
- fluid_stiff_tiles: float32 [128, 4, 128, 128], P(('row', 'col')), may hold values from -0.001953125 to 0.001953125
- fluid_mass_tiles: float32 [128, 4, 128, 128], P(('row', 'col')), may hold values from -0.001953125 to 0.001953125
- struct_cols: int32 [256, 4], P(('row', 'col')), may hold values from 0 to 3
- fluid_cols: int32 [128, 4], P(('row', 'col')), may hold values from 0 to 2
- wet_rows: int32 [16384], P(('row', 'col')), may hold values from 0 to 127
- wet_dest: int32 [16384, 1], P(('row', 'col')), may hold values from 0 to 127; in each aligned block of 128 rows (0 to 127, 128 to 255, ...) at most 2 rows name the same one
- coupling: float32 [32768, 256], P(('row', 'col')), may hold values from -0.001953125 to 0.001953125
Outputs:
- stiff_red: float32 [1024, 1024], P('row', 'col')
- mass_red: float32 [1024, 1024], P('row', 'col')
- fluid_stiff_red: float32 [1024, 1024], P('row', 'col')
- fluid_mass_red: float32 [1024, 1024], P('row', 'col')
- coupling_red: float32 [1024, 1024], P('row', 'col')
Inputs may be any that keep to these rules, and one draw needn't show every extreme that they name: `wet_dest`: among the 128 entries of one block, no block number is named more than 2 times, and some block number is named exactly 2 times in every draw.
All inputs are finite; a program needn't handle non-finite values.
Results may differ from a plain program's by a relative error of at most 0.0003.
Values sent between devices are 32-bit elements; how exact they have to be, the bound alone decides.
No kernel may reach another device: no remote copies, remote signals or barrier semaphores. Data moves between devices by JAX's collectives and lax.ppermute only.
A program may use at most 128 MiB of HBM per device.

v0:
```python
import functools

import jax
import jax.numpy as jnp
from jax import lax
from jax.experimental import pallas as pl
from jax.experimental.pallas import tpu as pltpu
from jax.sharding import Mesh
from jax.sharding import PartitionSpec as P


R = 1024
TILE = 128
CAP = 2
F32 = jnp.float32
BF16 = jnp.bfloat16

AXES = ("zhi", "x", "core", "y", "zlo")
ROW = ("zhi", "x", "core")
COL = ("y", "zlo")
X, Y, Z = "x", "y", ("zhi", "zlo")
HALF = 32


VMEM = pl.BlockSpec(memory_space=pltpu.VMEM)
SMEM = pl.BlockSpec(memory_space=pltpu.SMEM)
ANY = pl.BlockSpec(memory_space=pl.ANY)
PARAMS = pltpu.CompilerParams(vmem_limit_bytes=60 * 1024 * 1024)


def shape(*dims):
    return jax.ShapeDtypeStruct(dims, F32)


def parts(value):
    high = value.astype(BF16)
    low = (value - high.astype(F32)).astype(BF16)
    return high, low


def mul(a, b):
    return jnp.dot(a, b, preferred_element_type=F32)


def product(a, b):
    ah, al = a
    bh, bl = b
    return mul(ah, bh) + (mul(ah, bl) + mul(al, bh))


def shifted(value, axis, by):
    size = lax.axis_size(axis)
    return lax.ppermute(value, axis, [(i, (i + by) % size) for i in range(size)])


def from_behind(value, by):
    size = lax.axis_size(AXES)
    pairs = [(i, i + by) for i in range(size) if 0 <= i + by < size]
    return lax.ppermute(value, AXES, pairs)


def route_kernel(dest_col, dest_row, rows, fluid, out):
    n = dest_row.shape[1]
    earlier = lax.broadcasted_iota(jnp.int32, (n, n), 0) < lax.broadcasted_iota(jnp.int32, (n, n), 1)
    same = (dest_col[...] == dest_row[...]) & earlier
    slot = jnp.sum(jnp.where(same, 1.0, 0.0), axis=0, keepdims=True).astype(jnp.int32)
    target = dest_row[...] * CAP + slot
    q = out.shape[0]
    selector = jnp.where(lax.broadcasted_iota(jnp.int32, (q, n), 0) == target, 1.0, 0.0).astype(BF16)
    height = fluid.shape[0]
    picked = jnp.where(lax.broadcasted_iota(jnp.int32, (height, n), 0) == rows[...], 1.0, 0.0)
    chosen = lax.dot_general(
        selector, picked.astype(BF16), (((1,), (1,)), ((), ())), preferred_element_type=F32
    ).astype(BF16)
    value = fluid[...]
    high = value.astype(BF16)
    rest = value - high.astype(F32)
    mid = rest.astype(BF16)
    low = (rest - mid.astype(F32)).astype(BF16)
    out[...] = mul(chosen, high) + (mul(chosen, mid) + mul(chosen, low))


def turn_kernel(place, struct, fluid, own_s, send_s, own_f, send_f, held_s, held_f):
    core = place[3]
    held_s[...] = struct[...].T.reshape(held_s.shape)
    held_f[...] = fluid[...].T.reshape(held_f.shape)
    own_s[...] = held_s[:, core]
    send_s[...] = held_s[:, 1 - core]
    own_f[...] = held_f[:, core]
    send_f[...] = held_f[:, 1 - core]


def wet_kernel(coupling, received, out):
    out[...] = product(parts(coupling[...]), parts(received[...]))


def gathered(tiles, cols, total, at):
    total[:, at : at + TILE * tiles.shape[0]] = jnp.zeros(
        (total.shape[0], TILE * tiles.shape[0], TILE), F32
    )
    for i in range(tiles.shape[0]):
        rows = pl.ds(at + i * TILE, TILE)
        for k in range(tiles.shape[1]):
            c = cols[i, k]
            total[c, rows] = total[c, rows] + tiles[i, k]


def image(total, pieces):
    acc = None
    c = 0
    for piece in pieces:
        n = piece.shape[0] // TILE
        left = jnp.concatenate([total[c + i] for i in range(n)], axis=1) if n > 1 else total[c]
        term = product(parts(left), parts(piece))
        acc = term if acc is None else acc + term
        c += n
    return acc


def fluid_kernel(cols, stiff, mass, lo, own, hi, after_a, after_b, out, total):
    gathered(stiff, cols, total, 0)
    gathered(mass, cols, total, TILE)
    out[...] = image(total, (lo[...], own[...], hi[...])).reshape(out.shape)


def struct_kernel(cols, stiff, mass, lo, own, hi, after, out, total):
    gathered(stiff, cols, total, 0)
    gathered(mass, cols, total, 2 * TILE)
    out[...] = image(total, (lo[...], own[...], hi[...])).reshape(out.shape)


def joined(one, two):
    return jnp.concatenate([one[...].reshape(R // 2, -1), two[...].reshape(R // 2, -1)], axis=1)


def multiply(held, left, one, two):
    right = jnp.concatenate([one, two], axis=0)
    held[...] = product((left[0][...], left[1][...]), parts(right)).reshape(held.shape)


def send_off(place, held, outs):
    for o in range(4):
        dx = lax.rem(place[0] + o, 4)
        dy = lax.rem(place[1] + o, 4)
        for h in range(2):
            outs[o][0, h] = held[h * 4 + dx, 0:HALF, :]
        outs[4 + o][0] = held[:, HALF:, pl.ds(pl.multiple_of(dy * 256, 256), 256)]


def first_kernel(place, ls0, ls1, lf0, lf1, ic0, ic1, if0, if1, *rest):
    outs, (sh, sl, fh, fl, held) = rest[:8], rest[8:]
    m = pl.program_id(0)

    @pl.when(m == 0)
    def _():
        sh[...], sl[...] = parts(joined(ls0, ls1))
        fh[...], fl[...] = parts(joined(lf0, lf1))
        multiply(held, (sh, sl), ic0[...], ic1[...])

    @pl.when(m > 0)
    def _():
        multiply(held, (fh, fl), if0[0], if1[0])

    send_off(place, held, outs)


def second_kernel(place, ls0, ls1, is0, is1, *rest):
    outs, (sh, sl, held) = rest[:8], rest[8:]

    @pl.when(pl.program_id(0) == 0)
    def _():
        sh[...], sl[...] = parts(joined(ls0, ls1))

    multiply(held, (sh, sl), is0[0], is1[0])
    send_off(place, held, outs)


def split_kernel(axis, place, a0, a1, a2, a3, b0, b1, b2, b3, o0, o1, o2, o3, held):
    n = a0.shape[0]
    held[:n] = (a0[...] + a1[...]) + (a2[...] + a3[...])
    held[n:] = (b0[...] + b1[...]) + (b2[...] + b3[...])
    for o, out in enumerate((o0, o1, o2, o3)):
        d = lax.rem(place[axis] + o, 4)
        if axis == 1:
            out[...] = held[..., pl.ds(pl.multiple_of(d * 256, 256), 256)]
        else:
            for h in range(2):
                out[:, h] = held[:, h * 4 + d]


def spread_kernel(x0, x1, x2, x3, y0, y1, y2, y3, out):
    for h in range(2):
        top = (x0[:, h] + x1[:, h]) + (x2[:, h] + x3[:, h])
        low = (y0[:, h] + y1[:, h]) + (y2[:, h] + y3[:, h])
        for l in range(2):
            lanes = slice(l * 128, (l + 1) * 128)
            out[h * 2 + l, :, 0:HALF] = top[..., lanes]
            out[h * 2 + l, :, HALF:] = low[..., lanes]


def last_kernel(arrived, *outs):
    for m, out in enumerate(outs):
        out[...] = (arrived[0, m] + arrived[1, m]) + (arrived[2, m] + arrived[3, m])


def call(kernel, out, count, smem=0, anywhere=0, scratch=(), flops=0, moved=0):
    run = pl.pallas_call(
        kernel,
        out_shape=out,
        in_specs=[SMEM] * smem + [VMEM] * (count - smem - anywhere) + [ANY] * anywhere,
        out_specs=jax.tree.map(lambda _: VMEM, out),
        scratch_shapes=list(scratch),
        compiler_params=PARAMS,
        cost_estimate=pl.CostEstimate(flops=flops, bytes_accessed=moved, transcendentals=0),
    )
    return run


def exchanged(slots, axis):
    return [slots[0]] + [shifted(slots[o], axis, o) for o in range(1, 4)]


def split(place, one, two, axis):
    dims = (one[0].shape[0] + two[0].shape[0],) + one[0].shape[1:]
    size = one[0].size + two[0].size
    return call(
        functools.partial(split_kernel, axis),
        [shape(5, 2, HALF, 256)] * 4,
        9,
        smem=1,
        scratch=[pltpu.VMEM(dims, F32)],
        flops=3 * size,
        moved=20 * size,
    )(place, *one, *two)


def partial_sums(kernel, count, place, lefts, steps, operands, specs, scratch):
    run = pl.pallas_call(
        kernel,
        grid=(count,),
        out_shape=[shape(count, 2, HALF, R)] * 4 + [shape(count, 8, HALF, 256)] * 4,
        in_specs=[SMEM] + [VMEM] * len(lefts) + specs,
        out_specs=[pl.BlockSpec((1, 2, HALF, R), lambda m: (m, 0, 0, 0))] * 4
        + [pl.BlockSpec((1, 8, HALF, 256), lambda m: (m, 0, 0, 0))] * 4,
        scratch_shapes=scratch + [pltpu.VMEM((8, 64, R), F32)],
        compiler_params=PARAMS,
        cost_estimate=pl.CostEstimate(
            flops=6 * steps * 512 * 256 * R, bytes_accessed=4 * count * 2**20, transcendentals=0
        ),
    )
    return run(place, *lefts, *operands)


def compute(
    struct_basis,
    fluid_basis,
    stiff_tiles,
    mass_tiles,
    fluid_stiff_tiles,
    fluid_mass_tiles,
    struct_cols,
    fluid_cols,
    wet_rows,
    wet_dest,
    coupling,
):
    place = jnp.stack([lax.axis_index(X), lax.axis_index(Y), lax.axis_index(Z), lax.axis_index("core")]).astype(
        jnp.int32
    )
    below_s = from_behind(struct_basis[-TILE:], 1)
    above_s = from_behind(struct_basis[:TILE], -1)
    below_f = from_behind(fluid_basis, 1)
    above_f = from_behind(fluid_basis, -1)

    outgoing = call(route_kernel, shape(256, R), 4, flops=2 * 3 * 256 * 128 * R, moved=2**21)(
        wet_dest, wet_dest.reshape(1, -1), wet_rows.reshape(1, -1), fluid_basis
    )
    received = lax.all_to_all(outgoing, AXES, split_axis=0, concat_axis=0, tiled=True)

    own_s, send_s, own_f, send_f = call(
        turn_kernel,
        [shape(8, 64, 256)] * 2 + [shape(8, 64, 128)] * 2,
        3,
        smem=1,
        scratch=[pltpu.VMEM((8, 2, 64, 256), F32), pltpu.VMEM((8, 2, 64, 128), F32)],
        flops=2**20,
        moved=3 * 2**20,
    )(place, struct_basis, fluid_basis)
    left_s = shifted(send_s, "core", 1)
    left_f = shifted(send_f, "core", 1)

    image_c = call(wet_kernel, shape(256, R), 2, flops=6 * 256 * 256 * R, moved=2**21)(coupling, received)
    other_c = shifted(image_c, "core", 1)

    image_f = call(
        fluid_kernel,
        shape(2, 128, R),
        8,
        smem=1,
        anywhere=2,
        scratch=[pltpu.VMEM((3, 256, TILE), F32)],
        flops=6 * 256 * 384 * R,
        moved=3 * 2**20,
    )(fluid_cols, fluid_stiff_tiles, fluid_mass_tiles, below_f, fluid_basis, above_f, image_c, own_s)
    other_f = shifted(image_f, "core", 1)

    fblock = pl.BlockSpec((1, 128, R), lambda m: (jnp.maximum(m - 1, 0), 0, 0))
    slim = [pltpu.VMEM((512, 512), BF16)] * 2
    first = partial_sums(
        first_kernel,
        3,
        place,
        (own_s, left_s, own_f, left_f, image_c, other_c),
        4,
        (image_f, other_f),
        [fblock, fblock],
        slim + [pltpu.VMEM((512, 256), BF16)] * 2,
    )
    first_x = exchanged(first[0:4], X)
    first_y = exchanged(first[4:8], Y)

    image_s = call(
        struct_kernel,
        shape(2, 256, R),
        7,
        smem=1,
        anywhere=1,
        scratch=[pltpu.VMEM((4, 512, TILE), F32)],
        flops=6 * 512 * 512 * R,
        moved=5 * 2**20,
    )(struct_cols, stiff_tiles, mass_tiles, below_s, struct_basis, above_s, first[0])
    other_s = shifted(image_s, "core", 1)

    sblock = pl.BlockSpec((1, 256, R), lambda m: (m, 0, 0))
    second = partial_sums(second_kernel, 2, place, (own_s, left_s), 4, (image_s, other_s), [sblock, sblock], slim)
    second_x = exchanged(second[0:4], X)
    second_y = exchanged(second[4:8], Y)

    then_y = exchanged(split(place, first_x, second_x, 1), Y)
    then_x = exchanged(split(place, first_y, second_y, 0), X)
    blocks = call(spread_kernel, shape(4, 5, 64, 128), 8, flops=2**20, moved=2**22)(*then_y, *then_x)
    arrived = lax.all_to_all(blocks, Z, split_axis=0, concat_axis=0, tiled=True)
    wet, fstiff, fmass, stiff, mass = call(last_kernel, [shape(64, 128)] * 5, 1, flops=2**18, moved=2**20)(arrived)
    return stiff, mass, fstiff, fmass, wet


def solution(mesh):
    fine = Mesh(mesh.devices.reshape(2, 4, 2, 4, 2), AXES)
    return jax.shard_map(
        compute,
        mesh=fine,
        in_specs=(
            P(AXES, None),
            P(AXES, None),
            P(AXES, None, None, None),
            P(AXES, None, None, None),
            P(AXES, None, None, None),
            P(AXES, None, None, None),
            P(AXES, None),
            P(AXES, None),
            P(AXES),
            P(AXES, None),
            P(AXES, None),
        ),
        out_specs=(P(ROW, COL),) * 5,
        check_vma=False,
    )
```

profile of v0, /device:TPU:0, one launch (start us, length us, event | category | flops | bytes accessed | tf_op | source)
XLA Modules:
  0.0 224.5 jit_solution(1778449227243502610)
XLA Ops:
  0.6 1.4 copy.16.dest_col
  2.0 2.9 %shard_map.147 = f32[256,1024]{1,0:T(8,128)} custom-call(s32[128,1]{1,0:T(8,128)} %copy.16.dest_col, s32[1,128]{1,0:T(1,128)} %bitcast.6, s32[1,128]{1,0:T(1,128)} %bitcast.7, f32[128,1024]{1,0:T(8,128)} %own.2), custom_call_target="tpu_custom_call" | custom-call | flops 201326592 | bytes 2097152 | tf_op jit(solution)/shard_map/pallas_call | solution.py:275
  4.9 2.9 %all_to_all.10 = f32[128,2,1024]{2,1,0:T(2,128)} reshape(f32[256,1024]{1,0:T(8,128)} %shard_map.147) | data formatting | bytes 2097152 | tf_op jit(solution)/shard_map/all_to_all | solution.py:278
  7.8 11.2 %all-to-all-start = ((f32[128,2,1024]{2,1,0:T(2,128)}), f32[128,2,1024]{2,1,0:T(2,128)S(1)}, u32[]{:S(2)}, u32[]{:S(2)}) async-start(f32[128,2,1024]{2,1,0:T(2,128)} %all_to_all.10), calls=%async_computation | async-start | bytes 2097152 | tf_op jit(solution)/shard_map/all_to_all | solution.py:278
  19.0 3.0 %collective-permute-start.3 = (f32[128,1024]{1,0:T(8,128)S(1)}, f32[128,1024]{1,0:T(8,128)S(1)}, u32[]{:S(2)}, u32[]{:S(2)}) collective-permute-start(f32[128,1024]{1,0:T(8,128)S(1)} %copy-done.1), channel_id=1, source_target_pairs={{0,1},{1,2},{2,3},{3,4},{4,5},{5,6},{6,7},{7,8},{8,9},{9,10},{10,1... | collective-permute-start | bytes 1572872 | tf_op jit(solution)/shard_map/ppermute | solution.py:59
  22.0 1.3 collective-permute-start.4
  23.3 0.6 pad_add_fusion.place
  23.9 2.9 %shard_map.146 = (f32[8,64,256]{2,1,0:T(8,128)}, f32[8,64,256]{2,1,0:T(8,128)}, f32[8,64,128]{2,1,0:T(8,128)}, f32[8,64,128]{2,1,0:T(8,128)}) custom-call(s32[4]{0:T(128)} %pad_add_fusion.place, f32[256,1024]{1,0:T(8,128)} %own.3, f32[128,1024]{1,0:T(8,128)} %own.2), custom_call_target="tpu_custom_call" | custom-call | flops 1048576 | bytes 3145728 | tf_op jit(solution)/shard_map/pallas_call | solution.py:280
  26.8 11.2 %all-to-all-done = f32[128,2,1024]{2,1,0:T(2,128)S(1)} async-done(((f32[128,2,1024]{2,1,0:T(2,128)}), f32[128,2,1024]{2,1,0:T(2,128)S(1)}, u32[]{:S(2)}, u32[]{:S(2)}) %all-to-all-start) | async-done | bytes 1048608 | tf_op jit(solution)/shard_map/all_to_all | solution.py:278
  38.0 1.7 all_to_all.12.received
  39.7 2.9 %shard_map.148.after_a.ic0 = f32[256,1024]{1,0:T(8,128)} custom-call(f32[256,256]{1,0:T(8,128)} %coupling.1, f32[256,1024]{1,0:T(8,128)} %all_to_all.12.received), custom_call_target="tpu_custom_call" | custom-call | flops 402653184 | bytes 2097152 | tf_op jit(solution)/shard_map/pallas_call | solution.py:292
  42.6 10.7 %collective-permute-done.3.lo = f32[128,1024]{1,0:T(8,128)S(1)} collective-permute-done((f32[128,1024]{1,0:T(8,128)S(1)}, f32[128,1024]{1,0:T(8,128)S(1)}, u32[]{:S(2)}, u32[]{:S(2)}) %collective-permute-start.3) | collective-permute-done | bytes 524320 | tf_op jit(solution)/shard_map/ppermute | solution.py:59
  53.3 0.8 copy-done.7
  54.1 0.2 copy-done.8
  54.3 4.1 %shard_map.149.if0 = f32[2,128,1024]{2,1,0:T(8,128)} custom-call(s32[1,4]{1,0:T(1,128)} %cols.2, f32[1,4,128,128]{3,2,1,0:T(8,128)} %stiff.2, f32[1,4,128,128]{3,2,1,0:T(8,128)} %mass.2, f32[128,1024]{1,0:T(8,128)} %copy-done.7, f32[128,1024]{1,0:T(8,128)} %own.2, f32[128,1024]{1,0:T(8,128)} %copy-done.8, f32[256,1024]{1,0:T(8,128)} %shard_map.148.after_a.ic0, ...), custom_call_target="tpu_custom_call" | custom-call | flops 603979776 | bytes 3145728 | tf_op jit(solution)/shard_map/pallas_call | solution.py:295
  58.4 0.5 collective-permute-start
  58.9 0.0 collective-permute-start.1
  58.9 0.1 fusion
  59.1 1.3 collective-permute-start.10
  60.4 2.0 collective-permute-done.1.lf1
  62.4 4.4 %collective-permute-start.9 = (f32[128,1024]{1,0:T(8,128)S(1)}, f32[128,1024]{1,0:T(8,128)S(1)}, u32[]{:S(2)}, u32[]{:S(2)}) collective-permute-start(f32[128,1024]{1,0:T(8,128)S(1)} %get-tuple-element.72), channel_id=1, source_target_pairs={{0,1},{1,2},{2,3},{3,4},{4,5},{5,6},{6,7},{7,8},{8,9},{9,10},{10,1... | collective-permute-start | bytes 1572872 | tf_op jit(solution)/shard_map/ppermute | solution.py:59
  66.9 0.8 copy-done.19
  67.6 0.4 copy-done.18
  68.0 8.9 %shard_map.150 = (f32[3,2,32,1024]{3,2,1,0:T(8,128)}, f32[3,2,32,1024]{3,2,1,0:T(8,128)}, f32[3,2,32,1024]{3,2,1,0:T(8,128)}, f32[3,2,32,1024]{3,2,1,0:T(8,128)}...) custom-call(s32[4]{0:T(128)} %pad_add_fusion.place, ...), custom_call_target="tpu_custom_call" | custom-call | flops 3221225472 | bytes 12582912 | tf_op jit(solution)/shard_map/pallas_call | solution.py:251
  76.9 2.0 collective-permute-done.10.hi
  78.9 8.5 %collective-permute-done.9.lo = f32[128,1024]{1,0:T(8,128)S(1)} collective-permute-done((f32[128,1024]{1,0:T(8,128)S(1)}, f32[128,1024]{1,0:T(8,128)S(1)}, u32[]{:S(2)}, u32[]{:S(2)}) %collective-permute-start.9) | collective-permute-done | bytes 524320 | tf_op jit(solution)/shard_map/ppermute | solution.py:59
  87.4 0.8 copy-done.10
  88.2 5.9 %shard_map.151.is0 = f32[2,256,1024]{2,1,0:T(8,128)} custom-call(s32[2,4]{1,0:T(2,128)} %cols.3, f32[2,4,128,128]{3,2,1,0:T(8,128)} %stiff.3, f32[2,4,128,128]{3,2,1,0:T(8,128)} %mass.3, f32[128,1024]{1,0:T(8,128)} %copy-done.10, f32[256,1024]{1,0:T(8,128)} %own.3, f32[128,1024]{1,0:T(8,128)} %copy-done.9, f32[3,2,32,1024]{3,2,1,0:T(8,128)} %get-tuple-element.42.after.a0), custom_call_target="tpu_custom_call" | custom-call | flops 1610612736 | bytes 5242880 | tf_op jit(solution)/shard_map/pallas_call | solution.py:322
  94.2 2.5 %collective-permute-start.6 = (f32[3,2,32,1024]{3,2,1,0:T(8,128)}, f32[3,2,32,1024]{3,2,1,0:T(8,128)S(1)}, u32[]{:S(2)}, u32[]{:S(2)}) collective-permute-start(f32[3,2,32,1024]{3,2,1,0:T(8,128)} %get-tuple-element.43), channel_id=1, source_target_pairs={{0,16},{16,32},{32,48},{48,0},{1,17},{17,33},{33,49},{49,1},{2,18}... | collective-permute-start | bytes 2359304 | tf_op jit(solution)/shard_map/ppermute | solution.py:53
  96.7 2.3 %collective-permute-start.7 = (f32[3,2,32,1024]{3,2,1,0:T(8,128)}, f32[3,2,32,1024]{3,2,1,0:T(8,128)S(1)}, u32[]{:S(2)}, u32[]{:S(2)}) collective-permute-start(f32[3,2,32,1024]{3,2,1,0:T(8,128)} %get-tuple-element.44), channel_id=1, source_target_pairs={{0,32},{16,48},{32,0},{48,16},{1,33},{17,49},{33,1},{49,17},{2,34}... | collective-permute-start | bytes 2359304 | tf_op jit(solution)/shard_map/ppermute | solution.py:53
  99.0 1.8 collective-permute-start.8
  100.8 0.7 collective-permute-start.18
  101.5 1.4 copy-done.17
  102.9 2.6 %collective-permute-start.19 = (f32[3,8,32,256]{3,2,1,0:T(8,128)}, f32[3,8,32,256]{3,2,1,0:T(8,128)S(1)}, u32[]{:S(2)}, u32[]{:S(2)}) collective-permute-start(f32[3,8,32,256]{3,2,1,0:T(8,128)} %get-tuple-element.56), channel_id=1, source_target_pairs={{0,4},{2,6},{4,0},{6,2},{1,5},{3,7},{5,1},{7,3},{8,12},{10,14},{12... | collective-permute-start | bytes 2359304 | tf_op jit(solution)/shard_map/ppermute | solution.py:53
  105.4 7.4 %shard_map.152 = (f32[2,2,32,1024]{3,2,1,0:T(8,128)}, f32[2,2,32,1024]{3,2,1,0:T(8,128)}, f32[2,2,32,1024]{3,2,1,0:T(8,128)}, f32[2,2,32,1024]{3,2,1,0:T(8,128)}...) custom-call(s32[4]{0:T(128)} %pad_add_fusion.place, ...), custom_call_target="tpu_custom_call" | custom-call | flops 3221225472 | bytes 8388608 | tf_op jit(solution)/shard_map/pallas_call | solution.py:251
  112.8 3.2 %collective-permute-done.6.a1 = f32[3,2,32,1024]{3,2,1,0:T(8,128)S(1)} collective-permute-done((f32[3,2,32,1024]{3,2,1,0:T(8,128)}, f32[3,2,32,1024]{3,2,1,0:T(8,128)S(1)}, u32[]{:S(2)}, u32[]{:S(2)}) %collective-permute-start.6) | collective-permute-done | bytes 786464 | tf_op jit(solution)/shard_map/ppermute | solution.py:53
  116.0 1.4 collective-permute-start.12
  117.3 17.2 %collective-permute-done.7.a2 = f32[3,2,32,1024]{3,2,1,0:T(8,128)S(1)} collective-permute-done((f32[3,2,32,1024]{3,2,1,0:T(8,128)}, f32[3,2,32,1024]{3,2,1,0:T(8,128)S(1)}, u32[]{:S(2)}, u32[]{:S(2)}) %collective-permute-start.7) | collective-permute-done | bytes 786464 | tf_op jit(solution)/shard_map/ppermute | solution.py:53
  134.5 1.2 collective-permute-start.13
  135.7 0.8 collective-permute-start.14
  136.6 2.9 %collective-permute-start.20 = (f32[3,8,32,256]{3,2,1,0:T(8,128)}, f32[3,8,32,256]{3,2,1,0:T(8,128)}, u32[]{:S(2)}, u32[]{:S(2)}) collective-permute-start(f32[3,8,32,256]{3,2,1,0:T(8,128)} %get-tuple-element.57), channel_id=1, source_target_pairs={{0,6},{2,0},{4,2},{6,4},{1,7},{3,1},{5,3},{7,5},{8,14},{10,8},{12,... | collective-permute-start | bytes 2359304 | tf_op jit(solution)/shard_map/ppermute | solution.py:53
  139.5 6.3 %collective-permute-done.12.b1 = f32[2,2,32,1024]{3,2,1,0:T(8,128)} collective-permute-done((f32[2,2,32,1024]{3,2,1,0:T(8,128)}, f32[2,2,32,1024]{3,2,1,0:T(8,128)}, u32[]{:S(2)}, u32[]{:S(2)}) %collective-permute-start.12) | collective-permute-done | bytes 524320 | tf_op jit(solution)/shard_map/ppermute | solution.py:53
  145.8 1.0 collective-permute-start.21
  146.7 9.9 %collective-permute-done.13.b2 = f32[2,2,32,1024]{3,2,1,0:T(8,128)} collective-permute-done((f32[2,2,32,1024]{3,2,1,0:T(8,128)}, f32[2,2,32,1024]{3,2,1,0:T(8,128)}, u32[]{:S(2)}, u32[]{:S(2)}) %collective-permute-start.13) | collective-permute-done | bytes 524320 | tf_op jit(solution)/shard_map/ppermute | solution.py:53
  156.6 2.2 collective-permute-start.22
  158.8 1.5 collective-permute-start.23
  160.3 3.9 %shard_map.153 = (f32[5,2,32,256]{3,2,1,0:T(8,128)}, f32[5,2,32,256]{3,2,1,0:T(8,128)}, f32[5,2,32,256]{3,2,1,0:T(8,128)}, f32[5,2,32,256]{3,2,1,0:T(8,128)}) custom-call(s32[4]{0:T(128)} %pad_add_fusion.place, f32[3,2,32,1024]{3,2,1,0:T(8,128)} %get-tuple-element.42.after.a0, f32[3,2,32,1024]{3,2,1,0:T(8,128)} %copy-done.4, f32[3,2,32,1024]{3,2,1,0:T(8,128)} %copy-done.5, ...), custom_call_target="tpu_custom_call" | custom-call | flops 983040 | bytes 6553600 | tf_op jit(solution)/shard_map/pallas_call | solution.py:226
  164.2 0.6 collective-permute-start.15
  164.9 1.3 collective-permute-start.16
  166.2 2.1 collective-permute-start.17
  168.3 5.0 %collective-permute-done.22.b2 = f32[2,8,32,256]{3,2,1,0:T(8,128)} collective-permute-done((f32[2,8,32,256]{3,2,1,0:T(8,128)}, f32[2,8,32,256]{3,2,1,0:T(8,128)}, u32[]{:S(2)}, u32[]{:S(2)}) %collective-permute-start.22) | collective-permute-done | bytes 524320 | tf_op jit(solution)/shard_map/ppermute | solution.py:53
  173.3 10.6 %collective-permute-done.23.b3 = f32[2,8,32,256]{3,2,1,0:T(8,128)} collective-permute-done((f32[2,8,32,256]{3,2,1,0:T(8,128)}, f32[2,8,32,256]{3,2,1,0:T(8,128)}, u32[]{:S(2)}, u32[]{:S(2)}) %collective-permute-start.23) | collective-permute-done | bytes 524320 | tf_op jit(solution)/shard_map/ppermute | solution.py:53
  183.9 3.9 %shard_map.154 = (f32[5,2,32,256]{3,2,1,0:T(8,128)}, f32[5,2,32,256]{3,2,1,0:T(8,128)}, f32[5,2,32,256]{3,2,1,0:T(8,128)}, f32[5,2,32,256]{3,2,1,0:T(8,128)}) custom-call(s32[4]{0:T(128)} %pad_add_fusion.place, f32[3,8,32,256]{3,2,1,0:T(8,128)} %get-tuple-element.54.a0, f32[3,8,32,256]{3,2,1,0:T(8,128)} %copy-done.2, f32[3,8,32,256]{3,2,1,0:T(8,128)} %copy-done.3, ...), custom_call_target="tpu_custom_call" | custom-call | flops 983040 | bytes 6553600 | tf_op jit(solution)/shard_map/pallas_call | solution.py:226
  187.8 2.9 %collective-permute-start.25 = (f32[5,2,32,256]{3,2,1,0:T(8,128)}, f32[5,2,32,256]{3,2,1,0:T(8,128)S(1)}, u32[]{:S(2)}, u32[]{:S(2)}) collective-permute-start(f32[5,2,32,256]{3,2,1,0:T(8,128)} %get-tuple-element.64), channel_id=1, source_target_pairs={{0,32},{16,48},{32,0},{48,16},{1,33},{17,49},{33,1},{49,17},{2,34}... | collective-permute-start | bytes 983048 | tf_op jit(solution)/shard_map/ppermute | solution.py:53
  190.8 0.8 collective-permute-start.26
  191.6 5.0 %collective-permute-done.17.x3 = f32[5,2,32,256]{3,2,1,0:T(8,128)S(1)} collective-permute-done((f32[5,2,32,256]{3,2,1,0:T(8,128)}, f32[5,2,32,256]{3,2,1,0:T(8,128)S(1)}, u32[]{:S(2)}, u32[]{:S(2)}) %collective-permute-start.17) | collective-permute-done | bytes 327712 | tf_op jit(solution)/shard_map/ppermute | solution.py:53
  196.6 7.6 %collective-permute-done.24.y1 = f32[5,2,32,256]{3,2,1,0:T(8,128)S(1)} collective-permute-done((f32[5,2,32,256]{3,2,1,0:T(8,128)}, f32[5,2,32,256]{3,2,1,0:T(8,128)S(1)}, u32[]{:S(2)}, u32[]{:S(2)}) %collective-permute-start.24) | collective-permute-done | bytes 327712 | tf_op jit(solution)/shard_map/ppermute | solution.py:53
  204.2 0.6 collective-permute-done.26.y3
  204.8 0.1 copy-done.14
  204.9 0.1 copy-done.15
  205.1 0.5 copy-done.16
  205.6 2.7 %shard_map.155 = f32[4,5,64,128]{3,2,1,0:T(8,128)} custom-call(f32[5,2,32,256]{3,2,1,0:T(8,128)} %get-tuple-element.50.x0, f32[5,2,32,256]{3,2,1,0:T(8,128)} %copy-done.11, f32[5,2,32,256]{3,2,1,0:T(8,128)} %copy-done.12, f32[5,2,32,256]{3,2,1,0:T(8,128)} %copy-done.13, f32[5,2,32,256]{3,2,1,0:T(8,128)} %get-tuple-element.62.y0, ...), custom_call_target="tpu_custom_call" | custom-call | flops 1048576 | bytes 4194304 | tf_op jit(solution)/shard_map/pallas_call | solution.py:341
  208.2 14.5 %all_to_all.16.arrived = f32[4,5,64,128]{3,2,1,0:T(8,128)} all-to-all(f32[4,5,64,128]{3,2,1,0:T(8,128)} %shard_map.155), channel_id=1, replica_groups=mesh['zhi'=2,'x'=4,'core'=2,'y'=4,'zlo'=2] {'zhi','zlo'}, dimensions={0} | all-to-all | bytes 1310720 | tf_op jit(solution)/shard_map/all_to_all | solution.py:342
  222.8 1.8 shard_map.156
  (53 shorter events, 0.2 us)
Async XLA Ops:
  4.9 14.1 %copy-start.1 = (f32[128,1024]{1,0:T(8,128)S(1)}, f32[128,1024]{1,0:T(8,128)}, u32[]{:S(2)}) copy-start(f32[128,1024]{1,0:T(8,128)} %own.2) | copy-start | bytes 1572868
  7.8 30.2 %all-to-all-start = ((f32[128,2,1024]{2,1,0:T(2,128)}), f32[128,2,1024]{2,1,0:T(2,128)S(1)}, u32[]{:S(2)}, u32[]{:S(2)}) async-start(f32[128,2,1024]{2,1,0:T(2,128)} %all_to_all.10), calls=%async_computation | async-start | bytes 2097152 | tf_op jit(solution)/shard_map/all_to_all | solution.py:278
  19.0 34.3 %collective-permute-start.3 = (f32[128,1024]{1,0:T(8,128)S(1)}, f32[128,1024]{1,0:T(8,128)S(1)}, u32[]{:S(2)}, u32[]{:S(2)}) collective-permute-start(f32[128,1024]{1,0:T(8,128)S(1)} %copy-done.1), channel_id=1, source_target_pairs={{0,1},{1,2},{2,3},{3,4},{4,5},{5,6},{6,7},{7,8},{8,9},{9,10},{10,1... | collective-permute-start | bytes 1572872 | tf_op jit(solution)/shard_map/ppermute | solution.py:59
  22.0 31.3 %collective-permute-start.4 = (f32[128,1024]{1,0:T(8,128)S(1)}, f32[128,1024]{1,0:T(8,128)S(1)}, u32[]{:S(2)}, u32[]{:S(2)}) collective-permute-start(f32[128,1024]{1,0:T(8,128)S(1)} %copy-done.1), channel_id=1, source_target_pairs={{1,0},{2,1},{3,2},{4,3},{5,4},{6,5},{7,6},{8,7},{9,8},{10,9},{11,1... | collective-permute-start | bytes 1572872 | tf_op jit(solution)/shard_map/ppermute | solution.py:59
  42.6 24.2 %collective-permute-start.2 = (f32[256,1024]{1,0:T(8,128)}, f32[256,1024]{1,0:T(8,128)}, u32[]{:S(2)}, u32[]{:S(2)}) collective-permute-start(f32[256,1024]{1,0:T(8,128)} %shard_map.148.after_a.ic0), channel_id=1, source_target_pairs={{0,8},{8,0},{1,9},{9,1},{2,10},{10,2},{3,11},{11,3},{4,12},{12,4},... | collective-permute-start | bytes 3145736 | tf_op jit(solution)/shard_map/ppermute | solution.py:53
  53.3 0.8 copy-start.7
  53.3 1.0 copy-start.8
  54.3 4.6 %copy-start.20 = (f32[8,64,128]{2,1,0:T(8,128)S(1)}, f32[8,64,128]{2,1,0:T(8,128)}, u32[]{:S(2)}) copy-start(f32[8,64,128]{2,1,0:T(8,128)} %get-tuple-element.41) | copy-start | bytes 786436
  54.3 4.6 %copy-start = (f32[256,1024]{1,0:T(8,128)S(1)}, f32[256,1024]{1,0:T(8,128)}, u32[]{:S(2)}) copy-start(f32[256,1024]{1,0:T(8,128)} %own.3) | copy-start | bytes 3145732
  58.4 8.5 %collective-permute-start.5 = (f32[2,128,1024]{2,1,0:T(8,128)}, f32[2,128,1024]{2,1,0:T(8,128)S(1)}, u32[]{:S(2)}, u32[]{:S(2)}) collective-permute-start(f32[2,128,1024]{2,1,0:T(8,128)} %shard_map.149.if0), channel_id=1, source_target_pairs={{0,8},{8,0},{1,9},{9,1},{2,10},{10,2},{3,11},{11,3},{4,12},{12,4},... | collective-permute-start | bytes 3145736 | tf_op jit(solution)/shard_map/ppermute | solution.py:53
  58.4 8.4 %collective-permute-start = (f32[8,64,256]{2,1,0:T(8,128)}, f32[8,64,256]{2,1,0:T(8,128)S(1)}, u32[]{:S(2)}, u32[]{:S(2)}) collective-permute-start(f32[8,64,256]{2,1,0:T(8,128)} %get-tuple-element.39), channel_id=1, source_target_pairs={{0,8},{8,0},{1,9},{9,1},{2,10},{10,2},{3,11},{11,3},{4,12},{12,4},... | collective-permute-start | bytes 1572872 | tf_op jit(solution)/shard_map/ppermute | solution.py:53
  58.9 3.5 %collective-permute-start.1 = (f32[8,64,128]{2,1,0:T(8,128)S(1)}, f32[8,64,128]{2,1,0:T(8,128)S(1)}, u32[]{:S(2)}, u32[]{:S(2)}) collective-permute-start(f32[8,64,128]{2,1,0:T(8,128)S(1)} %copy-done.20), channel_id=1, source_target_pairs={{0,8},{8,0},{1,9},{9,1},{2,10},{10,2},{3,11},{11,3},{4,12},{12,4},... | collective-permute-start | bytes 786440 | tf_op jit(solution)/shard_map/ppermute | solution.py:53
  59.1 19.9 %collective-permute-start.10 = (f32[128,1024]{1,0:T(8,128)S(1)}, f32[128,1024]{1,0:T(8,128)S(1)}, u32[]{:S(2)}, u32[]{:S(2)}) collective-permute-start(f32[128,1024]{1,0:T(8,128)S(1)} %get-tuple-element.71), channel_id=1, source_target_pairs={{1,0},{2,1},{3,2},{4,3},{5,4},{6,5},{7,6},{8,7},{9,8},{10,9},{11,1... | collective-permute-start | bytes 1572872 | tf_op jit(solution)/shard_map/ppermute | solution.py:59
  62.4 4.5 %copy-start.21 = (f32[8,64,128]{2,1,0:T(8,128)}, f32[8,64,128]{2,1,0:T(8,128)S(1)}, u32[]{:S(2)}) copy-start(f32[8,64,128]{2,1,0:T(8,128)S(1)} %collective-permute-done.1.lf1) | copy-start | bytes 786436
  62.4 25.0 %collective-permute-start.9 = (f32[128,1024]{1,0:T(8,128)S(1)}, f32[128,1024]{1,0:T(8,128)S(1)}, u32[]{:S(2)}, u32[]{:S(2)}) collective-permute-start(f32[128,1024]{1,0:T(8,128)S(1)} %get-tuple-element.72), channel_id=1, source_target_pairs={{0,1},{1,2},{2,3},{3,4},{4,5},{5,6},{6,7},{7,8},{8,9},{9,10},{10,1... | collective-permute-start | bytes 1572872 | tf_op jit(solution)/shard_map/ppermute | solution.py:59
  66.8 0.8 copy-start.19
  66.9 1.1 copy-start.18
  78.9 8.5 %copy-start.9 = (f32[128,1024]{1,0:T(8,128)}, f32[128,1024]{1,0:T(8,128)S(1)}, u32[]{:S(2)}) copy-start(f32[128,1024]{1,0:T(8,128)S(1)} %collective-permute-done.10.hi) | copy-start | bytes 1572868
  87.4 0.8 copy-start.10
  94.2 7.3 %collective-permute-start.11 = (f32[2,256,1024]{2,1,0:T(8,128)}, f32[2,256,1024]{2,1,0:T(8,128)S(1)}, u32[]{:S(2)}, u32[]{:S(2)}) collective-permute-start(f32[2,256,1024]{2,1,0:T(8,128)} %shard_map.151.is0), channel_id=1, source_target_pairs={{0,8},{8,0},{1,9},{9,1},{2,10},{10,2},{3,11},{11,3},{4,12},{12,4},... | collective-permute-start | bytes 6291464 | tf_op jit(solution)/shard_map/ppermute | solution.py:53
  94.2 21.8 %collective-permute-start.6 = (f32[3,2,32,1024]{3,2,1,0:T(8,128)}, f32[3,2,32,1024]{3,2,1,0:T(8,128)S(1)}, u32[]{:S(2)}, u32[]{:S(2)}) collective-permute-start(f32[3,2,32,1024]{3,2,1,0:T(8,128)} %get-tuple-element.43), channel_id=1, source_target_pairs={{0,16},{16,32},{32,48},{48,0},{1,17},{17,33},{33,49},{49,1},{2,18}... | collective-permute-start | bytes 2359304 | tf_op jit(solution)/shard_map/ppermute | solution.py:53
  96.7 37.8 %collective-permute-start.7 = (f32[3,2,32,1024]{3,2,1,0:T(8,128)}, f32[3,2,32,1024]{3,2,1,0:T(8,128)S(1)}, u32[]{:S(2)}, u32[]{:S(2)}) collective-permute-start(f32[3,2,32,1024]{3,2,1,0:T(8,128)} %get-tuple-element.44), channel_id=1, source_target_pairs={{0,32},{16,48},{32,0},{48,16},{1,33},{17,49},{33,1},{49,17},{2,34}... | collective-permute-start | bytes 2359304 | tf_op jit(solution)/shard_map/ppermute | solution.py:53
  99.0 36.7 %collective-permute-start.8 = (f32[3,2,32,1024]{3,2,1,0:T(8,128)}, f32[3,2,32,1024]{3,2,1,0:T(8,128)S(1)}, u32[]{:S(2)}, u32[]{:S(2)}) collective-permute-start(f32[3,2,32,1024]{3,2,1,0:T(8,128)} %get-tuple-element.45), channel_id=1, source_target_pairs={{0,48},{16,0},{32,16},{48,32},{1,49},{17,1},{33,17},{49,33},{2,50}... | collective-permute-start | bytes 2359304 | tf_op jit(solution)/shard_map/ppermute | solution.py:53
  100.8 35.7 %collective-permute-start.18 = (f32[3,8,32,256]{3,2,1,0:T(8,128)}, f32[3,8,32,256]{3,2,1,0:T(8,128)S(1)}, u32[]{:S(2)}, u32[]{:S(2)}) collective-permute-start(f32[3,8,32,256]{3,2,1,0:T(8,128)} %get-tuple-element.55), channel_id=1, source_target_pairs={{0,2},{2,4},{4,6},{6,0},{1,3},{3,5},{5,7},{7,1},{8,10},{10,12},{12... | collective-permute-start | bytes 2359304 | tf_op jit(solution)/shard_map/ppermute | solution.py:53
  101.5 1.4 copy-start.17
  102.9 61.4 %collective-permute-start.19 = (f32[3,8,32,256]{3,2,1,0:T(8,128)}, f32[3,8,32,256]{3,2,1,0:T(8,128)S(1)}, u32[]{:S(2)}, u32[]{:S(2)}) collective-permute-start(f32[3,8,32,256]{3,2,1,0:T(8,128)} %get-tuple-element.56), channel_id=1, source_target_pairs={{0,4},{2,6},{4,0},{6,2},{1,5},{3,7},{5,1},{7,3},{8,12},{10,14},{12... | collective-permute-start | bytes 2359304 | tf_op jit(solution)/shard_map/ppermute | solution.py:53
  116.0 44.3 %copy-start.4 = (f32[3,2,32,1024]{3,2,1,0:T(8,128)}, f32[3,2,32,1024]{3,2,1,0:T(8,128)S(1)}, u32[]{:S(2)}) copy-start(f32[3,2,32,1024]{3,2,1,0:T(8,128)S(1)} %collective-permute-done.6.a1) | copy-start | bytes 2359300
  116.0 29.8 %collective-permute-start.12 = (f32[2,2,32,1024]{3,2,1,0:T(8,128)}, f32[2,2,32,1024]{3,2,1,0:T(8,128)}, u32[]{:S(2)}, u32[]{:S(2)}) collective-permute-start(f32[2,2,32,1024]{3,2,1,0:T(8,128)} %get-tuple-element.47), channel_id=1, source_target_pairs={{0,16},{16,32},{32,48},{48,0},{1,17},{17,33},{33,49},{49,1},{2,18}... | collective-permute-start | bytes 1572872 | tf_op jit(solution)/shard_map/ppermute | solution.py:53
  134.5 25.8 %copy-start.5 = (f32[3,2,32,1024]{3,2,1,0:T(8,128)}, f32[3,2,32,1024]{3,2,1,0:T(8,128)S(1)}, u32[]{:S(2)}) copy-start(f32[3,2,32,1024]{3,2,1,0:T(8,128)S(1)} %collective-permute-done.7.a2) | copy-start | bytes 2359300
  134.5 22.1 %collective-permute-start.13 = (f32[2,2,32,1024]{3,2,1,0:T(8,128)}, f32[2,2,32,1024]{3,2,1,0:T(8,128)}, u32[]{:S(2)}, u32[]{:S(2)}) collective-permute-start(f32[2,2,32,1024]{3,2,1,0:T(8,128)} %get-tuple-element.48), channel_id=1, source_target_pairs={{0,32},{16,48},{32,0},{48,16},{1,33},{17,49},{33,1},{49,17},{2,34}... | collective-permute-start | bytes 1572872 | tf_op jit(solution)/shard_map/ppermute | solution.py:53
  135.7 24.6 %copy-start.6 = (f32[3,2,32,1024]{3,2,1,0:T(8,128)}, f32[3,2,32,1024]{3,2,1,0:T(8,128)S(1)}, u32[]{:S(2)}) copy-start(f32[3,2,32,1024]{3,2,1,0:T(8,128)S(1)} %collective-permute-done.8.a3) | copy-start | bytes 2359300
  135.7 23.1 %collective-permute-start.14 = (f32[2,2,32,1024]{3,2,1,0:T(8,128)}, f32[2,2,32,1024]{3,2,1,0:T(8,128)}, u32[]{:S(2)}, u32[]{:S(2)}) collective-permute-start(f32[2,2,32,1024]{3,2,1,0:T(8,128)} %get-tuple-element.49), channel_id=1, source_target_pairs={{0,48},{16,0},{32,16},{48,32},{1,49},{17,1},{33,17},{49,33},{2,50}... | collective-permute-start | bytes 1572872 | tf_op jit(solution)/shard_map/ppermute | solution.py:53
  136.6 27.7 %copy-start.2 = (f32[3,8,32,256]{3,2,1,0:T(8,128)}, f32[3,8,32,256]{3,2,1,0:T(8,128)S(1)}, u32[]{:S(2)}) copy-start(f32[3,8,32,256]{3,2,1,0:T(8,128)S(1)} %collective-permute-done.18.a1) | copy-start | bytes 2359300
  136.6 28.3 %collective-permute-start.20 = (f32[3,8,32,256]{3,2,1,0:T(8,128)}, f32[3,8,32,256]{3,2,1,0:T(8,128)}, u32[]{:S(2)}, u32[]{:S(2)}) collective-permute-start(f32[3,8,32,256]{3,2,1,0:T(8,128)} %get-tuple-element.57), channel_id=1, source_target_pairs={{0,6},{2,0},{4,2},{6,4},{1,7},{3,1},{5,3},{7,5},{8,14},{10,8},{12,... | collective-permute-start | bytes 2359304 | tf_op jit(solution)/shard_map/ppermute | solution.py:53
  145.8 20.5 %collective-permute-start.21 = (f32[2,8,32,256]{3,2,1,0:T(8,128)}, f32[2,8,32,256]{3,2,1,0:T(8,128)}, u32[]{:S(2)}, u32[]{:S(2)}) collective-permute-start(f32[2,8,32,256]{3,2,1,0:T(8,128)} %get-tuple-element.59), channel_id=1, source_target_pairs={{0,2},{2,4},{4,6},{6,0},{1,3},{3,5},{5,7},{7,1},{8,10},{10,12},{12... | collective-permute-start | bytes 1572872 | tf_op jit(solution)/shard_map/ppermute | solution.py:53
  156.6 16.7 %collective-permute-start.22 = (f32[2,8,32,256]{3,2,1,0:T(8,128)}, f32[2,8,32,256]{3,2,1,0:T(8,128)}, u32[]{:S(2)}, u32[]{:S(2)}) collective-permute-start(f32[2,8,32,256]{3,2,1,0:T(8,128)} %get-tuple-element.60), channel_id=1, source_target_pairs={{0,4},{2,6},{4,0},{6,2},{1,5},{3,7},{5,1},{7,3},{8,12},{10,14},{12... | collective-permute-start | bytes 1572872 | tf_op jit(solution)/shard_map/ppermute | solution.py:53
  158.8 25.1 %collective-permute-start.23 = (f32[2,8,32,256]{3,2,1,0:T(8,128)}, f32[2,8,32,256]{3,2,1,0:T(8,128)}, u32[]{:S(2)}, u32[]{:S(2)}) collective-permute-start(f32[2,8,32,256]{3,2,1,0:T(8,128)} %get-tuple-element.61), channel_id=1, source_target_pairs={{0,6},{2,0},{4,2},{6,4},{1,7},{3,1},{5,3},{7,5},{8,14},{10,8},{12,... | collective-permute-start | bytes 1572872 | tf_op jit(solution)/shard_map/ppermute | solution.py:53
  164.2 19.7 %copy-start.3 = (f32[3,8,32,256]{3,2,1,0:T(8,128)}, f32[3,8,32,256]{3,2,1,0:T(8,128)S(1)}, u32[]{:S(2)}) copy-start(f32[3,8,32,256]{3,2,1,0:T(8,128)S(1)} %collective-permute-done.19.a2) | copy-start | bytes 2359300
  164.2 26.5 %collective-permute-start.15 = (f32[5,2,32,256]{3,2,1,0:T(8,128)}, f32[5,2,32,256]{3,2,1,0:T(8,128)S(1)}, u32[]{:S(2)}, u32[]{:S(2)}) collective-permute-start(f32[5,2,32,256]{3,2,1,0:T(8,128)} %get-tuple-element.51), channel_id=1, source_target_pairs={{0,2},{2,4},{4,6},{6,0},{1,3},{3,5},{5,7},{7,1},{8,10},{10,12},{12... | collective-permute-start | bytes 983048 | tf_op jit(solution)/shard_map/ppermute | solution.py:53
  164.9 26.7 %collective-permute-start.16 = (f32[5,2,32,256]{3,2,1,0:T(8,128)}, f32[5,2,32,256]{3,2,1,0:T(8,128)S(1)}, u32[]{:S(2)}, u32[]{:S(2)}) collective-permute-start(f32[5,2,32,256]{3,2,1,0:T(8,128)} %get-tuple-element.52), channel_id=1, source_target_pairs={{0,4},{2,6},{4,0},{6,2},{1,5},{3,7},{5,1},{7,3},{8,12},{10,14},{12... | collective-permute-start | bytes 983048 | tf_op jit(solution)/shard_map/ppermute | solution.py:53
  166.2 30.4 %collective-permute-start.17 = (f32[5,2,32,256]{3,2,1,0:T(8,128)}, f32[5,2,32,256]{3,2,1,0:T(8,128)S(1)}, u32[]{:S(2)}, u32[]{:S(2)}) collective-permute-start(f32[5,2,32,256]{3,2,1,0:T(8,128)} %get-tuple-element.53), channel_id=1, source_target_pairs={{0,6},{2,0},{4,2},{6,4},{1,7},{3,1},{5,3},{7,5},{8,14},{10,8},{12,... | collective-permute-start | bytes 983048 | tf_op jit(solution)/shard_map/ppermute | solution.py:53
  187.8 16.4 %collective-permute-start.24 = (f32[5,2,32,256]{3,2,1,0:T(8,128)}, f32[5,2,32,256]{3,2,1,0:T(8,128)S(1)}, u32[]{:S(2)}, u32[]{:S(2)}) collective-permute-start(f32[5,2,32,256]{3,2,1,0:T(8,128)} %get-tuple-element.63), channel_id=1, source_target_pairs={{0,16},{16,32},{32,48},{48,0},{1,17},{17,33},{33,49},{49,1},{2,18}... | collective-permute-start | bytes 983048 | tf_op jit(solution)/shard_map/ppermute | solution.py:53
  187.8 16.4 %collective-permute-start.25 = (f32[5,2,32,256]{3,2,1,0:T(8,128)}, f32[5,2,32,256]{3,2,1,0:T(8,128)S(1)}, u32[]{:S(2)}, u32[]{:S(2)}) collective-permute-start(f32[5,2,32,256]{3,2,1,0:T(8,128)} %get-tuple-element.64), channel_id=1, source_target_pairs={{0,32},{16,48},{32,0},{48,16},{1,33},{17,49},{33,1},{49,17},{2,34}... | collective-permute-start | bytes 983048 | tf_op jit(solution)/shard_map/ppermute | solution.py:53
  190.8 14.1 %copy-start.11 = (f32[5,2,32,256]{3,2,1,0:T(8,128)}, f32[5,2,32,256]{3,2,1,0:T(8,128)S(1)}, u32[]{:S(2)}) copy-start(f32[5,2,32,256]{3,2,1,0:T(8,128)S(1)} %collective-permute-done.15.x1) | copy-start | bytes 983044
  190.8 14.1 %collective-permute-start.26 = (f32[5,2,32,256]{3,2,1,0:T(8,128)}, f32[5,2,32,256]{3,2,1,0:T(8,128)S(1)}, u32[]{:S(2)}, u32[]{:S(2)}) collective-permute-start(f32[5,2,32,256]{3,2,1,0:T(8,128)} %get-tuple-element.65), channel_id=1, source_target_pairs={{0,48},{16,0},{32,16},{48,32},{1,49},{17,1},{33,17},{49,33},{2,50}... | collective-permute-start | bytes 983048 | tf_op jit(solution)/shard_map/ppermute | solution.py:53
  191.6 13.3 %copy-start.12 = (f32[5,2,32,256]{3,2,1,0:T(8,128)}, f32[5,2,32,256]{3,2,1,0:T(8,128)S(1)}, u32[]{:S(2)}) copy-start(f32[5,2,32,256]{3,2,1,0:T(8,128)S(1)} %collective-permute-done.16.x2) | copy-start | bytes 983044
  196.6 8.3 %copy-start.13 = (f32[5,2,32,256]{3,2,1,0:T(8,128)}, f32[5,2,32,256]{3,2,1,0:T(8,128)S(1)}, u32[]{:S(2)}) copy-start(f32[5,2,32,256]{3,2,1,0:T(8,128)S(1)} %collective-permute-done.17.x3) | copy-start | bytes 983044
  204.2 0.7 copy-start.14
  204.2 0.9 copy-start.15
  204.8 0.7 copy-start.16
where the time goes:
time: 227 us; the launch traced here: 225 us
  waiting for transfers between devices  99.8 us (44%)
  starting transfers between devices  50.4 us (22%)
  Pallas kernels  47.3 us (21%)
  blocking collectives  14.5 us (6%)
  local copies, waits for them, and re-layouts  11.1 us (5%)
    ppermute x23, waiting for transfers between devices, shifted(): lax.ppermute(value, axis, [(i, (i + by) % size) for i in range(size)])  67.4 us
    ppermute x23, starting transfers between devices, shifted(): lax.ppermute(value, axis, [(i, (i + by) % size) for i in range(size)])  29.2 us
    ppermute x4, waiting for transfers between devices, from_behind(): return lax.ppermute(value, AXES, pairs)  21.2 us
    pallas_call x2, Pallas kernels, partial_sums(): return run(place, *lefts, *operands)  16.3 us
    all_to_all x1, blocking collectives, compute(): arrived = lax.all_to_all(blocks, Z, split_axis=0, concat_axis=0, tiled=True)  14.5 us
    all_to_all x1, waiting for transfers between devices, compute(): lax.all_to_all(outgoing, AXES, split_axis=0, concat_axis=0, tiled=True)  11.2 us
    all_to_all x1, starting transfers between devices, compute(): lax.all_to_all(outgoing, AXES, split_axis=0, concat_axis=0, tiled=True)  11.2 us
    ppermute x4, starting transfers between devices, from_behind(): return lax.ppermute(value, AXES, pairs)  10 us
  transfers between devices with their start and end apart: 28, of which 14 were waited for; matrix products, arithmetic and copies ran while one was open for 0% of the time, Pallas kernels for 15%

commit v1 on v0

--- a/solution.py
+++ b/solution.py
@@ -117,7 +117,7 @@
     return acc
 
 
-def fluid_kernel(cols, stiff, mass, lo, own, hi, after_a, after_b, out, total):
+def fluid_kernel(cols, stiff, mass, lo, own, hi, after, out, total):
     gathered(stiff, cols, total, 0)
     gathered(mass, cols, total, TILE)
     out[...] = image(total, (lo[...], own[...], hi[...])).reshape(out.shape)
@@ -175,10 +175,8 @@
     send_off(place, held, outs)
 
 
-def split_kernel(axis, place, a0, a1, a2, a3, b0, b1, b2, b3, o0, o1, o2, o3, held):
-    n = a0.shape[0]
-    held[:n] = (a0[...] + a1[...]) + (a2[...] + a3[...])
-    held[n:] = (b0[...] + b1[...]) + (b2[...] + b3[...])
+def split_kernel(axis, place, a0, a1, a2, a3, o0, o1, o2, o3, held):
+    held[...] = (a0[...] + a1[...]) + (a2[...] + a3[...])
     for o, out in enumerate((o0, o1, o2, o3)):
         d = lax.rem(place[axis] + o, 4)
         if axis == 1:
@@ -188,14 +186,20 @@
                 out[:, h] = held[:, h * 4 + d]
 
 
-def spread_kernel(x0, x1, x2, x3, y0, y1, y2, y3, out):
-    for h in range(2):
-        top = (x0[:, h] + x1[:, h]) + (x2[:, h] + x3[:, h])
-        low = (y0[:, h] + y1[:, h]) + (y2[:, h] + y3[:, h])
-        for l in range(2):
-            lanes = slice(l * 128, (l + 1) * 128)
-            out[h * 2 + l, :, 0:HALF] = top[..., lanes]
-            out[h * 2 + l, :, HALF:] = low[..., lanes]
+def spread_kernel(*refs):
+    ins, out = refs[:16], refs[16]
+    at = 0
+    for group in range(2):
+        x, y = ins[group * 8 : group * 8 + 4], ins[group * 8 + 4 : group * 8 + 8]
+        n = x[0].shape[0]
+        for h in range(2):
+            top = (x[0][:, h] + x[1][:, h]) + (x[2][:, h] + x[3][:, h])
+            low = (y[0][:, h] + y[1][:, h]) + (y[2][:, h] + y[3][:, h])
+            for l in range(2):
+                lanes = slice(l * 128, (l + 1) * 128)
+                out[h * 2 + l, at : at + n, 0:HALF] = top[..., lanes]
+                out[h * 2 + l, at : at + n, HALF:] = low[..., lanes]
+        at += n
 
 
 def last_kernel(arrived, *outs):
@@ -220,18 +224,18 @@
     return [slots[0]] + [shifted(slots[o], axis, o) for o in range(1, 4)]
 
 
-def split(place, one, two, axis):
-    dims = (one[0].shape[0] + two[0].shape[0],) + one[0].shape[1:]
-    size = one[0].size + two[0].size
+def split(place, arrived, axis):
+    count = arrived[0].shape[0]
+    size = arrived[0].size
     return call(
         functools.partial(split_kernel, axis),
-        [shape(5, 2, HALF, 256)] * 4,
-        9,
+        [shape(count, 2, HALF, 256)] * 4,
+        5,
         smem=1,
-        scratch=[pltpu.VMEM(dims, F32)],
+        scratch=[pltpu.VMEM(arrived[0].shape, F32)],
         flops=3 * size,
         moved=20 * size,
-    )(place, *one, *two)
+    )(place, *arrived)
 
 
 def partial_sums(kernel, count, place, lefts, steps, operands, specs, scratch):
@@ -295,13 +299,13 @@
     image_f = call(
         fluid_kernel,
         shape(2, 128, R),
-        8,
+        7,
         smem=1,
-        anywhere=2,
+        anywhere=1,
         scratch=[pltpu.VMEM((3, 256, TILE), F32)],
         flops=6 * 256 * 384 * R,
         moved=3 * 2**20,
-    )(fluid_cols, fluid_stiff_tiles, fluid_mass_tiles, below_f, fluid_basis, above_f, image_c, own_s)
+    )(fluid_cols, fluid_stiff_tiles, fluid_mass_tiles, below_f, fluid_basis, above_f, own_s)
     other_f = shifted(image_f, "core", 1)
 
     fblock = pl.BlockSpec((1, 128, R), lambda m: (jnp.maximum(m - 1, 0), 0, 0))
@@ -336,9 +340,13 @@
     second_x = exchanged(second[0:4], X)
     second_y = exchanged(second[4:8], Y)
 
-    then_y = exchanged(split(place, first_x, second_x, 1), Y)
-    then_x = exchanged(split(place, first_y, second_y, 0), X)
-    blocks = call(spread_kernel, shape(4, 5, 64, 128), 8, flops=2**20, moved=2**22)(*then_y, *then_x)
+    first_xy = exchanged(split(place, first_x, 1), Y)
+    first_yx = exchanged(split(place, first_y, 0), X)
+    second_xy = exchanged(split(place, second_x, 1), Y)
+    second_yx = exchanged(split(place, second_y, 0), X)
+    blocks = call(spread_kernel, shape(4, 5, 64, 128), 16, flops=2**20, moved=2**22)(
+        *first_xy, *first_yx, *second_xy, *second_yx
+    )
     arrived = lax.all_to_all(blocks, Z, split_axis=0, concat_axis=0, tiled=True)
     wet, fstiff, fmass, stiff, mass = call(last_kernel, [shape(64, 128)] * 5, 1, flops=2**18, moved=2**20)(arrived)
     return stiff, mass, fstiff, fmass, wet

time: 227 us -> 227 us (level)
  waiting for transfers between devices: 99.8 us -> 92.3 us
  starting transfers between devices: 50.4 us -> 55.5 us
  Pallas kernels: 47.3 us -> 50.8 us
    ppermute x4, waiting for transfers between devices: 21.2 us -> 37.2 us  [from_behind(): return lax.ppermute(value, AXES, pairs)]
    ppermute x23 -> x29, waiting for transfers between devices: 67.4 us -> 55 us  [shifted(): lax.ppermute(value, axis, [(i, (i + by) % size) for i in range(size)])]
    all_to_all x1, waiting for transfers between devices: 11.2 us -> 0.01 us  [compute(): lax.all_to_all(outgoing, AXES, split_axis=0, concat_axis=0, tiled=True)]
    ppermute x23 -> x29, starting transfers between devices: 29.2 us -> 34.3 us  [shifted(): lax.ppermute(value, axis, [(i, (i + by) % size) for i in range(size)])]
    pallas_call x4 -> x6, Pallas kernels: 14.6 us -> 17.9 us  [the longest x4 11.2 us: split(): call(functools.partial(split_kernel, axis), [shape(count, 2, HALF, 256)]...]
    unnamed x45 -> x67, local copies, waits for them, and re-layouts: 6.44 us -> 7.73 us
  transfers between devices with their start and end apart: 28 -> 34, of which waited for: 14 -> 15; matrix products, arithmetic and copies ran while one was open for 0% -> 0% of each run, Pallas kernels for 15% -> 17%
where the time goes in v1:
time: 227 us; the launch traced here: 226 us
  waiting for transfers between devices  92.3 us (41%)
  starting transfers between devices  55.5 us (24%)
  Pallas kernels  50.8 us (22%)
  blocking collectives  13.4 us (6%)
  local copies, waits for them, and re-layouts  12.4 us (5%)
    ppermute x29, waiting for transfers between devices, shifted(): lax.ppermute(value, axis, [(i, (i + by) % size) for i in range(size)])  55 us
    ppermute x4, waiting for transfers between devices, from_behind(): return lax.ppermute(value, AXES, pairs)  37.2 us
    ppermute x29, starting transfers between devices, shifted(): lax.ppermute(value, axis, [(i, (i + by) % size) for i in range(size)])  34.3 us
    pallas_call x2, Pallas kernels, partial_sums(): return run(place, *lefts, *operands)  16.4 us
    all_to_all x1, blocking collectives, compute(): arrived = lax.all_to_all(blocks, Z, split_axis=0, concat_axis=0, tiled=True)  13.4 us
    all_to_all x1, starting transfers between devices, compute(): lax.all_to_all(outgoing, AXES, split_axis=0, concat_axis=0, tiled=True)  11.2 us
    pallas_call x4, Pallas kernels, split(): call(functools.partial(split_kernel, axis), [shape(count, 2, HALF, 256)]...  11.2 us
    ppermute x4, starting transfers between devices, from_behind(): return lax.ppermute(value, AXES, pairs)  10 us
  transfers between devices with their start and end apart: 34, of which 15 were waited for; matrix products, arithmetic and copies ran while one was open for 0% of the time, Pallas kernels for 17%

profile of v1, /device:TPU:0, one launch (start us, length us, event | category | flops | bytes accessed | tf_op | source)
XLA Modules:
  0.0 225.9 jit_solution(8274257523653552591)
XLA Ops:
  0.6 1.4 copy.16.dest_col
  2.0 2.9 %shard_map.147 = f32[256,1024]{1,0:T(8,128)} custom-call(s32[128,1]{1,0:T(8,128)} %copy.16.dest_col, s32[1,128]{1,0:T(1,128)} %bitcast.6, s32[1,128]{1,0:T(1,128)} %bitcast.7, f32[128,1024]{1,0:T(8,128)} %own.2), custom_call_target="tpu_custom_call" | custom-call | flops 201326592 | bytes 2097152 | tf_op jit(solution)/shard_map/pallas_call | solution.py:279
  4.9 2.9 %all_to_all.10 = f32[128,2,1024]{2,1,0:T(2,128)} reshape(f32[256,1024]{1,0:T(8,128)} %shard_map.147) | data formatting | bytes 2097152 | tf_op jit(solution)/shard_map/all_to_all | solution.py:282
  7.8 11.2 %all-to-all-start = ((f32[128,2,1024]{2,1,0:T(2,128)}), f32[128,2,1024]{2,1,0:T(2,128)S(1)}, u32[]{:S(2)}, u32[]{:S(2)}) async-start(f32[128,2,1024]{2,1,0:T(2,128)} %all_to_all.10), calls=%async_computation | async-start | bytes 2097152 | tf_op jit(solution)/shard_map/all_to_all | solution.py:282
  19.0 3.0 %collective-permute-start.3 = (f32[128,1024]{1,0:T(8,128)S(1)}, f32[128,1024]{1,0:T(8,128)S(1)}, u32[]{:S(2)}, u32[]{:S(2)}) collective-permute-start(f32[128,1024]{1,0:T(8,128)S(1)} %copy-done.1), channel_id=1, source_target_pairs={{0,1},{1,2},{2,3},{3,4},{4,5},{5,6},{6,7},{7,8},{8,9},{9,10},{10,1... | collective-permute-start | bytes 1572872 | tf_op jit(solution)/shard_map/ppermute | solution.py:59
  22.0 1.3 collective-permute-start.4
  23.3 0.6 pad_add_fusion.place
  23.9 3.0 %shard_map.146 = (f32[8,64,256]{2,1,0:T(8,128)}, f32[8,64,256]{2,1,0:T(8,128)}, f32[8,64,128]{2,1,0:T(8,128)}, f32[8,64,128]{2,1,0:T(8,128)}) custom-call(s32[4]{0:T(128)} %pad_add_fusion.place, f32[256,1024]{1,0:T(8,128)} %own.3, f32[128,1024]{1,0:T(8,128)} %own.2), custom_call_target="tpu_custom_call" | custom-call | flops 1048576 | bytes 3145728 | tf_op jit(solution)/shard_map/pallas_call | solution.py:284
  26.9 26.4 %collective-permute-done.3.lo = f32[128,1024]{1,0:T(8,128)S(1)} collective-permute-done((f32[128,1024]{1,0:T(8,128)S(1)}, f32[128,1024]{1,0:T(8,128)S(1)}, u32[]{:S(2)}, u32[]{:S(2)}) %collective-permute-start.3) | collective-permute-done | bytes 524320 | tf_op jit(solution)/shard_map/ppermute | solution.py:59
  53.3 0.8 copy-done.12
  54.3 4.0 %shard_map.149.if0 = f32[2,128,1024]{2,1,0:T(8,128)} custom-call(s32[1,4]{1,0:T(1,128)} %cols.2, f32[1,4,128,128]{3,2,1,0:T(8,128)} %stiff.2, f32[1,4,128,128]{3,2,1,0:T(8,128)} %mass.2, f32[128,1024]{1,0:T(8,128)} %copy-done.12, f32[128,1024]{1,0:T(8,128)} %own.2, f32[128,1024]{1,0:T(8,128)} %copy-done.13, f32[8,64,256]{2,1,0:T(8,128)} %get-tuple-element.46.after.ls0), custom_call_target="tpu_custom_call" | custom-call | flops 603979776 | bytes 3145728 | tf_op jit(solution)/shard_map/pallas_call | solution.py:299
  58.3 1.7 all_to_all.12.received
  60.0 2.9 %shard_map.148.ic0 = f32[256,1024]{1,0:T(8,128)} custom-call(f32[256,256]{1,0:T(8,128)} %coupling.1, f32[256,1024]{1,0:T(8,128)} %all_to_all.12.received), custom_call_target="tpu_custom_call" | custom-call | flops 402653184 | bytes 2097152 | tf_op jit(solution)/shard_map/pallas_call | solution.py:296
  62.9 0.5 collective-permute-start.2
  63.4 0.5 collective-permute-start.1
  64.0 4.4 %collective-permute-start.18 = (f32[128,1024]{1,0:T(8,128)S(1)}, f32[128,1024]{1,0:T(8,128)S(1)}, u32[]{:S(2)}, u32[]{:S(2)}) collective-permute-start(f32[128,1024]{1,0:T(8,128)S(1)} %get-tuple-element.88), channel_id=1, source_target_pairs={{0,1},{1,2},{2,3},{3,4},{4,5},{5,6},{6,7},{7,8},{8,9},{9,10},{10,1... | collective-permute-start | bytes 1572872 | tf_op jit(solution)/shard_map/ppermute | solution.py:59
  68.4 0.7 copy-done.30
  69.1 1.3 collective-permute-start.19
  70.5 0.8 copy-done.28
  71.2 8.9 %shard_map.150 = (f32[3,2,32,1024]{3,2,1,0:T(8,128)}, f32[3,2,32,1024]{3,2,1,0:T(8,128)}, f32[3,2,32,1024]{3,2,1,0:T(8,128)}, f32[3,2,32,1024]{3,2,1,0:T(8,128)}...) custom-call(s32[4]{0:T(128)} %pad_add_fusion.place, ...), custom_call_target="tpu_custom_call" | custom-call | flops 3221225472 | bytes 12582912 | tf_op jit(solution)/shard_map/pallas_call | solution.py:255
  80.2 10.8 %collective-permute-done.18.lo = f32[128,1024]{1,0:T(8,128)S(1)} collective-permute-done((f32[128,1024]{1,0:T(8,128)S(1)}, f32[128,1024]{1,0:T(8,128)S(1)}, u32[]{:S(2)}, u32[]{:S(2)}) %collective-permute-start.18) | collective-permute-done | bytes 524320 | tf_op jit(solution)/shard_map/ppermute | solution.py:59
  91.0 0.8 copy-done.10
  92.0 6.0 %shard_map.153.is0 = f32[2,256,1024]{2,1,0:T(8,128)} custom-call(s32[2,4]{1,0:T(2,128)} %cols.3, f32[2,4,128,128]{3,2,1,0:T(8,128)} %stiff.3, f32[2,4,128,128]{3,2,1,0:T(8,128)} %mass.3, f32[128,1024]{1,0:T(8,128)} %copy-done.10, f32[256,1024]{1,0:T(8,128)} %own.3, f32[128,1024]{1,0:T(8,128)} %copy-done.11, f32[3,2,32,1024]{3,2,1,0:T(8,128)} %get-tuple-element.50.a0.after), custom_call_target="tpu_custom_call" | custom-call | flops 1610612736 | bytes 5242880 | tf_op jit(solution)/shard_map/pallas_call | solution.py:326
  98.0 5.8 %collective-permute-start.6 = (f32[3,2,32,1024]{3,2,1,0:T(8,128)S(1)}, f32[3,2,32,1024]{3,2,1,0:T(8,128)S(1)}, u32[]{:S(2)}, u32[]{:S(2)}) collective-permute-start(f32[3,2,32,1024]{3,2,1,0:T(8,128)S(1)} %copy-done.27), channel_id=1, source_target_pairs={{0,16},{16,32},{32,48},{48,0},{1,17},{17,33},{33,49},{49,1},{2,18}... | collective-permute-start | bytes 2359304 | tf_op jit(solution)/shard_map/ppermute | solution.py:53
  103.8 2.3 %collective-permute-start.7 = (f32[3,2,32,1024]{3,2,1,0:T(8,128)}, f32[3,2,32,1024]{3,2,1,0:T(8,128)S(1)}, u32[]{:S(2)}, u32[]{:S(2)}) collective-permute-start(f32[3,2,32,1024]{3,2,1,0:T(8,128)} %get-tuple-element.52), channel_id=1, source_target_pairs={{0,32},{16,48},{32,0},{48,16},{1,33},{17,49},{33,1},{49,17},{2,34}... | collective-permute-start | bytes 2359304 | tf_op jit(solution)/shard_map/ppermute | solution.py:53
  106.2 1.8 collective-permute-start.8
  108.0 14.9 %collective-permute-done.6.a1 = f32[3,2,32,1024]{3,2,1,0:T(8,128)S(1)} collective-permute-done((f32[3,2,32,1024]{3,2,1,0:T(8,128)S(1)}, f32[3,2,32,1024]{3,2,1,0:T(8,128)S(1)}, u32[]{:S(2)}, u32[]{:S(2)}) %collective-permute-start.6) | collective-permute-done | bytes 786464 | tf_op jit(solution)/shard_map/ppermute | solution.py:53
  122.8 1.2 collective-permute-start.13
  124.1 1.4 copy-done.26
  125.4 1.5 collective-permute-start.14
  126.9 7.4 %shard_map.154 = (f32[2,2,32,1024]{3,2,1,0:T(8,128)}, f32[2,2,32,1024]{3,2,1,0:T(8,128)}, f32[2,2,32,1024]{3,2,1,0:T(8,128)}, f32[2,2,32,1024]{3,2,1,0:T(8,128)}...) custom-call(s32[4]{0:T(128)} %pad_add_fusion.place, ...), custom_call_target="tpu_custom_call" | custom-call | flops 3221225472 | bytes 8388608 | tf_op jit(solution)/shard_map/pallas_call | solution.py:255
  134.3 6.5 %collective-permute-done.7.a2 = f32[3,2,32,1024]{3,2,1,0:T(8,128)S(1)} collective-permute-done((f32[3,2,32,1024]{3,2,1,0:T(8,128)}, f32[3,2,32,1024]{3,2,1,0:T(8,128)S(1)}, u32[]{:S(2)}, u32[]{:S(2)}) %collective-permute-start.7) | collective-permute-done | bytes 786464 | tf_op jit(solution)/shard_map/ppermute | solution.py:53
  140.9 0.9 copy-done.6
  141.8 3.1 %shard_map.151 = (f32[3,2,32,256]{3,2,1,0:T(8,128)}, f32[3,2,32,256]{3,2,1,0:T(8,128)}, f32[3,2,32,256]{3,2,1,0:T(8,128)}, f32[3,2,32,256]{3,2,1,0:T(8,128)}) custom-call(s32[4]{0:T(128)} %pad_add_fusion.place, f32[3,2,32,1024]{3,2,1,0:T(8,128)} %get-tuple-element.50.a0.after, f32[3,2,32,1024]{3,2,1,0:T(8,128)} %copy-done.5, f32[3,2,32,1024]{3,2,1,0:T(8,128)} %copy-done.6, ...), custom_call_target="tpu_custom_call" | custom-call | flops 589824 | bytes 3932160 | tf_op jit(solution)/shard_map/pallas_call | solution.py:230
  145.3 1.4 collective-permute-start.10
  146.7 2.1 collective-permute-start.22
  148.7 11.4 %collective-permute-done.14.a3 = f32[3,8,32,256]{3,2,1,0:T(8,128)S(1)} collective-permute-done((f32[3,8,32,256]{3,2,1,0:T(8,128)}, f32[3,8,32,256]{3,2,1,0:T(8,128)S(1)}, u32[]{:S(2)}, u32[]{:S(2)}) %collective-permute-start.14) | collective-permute-done | bytes 786464 | tf_op jit(solution)/shard_map/ppermute | solution.py:53
  160.2 1.7 collective-permute-start.23
  161.9 1.4 collective-permute-start.27
  163.3 2.7 %collective-permute-start.28 = (f32[2,8,32,256]{3,2,1,0:T(8,128)}, f32[2,8,32,256]{3,2,1,0:T(8,128)}, u32[]{:S(2)}, u32[]{:S(2)}) collective-permute-start(f32[2,8,32,256]{3,2,1,0:T(8,128)} %get-tuple-element.76), channel_id=1, source_target_pairs={{0,4},{2,6},{4,0},{6,2},{1,5},{3,7},{5,1},{7,3},{8,12},{10,14},{12... | collective-permute-start | bytes 1572872 | tf_op jit(solution)/shard_map/ppermute | solution.py:53
  165.9 1.0 collective-permute-done.21.a1
  167.4 3.0 %shard_map.152 = (f32[3,2,32,256]{3,2,1,0:T(8,128)}, f32[3,2,32,256]{3,2,1,0:T(8,128)}, f32[3,2,32,256]{3,2,1,0:T(8,128)}, f32[3,2,32,256]{3,2,1,0:T(8,128)}) custom-call(s32[4]{0:T(128)} %pad_add_fusion.place, f32[3,8,32,256]{3,2,1,0:T(8,128)} %get-tuple-element.58.a0, f32[3,8,32,256]{3,2,1,0:T(8,128)} %copy-done.2, f32[3,8,32,256]{3,2,1,0:T(8,128)} %copy-done.3, ...), custom_call_target="tpu_custom_call" | custom-call | flops 589824 | bytes 3932160 | tf_op jit(solution)/shard_map/pallas_call | solution.py:230
  170.4 0.6 collective-permute-start.11
  171.0 1.7 collective-permute-done.23.a3
  172.7 1.2 collective-permute-start.15
  173.9 2.6 %collective-permute-done.27.a1 = f32[2,8,32,256]{3,2,1,0:T(8,128)S(1)} collective-permute-done((f32[2,8,32,256]{3,2,1,0:T(8,128)}, f32[2,8,32,256]{3,2,1,0:T(8,128)S(1)}, u32[]{:S(2)}, u32[]{:S(2)}) %collective-permute-start.27) | collective-permute-done | bytes 524320 | tf_op jit(solution)/shard_map/ppermute | solution.py:53
  176.5 1.0 collective-permute-start.16
  177.6 11.3 %collective-permute-done.28.a2 = f32[2,8,32,256]{3,2,1,0:T(8,128)} collective-permute-done((f32[2,8,32,256]{3,2,1,0:T(8,128)}, f32[2,8,32,256]{3,2,1,0:T(8,128)}, u32[]{:S(2)}, u32[]{:S(2)}) %collective-permute-start.28) | collective-permute-done | bytes 524320 | tf_op jit(solution)/shard_map/ppermute | solution.py:53
  188.9 0.7 collective-permute-start.17
  189.6 2.5 %shard_map.155 = (f32[2,2,32,256]{3,2,1,0:T(8,128)}, f32[2,2,32,256]{3,2,1,0:T(8,128)}, f32[2,2,32,256]{3,2,1,0:T(8,128)}, f32[2,2,32,256]{3,2,1,0:T(8,128)}) custom-call(s32[4]{0:T(128)} %pad_add_fusion.place, f32[2,2,32,1024]{3,2,1,0:T(8,128)} %get-tuple-element.66.a0, f32[2,2,32,1024]{3,2,1,0:T(8,128)} %copy-done.7, f32[2,2,32,1024]{3,2,1,0:T(8,128)} %copy-done.9, ...), custom_call_target="tpu_custom_call" | custom-call | flops 393216 | bytes 2621440 | tf_op jit(solution)/shard_map/pallas_call | solution.py:230
  192.2 2.5 %shard_map.156 = (f32[2,2,32,256]{3,2,1,0:T(8,128)}, f32[2,2,32,256]{3,2,1,0:T(8,128)}, f32[2,2,32,256]{3,2,1,0:T(8,128)}, f32[2,2,32,256]{3,2,1,0:T(8,128)}) custom-call(s32[4]{0:T(128)} %pad_add_fusion.place, f32[2,8,32,256]{3,2,1,0:T(8,128)} %get-tuple-element.74.a0, f32[2,8,32,256]{3,2,1,0:T(8,128)} %copy-done.8, ...), custom_call_target="tpu_custom_call" | custom-call | flops 393216 | bytes 2621440 | tf_op jit(solution)/shard_map/pallas_call | solution.py:230
  194.7 1.2 collective-permute-start.25
  196.0 2.6 %collective-permute-start.26 = (f32[2,2,32,256]{3,2,1,0:T(8,128)S(1)}, f32[2,2,32,256]{3,2,1,0:T(8,128)S(1)}, u32[]{:S(2)}, u32[]{:S(2)}) collective-permute-start(f32[2,2,32,256]{3,2,1,0:T(8,128)S(1)} %copy-done.31), channel_id=1, source_target_pairs={{0,6},{2,0},{4,2},{6,4},{1,7},{3,1},{5,3},{7,5},{8,14},{10,8},{12,... | collective-permute-start | bytes 393224 | tf_op jit(solution)/shard_map/ppermute | solution.py:53
  198.6 1.1 collective-permute-start.30
  199.7 0.9 collective-permute-start.31
  200.6 0.7 collective-permute-done.24.refs_9_
  201.4 1.6 collective-permute-start.32
  203.3 1.8 collective-permute-done.30.refs_13_
  205.0 1.4 collective-permute-done.31.refs_14_
  206.4 0.9 collective-permute-done.32.refs_15_
  207.4 0.6 copy-done.25
  208.0 2.8 %shard_map.157 = f32[4,5,64,128]{3,2,1,0:T(8,128)} custom-call(f32[3,2,32,256]{3,2,1,0:T(8,128)} %get-tuple-element.54.refs_0_, f32[3,2,32,256]{3,2,1,0:T(8,128)} %copy-done.14, f32[3,2,32,256]{3,2,1,0:T(8,128)} %copy-done.15, f32[3,2,32,256]{3,2,1,0:T(8,128)} %copy-done.16, f32[3,2,32,256]{3,2,1,0:T(8,128)} %get-tuple-element.62.refs_4_, ...), custom_call_target="tpu_custom_call" | custom-call | flops 1048576 | bytes 4194304 | tf_op jit(solution)/shard_map/pallas_call | solution.py:347
  210.7 13.4 %all_to_all.16.arrived = f32[4,5,64,128]{3,2,1,0:T(8,128)} all-to-all(f32[4,5,64,128]{3,2,1,0:T(8,128)} %shard_map.157), channel_id=1, replica_groups=mesh['zhi'=2,'x'=4,'core'=2,'y'=4,'zlo'=2] {'zhi','zlo'}, dimensions={0} | all-to-all | bytes 1310720 | tf_op jit(solution)/shard_map/all_to_all | solution.py:350
  224.1 1.8 shard_map.158
  (89 shorter events, 1.9 us)
Async XLA Ops:
  4.9 14.1 %copy-start.1 = (f32[128,1024]{1,0:T(8,128)S(1)}, f32[128,1024]{1,0:T(8,128)}, u32[]{:S(2)}) copy-start(f32[128,1024]{1,0:T(8,128)} %own.2) | copy-start | bytes 1572868
  7.8 50.5 %all-to-all-start = ((f32[128,2,1024]{2,1,0:T(2,128)}), f32[128,2,1024]{2,1,0:T(2,128)S(1)}, u32[]{:S(2)}, u32[]{:S(2)}) async-start(f32[128,2,1024]{2,1,0:T(2,128)} %all_to_all.10), calls=%async_computation | async-start | bytes 2097152 | tf_op jit(solution)/shard_map/all_to_all | solution.py:282
  19.0 34.3 %collective-permute-start.3 = (f32[128,1024]{1,0:T(8,128)S(1)}, f32[128,1024]{1,0:T(8,128)S(1)}, u32[]{:S(2)}, u32[]{:S(2)}) collective-permute-start(f32[128,1024]{1,0:T(8,128)S(1)} %copy-done.1), channel_id=1, source_target_pairs={{0,1},{1,2},{2,3},{3,4},{4,5},{5,6},{6,7},{7,8},{8,9},{9,10},{10,1... | collective-permute-start | bytes 1572872 | tf_op jit(solution)/shard_map/ppermute | solution.py:59
  22.0 31.3 %collective-permute-start.4 = (f32[128,1024]{1,0:T(8,128)S(1)}, f32[128,1024]{1,0:T(8,128)S(1)}, u32[]{:S(2)}, u32[]{:S(2)}) collective-permute-start(f32[128,1024]{1,0:T(8,128)S(1)} %copy-done.1), channel_id=1, source_target_pairs={{1,0},{2,1},{3,2},{4,3},{5,4},{6,5},{7,6},{8,7},{9,8},{10,9},{11,1... | collective-permute-start | bytes 1572872 | tf_op jit(solution)/shard_map/ppermute | solution.py:59
  53.3 0.8 copy-start.12
  53.3 1.0 copy-start.13
  58.3 5.1 %copy-start.29 = (f32[8,64,128]{2,1,0:T(8,128)S(1)}, f32[8,64,128]{2,1,0:T(8,128)}, u32[]{:S(2)}) copy-start(f32[8,64,128]{2,1,0:T(8,128)} %get-tuple-element.49) | copy-start | bytes 786436
  58.3 5.6 %copy-start = (f32[256,1024]{1,0:T(8,128)S(1)}, f32[256,1024]{1,0:T(8,128)}, u32[]{:S(2)}) copy-start(f32[256,1024]{1,0:T(8,128)} %own.3) | copy-start | bytes 3145732
  58.3 12.2 %collective-permute-start.5 = (f32[2,128,1024]{2,1,0:T(8,128)}, f32[2,128,1024]{2,1,0:T(8,128)}, u32[]{:S(2)}, u32[]{:S(2)}) collective-permute-start(f32[2,128,1024]{2,1,0:T(8,128)} %shard_map.149.if0), channel_id=1, source_target_pairs={{0,8},{8,0},{1,9},{9,1},{2,10},{10,2},{3,11},{11,3},{4,12},{12,4},... | collective-permute-start | bytes 3145736 | tf_op jit(solution)/shard_map/ppermute | solution.py:53
  62.9 7.5 %collective-permute-start.2 = (f32[256,1024]{1,0:T(8,128)}, f32[256,1024]{1,0:T(8,128)}, u32[]{:S(2)}, u32[]{:S(2)}) collective-permute-start(f32[256,1024]{1,0:T(8,128)} %shard_map.148.ic0), channel_id=1, source_target_pairs={{0,8},{8,0},{1,9},{9,1},{2,10},{10,2},{3,11},{11,3},{4,12},{12,4},... | collective-permute-start | bytes 3145736 | tf_op jit(solution)/shard_map/ppermute | solution.py:53
  63.4 7.0 %collective-permute-start = (f32[8,64,256]{2,1,0:T(8,128)}, f32[8,64,256]{2,1,0:T(8,128)S(1)}, u32[]{:S(2)}, u32[]{:S(2)}) collective-permute-start(f32[8,64,256]{2,1,0:T(8,128)} %get-tuple-element.47), channel_id=1, source_target_pairs={{0,8},{8,0},{1,9},{9,1},{2,10},{10,2},{3,11},{11,3},{4,12},{12,4},... | collective-permute-start | bytes 1572872 | tf_op jit(solution)/shard_map/ppermute | solution.py:53
  63.4 5.0 %collective-permute-start.1 = (f32[8,64,128]{2,1,0:T(8,128)S(1)}, f32[8,64,128]{2,1,0:T(8,128)S(1)}, u32[]{:S(2)}, u32[]{:S(2)}) collective-permute-start(f32[8,64,128]{2,1,0:T(8,128)S(1)} %copy-done.29), channel_id=1, source_target_pairs={{0,8},{8,0},{1,9},{9,1},{2,10},{10,2},{3,11},{11,3},{4,12},{12,4},... | collective-permute-start | bytes 786440 | tf_op jit(solution)/shard_map/ppermute | solution.py:53
  64.0 27.0 %collective-permute-start.18 = (f32[128,1024]{1,0:T(8,128)S(1)}, f32[128,1024]{1,0:T(8,128)S(1)}, u32[]{:S(2)}, u32[]{:S(2)}) collective-permute-start(f32[128,1024]{1,0:T(8,128)S(1)} %get-tuple-element.88), channel_id=1, source_target_pairs={{0,1},{1,2},{2,3},{3,4},{4,5},{5,6},{6,7},{7,8},{8,9},{9,10},{10,1... | collective-permute-start | bytes 1572872 | tf_op jit(solution)/shard_map/ppermute | solution.py:59
  69.1 21.9 %collective-permute-start.19 = (f32[128,1024]{1,0:T(8,128)S(1)}, f32[128,1024]{1,0:T(8,128)S(1)}, u32[]{:S(2)}, u32[]{:S(2)}) collective-permute-start(f32[128,1024]{1,0:T(8,128)S(1)} %get-tuple-element.87), channel_id=1, source_target_pairs={{1,0},{2,1},{3,2},{4,3},{5,4},{6,5},{7,6},{8,7},{9,8},{10,9},{11,1... | collective-permute-start | bytes 1572872 | tf_op jit(solution)/shard_map/ppermute | solution.py:59
  91.0 0.8 copy-start.10
  91.0 1.0 copy-start.11
  92.0 6.0 %copy-start.27 = (f32[3,2,32,1024]{3,2,1,0:T(8,128)S(1)}, f32[3,2,32,1024]{3,2,1,0:T(8,128)}, u32[]{:S(2)}) copy-start(f32[3,2,32,1024]{3,2,1,0:T(8,128)} %get-tuple-element.51) | copy-start | bytes 2359300
  98.0 26.1 %collective-permute-start.20 = (f32[2,256,1024]{2,1,0:T(8,128)}, f32[2,256,1024]{2,1,0:T(8,128)S(1)}, u32[]{:S(2)}, u32[]{:S(2)}) collective-permute-start(f32[2,256,1024]{2,1,0:T(8,128)} %shard_map.153.is0), channel_id=1, source_target_pairs={{0,8},{8,0},{1,9},{9,1},{2,10},{10,2},{3,11},{11,3},{4,12},{12,4},... | collective-permute-start | bytes 6291464 | tf_op jit(solution)/shard_map/ppermute | solution.py:53
  98.0 24.9 %collective-permute-start.6 = (f32[3,2,32,1024]{3,2,1,0:T(8,128)S(1)}, f32[3,2,32,1024]{3,2,1,0:T(8,128)S(1)}, u32[]{:S(2)}, u32[]{:S(2)}) collective-permute-start(f32[3,2,32,1024]{3,2,1,0:T(8,128)S(1)} %copy-done.27), channel_id=1, source_target_pairs={{0,16},{16,32},{32,48},{48,0},{1,17},{17,33},{33,49},{49,1},{2,18}... | collective-permute-start | bytes 2359304 | tf_op jit(solution)/shard_map/ppermute | solution.py:53
  103.8 37.0 %collective-permute-start.7 = (f32[3,2,32,1024]{3,2,1,0:T(8,128)}, f32[3,2,32,1024]{3,2,1,0:T(8,128)S(1)}, u32[]{:S(2)}, u32[]{:S(2)}) collective-permute-start(f32[3,2,32,1024]{3,2,1,0:T(8,128)} %get-tuple-element.52), channel_id=1, source_target_pairs={{0,32},{16,48},{32,0},{48,16},{1,33},{17,49},{33,1},{49,17},{2,34}... | collective-permute-start | bytes 2359304 | tf_op jit(solution)/shard_map/ppermute | solution.py:53
  106.2 34.7 %collective-permute-start.8 = (f32[3,2,32,1024]{3,2,1,0:T(8,128)}, f32[3,2,32,1024]{3,2,1,0:T(8,128)}, u32[]{:S(2)}, u32[]{:S(2)}) collective-permute-start(f32[3,2,32,1024]{3,2,1,0:T(8,128)} %get-tuple-element.53), channel_id=1, source_target_pairs={{0,48},{16,0},{32,16},{48,32},{1,49},{17,1},{33,17},{49,33},{2,50}... | collective-permute-start | bytes 2359304 | tf_op jit(solution)/shard_map/ppermute | solution.py:53
  108.0 37.3 %collective-permute-start.12 = (f32[3,8,32,256]{3,2,1,0:T(8,128)}, f32[3,8,32,256]{3,2,1,0:T(8,128)S(1)}, u32[]{:S(2)}, u32[]{:S(2)}) collective-permute-start(f32[3,8,32,256]{3,2,1,0:T(8,128)} %get-tuple-element.59), channel_id=1, source_target_pairs={{0,2},{2,4},{4,6},{6,0},{1,3},{3,5},{5,7},{7,1},{8,10},{10,12},{12... | collective-permute-start | bytes 2359304 | tf_op jit(solution)/shard_map/ppermute | solution.py:53
  122.8 11.5 %copy-start.5 = (f32[3,2,32,1024]{3,2,1,0:T(8,128)}, f32[3,2,32,1024]{3,2,1,0:T(8,128)S(1)}, u32[]{:S(2)}) copy-start(f32[3,2,32,1024]{3,2,1,0:T(8,128)S(1)} %collective-permute-done.6.a1) | copy-start | bytes 2359300
  122.8 23.8 %collective-permute-start.13 = (f32[3,8,32,256]{3,2,1,0:T(8,128)}, f32[3,8,32,256]{3,2,1,0:T(8,128)S(1)}, u32[]{:S(2)}, u32[]{:S(2)}) collective-permute-start(f32[3,8,32,256]{3,2,1,0:T(8,128)} %get-tuple-element.60), channel_id=1, source_target_pairs={{0,4},{2,6},{4,0},{6,2},{1,5},{3,7},{5,1},{7,3},{8,12},{10,14},{12... | collective-permute-start | bytes 2359304 | tf_op jit(solution)/shard_map/ppermute | solution.py:53
  124.1 1.4 copy-start.26
  125.4 34.7 %collective-permute-start.14 = (f32[3,8,32,256]{3,2,1,0:T(8,128)}, f32[3,8,32,256]{3,2,1,0:T(8,128)S(1)}, u32[]{:S(2)}, u32[]{:S(2)}) collective-permute-start(f32[3,8,32,256]{3,2,1,0:T(8,128)} %get-tuple-element.61), channel_id=1, source_target_pairs={{0,6},{2,0},{4,2},{6,4},{1,7},{3,1},{5,3},{7,5},{8,14},{10,8},{12,... | collective-permute-start | bytes 2359304 | tf_op jit(solution)/shard_map/ppermute | solution.py:53
  140.9 0.9 copy-start.6
  140.9 26.1 %collective-permute-start.21 = (f32[2,2,32,1024]{3,2,1,0:T(8,128)}, f32[2,2,32,1024]{3,2,1,0:T(8,128)S(1)}, u32[]{:S(2)}, u32[]{:S(2)}) collective-permute-start(f32[2,2,32,1024]{3,2,1,0:T(8,128)} %get-tuple-element.67), channel_id=1, source_target_pairs={{0,16},{16,32},{32,48},{48,0},{1,17},{17,33},{33,49},{49,1},{2,18}... | collective-permute-start | bytes 1572872 | tf_op jit(solution)/shard_map/ppermute | solution.py:53
  144.8 17.0 %collective-permute-start.9 = (f32[3,2,32,256]{3,2,1,0:T(8,128)}, f32[3,2,32,256]{3,2,1,0:T(8,128)S(1)}, u32[]{:S(2)}, u32[]{:S(2)}) collective-permute-start(f32[3,2,32,256]{3,2,1,0:T(8,128)} %get-tuple-element.55), channel_id=1, source_target_pairs={{0,2},{2,4},{4,6},{6,0},{1,3},{3,5},{5,7},{7,1},{8,10},{10,12},{12... | collective-permute-start | bytes 589832 | tf_op jit(solution)/shard_map/ppermute | solution.py:53
  145.3 22.1 %copy-start.2 = (f32[3,8,32,256]{3,2,1,0:T(8,128)}, f32[3,8,32,256]{3,2,1,0:T(8,128)S(1)}, u32[]{:S(2)}) copy-start(f32[3,8,32,256]{3,2,1,0:T(8,128)S(1)} %collective-permute-done.12.a1) | copy-start | bytes 2359300
  145.3 18.0 %collective-permute-start.10 = (f32[3,2,32,256]{3,2,1,0:T(8,128)}, f32[3,2,32,256]{3,2,1,0:T(8,128)S(1)}, u32[]{:S(2)}, u32[]{:S(2)}) collective-permute-start(f32[3,2,32,256]{3,2,1,0:T(8,128)} %get-tuple-element.56), channel_id=1, source_target_pairs={{0,4},{2,6},{4,0},{6,2},{1,5},{3,7},{5,1},{7,3},{8,12},{10,14},{12... | collective-permute-start | bytes 589832 | tf_op jit(solution)/shard_map/ppermute | solution.py:53
  146.7 20.7 %copy-start.3 = (f32[3,8,32,256]{3,2,1,0:T(8,128)}, f32[3,8,32,256]{3,2,1,0:T(8,128)S(1)}, u32[]{:S(2)}) copy-start(f32[3,8,32,256]{3,2,1,0:T(8,128)S(1)} %collective-permute-done.13.a2) | copy-start | bytes 2359300
  146.7 23.7 %collective-permute-start.22 = (f32[2,2,32,1024]{3,2,1,0:T(8,128)}, f32[2,2,32,1024]{3,2,1,0:T(8,128)S(1)}, u32[]{:S(2)}, u32[]{:S(2)}) collective-permute-start(f32[2,2,32,1024]{3,2,1,0:T(8,128)} %get-tuple-element.68), channel_id=1, source_target_pairs={{0,32},{16,48},{32,0},{48,16},{1,33},{17,49},{33,1},{49,17},{2,34}... | collective-permute-start | bytes 1572872 | tf_op jit(solution)/shard_map/ppermute | solution.py:53
  160.2 7.2 %copy-start.4 = (f32[3,8,32,256]{3,2,1,0:T(8,128)}, f32[3,8,32,256]{3,2,1,0:T(8,128)S(1)}, u32[]{:S(2)}) copy-start(f32[3,8,32,256]{3,2,1,0:T(8,128)S(1)} %collective-permute-done.14.a3) | copy-start | bytes 2359300
  160.2 12.6 %collective-permute-start.23 = (f32[2,2,32,1024]{3,2,1,0:T(8,128)}, f32[2,2,32,1024]{3,2,1,0:T(8,128)}, u32[]{:S(2)}, u32[]{:S(2)}) collective-permute-start(f32[2,2,32,1024]{3,2,1,0:T(8,128)} %get-tuple-element.69), channel_id=1, source_target_pairs={{0,48},{16,0},{32,16},{48,32},{1,49},{17,1},{33,17},{49,33},{2,50}... | collective-permute-start | bytes 1572872 | tf_op jit(solution)/shard_map/ppermute | solution.py:53
  161.8 30.2 %copy-start.14 = (f32[3,2,32,256]{3,2,1,0:T(8,128)}, f32[3,2,32,256]{3,2,1,0:T(8,128)S(1)}, u32[]{:S(2)}) copy-start(f32[3,2,32,256]{3,2,1,0:T(8,128)S(1)} %collective-permute-done.9.refs_1_) | copy-start | bytes 589828
  161.9 14.7 %collective-permute-start.27 = (f32[2,8,32,256]{3,2,1,0:T(8,128)}, f32[2,8,32,256]{3,2,1,0:T(8,128)S(1)}, u32[]{:S(2)}, u32[]{:S(2)}) collective-permute-start(f32[2,8,32,256]{3,2,1,0:T(8,128)} %get-tuple-element.75), channel_id=1, source_target_pairs={{0,2},{2,4},{4,6},{6,0},{1,3},{3,5},{5,7},{7,1},{8,10},{10,12},{12... | collective-permute-start | bytes 1572872 | tf_op jit(solution)/shard_map/ppermute | solution.py:53
  163.2 3.7 %copy-start.15 = (f32[3,2,32,256]{3,2,1,0:T(8,128)}, f32[3,2,32,256]{3,2,1,0:T(8,128)S(1)}, u32[]{:S(2)}) copy-start(f32[3,2,32,256]{3,2,1,0:T(8,128)S(1)} %collective-permute-done.10.refs_2_) | copy-start | bytes 589828
  163.3 25.6 %collective-permute-start.28 = (f32[2,8,32,256]{3,2,1,0:T(8,128)}, f32[2,8,32,256]{3,2,1,0:T(8,128)}, u32[]{:S(2)}, u32[]{:S(2)}) collective-permute-start(f32[2,8,32,256]{3,2,1,0:T(8,128)} %get-tuple-element.76), channel_id=1, source_target_pairs={{0,4},{2,6},{4,0},{6,2},{1,5},{3,7},{5,1},{7,3},{8,12},{10,14},{12... | collective-permute-start | bytes 1572872 | tf_op jit(solution)/shard_map/ppermute | solution.py:53
  166.9 22.6 %copy-start.7 = (f32[2,2,32,1024]{3,2,1,0:T(8,128)}, f32[2,2,32,1024]{3,2,1,0:T(8,128)S(1)}, u32[]{:S(2)}) copy-start(f32[2,2,32,1024]{3,2,1,0:T(8,128)S(1)} %collective-permute-done.21.a1) | copy-start | bytes 1572868
  166.9 25.2 %collective-permute-start.29 = (f32[2,8,32,256]{3,2,1,0:T(8,128)}, f32[2,8,32,256]{3,2,1,0:T(8,128)}, u32[]{:S(2)}, u32[]{:S(2)}) collective-permute-start(f32[2,8,32,256]{3,2,1,0:T(8,128)} %get-tuple-element.77), channel_id=1, source_target_pairs={{0,6},{2,0},{4,2},{6,4},{1,7},{3,1},{5,3},{7,5},{8,14},{10,8},{12,... | collective-permute-start | bytes 1572872 | tf_op jit(solution)/shard_map/ppermute | solution.py:53
  170.4 19.1 %copy-start.9 = (f32[2,2,32,1024]{3,2,1,0:T(8,128)}, f32[2,2,32,1024]{3,2,1,0:T(8,128)S(1)}, u32[]{:S(2)}) copy-start(f32[2,2,32,1024]{3,2,1,0:T(8,128)S(1)} %collective-permute-done.22.a2) | copy-start | bytes 1572868
  170.4 24.3 %collective-permute-start.11 = (f32[3,2,32,256]{3,2,1,0:T(8,128)}, f32[3,2,32,256]{3,2,1,0:T(8,128)S(1)}, u32[]{:S(2)}, u32[]{:S(2)}) collective-permute-start(f32[3,2,32,256]{3,2,1,0:T(8,128)} %get-tuple-element.57), channel_id=1, source_target_pairs={{0,6},{2,0},{4,2},{6,4},{1,7},{3,1},{5,3},{7,5},{8,14},{10,8},{12,... | collective-permute-start | bytes 589832 | tf_op jit(solution)/shard_map/ppermute | solution.py:53
  172.7 23.3 %collective-permute-start.15 = (f32[3,2,32,256]{3,2,1,0:T(8,128)}, f32[3,2,32,256]{3,2,1,0:T(8,128)S(1)}, u32[]{:S(2)}, u32[]{:S(2)}) collective-permute-start(f32[3,2,32,256]{3,2,1,0:T(8,128)} %get-tuple-element.63), channel_id=1, source_target_pairs={{0,16},{16,32},{32,48},{48,0},{1,17},{17,33},{33,49},{49,1},{2,18}... | collective-permute-start | bytes 589832 | tf_op jit(solution)/shard_map/ppermute | solution.py:53
  176.5 15.7 %copy-start.8 = (f32[2,8,32,256]{3,2,1,0:T(8,128)}, f32[2,8,32,256]{3,2,1,0:T(8,128)S(1)}, u32[]{:S(2)}) copy-start(f32[2,8,32,256]{3,2,1,0:T(8,128)S(1)} %collective-permute-done.27.a1) | copy-start | bytes 1572868
  176.5 22.1 %collective-permute-start.16 = (f32[3,2,32,256]{3,2,1,0:T(8,128)}, f32[3,2,32,256]{3,2,1,0:T(8,128)S(1)}, u32[]{:S(2)}, u32[]{:S(2)}) collective-permute-start(f32[3,2,32,256]{3,2,1,0:T(8,128)} %get-tuple-element.64), channel_id=1, source_target_pairs={{0,32},{16,48},{32,0},{48,16},{1,33},{17,49},{33,1},{49,17},{2,34}... | collective-permute-start | bytes 589832 | tf_op jit(solution)/shard_map/ppermute | solution.py:53
  188.9 10.8 %collective-permute-start.17 = (f32[3,2,32,256]{3,2,1,0:T(8,128)}, f32[3,2,32,256]{3,2,1,0:T(8,128)S(1)}, u32[]{:S(2)}, u32[]{:S(2)}) collective-permute-start(f32[3,2,32,256]{3,2,1,0:T(8,128)} %get-tuple-element.65), channel_id=1, source_target_pairs={{0,48},{16,0},{32,16},{48,32},{1,49},{17,1},{33,17},{49,33},{2,50}... | collective-permute-start | bytes 589832 | tf_op jit(solution)/shard_map/ppermute | solution.py:53
  192.1 2.7 %copy-start.32 = (f32[2,2,32,256]{3,2,1,0:T(8,128)S(1)}, f32[2,2,32,256]{3,2,1,0:T(8,128)}, u32[]{:S(2)}) copy-start(f32[2,2,32,256]{3,2,1,0:T(8,128)} %get-tuple-element.72) | copy-start | bytes 393220
  192.1 3.9 %copy-start.31 = (f32[2,2,32,256]{3,2,1,0:T(8,128)S(1)}, f32[2,2,32,256]{3,2,1,0:T(8,128)}, u32[]{:S(2)}) copy-start(f32[2,2,32,256]{3,2,1,0:T(8,128)} %get-tuple-element.73) | copy-start | bytes 393220
  192.1 9.3 %collective-permute-start.24 = (f32[2,2,32,256]{3,2,1,0:T(8,128)}, f32[2,2,32,256]{3,2,1,0:T(8,128)S(1)}, u32[]{:S(2)}, u32[]{:S(2)}) collective-permute-start(f32[2,2,32,256]{3,2,1,0:T(8,128)} %get-tuple-element.71), channel_id=1, source_target_pairs={{0,2},{2,4},{4,6},{6,0},{1,3},{3,5},{5,7},{7,1},{8,10},{10,12},{12... | collective-permute-start | bytes 393224 | tf_op jit(solution)/shard_map/ppermute | solution.py:53
  194.7 12.6 %copy-start.16 = (f32[3,2,32,256]{3,2,1,0:T(8,128)}, f32[3,2,32,256]{3,2,1,0:T(8,128)S(1)}, u32[]{:S(2)}) copy-start(f32[3,2,32,256]{3,2,1,0:T(8,128)S(1)} %collective-permute-done.11.refs_3_) | copy-start | bytes 589828
  194.7 8.2 %collective-permute-start.25 = (f32[2,2,32,256]{3,2,1,0:T(8,128)S(1)}, f32[2,2,32,256]{3,2,1,0:T(8,128)S(1)}, u32[]{:S(2)}, u32[]{:S(2)}) collective-permute-start(f32[2,2,32,256]{3,2,1,0:T(8,128)S(1)} %copy-done.32), channel_id=1, source_target_pairs={{0,4},{2,6},{4,0},{6,2},{1,5},{3,7},{5,1},{7,3},{8,12},{10,14},{12... | collective-permute-start | bytes 393224 | tf_op jit(solution)/shard_map/ppermute | solution.py:53
  196.0 11.3 %copy-start.17 = (f32[3,2,32,256]{3,2,1,0:T(8,128)}, f32[3,2,32,256]{3,2,1,0:T(8,128)S(1)}, u32[]{:S(2)}) copy-start(f32[3,2,32,256]{3,2,1,0:T(8,128)S(1)} %collective-permute-done.15.refs_5_) | copy-start | bytes 589828
  196.0 7.3 %collective-permute-start.26 = (f32[2,2,32,256]{3,2,1,0:T(8,128)S(1)}, f32[2,2,32,256]{3,2,1,0:T(8,128)S(1)}, u32[]{:S(2)}, u32[]{:S(2)}) collective-permute-start(f32[2,2,32,256]{3,2,1,0:T(8,128)S(1)} %copy-done.31), channel_id=1, source_target_pairs={{0,6},{2,0},{4,2},{6,4},{1,7},{3,1},{5,3},{7,5},{8,14},{10,8},{12,... | collective-permute-start | bytes 393224 | tf_op jit(solution)/shard_map/ppermute | solution.py:53
  198.6 8.7 %copy-start.18 = (f32[3,2,32,256]{3,2,1,0:T(8,128)}, f32[3,2,32,256]{3,2,1,0:T(8,128)S(1)}, u32[]{:S(2)}) copy-start(f32[3,2,32,256]{3,2,1,0:T(8,128)S(1)} %collective-permute-done.16.refs_6_) | copy-start | bytes 589828
  198.6 6.4 %collective-permute-start.30 = (f32[2,2,32,256]{3,2,1,0:T(8,128)}, f32[2,2,32,256]{3,2,1,0:T(8,128)S(1)}, u32[]{:S(2)}, u32[]{:S(2)}) collective-permute-start(f32[2,2,32,256]{3,2,1,0:T(8,128)} %get-tuple-element.79), channel_id=1, source_target_pairs={{0,16},{16,32},{32,48},{48,0},{1,17},{17,33},{33,49},{49,1},{2,18}... | collective-permute-start | bytes 393224 | tf_op jit(solution)/shard_map/ppermute | solution.py:53
  199.7 7.6 %copy-start.19 = (f32[3,2,32,256]{3,2,1,0:T(8,128)}, f32[3,2,32,256]{3,2,1,0:T(8,128)S(1)}, u32[]{:S(2)}) copy-start(f32[3,2,32,256]{3,2,1,0:T(8,128)S(1)} %collective-permute-done.17.refs_7_) | copy-start | bytes 589828
  199.7 6.7 %collective-permute-start.31 = (f32[2,2,32,256]{3,2,1,0:T(8,128)}, f32[2,2,32,256]{3,2,1,0:T(8,128)S(1)}, u32[]{:S(2)}, u32[]{:S(2)}) collective-permute-start(f32[2,2,32,256]{3,2,1,0:T(8,128)} %get-tuple-element.80), channel_id=1, source_target_pairs={{0,32},{16,48},{32,0},{48,16},{1,33},{17,49},{33,1},{49,17},{2,34}... | collective-permute-start | bytes 393224 | tf_op jit(solution)/shard_map/ppermute | solution.py:53
  201.4 6.0 %copy-start.20 = (f32[2,2,32,256]{3,2,1,0:T(8,128)}, f32[2,2,32,256]{3,2,1,0:T(8,128)S(1)}, u32[]{:S(2)}) copy-start(f32[2,2,32,256]{3,2,1,0:T(8,128)S(1)} %collective-permute-done.24.refs_9_) | copy-start | bytes 393220
  201.4 5.9 %collective-permute-start.32 = (f32[2,2,32,256]{3,2,1,0:T(8,128)}, f32[2,2,32,256]{3,2,1,0:T(8,128)S(1)}, u32[]{:S(2)}, u32[]{:S(2)}) collective-permute-start(f32[2,2,32,256]{3,2,1,0:T(8,128)} %get-tuple-element.81), channel_id=1, source_target_pairs={{0,48},{16,0},{32,16},{48,32},{1,49},{17,1},{33,17},{49,33},{2,50}... | collective-permute-start | bytes 393224 | tf_op jit(solution)/shard_map/ppermute | solution.py:53
  203.0 4.4 %copy-start.21 = (f32[2,2,32,256]{3,2,1,0:T(8,128)}, f32[2,2,32,256]{3,2,1,0:T(8,128)S(1)}, u32[]{:S(2)}) copy-start(f32[2,2,32,256]{3,2,1,0:T(8,128)S(1)} %collective-permute-done.25.refs_10_) | copy-start | bytes 393220
  203.3 4.1 %copy-start.22 = (f32[2,2,32,256]{3,2,1,0:T(8,128)}, f32[2,2,32,256]{3,2,1,0:T(8,128)S(1)}, u32[]{:S(2)}) copy-start(f32[2,2,32,256]{3,2,1,0:T(8,128)S(1)} %collective-permute-done.26.refs_11_) | copy-start | bytes 393220
  205.0 2.3 %copy-start.23 = (f32[2,2,32,256]{3,2,1,0:T(8,128)}, f32[2,2,32,256]{3,2,1,0:T(8,128)S(1)}, u32[]{:S(2)}) copy-start(f32[2,2,32,256]{3,2,1,0:T(8,128)S(1)} %collective-permute-done.30.refs_13_) | copy-start | bytes 393220
  206.4 0.9 copy-start.24
  (3 other events, 2.2 us)

commit v2 on v1

--- a/solution.py
+++ b/solution.py
@@ -65,7 +65,7 @@
     same = (dest_col[...] == dest_row[...]) & earlier
     slot = jnp.sum(jnp.where(same, 1.0, 0.0), axis=0, keepdims=True).astype(jnp.int32)
     target = dest_row[...] * CAP + slot
-    q = out.shape[0]
+    q = out.shape[0] * CAP
     selector = jnp.where(lax.broadcasted_iota(jnp.int32, (q, n), 0) == target, 1.0, 0.0).astype(BF16)
     height = fluid.shape[0]
     picked = jnp.where(lax.broadcasted_iota(jnp.int32, (height, n), 0) == rows[...], 1.0, 0.0)
@@ -77,7 +77,8 @@
     rest = value - high.astype(F32)
     mid = rest.astype(BF16)
     low = (rest - mid.astype(F32)).astype(BF16)
-    out[...] = mul(chosen, high) + (mul(chosen, mid) + mul(chosen, low))
+    value = mul(chosen, high) + (mul(chosen, mid) + mul(chosen, low))
+    out[...] = value.reshape(out.shape)
 
 
 def turn_kernel(place, struct, fluid, own_s, send_s, own_f, send_f, held_s, held_f):
@@ -91,7 +92,8 @@
 
 
 def wet_kernel(coupling, received, out):
-    out[...] = product(parts(coupling[...]), parts(received[...]))
+    right = received[...].reshape(coupling.shape[1], R)
+    out[...] = product(parts(coupling[...]), parts(right))
 
 
 def gathered(tiles, cols, total, at):
@@ -147,20 +149,21 @@
         outs[4 + o][0] = held[:, HALF:, pl.ds(pl.multiple_of(dy * 256, 256), 256)]
 
 
-def first_kernel(place, ls0, ls1, lf0, lf1, ic0, ic1, if0, if1, *rest):
-    outs, (sh, sl, fh, fl, held) = rest[:8], rest[8:]
-    m = pl.program_id(0)
-
-    @pl.when(m == 0)
+def fluid_product_kernel(place, lf0, lf1, if0, if1, *rest):
+    outs, (fh, fl, held) = rest[:8], rest[8:]
+
+    @pl.when(pl.program_id(0) == 0)
     def _():
-        sh[...], sl[...] = parts(joined(ls0, ls1))
         fh[...], fl[...] = parts(joined(lf0, lf1))
-        multiply(held, (sh, sl), ic0[...], ic1[...])
-
-    @pl.when(m > 0)
-    def _():
-        multiply(held, (fh, fl), if0[0], if1[0])
-
+
+    multiply(held, (fh, fl), if0[0], if1[0])
+    send_off(place, held, outs)
+
+
+def wet_product_kernel(place, ls0, ls1, ic0, ic1, *rest):
+    outs, (sh, sl, held) = rest[8:16], rest[16:]
+    sh[...], sl[...] = parts(joined(ls0, ls1))
+    multiply(held, (sh, sl), ic0[...], ic1[...])
     send_off(place, held, outs)
 
 
@@ -186,25 +189,20 @@
                 out[:, h] = held[:, h * 4 + d]
 
 
-def spread_kernel(*refs):
-    ins, out = refs[:16], refs[16]
-    at = 0
-    for group in range(2):
-        x, y = ins[group * 8 : group * 8 + 4], ins[group * 8 + 4 : group * 8 + 8]
-        n = x[0].shape[0]
-        for h in range(2):
-            top = (x[0][:, h] + x[1][:, h]) + (x[2][:, h] + x[3][:, h])
-            low = (y[0][:, h] + y[1][:, h]) + (y[2][:, h] + y[3][:, h])
-            for l in range(2):
-                lanes = slice(l * 128, (l + 1) * 128)
-                out[h * 2 + l, at : at + n, 0:HALF] = top[..., lanes]
-                out[h * 2 + l, at : at + n, HALF:] = low[..., lanes]
-        at += n
-
-
-def last_kernel(arrived, *outs):
-    for m, out in enumerate(outs):
-        out[...] = (arrived[0, m] + arrived[1, m]) + (arrived[2, m] + arrived[3, m])
+def spread_kernel(place, x0, x1, x2, x3, y0, y1, y2, y3, o0, o1, o2, o3, held):
+    held[:, :, 0:HALF] = (x0[...] + x1[...]) + (x2[...] + x3[...])
+    held[:, :, HALF:] = (y0[...] + y1[...]) + (y2[...] + y3[...])
+    for o, out in enumerate((o0, o1, o2, o3)):
+        d = lax.rem(place[2] + o, 4)
+        lanes = pl.ds(pl.multiple_of(lax.rem(d, 2) * 128, 128), 128)
+        out[...] = held[:, d // 2, :, lanes]
+
+
+def last_kernel(a0, a1, a2, a3, b0, b1, b2, b3, fstiff, fmass, wet, stiff, mass):
+    for m, out in enumerate((fstiff, fmass, wet)):
+        out[...] = (a0[m] + a1[m]) + (a2[m] + a3[m])
+    for m, out in enumerate((stiff, mass)):
+        out[...] = (b0[m] + b1[m]) + (b2[m] + b3[m])
 
 
 def call(kernel, out, count, smem=0, anywhere=0, scratch=(), flops=0, moved=0):
@@ -238,21 +236,36 @@
     )(place, *arrived)
 
 
-def partial_sums(kernel, count, place, lefts, steps, operands, specs, scratch):
+def spread(place, x, y):
+    count = x[0].shape[0]
+    return call(
+        spread_kernel,
+        [shape(count, 64, 128)] * 4,
+        9,
+        smem=1,
+        scratch=[pltpu.VMEM((count, 2, 64, 256), F32)],
+        flops=6 * x[0].size,
+        moved=40 * x[0].size,
+    )(place, *x, *y)
+
+
+def partial_sums(kernel, steps, at, count, place, lefts, depth, operands, specs, carried=()):
+    left = pltpu.VMEM((512, depth), BF16)
     run = pl.pallas_call(
         kernel,
-        grid=(count,),
+        grid=(steps,),
         out_shape=[shape(count, 2, HALF, R)] * 4 + [shape(count, 8, HALF, 256)] * 4,
-        in_specs=[SMEM] + [VMEM] * len(lefts) + specs,
-        out_specs=[pl.BlockSpec((1, 2, HALF, R), lambda m: (m, 0, 0, 0))] * 4
-        + [pl.BlockSpec((1, 8, HALF, 256), lambda m: (m, 0, 0, 0))] * 4,
-        scratch_shapes=scratch + [pltpu.VMEM((8, 64, R), F32)],
+        in_specs=[SMEM] + [VMEM] * len(lefts) + specs + [ANY] * len(carried),
+        out_specs=[pl.BlockSpec((1, 2, HALF, R), lambda m: (m + at, 0, 0, 0))] * 4
+        + [pl.BlockSpec((1, 8, HALF, 256), lambda m: (m + at, 0, 0, 0))] * 4,
+        scratch_shapes=[left, left, pltpu.VMEM((8, 64, R), F32)],
+        input_output_aliases={1 + len(lefts) + len(specs) + i: i for i in range(len(carried))},
         compiler_params=PARAMS,
         cost_estimate=pl.CostEstimate(
-            flops=6 * steps * 512 * 256 * R, bytes_accessed=4 * count * 2**20, transcendentals=0
+            flops=6 * steps * 512 * depth * R, bytes_accessed=4 * steps * 2**20, transcendentals=0
         ),
     )
-    return run(place, *lefts, *operands)
+    return run(place, *lefts, *operands, *carried)
 
 
 def compute(
@@ -276,7 +289,7 @@
     below_f = from_behind(fluid_basis, 1)
     above_f = from_behind(fluid_basis, -1)
 
-    outgoing = call(route_kernel, shape(256, R), 4, flops=2 * 3 * 256 * 128 * R, moved=2**21)(
+    outgoing = call(route_kernel, shape(128, CAP, R), 4, flops=2 * 3 * 256 * 128 * R, moved=2**21)(
         wet_dest, wet_dest.reshape(1, -1), wet_rows.reshape(1, -1), fluid_basis
     )
     received = lax.all_to_all(outgoing, AXES, split_axis=0, concat_axis=0, tiled=True)
@@ -308,17 +321,14 @@
     )(fluid_cols, fluid_stiff_tiles, fluid_mass_tiles, below_f, fluid_basis, above_f, own_s)
     other_f = shifted(image_f, "core", 1)
 
-    fblock = pl.BlockSpec((1, 128, R), lambda m: (jnp.maximum(m - 1, 0), 0, 0))
-    slim = [pltpu.VMEM((512, 512), BF16)] * 2
+    def block(rows):
+        return pl.BlockSpec((1, rows, R), lambda m: (m, 0, 0))
+
+    fluid = partial_sums(
+        fluid_product_kernel, 2, 0, 3, place, (own_f, left_f), 256, (image_f, other_f), [block(128)] * 2
+    )
     first = partial_sums(
-        first_kernel,
-        3,
-        place,
-        (own_s, left_s, own_f, left_f, image_c, other_c),
-        4,
-        (image_f, other_f),
-        [fblock, fblock],
-        slim + [pltpu.VMEM((512, 256), BF16)] * 2,
+        wet_product_kernel, 1, 2, 3, place, (own_s, left_s), 512, (image_c, other_c), [VMEM] * 2, fluid
     )
     first_x = exchanged(first[0:4], X)
     first_y = exchanged(first[4:8], Y)
@@ -335,8 +345,7 @@
     )(struct_cols, stiff_tiles, mass_tiles, below_s, struct_basis, above_s, first[0])
     other_s = shifted(image_s, "core", 1)
 
-    sblock = pl.BlockSpec((1, 256, R), lambda m: (m, 0, 0))
-    second = partial_sums(second_kernel, 2, place, (own_s, left_s), 4, (image_s, other_s), [sblock, sblock], slim)
+    second = partial_sums(second_kernel, 2, 0, 2, place, (own_s, left_s), 512, (image_s, other_s), [block(256)] * 2)
     second_x = exchanged(second[0:4], X)
     second_y = exchanged(second[4:8], Y)
 
@@ -344,11 +353,11 @@
     first_yx = exchanged(split(place, first_y, 0), X)
     second_xy = exchanged(split(place, second_x, 1), Y)
     second_yx = exchanged(split(place, second_y, 0), X)
-    blocks = call(spread_kernel, shape(4, 5, 64, 128), 16, flops=2**20, moved=2**22)(
-        *first_xy, *first_yx, *second_xy, *second_yx
-    )
-    arrived = lax.all_to_all(blocks, Z, split_axis=0, concat_axis=0, tiled=True)
-    wet, fstiff, fmass, stiff, mass = call(last_kernel, [shape(64, 128)] * 5, 1, flops=2**18, moved=2**20)(arrived)
+    first_z = exchanged(spread(place, first_xy, first_yx), Z)
+    second_z = exchanged(spread(place, second_xy, second_yx), Z)
+    fstiff, fmass, wet, stiff, mass = call(
+        last_kernel, [shape(64, 128)] * 5, 8, flops=2**18, moved=2**20
+    )(*first_z, *second_z)
     return stiff, mass, fstiff, fmass, wet
 
 

time: 227 us -> 224 us (0.987)
  starting transfers between devices: 55.5 us -> 74.3 us
  blocking collectives: 13.4 us -> 0 us
  waiting for transfers between devices: 92.3 us -> 83.5 us
  Pallas kernels: 50.8 us -> 54.2 us
  local copies, waits for them, and re-layouts: 12.4 us -> 9.89 us
    ppermute x29 -> x35, starting transfers between devices: 34.3 us -> 53.1 us  [shifted(): lax.ppermute(value, axis, [(i, (i + by) % size) for i in range(size)])]
    all_to_all x1 -> x0, blocking collectives: 13.4 us -> none  [compute(): arrived = lax.all_to_all(blocks, Z, split_axis=0, concat_axis=0, tiled=True)]
    ppermute x29 -> x35, waiting for transfers between devices: 55 us -> 47.2 us  [shifted(): lax.ppermute(value, axis, [(i, (i + by) % size) for i in range(size)])]
    all_to_all x2 -> x0, local copies, waits for them, and re-layouts: 4.58 us -> none  [compute(): lax.all_to_all(outgoing, AXES, split_axis=0, concat_axis=0, tiled=True)]
    pallas_call x5 -> x7, Pallas kernels: 23.8 us -> 26.9 us  [the longest x3 17.9 us: partial_sums(): return run(place, *lefts, *operands, *carried)]
    unnamed x67 -> x89, local copies, waits for them, and re-layouts: 7.73 us -> 8.93 us
  transfers between devices with their start and end apart: 34 -> 40, of which waited for: 15 -> 10; matrix products, arithmetic and copies ran while one was open for 0% -> 1% of each run, Pallas kernels for 17% -> 19%
where the time goes in v2:
time: 224 us; the launch traced here: 223 us
  waiting for transfers between devices  83.5 us (37%)
  starting transfers between devices  74.3 us (33%)
  Pallas kernels  54.2 us (24%)
  local copies, waits for them, and re-layouts  9.89 us (4%)
    ppermute x35, starting transfers between devices, shifted(): lax.ppermute(value, axis, [(i, (i + by) % size) for i in range(size)])  53.1 us
    ppermute x35, waiting for transfers between devices, shifted(): lax.ppermute(value, axis, [(i, (i + by) % size) for i in range(size)])  47.2 us
    ppermute x4, waiting for transfers between devices, from_behind(): return lax.ppermute(value, AXES, pairs)  36.3 us
    pallas_call x3, Pallas kernels, partial_sums(): return run(place, *lefts, *operands, *carried)  17.9 us
    all_to_all x1, starting transfers between devices, compute(): lax.all_to_all(outgoing, AXES, split_axis=0, concat_axis=0, tiled=True)  11.2 us
    pallas_call x4, Pallas kernels, split(): call(functools.partial(split_kernel, axis), [shape(count, 2, HALF, 256)]...  11.1 us
    ppermute x4, starting transfers between devices, from_behind(): return lax.ppermute(value, AXES, pairs)  10 us
    unnamed x89, local copies, waits for them, and re-layouts  8.93 us
  transfers between devices with their start and end apart: 40, of which 10 were waited for; matrix products, arithmetic and copies ran while one was open for 1% of the time, Pallas kernels for 19%

profile of v2, /device:TPU:0, one launch (start us, length us, event | category | flops | bytes accessed | tf_op | source)
XLA Modules:
  0.0 223.5 jit_solution(12845416672293247141)
XLA Ops:
  0.6 1.4 copy.24.dest_col
  2.1 2.9 %shard_map.147 = f32[128,2,1024]{2,1,0:T(2,128)} custom-call(s32[128,1]{1,0:T(8,128)} %copy.24.dest_col, s32[1,128]{1,0:T(1,128)} %bitcast.6, s32[1,128]{1,0:T(1,128)} %bitcast.7, f32[128,1024]{1,0:T(8,128)} %own.2), custom_call_target="tpu_custom_call" | custom-call | flops 201326592 | bytes 2097152 | tf_op jit(solution)/shard_map/pallas_call | solution.py:292
  5.0 11.2 %all-to-all-start = ((f32[128,2,1024]{2,1,0:T(2,128)}), f32[128,2,1024]{2,1,0:T(2,128)S(1)}, u32[]{:S(2)}, u32[]{:S(2)}) async-start(f32[128,2,1024]{2,1,0:T(2,128)} %shard_map.147), calls=%async_computation | async-start | bytes 2097152 | tf_op jit(solution)/shard_map/all_to_all | solution.py:295
  16.1 3.0 %collective-permute-start.3 = (f32[128,1024]{1,0:T(8,128)S(1)}, f32[128,1024]{1,0:T(8,128)S(1)}, u32[]{:S(2)}, u32[]{:S(2)}) collective-permute-start(f32[128,1024]{1,0:T(8,128)S(1)} %copy-done.1), channel_id=1, source_target_pairs={{0,1},{1,2},{2,3},{3,4},{4,5},{5,6},{6,7},{7,8},{8,9},{9,10},{10,1... | collective-permute-start | bytes 1572872 | tf_op jit(solution)/shard_map/ppermute | solution.py:59
  19.2 1.3 collective-permute-start.4
  21.1 2.9 %shard_map.146 = (f32[8,64,256]{2,1,0:T(8,128)}, f32[8,64,256]{2,1,0:T(8,128)}, f32[8,64,128]{2,1,0:T(8,128)}, f32[8,64,128]{2,1,0:T(8,128)}) custom-call(s32[4]{0:T(128)} %pad_add_fusion.place, f32[256,1024]{1,0:T(8,128)} %own.3, f32[128,1024]{1,0:T(8,128)} %own.2), custom_call_target="tpu_custom_call" | custom-call | flops 1048576 | bytes 3145728 | tf_op jit(solution)/shard_map/pallas_call | solution.py:297
  24.0 26.5 %collective-permute-done.3.lo = f32[128,1024]{1,0:T(8,128)S(1)} collective-permute-done((f32[128,1024]{1,0:T(8,128)S(1)}, f32[128,1024]{1,0:T(8,128)S(1)}, u32[]{:S(2)}, u32[]{:S(2)}) %collective-permute-start.3) | collective-permute-done | bytes 524320 | tf_op jit(solution)/shard_map/ppermute | solution.py:59
  50.5 0.8 copy-done.20
  51.5 3.9 %shard_map.149.if0 = f32[2,128,1024]{2,1,0:T(8,128)} custom-call(s32[1,4]{1,0:T(1,128)} %cols.2, f32[1,4,128,128]{3,2,1,0:T(8,128)} %stiff.2, f32[1,4,128,128]{3,2,1,0:T(8,128)} %mass.2, f32[128,1024]{1,0:T(8,128)} %copy-done.20, f32[128,1024]{1,0:T(8,128)} %own.2, f32[128,1024]{1,0:T(8,128)} %copy-done.21, f32[8,64,256]{2,1,0:T(8,128)} %get-tuple-element.62.after.ls0), custom_call_target="tpu_custom_call" | custom-call | flops 603979776 | bytes 3145728 | tf_op jit(solution)/shard_map/pallas_call | solution.py:312
  55.4 1.0 copy-done.2
  56.4 3.1 %shard_map.148.ic0 = f32[256,1024]{1,0:T(8,128)} custom-call(f32[256,256]{1,0:T(8,128)} %coupling.1, f32[128,2,1024]{2,1,0:T(2,128)} %copy-done.2), custom_call_target="tpu_custom_call" | custom-call | flops 402653184 | bytes 2097152 | tf_op jit(solution)/shard_map/pallas_call | solution.py:309
  60.6 1.0 fusion
  61.5 4.4 %collective-permute-start.21 = (f32[128,1024]{1,0:T(8,128)}, f32[128,1024]{1,0:T(8,128)S(1)}, u32[]{:S(2)}, u32[]{:S(2)}) collective-permute-start(f32[128,1024]{1,0:T(8,128)} %get-tuple-element.120), channel_id=1, source_target_pairs={{0,1},{1,2},{2,3},{3,4},{4,5},{5,6},{6,7},{7,8},{8,9},{9,10},{10,1... | collective-permute-start | bytes 1572872 | tf_op jit(solution)/shard_map/ppermute | solution.py:59
  66.0 1.3 collective-permute-start.22
  67.3 5.3 %shard_map.150 = (f32[3,2,32,1024]{3,2,1,0:T(8,128)}, f32[3,2,32,1024]{3,2,1,0:T(8,128)}, f32[3,2,32,1024]{3,2,1,0:T(8,128)}, f32[3,2,32,1024]{3,2,1,0:T(8,128)}...) custom-call(s32[4]{0:T(128)} %pad_add_fusion.place, ...), custom_call_target="tpu_custom_call" | custom-call | flops 1610612736 | bytes 8388608 | tf_op jit(solution)/shard_map/pallas_call | solution.py:268
  72.6 0.8 copy-done.11
  73.8 5.2 %shard_map.151 = (f32[3,2,32,1024]{3,2,1,0:T(8,128)}, f32[3,2,32,1024]{3,2,1,0:T(8,128)}, f32[3,2,32,1024]{3,2,1,0:T(8,128)}, f32[3,2,32,1024]{3,2,1,0:T(8,128)}...) custom-call(s32[4]{0:T(128)} %pad_add_fusion.place, ...), custom_call_target="tpu_custom_call", output_to_operand_aliasing={{0}: (5, {}), {1}: (6, {}), {2}: (7, {}), {3}: (8, {}), {4}... | custom-call | flops 1610612736 | bytes 4194304 | tf_op jit(solution)/shard_map/pallas_call | solution.py:268
  79.0 9.8 %collective-permute-done.21.lo = f32[128,1024]{1,0:T(8,128)S(1)} collective-permute-done((f32[128,1024]{1,0:T(8,128)}, f32[128,1024]{1,0:T(8,128)S(1)}, u32[]{:S(2)}, u32[]{:S(2)}) %collective-permute-start.21) | collective-permute-done | bytes 524320 | tf_op jit(solution)/shard_map/ppermute | solution.py:59
  88.8 0.9 copy-done.18
  89.7 0.8 copy-done.19
  90.5 6.1 %shard_map.155.is0 = f32[2,256,1024]{2,1,0:T(8,128)} custom-call(s32[2,4]{1,0:T(2,128)} %cols.3, f32[2,4,128,128]{3,2,1,0:T(8,128)} %stiff.3, f32[2,4,128,128]{3,2,1,0:T(8,128)} %mass.3, f32[128,1024]{1,0:T(8,128)} %copy-done.18, f32[256,1024]{1,0:T(8,128)} %own.3, f32[128,1024]{1,0:T(8,128)} %copy-done.19, f32[3,2,32,1024]{3,2,1,0:T(8,128)} %get-tuple-element.74.a0.after), custom_call_target="tpu_custom_call" | custom-call | flops 1610612736 | bytes 5242880 | tf_op jit(solution)/shard_map/pallas_call | solution.py:336
  96.7 4.7 %collective-permute-start.6 = (f32[3,2,32,1024]{3,2,1,0:T(8,128)S(1)}, f32[3,2,32,1024]{3,2,1,0:T(8,128)S(1)}, u32[]{:S(2)}, u32[]{:S(2)}) collective-permute-start(f32[3,2,32,1024]{3,2,1,0:T(8,128)S(1)} %copy-done.4), channel_id=1, source_target_pairs={{0,16},{16,32},{32,48},{48,0},{1,17},{17,33},{33,49},{49,1},{2,18}... | collective-permute-start | bytes 2359304 | tf_op jit(solution)/shard_map/ppermute | solution.py:53
  101.3 2.3 %collective-permute-start.7 = (f32[3,2,32,1024]{3,2,1,0:T(8,128)S(1)}, f32[3,2,32,1024]{3,2,1,0:T(8,128)}, u32[]{:S(2)}, u32[]{:S(2)}) collective-permute-start(f32[3,2,32,1024]{3,2,1,0:T(8,128)S(1)} %copy-done.5), channel_id=1, source_target_pairs={{0,32},{16,48},{32,0},{48,16},{1,33},{17,49},{33,1},{49,17},{2,34}... | collective-permute-start | bytes 2359304 | tf_op jit(solution)/shard_map/ppermute | solution.py:53
  103.7 1.8 collective-permute-start.8
  105.5 14.9 %collective-permute-done.6.a1 = f32[3,2,32,1024]{3,2,1,0:T(8,128)S(1)} collective-permute-done((f32[3,2,32,1024]{3,2,1,0:T(8,128)S(1)}, f32[3,2,32,1024]{3,2,1,0:T(8,128)S(1)}, u32[]{:S(2)}, u32[]{:S(2)}) %collective-permute-start.6) | collective-permute-done | bytes 786464 | tf_op jit(solution)/shard_map/ppermute | solution.py:53
  120.3 1.6 collective-permute-start.13
  122.0 1.3 copy-done.40
  123.3 1.5 collective-permute-start.14
  124.8 7.4 %shard_map.156 = (f32[2,2,32,1024]{3,2,1,0:T(8,128)}, f32[2,2,32,1024]{3,2,1,0:T(8,128)}, f32[2,2,32,1024]{3,2,1,0:T(8,128)}, f32[2,2,32,1024]{3,2,1,0:T(8,128)}...) custom-call(s32[4]{0:T(128)} %pad_add_fusion.place, ...), custom_call_target="tpu_custom_call" | custom-call | flops 3221225472 | bytes 8388608 | tf_op jit(solution)/shard_map/pallas_call | solution.py:268
  132.2 6.3 %collective-permute-done.7.a2 = f32[3,2,32,1024]{3,2,1,0:T(8,128)} collective-permute-done((f32[3,2,32,1024]{3,2,1,0:T(8,128)S(1)}, f32[3,2,32,1024]{3,2,1,0:T(8,128)}, u32[]{:S(2)}, u32[]{:S(2)}) %collective-permute-start.7) | collective-permute-done | bytes 786464 | tf_op jit(solution)/shard_map/ppermute | solution.py:53
  138.5 3.0 %shard_map.152 = (f32[3,2,32,256]{3,2,1,0:T(8,128)}, f32[3,2,32,256]{3,2,1,0:T(8,128)}, f32[3,2,32,256]{3,2,1,0:T(8,128)}, f32[3,2,32,256]{3,2,1,0:T(8,128)}) custom-call(s32[4]{0:T(128)} %pad_add_fusion.place, f32[3,2,32,1024]{3,2,1,0:T(8,128)} %get-tuple-element.74.a0.after, f32[3,2,32,1024]{3,2,1,0:T(8,128)} %copy-done.10, ...), custom_call_target="tpu_custom_call" | custom-call | flops 589824 | bytes 3932160 | tf_op jit(solution)/shard_map/pallas_call | solution.py:228
  141.5 1.2 collective-permute-done.12.a1
  142.7 1.1 collective-permute-start.10
  143.8 1.3 collective-permute-start.11
  145.1 12.8 %collective-permute-done.14.a3 = f32[3,8,32,256]{3,2,1,0:T(8,128)} collective-permute-done((f32[3,8,32,256]{3,2,1,0:T(8,128)}, f32[3,8,32,256]{3,2,1,0:T(8,128)}, u32[]{:S(2)}, u32[]{:S(2)}) %collective-permute-start.14) | collective-permute-done | bytes 786464 | tf_op jit(solution)/shard_map/ppermute | solution.py:53
  157.9 1.9 collective-permute-start.25
  159.8 1.4 collective-permute-start.26
  161.2 2.6 %collective-permute-start.30 = (f32[2,8,32,256]{3,2,1,0:T(8,128)}, f32[2,8,32,256]{3,2,1,0:T(8,128)S(1)}, u32[]{:S(2)}, u32[]{:S(2)}) collective-permute-start(f32[2,8,32,256]{3,2,1,0:T(8,128)} %get-tuple-element.103), channel_id=1, source_target_pairs={{0,2},{2,4},{4,6},{6,0},{1,3},{3,5},{5,7},{7,1},{8,10},{10,12},{12... | collective-permute-start | bytes 1572872 | tf_op jit(solution)/shard_map/ppermute | solution.py:53
  163.8 1.0 collective-permute-done.11.x3
  164.8 2.3 %collective-permute-start.31 = (f32[2,8,32,256]{3,2,1,0:T(8,128)}, f32[2,8,32,256]{3,2,1,0:T(8,128)S(1)}, u32[]{:S(2)}, u32[]{:S(2)}) collective-permute-start(f32[2,8,32,256]{3,2,1,0:T(8,128)} %get-tuple-element.104), channel_id=1, source_target_pairs={{0,4},{2,6},{4,0},{6,2},{1,5},{3,7},{5,1},{7,3},{8,12},{10,14},{12... | collective-permute-start | bytes 1572872 | tf_op jit(solution)/shard_map/ppermute | solution.py:53
  167.2 2.0 collective-permute-start.32
  169.3 3.0 %shard_map.153 = (f32[3,2,32,256]{3,2,1,0:T(8,128)}, f32[3,2,32,256]{3,2,1,0:T(8,128)}, f32[3,2,32,256]{3,2,1,0:T(8,128)}, f32[3,2,32,256]{3,2,1,0:T(8,128)}) custom-call(s32[4]{0:T(128)} %pad_add_fusion.place, f32[3,8,32,256]{3,2,1,0:T(8,128)} %get-tuple-element.82.a0, f32[3,8,32,256]{3,2,1,0:T(8,128)} %collective-permute-done.12.a1, ...), custom_call_target="tpu_custom_call" | custom-call | flops 589824 | bytes 3932160 | tf_op jit(solution)/shard_map/pallas_call | solution.py:228
  172.3 2.8 %collective-permute-start.15 = (f32[3,2,32,256]{3,2,1,0:T(8,128)}, f32[3,2,32,256]{3,2,1,0:T(8,128)S(1)}, u32[]{:S(2)}, u32[]{:S(2)}) collective-permute-start(f32[3,2,32,256]{3,2,1,0:T(8,128)} %get-tuple-element.87), channel_id=1, source_target_pairs={{0,16},{16,32},{32,48},{48,0},{1,17},{17,33},{33,49},{49,1},{2,18}... | collective-permute-start | bytes 589832 | tf_op jit(solution)/shard_map/ppermute | solution.py:53
  175.1 7.1 %collective-permute-done.26.a3 = f32[2,2,32,1024]{3,2,1,0:T(8,128)S(1)} collective-permute-done((f32[2,2,32,1024]{3,2,1,0:T(8,128)}, f32[2,2,32,1024]{3,2,1,0:T(8,128)S(1)}, u32[]{:S(2)}, u32[]{:S(2)}) %collective-permute-start.26) | collective-permute-done | bytes 524320 | tf_op jit(solution)/shard_map/ppermute | solution.py:53
  182.1 2.2 collective-permute-start.16
  184.3 2.0 collective-permute-start.17
  186.3 2.5 %shard_map.157 = (f32[2,2,32,256]{3,2,1,0:T(8,128)}, f32[2,2,32,256]{3,2,1,0:T(8,128)}, f32[2,2,32,256]{3,2,1,0:T(8,128)}, f32[2,2,32,256]{3,2,1,0:T(8,128)}) custom-call(s32[4]{0:T(128)} %pad_add_fusion.place, f32[2,2,32,1024]{3,2,1,0:T(8,128)} %get-tuple-element.94.a0, f32[2,2,32,1024]{3,2,1,0:T(8,128)} %copy-done.12, f32[2,2,32,1024]{3,2,1,0:T(8,128)} %copy-done.15, ...), custom_call_target="tpu_custom_call" | custom-call | flops 393216 | bytes 2621440 | tf_op jit(solution)/shard_map/pallas_call | solution.py:228
  188.9 3.0 %collective-permute-start.27 = (f32[2,2,32,256]{3,2,1,0:T(8,128)}, f32[2,2,32,256]{3,2,1,0:T(8,128)S(1)}, u32[]{:S(2)}, u32[]{:S(2)}) collective-permute-start(f32[2,2,32,256]{3,2,1,0:T(8,128)} %get-tuple-element.99), channel_id=1, source_target_pairs={{0,2},{2,4},{4,6},{6,0},{1,3},{3,5},{5,7},{7,1},{8,10},{10,12},{12... | collective-permute-start | bytes 393224 | tf_op jit(solution)/shard_map/ppermute | solution.py:53
  191.9 2.7 %collective-permute-start.28 = (f32[2,2,32,256]{3,2,1,0:T(8,128)}, f32[2,2,32,256]{3,2,1,0:T(8,128)S(1)}, u32[]{:S(2)}, u32[]{:S(2)}) collective-permute-start(f32[2,2,32,256]{3,2,1,0:T(8,128)} %get-tuple-element.100), channel_id=1, source_target_pairs={{0,4},{2,6},{4,0},{6,2},{1,5},{3,7},{5,1},{7,3},{8,12},{10,14},{12... | collective-permute-start | bytes 393224 | tf_op jit(solution)/shard_map/ppermute | solution.py:53
  194.6 2.5 %shard_map.158 = (f32[2,2,32,256]{3,2,1,0:T(8,128)}, f32[2,2,32,256]{3,2,1,0:T(8,128)}, f32[2,2,32,256]{3,2,1,0:T(8,128)}, f32[2,2,32,256]{3,2,1,0:T(8,128)}) custom-call(s32[4]{0:T(128)} %pad_add_fusion.place, f32[2,8,32,256]{3,2,1,0:T(8,128)} %get-tuple-element.102.a0, f32[2,8,32,256]{3,2,1,0:T(8,128)} %copy-done.13, f32[2,8,32,256]{3,2,1,0:T(8,128)} %copy-done.14, ...), custom_call_target="tpu_custom_call" | custom-call | flops 393216 | bytes 2621440 | tf_op jit(solution)/shard_map/pallas_call | solution.py:228
  197.2 1.4 collective-permute-start.29
  198.6 2.5 %collective-permute-start.34 = (f32[2,2,32,256]{3,2,1,0:T(8,128)}, f32[2,2,32,256]{3,2,1,0:T(8,128)S(1)}, u32[]{:S(2)}, u32[]{:S(2)}) collective-permute-start(f32[2,2,32,256]{3,2,1,0:T(8,128)} %get-tuple-element.108), channel_id=1, source_target_pairs={{0,32},{16,48},{32,0},{48,16},{1,33},{17,49},{33,1},{49,17},{2,34}... | collective-permute-start | bytes 393224 | tf_op jit(solution)/shard_map/ppermute | solution.py:53
  201.2 1.6 collective-permute-start.35
  202.8 2.3 %shard_map.154 = (f32[3,64,128]{2,1,0:T(8,128)}, f32[3,64,128]{2,1,0:T(8,128)}, f32[3,64,128]{2,1,0:T(8,128)}, f32[3,64,128]{2,1,0:T(8,128)}) custom-call(s32[4]{0:T(128)} %pad_add_fusion.place, f32[3,2,32,256]{3,2,1,0:T(8,128)} %get-tuple-element.78.x0, f32[3,2,32,256]{3,2,1,0:T(8,128)} %copy-done.22, f32[3,2,32,256]{3,2,1,0:T(8,128)} %copy-done.23, ...), custom_call_target="tpu_custom_call" | custom-call | flops 294912 | bytes 1966080 | tf_op jit(solution)/shard_map/pallas_call | solution.py:241
  205.5 3.6 %collective-permute-start.19 = (f32[3,64,128]{2,1,0:T(8,128)}, f32[3,64,128]{2,1,0:T(8,128)S(1)}, u32[]{:S(2)}, u32[]{:S(2)}) collective-permute-start(f32[3,64,128]{2,1,0:T(8,128)} %get-tuple-element.92), channel_id=1, source_target_pairs={{0,64},{1,65},{64,0},{65,1},{2,66},{3,67},{66,2},{67,3},{4,68},{5,... | collective-permute-start | bytes 294920 | tf_op jit(solution)/shard_map/ppermute | solution.py:53
  209.1 2.0 collective-permute-start.20
  211.1 0.6 copy-done.32
  211.8 2.1 shard_map.159
  213.9 1.8 collective-permute-start.37
  215.7 1.4 collective-permute-start.38
  217.2 3.1 %collective-permute-done.36.b1 = f32[2,64,128]{2,1,0:T(8,128)S(1)} collective-permute-done((f32[2,64,128]{2,1,0:T(8,128)}, f32[2,64,128]{2,1,0:T(8,128)S(1)}, u32[]{:S(2)}, u32[]{:S(2)}) %collective-permute-start.36) | collective-permute-done | bytes 65568 | tf_op jit(solution)/shard_map/ppermute | solution.py:53
  220.2 0.8 collective-permute-done.38.b3
  221.1 0.6 copy-done.39
  221.7 1.8 shard_map.160
  (122 shorter events, 2.9 us)
Async XLA Ops:
  0.6 15.5 %copy-start.1 = (f32[128,1024]{1,0:T(8,128)S(1)}, f32[128,1024]{1,0:T(8,128)}, u32[]{:S(2)}) copy-start(f32[128,1024]{1,0:T(8,128)} %own.2) | copy-start | bytes 1572868
  5.0 50.5 %all-to-all-start = ((f32[128,2,1024]{2,1,0:T(2,128)}), f32[128,2,1024]{2,1,0:T(2,128)S(1)}, u32[]{:S(2)}, u32[]{:S(2)}) async-start(f32[128,2,1024]{2,1,0:T(2,128)} %shard_map.147), calls=%async_computation | async-start | bytes 2097152 | tf_op jit(solution)/shard_map/all_to_all | solution.py:295
  16.1 34.3 %collective-permute-start.3 = (f32[128,1024]{1,0:T(8,128)S(1)}, f32[128,1024]{1,0:T(8,128)S(1)}, u32[]{:S(2)}, u32[]{:S(2)}) collective-permute-start(f32[128,1024]{1,0:T(8,128)S(1)} %copy-done.1), channel_id=1, source_target_pairs={{0,1},{1,2},{2,3},{3,4},{4,5},{5,6},{6,7},{7,8},{8,9},{9,10},{10,1... | collective-permute-start | bytes 1572872 | tf_op jit(solution)/shard_map/ppermute | solution.py:59
  19.2 31.3 %collective-permute-start.4 = (f32[128,1024]{1,0:T(8,128)S(1)}, f32[128,1024]{1,0:T(8,128)S(1)}, u32[]{:S(2)}, u32[]{:S(2)}) collective-permute-start(f32[128,1024]{1,0:T(8,128)S(1)} %copy-done.1), channel_id=1, source_target_pairs={{1,0},{2,1},{3,2},{4,3},{5,4},{6,5},{7,6},{8,7},{9,8},{10,9},{11,1... | collective-permute-start | bytes 1572872 | tf_op jit(solution)/shard_map/ppermute | solution.py:59
  55.4 4.7 %copy-start.41 = (f32[8,64,128]{2,1,0:T(8,128)S(1)}, f32[8,64,128]{2,1,0:T(8,128)}, u32[]{:S(2)}) copy-start(f32[8,64,128]{2,1,0:T(8,128)} %get-tuple-element.65) | copy-start | bytes 786436
  55.4 5.1 %copy-start = (f32[256,1024]{1,0:T(8,128)S(1)}, f32[256,1024]{1,0:T(8,128)}, u32[]{:S(2)}) copy-start(f32[256,1024]{1,0:T(8,128)} %own.3) | copy-start | bytes 3145732
  55.4 11.9 %collective-permute-start.5 = (f32[2,128,1024]{2,1,0:T(8,128)}, f32[2,128,1024]{2,1,0:T(8,128)}, u32[]{:S(2)}, u32[]{:S(2)}) collective-permute-start(f32[2,128,1024]{2,1,0:T(8,128)} %shard_map.149.if0), channel_id=1, source_target_pairs={{0,8},{8,0},{1,9},{9,1},{2,10},{10,2},{3,11},{11,3},{4,12},{12,4},... | collective-permute-start | bytes 3145736 | tf_op jit(solution)/shard_map/ppermute | solution.py:53
  59.6 13.1 %collective-permute-start.1 = (f32[256,1024]{1,0:T(8,128)}, f32[256,1024]{1,0:T(8,128)S(1)}, u32[]{:S(2)}, u32[]{:S(2)}) collective-permute-start(f32[256,1024]{1,0:T(8,128)} %shard_map.148.ic0), channel_id=1, source_target_pairs={{0,8},{8,0},{1,9},{9,1},{2,10},{10,2},{3,11},{11,3},{4,12},{12,4},... | collective-permute-start | bytes 3145736 | tf_op jit(solution)/shard_map/ppermute | solution.py:53
  60.0 12.6 %collective-permute-start = (f32[8,64,256]{2,1,0:T(8,128)}, f32[8,64,256]{2,1,0:T(8,128)S(1)}, u32[]{:S(2)}, u32[]{:S(2)}) collective-permute-start(f32[8,64,256]{2,1,0:T(8,128)} %get-tuple-element.63), channel_id=1, source_target_pairs={{0,8},{8,0},{1,9},{9,1},{2,10},{10,2},{3,11},{11,3},{4,12},{12,4},... | collective-permute-start | bytes 1572872 | tf_op jit(solution)/shard_map/ppermute | solution.py:53
  60.1 5.9 %collective-permute-start.2 = (f32[8,64,128]{2,1,0:T(8,128)S(1)}, f32[8,64,128]{2,1,0:T(8,128)S(1)}, u32[]{:S(2)}, u32[]{:S(2)}) collective-permute-start(f32[8,64,128]{2,1,0:T(8,128)S(1)} %copy-done.41), channel_id=1, source_target_pairs={{0,8},{8,0},{1,9},{9,1},{2,10},{10,2},{3,11},{11,3},{4,12},{12,4},... | collective-permute-start | bytes 786440 | tf_op jit(solution)/shard_map/ppermute | solution.py:53
  61.5 27.3 %collective-permute-start.21 = (f32[128,1024]{1,0:T(8,128)}, f32[128,1024]{1,0:T(8,128)S(1)}, u32[]{:S(2)}, u32[]{:S(2)}) collective-permute-start(f32[128,1024]{1,0:T(8,128)} %get-tuple-element.120), channel_id=1, source_target_pairs={{0,1},{1,2},{2,3},{3,4},{4,5},{5,6},{6,7},{7,8},{8,9},{9,10},{10,1... | collective-permute-start | bytes 1572872 | tf_op jit(solution)/shard_map/ppermute | solution.py:59
  66.0 22.9 %collective-permute-start.22 = (f32[128,1024]{1,0:T(8,128)S(1)}, f32[128,1024]{1,0:T(8,128)S(1)}, u32[]{:S(2)}, u32[]{:S(2)}) collective-permute-start(f32[128,1024]{1,0:T(8,128)S(1)} %get-tuple-element.119), channel_id=1, source_target_pairs={{1,0},{2,1},{3,2},{4,3},{5,4},{6,5},{7,6},{8,7},{9,8},{10,9},{11,1... | collective-permute-start | bytes 1572872 | tf_op jit(solution)/shard_map/ppermute | solution.py:59
  90.5 6.2 %copy-start.4 = (f32[3,2,32,1024]{3,2,1,0:T(8,128)S(1)}, f32[3,2,32,1024]{3,2,1,0:T(8,128)}, u32[]{:S(2)}) copy-start(f32[3,2,32,1024]{3,2,1,0:T(8,128)} %get-tuple-element.75) | copy-start | bytes 2359300
  90.5 10.8 %copy-start.5 = (f32[3,2,32,1024]{3,2,1,0:T(8,128)S(1)}, f32[3,2,32,1024]{3,2,1,0:T(8,128)}, u32[]{:S(2)}) copy-start(f32[3,2,32,1024]{3,2,1,0:T(8,128)} %get-tuple-element.76) | copy-start | bytes 2359300
  90.5 13.2 %copy-start.6 = (f32[3,2,32,1024]{3,2,1,0:T(8,128)S(1)}, f32[3,2,32,1024]{3,2,1,0:T(8,128)}, u32[]{:S(2)}) copy-start(f32[3,2,32,1024]{3,2,1,0:T(8,128)} %get-tuple-element.77) | copy-start | bytes 2359300
  90.5 15.0 %copy-start.7 = (f32[3,8,32,256]{3,2,1,0:T(8,128)S(1)}, f32[3,8,32,256]{3,2,1,0:T(8,128)}, u32[]{:S(2)}) copy-start(f32[3,8,32,256]{3,2,1,0:T(8,128)} %get-tuple-element.83) | copy-start | bytes 2359300
  90.5 29.8 %copy-start.8 = (f32[3,8,32,256]{3,2,1,0:T(8,128)S(1)}, f32[3,8,32,256]{3,2,1,0:T(8,128)}, u32[]{:S(2)}) copy-start(f32[3,8,32,256]{3,2,1,0:T(8,128)} %get-tuple-element.84) | copy-start | bytes 2359300
  96.7 25.3 %collective-permute-start.23 = (f32[2,256,1024]{2,1,0:T(8,128)}, f32[2,256,1024]{2,1,0:T(8,128)S(1)}, u32[]{:S(2)}, u32[]{:S(2)}) collective-permute-start(f32[2,256,1024]{2,1,0:T(8,128)} %shard_map.155.is0), channel_id=1, source_target_pairs={{0,8},{8,0},{1,9},{9,1},{2,10},{10,2},{3,11},{11,3},{4,12},{12,4},... | collective-permute-start | bytes 6291464 | tf_op jit(solution)/shard_map/ppermute | solution.py:53
  96.7 23.7 %collective-permute-start.6 = (f32[3,2,32,1024]{3,2,1,0:T(8,128)S(1)}, f32[3,2,32,1024]{3,2,1,0:T(8,128)S(1)}, u32[]{:S(2)}, u32[]{:S(2)}) collective-permute-start(f32[3,2,32,1024]{3,2,1,0:T(8,128)S(1)} %copy-done.4), channel_id=1, source_target_pairs={{0,16},{16,32},{32,48},{48,0},{1,17},{17,33},{33,49},{49,1},{2,18}... | collective-permute-start | bytes 2359304 | tf_op jit(solution)/shard_map/ppermute | solution.py:53
  101.3 37.1 %collective-permute-start.7 = (f32[3,2,32,1024]{3,2,1,0:T(8,128)S(1)}, f32[3,2,32,1024]{3,2,1,0:T(8,128)}, u32[]{:S(2)}, u32[]{:S(2)}) collective-permute-start(f32[3,2,32,1024]{3,2,1,0:T(8,128)S(1)} %copy-done.5), channel_id=1, source_target_pairs={{0,32},{16,48},{32,0},{48,16},{1,33},{17,49},{33,1},{49,17},{2,34}... | collective-permute-start | bytes 2359304 | tf_op jit(solution)/shard_map/ppermute | solution.py:53
  103.7 34.8 %collective-permute-start.8 = (f32[3,2,32,1024]{3,2,1,0:T(8,128)S(1)}, f32[3,2,32,1024]{3,2,1,0:T(8,128)}, u32[]{:S(2)}, u32[]{:S(2)}) collective-permute-start(f32[3,2,32,1024]{3,2,1,0:T(8,128)S(1)} %copy-done.6), channel_id=1, source_target_pairs={{0,48},{16,0},{32,16},{48,32},{1,49},{17,1},{33,17},{49,33},{2,50}... | collective-permute-start | bytes 2359304 | tf_op jit(solution)/shard_map/ppermute | solution.py:53
  105.5 37.2 %collective-permute-start.12 = (f32[3,8,32,256]{3,2,1,0:T(8,128)S(1)}, f32[3,8,32,256]{3,2,1,0:T(8,128)}, u32[]{:S(2)}, u32[]{:S(2)}) collective-permute-start(f32[3,8,32,256]{3,2,1,0:T(8,128)S(1)} %copy-done.7), channel_id=1, source_target_pairs={{0,2},{2,4},{4,6},{6,0},{1,3},{3,5},{5,7},{7,1},{8,10},{10,12},{12... | collective-permute-start | bytes 2359304 | tf_op jit(solution)/shard_map/ppermute | solution.py:53
  120.3 23.4 %collective-permute-start.13 = (f32[3,8,32,256]{3,2,1,0:T(8,128)S(1)}, f32[3,8,32,256]{3,2,1,0:T(8,128)S(1)}, u32[]{:S(2)}, u32[]{:S(2)}) collective-permute-start(f32[3,8,32,256]{3,2,1,0:T(8,128)S(1)} %copy-done.8), channel_id=1, source_target_pairs={{0,4},{2,6},{4,0},{6,2},{1,5},{3,7},{5,1},{7,3},{8,12},{10,14},{12... | collective-permute-start | bytes 2359304 | tf_op jit(solution)/shard_map/ppermute | solution.py:53
  123.3 34.6 %collective-permute-start.14 = (f32[3,8,32,256]{3,2,1,0:T(8,128)}, f32[3,8,32,256]{3,2,1,0:T(8,128)}, u32[]{:S(2)}, u32[]{:S(2)}) collective-permute-start(f32[3,8,32,256]{3,2,1,0:T(8,128)} %get-tuple-element.85), channel_id=1, source_target_pairs={{0,6},{2,0},{4,2},{6,4},{1,7},{3,1},{5,3},{7,5},{8,14},{10,8},{12,... | collective-permute-start | bytes 2359304 | tf_op jit(solution)/shard_map/ppermute | solution.py:53
  138.5 28.7 %collective-permute-start.24 = (f32[2,2,32,1024]{3,2,1,0:T(8,128)}, f32[2,2,32,1024]{3,2,1,0:T(8,128)S(1)}, u32[]{:S(2)}, u32[]{:S(2)}) collective-permute-start(f32[2,2,32,1024]{3,2,1,0:T(8,128)} %get-tuple-element.95), channel_id=1, source_target_pairs={{0,16},{16,32},{32,48},{48,0},{1,17},{17,33},{33,49},{49,1},{2,18}... | collective-permute-start | bytes 1572872 | tf_op jit(solution)/shard_map/ppermute | solution.py:53
  141.5 18.3 %collective-permute-start.9 = (f32[3,2,32,256]{3,2,1,0:T(8,128)}, f32[3,2,32,256]{3,2,1,0:T(8,128)S(1)}, u32[]{:S(2)}, u32[]{:S(2)}) collective-permute-start(f32[3,2,32,256]{3,2,1,0:T(8,128)} %get-tuple-element.79), channel_id=1, source_target_pairs={{0,2},{2,4},{4,6},{6,0},{1,3},{3,5},{5,7},{7,1},{8,10},{10,12},{12... | collective-permute-start | bytes 589832 | tf_op jit(solution)/shard_map/ppermute | solution.py:53
  142.7 18.5 %collective-permute-start.10 = (f32[3,2,32,256]{3,2,1,0:T(8,128)}, f32[3,2,32,256]{3,2,1,0:T(8,128)S(1)}, u32[]{:S(2)}, u32[]{:S(2)}) collective-permute-start(f32[3,2,32,256]{3,2,1,0:T(8,128)} %get-tuple-element.80), channel_id=1, source_target_pairs={{0,4},{2,6},{4,0},{6,2},{1,5},{3,7},{5,1},{7,3},{8,12},{10,14},{12... | collective-permute-start | bytes 589832 | tf_op jit(solution)/shard_map/ppermute | solution.py:53
  143.8 25.5 %copy-start.9 = (f32[3,8,32,256]{3,2,1,0:T(8,128)}, f32[3,8,32,256]{3,2,1,0:T(8,128)S(1)}, u32[]{:S(2)}) copy-start(f32[3,8,32,256]{3,2,1,0:T(8,128)S(1)} %collective-permute-done.13.a2) | copy-start | bytes 2359300
  143.8 21.1 %collective-permute-start.11 = (f32[3,2,32,256]{3,2,1,0:T(8,128)}, f32[3,2,32,256]{3,2,1,0:T(8,128)S(1)}, u32[]{:S(2)}, u32[]{:S(2)}) collective-permute-start(f32[3,2,32,256]{3,2,1,0:T(8,128)} %get-tuple-element.81), channel_id=1, source_target_pairs={{0,6},{2,0},{4,2},{6,4},{1,7},{3,1},{5,3},{7,5},{8,14},{10,8},{12,... | collective-permute-start | bytes 589832 | tf_op jit(solution)/shard_map/ppermute | solution.py:53
  157.9 14.4 %collective-permute-start.25 = (f32[2,2,32,1024]{3,2,1,0:T(8,128)}, f32[2,2,32,1024]{3,2,1,0:T(8,128)S(1)}, u32[]{:S(2)}, u32[]{:S(2)}) collective-permute-start(f32[2,2,32,1024]{3,2,1,0:T(8,128)} %get-tuple-element.96), channel_id=1, source_target_pairs={{0,32},{16,48},{32,0},{48,16},{1,33},{17,49},{33,1},{49,17},{2,34}... | collective-permute-start | bytes 1572872 | tf_op jit(solution)/shard_map/ppermute | solution.py:53
  159.8 29.1 %copy-start.22 = (f32[3,2,32,256]{3,2,1,0:T(8,128)}, f32[3,2,32,256]{3,2,1,0:T(8,128)S(1)}, u32[]{:S(2)}) copy-start(f32[3,2,32,256]{3,2,1,0:T(8,128)S(1)} %collective-permute-done.9.x1) | copy-start | bytes 589828
  159.8 22.3 %collective-permute-start.26 = (f32[2,2,32,1024]{3,2,1,0:T(8,128)}, f32[2,2,32,1024]{3,2,1,0:T(8,128)S(1)}, u32[]{:S(2)}, u32[]{:S(2)}) collective-permute-start(f32[2,2,32,1024]{3,2,1,0:T(8,128)} %get-tuple-element.97), channel_id=1, source_target_pairs={{0,48},{16,0},{32,16},{48,32},{1,49},{17,1},{33,17},{49,33},{2,50}... | collective-permute-start | bytes 1572872 | tf_op jit(solution)/shard_map/ppermute | solution.py:53
  161.2 5.9 %copy-start.23 = (f32[3,2,32,256]{3,2,1,0:T(8,128)}, f32[3,2,32,256]{3,2,1,0:T(8,128)S(1)}, u32[]{:S(2)}) copy-start(f32[3,2,32,256]{3,2,1,0:T(8,128)S(1)} %collective-permute-done.10.x2) | copy-start | bytes 589828
  161.2 23.1 %collective-permute-start.30 = (f32[2,8,32,256]{3,2,1,0:T(8,128)}, f32[2,8,32,256]{3,2,1,0:T(8,128)S(1)}, u32[]{:S(2)}, u32[]{:S(2)}) collective-permute-start(f32[2,8,32,256]{3,2,1,0:T(8,128)} %get-tuple-element.103), channel_id=1, source_target_pairs={{0,2},{2,4},{4,6},{6,0},{1,3},{3,5},{5,7},{7,1},{8,10},{10,12},{12... | collective-permute-start | bytes 1572872 | tf_op jit(solution)/shard_map/ppermute | solution.py:53
  164.8 24.1 %collective-permute-start.31 = (f32[2,8,32,256]{3,2,1,0:T(8,128)}, f32[2,8,32,256]{3,2,1,0:T(8,128)S(1)}, u32[]{:S(2)}, u32[]{:S(2)}) collective-permute-start(f32[2,8,32,256]{3,2,1,0:T(8,128)} %get-tuple-element.104), channel_id=1, source_target_pairs={{0,4},{2,6},{4,0},{6,2},{1,5},{3,7},{5,1},{7,3},{8,12},{10,14},{12... | collective-permute-start | bytes 1572872 | tf_op jit(solution)/shard_map/ppermute | solution.py:53
  167.2 19.1 %copy-start.12 = (f32[2,2,32,1024]{3,2,1,0:T(8,128)}, f32[2,2,32,1024]{3,2,1,0:T(8,128)S(1)}, u32[]{:S(2)}) copy-start(f32[2,2,32,1024]{3,2,1,0:T(8,128)S(1)} %collective-permute-done.24.a1) | copy-start | bytes 1572868
  167.2 24.7 %collective-permute-start.32 = (f32[2,8,32,256]{3,2,1,0:T(8,128)}, f32[2,8,32,256]{3,2,1,0:T(8,128)S(1)}, u32[]{:S(2)}, u32[]{:S(2)}) collective-permute-start(f32[2,8,32,256]{3,2,1,0:T(8,128)} %get-tuple-element.105), channel_id=1, source_target_pairs={{0,6},{2,0},{4,2},{6,4},{1,7},{3,1},{5,3},{7,5},{8,14},{10,8},{12,... | collective-permute-start | bytes 1572872 | tf_op jit(solution)/shard_map/ppermute | solution.py:53
  172.3 14.1 %copy-start.15 = (f32[2,2,32,1024]{3,2,1,0:T(8,128)}, f32[2,2,32,1024]{3,2,1,0:T(8,128)S(1)}, u32[]{:S(2)}) copy-start(f32[2,2,32,1024]{3,2,1,0:T(8,128)S(1)} %collective-permute-done.25.a2) | copy-start | bytes 1572868
  172.3 24.9 %collective-permute-start.15 = (f32[3,2,32,256]{3,2,1,0:T(8,128)}, f32[3,2,32,256]{3,2,1,0:T(8,128)S(1)}, u32[]{:S(2)}, u32[]{:S(2)}) collective-permute-start(f32[3,2,32,256]{3,2,1,0:T(8,128)} %get-tuple-element.87), channel_id=1, source_target_pairs={{0,16},{16,32},{32,48},{48,0},{1,17},{17,33},{33,49},{49,1},{2,18}... | collective-permute-start | bytes 589832 | tf_op jit(solution)/shard_map/ppermute | solution.py:53
  182.1 4.2 %copy-start.17 = (f32[2,2,32,1024]{3,2,1,0:T(8,128)}, f32[2,2,32,1024]{3,2,1,0:T(8,128)S(1)}, u32[]{:S(2)}) copy-start(f32[2,2,32,1024]{3,2,1,0:T(8,128)S(1)} %collective-permute-done.26.a3) | copy-start | bytes 1572868
  182.1 16.4 %collective-permute-start.16 = (f32[3,2,32,256]{3,2,1,0:T(8,128)}, f32[3,2,32,256]{3,2,1,0:T(8,128)S(1)}, u32[]{:S(2)}, u32[]{:S(2)}) collective-permute-start(f32[3,2,32,256]{3,2,1,0:T(8,128)} %get-tuple-element.88), channel_id=1, source_target_pairs={{0,32},{16,48},{32,0},{48,16},{1,33},{17,49},{33,1},{49,17},{2,34}... | collective-permute-start | bytes 589832 | tf_op jit(solution)/shard_map/ppermute | solution.py:53
  184.3 10.3 %copy-start.13 = (f32[2,8,32,256]{3,2,1,0:T(8,128)}, f32[2,8,32,256]{3,2,1,0:T(8,128)S(1)}, u32[]{:S(2)}) copy-start(f32[2,8,32,256]{3,2,1,0:T(8,128)S(1)} %collective-permute-done.30.a1) | copy-start | bytes 1572868
  184.3 14.3 %collective-permute-start.17 = (f32[3,2,32,256]{3,2,1,0:T(8,128)}, f32[3,2,32,256]{3,2,1,0:T(8,128)S(1)}, u32[]{:S(2)}, u32[]{:S(2)}) collective-permute-start(f32[3,2,32,256]{3,2,1,0:T(8,128)} %get-tuple-element.89), channel_id=1, source_target_pairs={{0,48},{16,0},{32,16},{48,32},{1,49},{17,1},{33,17},{49,33},{2,50}... | collective-permute-start | bytes 589832 | tf_op jit(solution)/shard_map/ppermute | solution.py:53
  188.9 8.3 %copy-start.43 = (f32[2,2,32,256]{3,2,1,0:T(8,128)S(1)}, f32[2,2,32,256]{3,2,1,0:T(8,128)}, u32[]{:S(2)}) copy-start(f32[2,2,32,256]{3,2,1,0:T(8,128)} %get-tuple-element.101) | copy-start | bytes 393220
  188.9 5.7 %copy-start.14 = (f32[2,8,32,256]{3,2,1,0:T(8,128)}, f32[2,8,32,256]{3,2,1,0:T(8,128)S(1)}, u32[]{:S(2)}) copy-start(f32[2,8,32,256]{3,2,1,0:T(8,128)S(1)} %collective-permute-done.31.a2) | copy-start | bytes 1572868
  188.9 12.2 %collective-permute-start.27 = (f32[2,2,32,256]{3,2,1,0:T(8,128)}, f32[2,2,32,256]{3,2,1,0:T(8,128)S(1)}, u32[]{:S(2)}, u32[]{:S(2)}) collective-permute-start(f32[2,2,32,256]{3,2,1,0:T(8,128)} %get-tuple-element.99), channel_id=1, source_target_pairs={{0,2},{2,4},{4,6},{6,0},{1,3},{3,5},{5,7},{7,1},{8,10},{10,12},{12... | collective-permute-start | bytes 393224 | tf_op jit(solution)/shard_map/ppermute | solution.py:53
  191.9 13.2 %collective-permute-start.28 = (f32[2,2,32,256]{3,2,1,0:T(8,128)}, f32[2,2,32,256]{3,2,1,0:T(8,128)S(1)}, u32[]{:S(2)}, u32[]{:S(2)}) collective-permute-start(f32[2,2,32,256]{3,2,1,0:T(8,128)} %get-tuple-element.100), channel_id=1, source_target_pairs={{0,4},{2,6},{4,0},{6,2},{1,5},{3,7},{5,1},{7,3},{8,12},{10,14},{12... | collective-permute-start | bytes 393224 | tf_op jit(solution)/shard_map/ppermute | solution.py:53
  197.2 5.6 %copy-start.25 = (f32[3,2,32,256]{3,2,1,0:T(8,128)}, f32[3,2,32,256]{3,2,1,0:T(8,128)S(1)}, u32[]{:S(2)}) copy-start(f32[3,2,32,256]{3,2,1,0:T(8,128)S(1)} %collective-permute-done.15.y1) | copy-start | bytes 589828
  197.2 8.3 %collective-permute-start.29 = (f32[2,2,32,256]{3,2,1,0:T(8,128)S(1)}, f32[2,2,32,256]{3,2,1,0:T(8,128)S(1)}, u32[]{:S(2)}, u32[]{:S(2)}) collective-permute-start(f32[2,2,32,256]{3,2,1,0:T(8,128)S(1)} %copy-done.43), channel_id=1, source_target_pairs={{0,6},{2,0},{4,2},{6,4},{1,7},{3,1},{5,3},{7,5},{8,14},{10,8},{12,... | collective-permute-start | bytes 393224 | tf_op jit(solution)/shard_map/ppermute | solution.py:53
  198.6 4.2 %copy-start.26 = (f32[3,2,32,256]{3,2,1,0:T(8,128)}, f32[3,2,32,256]{3,2,1,0:T(8,128)S(1)}, u32[]{:S(2)}) copy-start(f32[3,2,32,256]{3,2,1,0:T(8,128)S(1)} %collective-permute-done.16.y2) | copy-start | bytes 589828
  198.6 10.5 %collective-permute-start.33 = (f32[2,2,32,256]{3,2,1,0:T(8,128)}, f32[2,2,32,256]{3,2,1,0:T(8,128)S(1)}, u32[]{:S(2)}, u32[]{:S(2)}) collective-permute-start(f32[2,2,32,256]{3,2,1,0:T(8,128)} %get-tuple-element.107), channel_id=1, source_target_pairs={{0,16},{16,32},{32,48},{48,0},{1,17},{17,33},{33,49},{49,1},{2,18}... | collective-permute-start | bytes 393224 | tf_op jit(solution)/shard_map/ppermute | solution.py:53
  198.6 4.2 %copy-start.27 = (f32[3,2,32,256]{3,2,1,0:T(8,128)}, f32[3,2,32,256]{3,2,1,0:T(8,128)S(1)}, u32[]{:S(2)}) copy-start(f32[3,2,32,256]{3,2,1,0:T(8,128)S(1)} %collective-permute-done.17.y3) | copy-start | bytes 589828
  198.6 12.5 %collective-permute-start.34 = (f32[2,2,32,256]{3,2,1,0:T(8,128)}, f32[2,2,32,256]{3,2,1,0:T(8,128)S(1)}, u32[]{:S(2)}, u32[]{:S(2)}) collective-permute-start(f32[2,2,32,256]{3,2,1,0:T(8,128)} %get-tuple-element.108), channel_id=1, source_target_pairs={{0,32},{16,48},{32,0},{48,16},{1,33},{17,49},{33,1},{49,17},{2,34}... | collective-permute-start | bytes 393224 | tf_op jit(solution)/shard_map/ppermute | solution.py:53
  201.2 9.9 %copy-start.28 = (f32[2,2,32,256]{3,2,1,0:T(8,128)}, f32[2,2,32,256]{3,2,1,0:T(8,128)S(1)}, u32[]{:S(2)}) copy-start(f32[2,2,32,256]{3,2,1,0:T(8,128)S(1)} %collective-permute-done.27.x1) | copy-start | bytes 393220
  201.2 9.9 %collective-permute-start.35 = (f32[2,2,32,256]{3,2,1,0:T(8,128)}, f32[2,2,32,256]{3,2,1,0:T(8,128)S(1)}, u32[]{:S(2)}, u32[]{:S(2)}) collective-permute-start(f32[2,2,32,256]{3,2,1,0:T(8,128)} %get-tuple-element.109), channel_id=1, source_target_pairs={{0,48},{16,0},{32,16},{48,32},{1,49},{17,1},{33,17},{49,33},{2,50}... | collective-permute-start | bytes 393224 | tf_op jit(solution)/shard_map/ppermute | solution.py:53
  205.1 6.0 %copy-start.29 = (f32[2,2,32,256]{3,2,1,0:T(8,128)}, f32[2,2,32,256]{3,2,1,0:T(8,128)S(1)}, u32[]{:S(2)}) copy-start(f32[2,2,32,256]{3,2,1,0:T(8,128)S(1)} %collective-permute-done.28.x2) | copy-start | bytes 393220
  205.1 10.6 %collective-permute-start.18 = (f32[3,64,128]{2,1,0:T(8,128)}, f32[3,64,128]{2,1,0:T(8,128)S(1)}, u32[]{:S(2)}, u32[]{:S(2)}) collective-permute-start(f32[3,64,128]{2,1,0:T(8,128)} %get-tuple-element.91), channel_id=1, source_target_pairs={{0,1},{1,64},{64,65},{65,0},{2,3},{3,66},{66,67},{67,2},{4,5},{5,6... | collective-permute-start | bytes 294920 | tf_op jit(solution)/shard_map/ppermute | solution.py:53
  205.5 5.6 %copy-start.30 = (f32[2,2,32,256]{3,2,1,0:T(8,128)}, f32[2,2,32,256]{3,2,1,0:T(8,128)S(1)}, u32[]{:S(2)}) copy-start(f32[2,2,32,256]{3,2,1,0:T(8,128)S(1)} %collective-permute-done.29.x3) | copy-start | bytes 393220
  205.5 11.6 %collective-permute-start.19 = (f32[3,64,128]{2,1,0:T(8,128)}, f32[3,64,128]{2,1,0:T(8,128)S(1)}, u32[]{:S(2)}, u32[]{:S(2)}) collective-permute-start(f32[3,64,128]{2,1,0:T(8,128)} %get-tuple-element.92), channel_id=1, source_target_pairs={{0,64},{1,65},{64,0},{65,1},{2,66},{3,67},{66,2},{67,3},{4,68},{5,... | collective-permute-start | bytes 294920 | tf_op jit(solution)/shard_map/ppermute | solution.py:53
  209.1 8.1 %collective-permute-start.20 = (f32[3,64,128]{2,1,0:T(8,128)}, f32[3,64,128]{2,1,0:T(8,128)S(1)}, u32[]{:S(2)}, u32[]{:S(2)}) collective-permute-start(f32[3,64,128]{2,1,0:T(8,128)} %get-tuple-element.93), channel_id=1, source_target_pairs={{0,65},{1,0},{64,1},{65,64},{2,67},{3,2},{66,3},{67,66},{4,69},{5,... | collective-permute-start | bytes 294920 | tf_op jit(solution)/shard_map/ppermute | solution.py:53
  213.8 6.4 %collective-permute-start.36 = (f32[2,64,128]{2,1,0:T(8,128)}, f32[2,64,128]{2,1,0:T(8,128)S(1)}, u32[]{:S(2)}, u32[]{:S(2)}) collective-permute-start(f32[2,64,128]{2,1,0:T(8,128)} %get-tuple-element.111), channel_id=1, source_target_pairs={{0,1},{1,64},{64,65},{65,0},{2,3},{3,66},{66,67},{67,2},{4,5},{5,6... | collective-permute-start | bytes 196616 | tf_op jit(solution)/shard_map/ppermute | solution.py:53
  213.9 6.3 %collective-permute-start.37 = (f32[2,64,128]{2,1,0:T(8,128)}, f32[2,64,128]{2,1,0:T(8,128)S(1)}, u32[]{:S(2)}, u32[]{:S(2)}) collective-permute-start(f32[2,64,128]{2,1,0:T(8,128)} %get-tuple-element.112), channel_id=1, source_target_pairs={{0,64},{1,65},{64,0},{65,1},{2,66},{3,67},{66,2},{67,3},{4,68},{5,... | collective-permute-start | bytes 196616 | tf_op jit(solution)/shard_map/ppermute | solution.py:53
  215.7 5.4 %copy-start.34 = (f32[3,64,128]{2,1,0:T(8,128)}, f32[3,64,128]{2,1,0:T(8,128)S(1)}, u32[]{:S(2)}) copy-start(f32[3,64,128]{2,1,0:T(8,128)S(1)} %collective-permute-done.18.a1) | copy-start | bytes 294916
  215.7 5.4 %collective-permute-start.38 = (f32[2,64,128]{2,1,0:T(8,128)}, f32[2,64,128]{2,1,0:T(8,128)S(1)}, u32[]{:S(2)}, u32[]{:S(2)}) collective-permute-start(f32[2,64,128]{2,1,0:T(8,128)} %get-tuple-element.113), channel_id=1, source_target_pairs={{0,65},{1,0},{64,1},{65,64},{2,67},{3,2},{66,3},{67,66},{4,69},{5,... | collective-permute-start | bytes 196616 | tf_op jit(solution)/shard_map/ppermute | solution.py:53
  (20 other events, 29.4 us)

commit v3 on v2

--- a/solution.py
+++ b/solution.py
@@ -59,10 +59,11 @@
     return lax.ppermute(value, AXES, pairs)
 
 
-def route_kernel(dest_col, dest_row, rows, fluid, out):
+def route_kernel(dest_row, rows, fluid, out):
     n = dest_row.shape[1]
+    dest = jnp.broadcast_to(dest_row[...].astype(F32), (n, n))
     earlier = lax.broadcasted_iota(jnp.int32, (n, n), 0) < lax.broadcasted_iota(jnp.int32, (n, n), 1)
-    same = (dest_col[...] == dest_row[...]) & earlier
+    same = (dest.T == dest) & earlier
     slot = jnp.sum(jnp.where(same, 1.0, 0.0), axis=0, keepdims=True).astype(jnp.int32)
     target = dest_row[...] * CAP + slot
     q = out.shape[0] * CAP
@@ -161,14 +162,14 @@
 
 
 def wet_product_kernel(place, ls0, ls1, ic0, ic1, *rest):
-    outs, (sh, sl, held) = rest[8:16], rest[16:]
+    outs, (sh, sl, held) = rest[:8], rest[8:]
     sh[...], sl[...] = parts(joined(ls0, ls1))
     multiply(held, (sh, sl), ic0[...], ic1[...])
     send_off(place, held, outs)
 
 
 def second_kernel(place, ls0, ls1, is0, is1, *rest):
-    outs, (sh, sl, held) = rest[:8], rest[8:]
+    outs, (sh, sl, held) = rest[8:16], rest[16:]
 
     @pl.when(pl.program_id(0) == 0)
     def _():
@@ -189,20 +190,23 @@
                 out[:, h] = held[:, h * 4 + d]
 
 
-def spread_kernel(place, x0, x1, x2, x3, y0, y1, y2, y3, o0, o1, o2, o3, held):
-    held[:, :, 0:HALF] = (x0[...] + x1[...]) + (x2[...] + x3[...])
-    held[:, :, HALF:] = (y0[...] + y1[...]) + (y2[...] + y3[...])
-    for o, out in enumerate((o0, o1, o2, o3)):
+def spread_kernel(place, *refs):
+    ins, outs, held = refs[:16], refs[16:20], refs[20]
+    at = 0
+    for x, y in ((ins[0:4], ins[4:8]), (ins[8:12], ins[12:16])):
+        rows = slice(at, at + x[0].shape[0])
+        held[rows, :, 0:HALF] = (x[0][...] + x[1][...]) + (x[2][...] + x[3][...])
+        held[rows, :, HALF:] = (y[0][...] + y[1][...]) + (y[2][...] + y[3][...])
+        at = rows.stop
+    for o, out in enumerate(outs):
         d = lax.rem(place[2] + o, 4)
         lanes = pl.ds(pl.multiple_of(lax.rem(d, 2) * 128, 128), 128)
         out[...] = held[:, d // 2, :, lanes]
 
 
-def last_kernel(a0, a1, a2, a3, b0, b1, b2, b3, fstiff, fmass, wet, stiff, mass):
-    for m, out in enumerate((fstiff, fmass, wet)):
+def last_kernel(a0, a1, a2, a3, *outs):
+    for m, out in enumerate(outs):
         out[...] = (a0[m] + a1[m]) + (a2[m] + a3[m])
-    for m, out in enumerate((stiff, mass)):
-        out[...] = (b0[m] + b1[m]) + (b2[m] + b3[m])
 
 
 def call(kernel, out, count, smem=0, anywhere=0, scratch=(), flops=0, moved=0):
@@ -236,17 +240,16 @@
     )(place, *arrived)
 
 
-def spread(place, x, y):
-    count = x[0].shape[0]
+def spread(place, *arrived):
     return call(
         spread_kernel,
-        [shape(count, 64, 128)] * 4,
-        9,
-        smem=1,
-        scratch=[pltpu.VMEM((count, 2, 64, 256), F32)],
-        flops=6 * x[0].size,
-        moved=40 * x[0].size,
-    )(place, *x, *y)
+        [shape(5, 64, 128)] * 4,
+        17,
+        smem=1,
+        scratch=[pltpu.VMEM((5, 2, 64, 256), F32)],
+        flops=2**20,
+        moved=2**22,
+    )(place, *arrived)
 
 
 def partial_sums(kernel, steps, at, count, place, lefts, depth, operands, specs, carried=()):
@@ -289,8 +292,8 @@
     below_f = from_behind(fluid_basis, 1)
     above_f = from_behind(fluid_basis, -1)
 
-    outgoing = call(route_kernel, shape(128, CAP, R), 4, flops=2 * 3 * 256 * 128 * R, moved=2**21)(
-        wet_dest, wet_dest.reshape(1, -1), wet_rows.reshape(1, -1), fluid_basis
+    outgoing = call(route_kernel, shape(128, CAP, R), 3, flops=2 * 3 * 256 * 128 * R, moved=2**21)(
+        wet_dest.reshape(1, -1), wet_rows.reshape(1, -1), fluid_basis
     )
     received = lax.all_to_all(outgoing, AXES, split_axis=0, concat_axis=0, tiled=True)
 
@@ -324,11 +327,8 @@
     def block(rows):
         return pl.BlockSpec((1, rows, R), lambda m: (m, 0, 0))
 
-    fluid = partial_sums(
-        fluid_product_kernel, 2, 0, 3, place, (own_f, left_f), 256, (image_f, other_f), [block(128)] * 2
-    )
     first = partial_sums(
-        wet_product_kernel, 1, 2, 3, place, (own_s, left_s), 512, (image_c, other_c), [VMEM] * 2, fluid
+        fluid_product_kernel, 2, 0, 2, place, (own_f, left_f), 256, (image_f, other_f), [block(128)] * 2
     )
     first_x = exchanged(first[0:4], X)
     first_y = exchanged(first[4:8], Y)
@@ -345,7 +345,10 @@
     )(struct_cols, stiff_tiles, mass_tiles, below_s, struct_basis, above_s, first[0])
     other_s = shifted(image_s, "core", 1)
 
-    second = partial_sums(second_kernel, 2, 0, 2, place, (own_s, left_s), 512, (image_s, other_s), [block(256)] * 2)
+    wet = partial_sums(wet_product_kernel, 1, 2, 3, place, (own_s, left_s), 512, (image_c, other_c), [VMEM] * 2)
+    second = partial_sums(
+        second_kernel, 2, 0, 3, place, (own_s, left_s), 512, (image_s, other_s), [block(256)] * 2, wet
+    )
     second_x = exchanged(second[0:4], X)
     second_y = exchanged(second[4:8], Y)
 
@@ -353,11 +356,8 @@
     first_yx = exchanged(split(place, first_y, 0), X)
     second_xy = exchanged(split(place, second_x, 1), Y)
     second_yx = exchanged(split(place, second_y, 0), X)
-    first_z = exchanged(spread(place, first_xy, first_yx), Z)
-    second_z = exchanged(spread(place, second_xy, second_yx), Z)
-    fstiff, fmass, wet, stiff, mass = call(
-        last_kernel, [shape(64, 128)] * 5, 8, flops=2**18, moved=2**20
-    )(*first_z, *second_z)
+    summed = exchanged(spread(place, *first_xy, *first_yx, *second_xy, *second_yx), Z)
+    fstiff, fmass, stiff, mass, wet = call(last_kernel, [shape(64, 128)] * 5, 4, flops=2**18, moved=2**20)(*summed)
     return stiff, mass, fstiff, fmass, wet
 
 

time: 224 us -> 220 us (0.982)
  starting transfers between devices: 74.3 us -> 79 us
  waiting for transfers between devices: 83.5 us -> 79 us
  local copies, waits for them, and re-layouts: 9.89 us -> 6.77 us
    ppermute x4, waiting for transfers between devices: 36.3 us -> 25 us  [from_behind(): return lax.ppermute(value, AXES, pairs)]
    ppermute x35 -> x32, waiting for transfers between devices: 47.2 us -> 54.1 us  [shifted(): lax.ppermute(value, axis, [(i, (i + by) % size) for i in range(size)])]
    ppermute x4, starting transfers between devices: 10 us -> 12.8 us  [from_behind(): return lax.ppermute(value, AXES, pairs)]
    unnamed x89 -> x72, local copies, waits for them, and re-layouts: 8.93 us -> 6.7 us
    pallas_call x4 -> x3, Pallas kernels: 9.05 us -> 7.46 us  [the longest x1 2.86 us: compute(): call(route_kernel, shape(128, CAP, R), 3, flops=2 * 3 * 256 * 128 * R, mo...]
    ppermute x35 -> x32, starting transfers between devices: 53.1 us -> 54.6 us  [shifted(): lax.ppermute(value, axis, [(i, (i + by) % size) for i in range(size)])]
  transfers between devices with their start and end apart: 40 -> 37, of which waited for: 10 -> 17; matrix products, arithmetic and copies ran while one was open for 1% -> 0% of each run, Pallas kernels for 19% -> 20%
where the time goes in v3:
time: 220 us; the launch traced here: 219 us
  starting transfers between devices  79 us (36%)
  waiting for transfers between devices  79 us (36%)
  Pallas kernels  52.7 us (24%)
  local copies, waits for them, and re-layouts  6.77 us (3%)
    ppermute x32, starting transfers between devices, shifted(): lax.ppermute(value, axis, [(i, (i + by) % size) for i in range(size)])  54.6 us
    ppermute x32, waiting for transfers between devices, shifted(): lax.ppermute(value, axis, [(i, (i + by) % size) for i in range(size)])  54.1 us
    ppermute x4, waiting for transfers between devices, from_behind(): return lax.ppermute(value, AXES, pairs)  25 us
    pallas_call x3, Pallas kernels, partial_sums(): return run(place, *lefts, *operands, *carried)  18 us
    ppermute x4, starting transfers between devices, from_behind(): return lax.ppermute(value, AXES, pairs)  12.8 us
    all_to_all x1, starting transfers between devices, compute(): lax.all_to_all(outgoing, AXES, split_axis=0, concat_axis=0, tiled=True)  11.6 us
    pallas_call x4, Pallas kernels, split(): call(functools.partial(split_kernel, axis), [shape(count, 2, HALF, 256)]...  11.2 us
    unnamed x72, local copies, waits for them, and re-layouts  6.7 us
  transfers between devices with their start and end apart: 37, of which 17 were waited for; matrix products, arithmetic and copies ran while one was open for 0% of the time, Pallas kernels for 20%

profile of v3, /device:TPU:0, one launch (start us, length us, event | category | flops | bytes accessed | tf_op | source)
XLA Modules:
  0.0 219.1 jit_solution(3762734412195330739)
XLA Ops:
  0.6 1.3 collective-permute-start.2
  1.9 4.6 %collective-permute-start.1 = (f32[128,1024]{1,0:T(8,128)}, f32[128,1024]{1,0:T(8,128)S(1)}, u32[]{:S(2)}, u32[]{:S(2)}) collective-permute-start(f32[128,1024]{1,0:T(8,128)} %fluid.3), channel_id=1, source_target_pairs={{0,1},{1,2},{2,3},{3,4},{4,5},{5,6},{6,7},{7,8},{8,9},{9,10},{10,1... | collective-permute-start | bytes 1572872 | tf_op jit(solution)/shard_map/ppermute | solution.py:59
  6.5 0.6 pad_add_fusion.place
  7.1 3.0 %shard_map.146 = (f32[8,64,256]{2,1,0:T(8,128)}, f32[8,64,256]{2,1,0:T(8,128)}, f32[8,64,128]{2,1,0:T(8,128)}, f32[8,64,128]{2,1,0:T(8,128)}) custom-call(s32[4]{0:T(128)} %pad_add_fusion.place, f32[256,1024]{1,0:T(8,128)} %own.3, f32[128,1024]{1,0:T(8,128)} %fluid.3), custom_call_target="tpu_custom_call" | custom-call | flops 1048576 | bytes 3145728 | tf_op jit(solution)/shard_map/pallas_call | solution.py:300
  10.1 10.1 %collective-permute-done.2.hi = f32[128,1024]{1,0:T(8,128)S(1)} collective-permute-done((f32[128,1024]{1,0:T(8,128)}, f32[128,1024]{1,0:T(8,128)S(1)}, u32[]{:S(2)}, u32[]{:S(2)}) %collective-permute-start.2) | collective-permute-done | bytes 524320 | tf_op jit(solution)/shard_map/ppermute | solution.py:59
  20.2 7.9 %collective-permute-done.1.lo = f32[128,1024]{1,0:T(8,128)S(1)} collective-permute-done((f32[128,1024]{1,0:T(8,128)}, f32[128,1024]{1,0:T(8,128)S(1)}, u32[]{:S(2)}, u32[]{:S(2)}) %collective-permute-start.1) | collective-permute-done | bytes 524320 | tf_op jit(solution)/shard_map/ppermute | solution.py:59
  28.1 0.8 copy-done.14
  28.9 4.0 %shard_map.147.if0 = f32[2,128,1024]{2,1,0:T(8,128)} custom-call(s32[1,4]{1,0:T(1,128)} %cols.2, f32[1,4,128,128]{3,2,1,0:T(8,128)} %stiff.2, f32[1,4,128,128]{3,2,1,0:T(8,128)} %mass.2, f32[128,1024]{1,0:T(8,128)} %copy-done.14, f32[128,1024]{1,0:T(8,128)} %fluid.3, f32[128,1024]{1,0:T(8,128)} %copy-done.13, f32[8,64,256]{2,1,0:T(8,128)} %get-tuple-element.60.after.ls0), custom_call_target="tpu_custom_call" | custom-call | flops 603979776 | bytes 3145728 | tf_op jit(solution)/shard_map/pallas_call | solution.py:315
  33.2 1.3 collective-permute-start.18
  34.5 5.6 %collective-permute-start.17 = (f32[128,1024]{1,0:T(8,128)S(1)}, f32[128,1024]{1,0:T(8,128)}, u32[]{:S(2)}, u32[]{:S(2)}) collective-permute-start(f32[128,1024]{1,0:T(8,128)S(1)} %get-tuple-element.112), channel_id=1, source_target_pairs={{0,1},{1,2},{2,3},{3,4},{4,5},{5,6},{6,7},{7,8},{8,9},{9,10},{10,1... | collective-permute-start | bytes 1572872 | tf_op jit(solution)/shard_map/ppermute | solution.py:59
  40.1 3.1 %collective-permute-start = (f32[8,64,128]{2,1,0:T(8,128)S(1)}, f32[8,64,128]{2,1,0:T(8,128)}, u32[]{:S(2)}, u32[]{:S(2)}) collective-permute-start(f32[8,64,128]{2,1,0:T(8,128)S(1)} %copy-done.32), channel_id=1, source_target_pairs={{0,8},{8,0},{1,9},{9,1},{2,10},{10,2},{3,11},{11,3},{4,12},{12,4},... | collective-permute-start | bytes 786440 | tf_op jit(solution)/shard_map/ppermute | solution.py:53
  43.1 2.9 %shard_map.152 = f32[128,2,1024]{2,1,0:T(2,128)} custom-call(s32[1,128]{1,0:T(1,128)} %bitcast.6, s32[1,128]{1,0:T(1,128)} %bitcast.7, f32[128,1024]{1,0:T(8,128)} %fluid.3), custom_call_target="tpu_custom_call" | custom-call | flops 201326592 | bytes 2097152 | tf_op jit(solution)/shard_map/pallas_call | solution.py:295
  46.0 11.6 %all-to-all-start = ((f32[128,2,1024]{2,1,0:T(2,128)}), f32[128,2,1024]{2,1,0:T(2,128)S(1)}, u32[]{:S(2)}, u32[]{:S(2)}) async-start(f32[128,2,1024]{2,1,0:T(2,128)} %shard_map.152), calls=%async_computation | async-start | bytes 2097152 | tf_op jit(solution)/shard_map/all_to_all | solution.py:298
  57.7 1.0 copy-done.30
  58.7 5.3 %shard_map.148 = (f32[2,2,32,1024]{3,2,1,0:T(8,128)}, f32[2,2,32,1024]{3,2,1,0:T(8,128)}, f32[2,2,32,1024]{3,2,1,0:T(8,128)}, f32[2,2,32,1024]{3,2,1,0:T(8,128)}...) custom-call(s32[4]{0:T(128)} %pad_add_fusion.place, ...), custom_call_target="tpu_custom_call" | custom-call | flops 1610612736 | bytes 8388608 | tf_op jit(solution)/shard_map/pallas_call | solution.py:271
  64.0 7.0 %collective-permute-done.17.lo = f32[128,1024]{1,0:T(8,128)} collective-permute-done((f32[128,1024]{1,0:T(8,128)S(1)}, f32[128,1024]{1,0:T(8,128)}, u32[]{:S(2)}, u32[]{:S(2)}) %collective-permute-start.17) | collective-permute-done | bytes 524320 | tf_op jit(solution)/shard_map/ppermute | solution.py:59
  71.0 5.9 %shard_map.151.is0 = f32[2,256,1024]{2,1,0:T(8,128)} custom-call(s32[2,4]{1,0:T(2,128)} %cols.3, f32[2,4,128,128]{3,2,1,0:T(8,128)} %stiff.3, f32[2,4,128,128]{3,2,1,0:T(8,128)} %mass.3, f32[128,1024]{1,0:T(8,128)} %collective-permute-done.17.lo, f32[256,1024]{1,0:T(8,128)} %own.3, f32[128,1024]{1,0:T(8,128)} %collective-permute-done.18.hi, ...), custom_call_target="tpu_custom_call" | custom-call | flops 1610612736 | bytes 5242880 | tf_op jit(solution)/shard_map/pallas_call | solution.py:336
  76.9 0.4 collective-permute-start.19
  77.4 1.0 copy-done.1
  78.4 3.1 %shard_map.153.ic0 = f32[256,1024]{1,0:T(8,128)} custom-call(f32[256,256]{1,0:T(8,128)} %coupling.1, f32[128,2,1024]{2,1,0:T(2,128)} %copy-done.1), custom_call_target="tpu_custom_call" | custom-call | flops 402653184 | bytes 2097152 | tf_op jit(solution)/shard_map/pallas_call | solution.py:312
  81.6 0.4 collective-permute-start.16
  82.0 1.9 collective-permute-start.4
  83.9 2.7 %collective-permute-start.5 = (f32[2,2,32,1024]{3,2,1,0:T(8,128)}, f32[2,2,32,1024]{3,2,1,0:T(8,128)S(1)}, u32[]{:S(2)}, u32[]{:S(2)}) collective-permute-start(f32[2,2,32,1024]{3,2,1,0:T(8,128)} %get-tuple-element.63), channel_id=1, source_target_pairs={{0,32},{16,48},{32,0},{48,16},{1,33},{17,49},{33,1},{49,17},{2,34}... | collective-permute-start | bytes 1572872 | tf_op jit(solution)/shard_map/ppermute | solution.py:53
  86.7 0.8 copy-done.31
  87.5 5.2 %shard_map.154 = (f32[3,2,32,1024]{3,2,1,0:T(8,128)}, f32[3,2,32,1024]{3,2,1,0:T(8,128)}, f32[3,2,32,1024]{3,2,1,0:T(8,128)}, f32[3,2,32,1024]{3,2,1,0:T(8,128)}...) custom-call(s32[4]{0:T(128)} %pad_add_fusion.place, ...), custom_call_target="tpu_custom_call" | custom-call | flops 1610612736 | bytes 4194304 | tf_op jit(solution)/shard_map/pallas_call | solution.py:271
  92.7 1.4 copy-done.29
  94.0 7.5 %shard_map.155 = (f32[3,2,32,1024]{3,2,1,0:T(8,128)}, f32[3,2,32,1024]{3,2,1,0:T(8,128)}, f32[3,2,32,1024]{3,2,1,0:T(8,128)}, f32[3,2,32,1024]{3,2,1,0:T(8,128)}...) custom-call(s32[4]{0:T(128)} %pad_add_fusion.place, ...), custom_call_target="tpu_custom_call", output_to_operand_aliasing={{0}: (5, {}), {1}: (6, {}), {2}: (7, {}), {3}: (8, {}), {4}... | custom-call | flops 3221225472 | bytes 8388608 | tf_op jit(solution)/shard_map/pallas_call | solution.py:271
  101.5 0.7 collective-permute-start.21
  102.2 2.7 %collective-permute-start.6 = (f32[2,2,32,1024]{3,2,1,0:T(8,128)}, f32[2,2,32,1024]{3,2,1,0:T(8,128)S(1)}, u32[]{:S(2)}, u32[]{:S(2)}) collective-permute-start(f32[2,2,32,1024]{3,2,1,0:T(8,128)} %get-tuple-element.64), channel_id=1, source_target_pairs={{0,48},{16,0},{32,16},{48,32},{1,49},{17,1},{33,17},{49,33},{2,50}... | collective-permute-start | bytes 1572872 | tf_op jit(solution)/shard_map/ppermute | solution.py:53
  105.0 1.6 collective-permute-start.10
  106.6 4.3 %collective-permute-start.11 = (f32[2,8,32,256]{3,2,1,0:T(8,128)}, f32[2,8,32,256]{3,2,1,0:T(8,128)S(1)}, u32[]{:S(2)}, u32[]{:S(2)}) collective-permute-start(f32[2,8,32,256]{3,2,1,0:T(8,128)} %get-tuple-element.71), channel_id=1, source_target_pairs={{0,4},{2,6},{4,0},{6,2},{1,5},{3,7},{5,1},{7,3},{8,12},{10,14},{12... | collective-permute-start | bytes 1572872 | tf_op jit(solution)/shard_map/ppermute | solution.py:53
  110.9 4.2 %collective-permute-start.12 = (f32[2,8,32,256]{3,2,1,0:T(8,128)}, f32[2,8,32,256]{3,2,1,0:T(8,128)S(1)}, u32[]{:S(2)}, u32[]{:S(2)}) collective-permute-start(f32[2,8,32,256]{3,2,1,0:T(8,128)} %get-tuple-element.72), channel_id=1, source_target_pairs={{0,6},{2,0},{4,2},{6,4},{1,7},{3,1},{5,3},{7,5},{8,14},{10,8},{12,... | collective-permute-start | bytes 1572872 | tf_op jit(solution)/shard_map/ppermute | solution.py:53
  115.1 1.3 collective-permute-done.6.a3
  116.4 2.7 %collective-permute-start.22 = (f32[3,2,32,1024]{3,2,1,0:T(8,128)}, f32[3,2,32,1024]{3,2,1,0:T(8,128)S(1)}, u32[]{:S(2)}, u32[]{:S(2)}) collective-permute-start(f32[3,2,32,1024]{3,2,1,0:T(8,128)} %get-tuple-element.88), channel_id=1, source_target_pairs={{0,32},{16,48},{32,0},{48,16},{1,33},{17,49},{33,1},{49,17},{2,34}... | collective-permute-start | bytes 2359304 | tf_op jit(solution)/shard_map/ppermute | solution.py:53
  119.1 2.4 %collective-permute-done.10.a1 = f32[2,8,32,256]{3,2,1,0:T(8,128)S(1)} collective-permute-done((f32[2,8,32,256]{3,2,1,0:T(8,128)}, f32[2,8,32,256]{3,2,1,0:T(8,128)S(1)}, u32[]{:S(2)}, u32[]{:S(2)}) %collective-permute-start.10) | collective-permute-done | bytes 524320 | tf_op jit(solution)/shard_map/ppermute | solution.py:53
  121.5 1.2 collective-permute-start.23
  122.7 11.6 %collective-permute-done.11.a2 = f32[2,8,32,256]{3,2,1,0:T(8,128)S(1)} collective-permute-done((f32[2,8,32,256]{3,2,1,0:T(8,128)}, f32[2,8,32,256]{3,2,1,0:T(8,128)S(1)}, u32[]{:S(2)}, u32[]{:S(2)}) %collective-permute-start.11) | collective-permute-done | bytes 524320 | tf_op jit(solution)/shard_map/ppermute | solution.py:53
  135.3 3.1 %collective-permute-start.29 = (f32[3,8,32,256]{3,2,1,0:T(8,128)}, f32[3,8,32,256]{3,2,1,0:T(8,128)S(1)}, u32[]{:S(2)}, u32[]{:S(2)}) collective-permute-start(f32[3,8,32,256]{3,2,1,0:T(8,128)} %get-tuple-element.97), channel_id=1, source_target_pairs={{0,6},{2,0},{4,2},{6,4},{1,7},{3,1},{5,3},{7,5},{8,14},{10,8},{12,... | collective-permute-start | bytes 2359304 | tf_op jit(solution)/shard_map/ppermute | solution.py:53
  138.4 2.5 %shard_map.149 = (f32[2,2,32,256]{3,2,1,0:T(8,128)}, f32[2,2,32,256]{3,2,1,0:T(8,128)}, f32[2,2,32,256]{3,2,1,0:T(8,128)}, f32[2,2,32,256]{3,2,1,0:T(8,128)}) custom-call(s32[4]{0:T(128)} %pad_add_fusion.place, f32[2,2,32,1024]{3,2,1,0:T(8,128)} %get-tuple-element.61.a0.after, f32[2,2,32,1024]{3,2,1,0:T(8,128)} %copy-done.7, f32[2,2,32,1024]{3,2,1,0:T(8,128)} %copy-done.8, ...), custom_call_target="tpu_custom_call" | custom-call | flops 393216 | bytes 2621440 | tf_op jit(solution)/shard_map/pallas_call | solution.py:232
  140.9 3.3 %collective-permute-done.22.a2 = f32[3,2,32,1024]{3,2,1,0:T(8,128)S(1)} collective-permute-done((f32[3,2,32,1024]{3,2,1,0:T(8,128)}, f32[3,2,32,1024]{3,2,1,0:T(8,128)S(1)}, u32[]{:S(2)}, u32[]{:S(2)}) %collective-permute-start.22) | collective-permute-done | bytes 786464 | tf_op jit(solution)/shard_map/ppermute | solution.py:53
  144.2 1.6 collective-permute-start.7
  145.7 8.4 %collective-permute-done.23.a3 = f32[3,2,32,1024]{3,2,1,0:T(8,128)} collective-permute-done((f32[3,2,32,1024]{3,2,1,0:T(8,128)}, f32[3,2,32,1024]{3,2,1,0:T(8,128)}, u32[]{:S(2)}, u32[]{:S(2)}) %collective-permute-start.23) | collective-permute-done | bytes 786464 | tf_op jit(solution)/shard_map/ppermute | solution.py:53
  154.2 3.3 %collective-permute-start.8 = (f32[2,2,32,256]{3,2,1,0:T(8,128)}, f32[2,2,32,256]{3,2,1,0:T(8,128)}, u32[]{:S(2)}, u32[]{:S(2)}) collective-permute-start(f32[2,2,32,256]{3,2,1,0:T(8,128)} %get-tuple-element.67), channel_id=1, source_target_pairs={{0,4},{2,6},{4,0},{6,2},{1,5},{3,7},{5,1},{7,3},{8,12},{10,14},{12... | collective-permute-start | bytes 393224 | tf_op jit(solution)/shard_map/ppermute | solution.py:53
  157.5 3.1 %shard_map.156 = (f32[3,2,32,256]{3,2,1,0:T(8,128)}, f32[3,2,32,256]{3,2,1,0:T(8,128)}, f32[3,2,32,256]{3,2,1,0:T(8,128)}, f32[3,2,32,256]{3,2,1,0:T(8,128)}) custom-call(s32[4]{0:T(128)} %pad_add_fusion.place, f32[3,2,32,1024]{3,2,1,0:T(8,128)} %get-tuple-element.86.a0, f32[3,2,32,1024]{3,2,1,0:T(8,128)} %copy-done.4, f32[3,2,32,1024]{3,2,1,0:T(8,128)} %copy-done.6, ...), custom_call_target="tpu_custom_call" | custom-call | flops 589824 | bytes 3932160 | tf_op jit(solution)/shard_map/pallas_call | solution.py:232
  160.6 15.7 %collective-permute-done.7.refs_1_ = f32[2,2,32,256]{3,2,1,0:T(8,128)S(1)} collective-permute-done((f32[2,2,32,256]{3,2,1,0:T(8,128)}, f32[2,2,32,256]{3,2,1,0:T(8,128)S(1)}, u32[]{:S(2)}, u32[]{:S(2)}) %collective-permute-start.7) | collective-permute-done | bytes 131104 | tf_op jit(solution)/shard_map/ppermute | solution.py:53
  176.3 2.6 %shard_map.150 = (f32[2,2,32,256]{3,2,1,0:T(8,128)}, f32[2,2,32,256]{3,2,1,0:T(8,128)}, f32[2,2,32,256]{3,2,1,0:T(8,128)}, f32[2,2,32,256]{3,2,1,0:T(8,128)}) custom-call(s32[4]{0:T(128)} %pad_add_fusion.place, f32[2,8,32,256]{3,2,1,0:T(8,128)} %get-tuple-element.69.a0, f32[2,8,32,256]{3,2,1,0:T(8,128)} %copy-done.9, f32[2,8,32,256]{3,2,1,0:T(8,128)} %copy-done.10, ...), custom_call_target="tpu_custom_call" | custom-call | flops 393216 | bytes 2621440 | tf_op jit(solution)/shard_map/pallas_call | solution.py:232
  178.9 3.3 %collective-permute-start.9 = (f32[2,2,32,256]{3,2,1,0:T(8,128)S(1)}, f32[2,2,32,256]{3,2,1,0:T(8,128)S(1)}, u32[]{:S(2)}, u32[]{:S(2)}) collective-permute-start(f32[2,2,32,256]{3,2,1,0:T(8,128)S(1)} %copy-done.35), channel_id=1, source_target_pairs={{0,6},{2,0},{4,2},{6,4},{1,7},{3,1},{5,3},{7,5},{8,14},{10,8},{12,... | collective-permute-start | bytes 393224 | tf_op jit(solution)/shard_map/ppermute | solution.py:53
  182.4 2.0 collective-permute-start.14
  184.4 2.2 collective-permute-start.15
  186.6 3.0 %shard_map.157 = (f32[3,2,32,256]{3,2,1,0:T(8,128)}, f32[3,2,32,256]{3,2,1,0:T(8,128)}, f32[3,2,32,256]{3,2,1,0:T(8,128)}, f32[3,2,32,256]{3,2,1,0:T(8,128)}) custom-call(s32[4]{0:T(128)} %pad_add_fusion.place, f32[3,8,32,256]{3,2,1,0:T(8,128)} %get-tuple-element.94.a0, f32[3,8,32,256]{3,2,1,0:T(8,128)} %copy-done.2, f32[3,8,32,256]{3,2,1,0:T(8,128)} %copy-done.3, ...), custom_call_target="tpu_custom_call" | custom-call | flops 589824 | bytes 3932160 | tf_op jit(solution)/shard_map/pallas_call | solution.py:232
  189.9 1.4 collective-permute-start.26
  191.3 0.5 collective-permute-start.30
  191.9 1.8 collective-permute-start.31
  193.7 2.0 collective-permute-start.32
  195.7 1.2 collective-permute-done.25.refs_10_
  196.9 3.6 %collective-permute-done.30.refs_13_ = f32[3,2,32,256]{3,2,1,0:T(8,128)S(1)} collective-permute-done((f32[3,2,32,256]{3,2,1,0:T(8,128)}, f32[3,2,32,256]{3,2,1,0:T(8,128)S(1)}, u32[]{:S(2)}, u32[]{:S(2)}) %collective-permute-start.30) | collective-permute-done | bytes 196640 | tf_op jit(solution)/shard_map/ppermute | solution.py:53
  200.5 0.9 collective-permute-done.32.refs_15_
  201.5 0.6 copy-done.20
  202.1 2.8 %shard_map.158 = (f32[5,64,128]{2,1,0:T(8,128)}, f32[5,64,128]{2,1,0:T(8,128)}, f32[5,64,128]{2,1,0:T(8,128)}, f32[5,64,128]{2,1,0:T(8,128)}) custom-call(s32[4]{0:T(128)} %pad_add_fusion.place, f32[2,2,32,256]{3,2,1,0:T(8,128)} %get-tuple-element.65.refs_0_, f32[2,2,32,256]{3,2,1,0:T(8,128)} %copy-done.24, ...), custom_call_target="tpu_custom_call" | custom-call | flops 1048576 | bytes 4194304 | tf_op jit(solution)/shard_map/pallas_call | solution.py:244
  204.8 2.6 %collective-permute-start.33 = (f32[5,64,128]{2,1,0:T(8,128)}, f32[5,64,128]{2,1,0:T(8,128)S(1)}, u32[]{:S(2)}, u32[]{:S(2)}) collective-permute-start(f32[5,64,128]{2,1,0:T(8,128)} %get-tuple-element.103), channel_id=1, source_target_pairs={{0,1},{1,64},{64,65},{65,0},{2,3},{3,66},{66,67},{67,2},{4,5},{5,6... | collective-permute-start | bytes 491528 | tf_op jit(solution)/shard_map/ppermute | solution.py:53
  207.4 3.6 %collective-permute-start.34 = (f32[5,64,128]{2,1,0:T(8,128)}, f32[5,64,128]{2,1,0:T(8,128)S(1)}, u32[]{:S(2)}, u32[]{:S(2)}) collective-permute-start(f32[5,64,128]{2,1,0:T(8,128)} %get-tuple-element.104), channel_id=1, source_target_pairs={{0,64},{1,65},{64,0},{65,1},{2,66},{3,67},{66,2},{67,3},{4,68},{5,... | collective-permute-start | bytes 491528 | tf_op jit(solution)/shard_map/ppermute | solution.py:53
  211.1 2.0 collective-permute-done.33.a1
  213.1 3.2 %collective-permute-done.34.a2 = f32[5,64,128]{2,1,0:T(8,128)S(1)} collective-permute-done((f32[5,64,128]{2,1,0:T(8,128)}, f32[5,64,128]{2,1,0:T(8,128)S(1)}, u32[]{:S(2)}, u32[]{:S(2)}) %collective-permute-start.34) | collective-permute-done | bytes 163872 | tf_op jit(solution)/shard_map/ppermute | solution.py:53
  217.2 1.8 shard_map.159
  (98 shorter events, 3.0 us)
Async XLA Ops:
  0.6 19.6 %collective-permute-start.2 = (f32[128,1024]{1,0:T(8,128)}, f32[128,1024]{1,0:T(8,128)S(1)}, u32[]{:S(2)}, u32[]{:S(2)}) collective-permute-start(f32[128,1024]{1,0:T(8,128)} %fluid.3), channel_id=1, source_target_pairs={{1,0},{2,1},{3,2},{4,3},{5,4},{6,5},{7,6},{8,7},{9,8},{10,9},{11,1... | collective-permute-start | bytes 1572872 | tf_op jit(solution)/shard_map/ppermute | solution.py:59
  1.9 26.2 %collective-permute-start.1 = (f32[128,1024]{1,0:T(8,128)}, f32[128,1024]{1,0:T(8,128)S(1)}, u32[]{:S(2)}, u32[]{:S(2)}) collective-permute-start(f32[128,1024]{1,0:T(8,128)} %fluid.3), channel_id=1, source_target_pairs={{0,1},{1,2},{2,3},{3,4},{4,5},{5,6},{6,7},{7,8},{8,9},{9,10},{10,1... | collective-permute-start | bytes 1572872 | tf_op jit(solution)/shard_map/ppermute | solution.py:59
  10.1 23.0 %copy-start = (f32[256,1024]{1,0:T(8,128)S(1)}, f32[256,1024]{1,0:T(8,128)}, u32[]{:S(2)}) copy-start(f32[256,1024]{1,0:T(8,128)} %own.3) | copy-start | bytes 3145732
  20.2 7.9 %copy-start.13 = (f32[128,1024]{1,0:T(8,128)}, f32[128,1024]{1,0:T(8,128)S(1)}, u32[]{:S(2)}) copy-start(f32[128,1024]{1,0:T(8,128)S(1)} %collective-permute-done.2.hi) | copy-start | bytes 1572868
  28.9 11.2 %copy-start.32 = (f32[8,64,128]{2,1,0:T(8,128)S(1)}, f32[8,64,128]{2,1,0:T(8,128)}, u32[]{:S(2)}) copy-start(f32[8,64,128]{2,1,0:T(8,128)} %get-tuple-element.59) | copy-start | bytes 786436
  32.9 24.8 %collective-permute-start.3 = (f32[2,128,1024]{2,1,0:T(8,128)}, f32[2,128,1024]{2,1,0:T(8,128)S(1)}, u32[]{:S(2)}, u32[]{:S(2)}) collective-permute-start(f32[2,128,1024]{2,1,0:T(8,128)} %shard_map.147.if0), channel_id=1, source_target_pairs={{0,8},{8,0},{1,9},{9,1},{2,10},{10,2},{3,11},{11,3},{4,12},{12,4},... | collective-permute-start | bytes 3145736 | tf_op jit(solution)/shard_map/ppermute | solution.py:53
  33.2 30.8 %collective-permute-start.18 = (f32[128,1024]{1,0:T(8,128)S(1)}, f32[128,1024]{1,0:T(8,128)}, u32[]{:S(2)}, u32[]{:S(2)}) collective-permute-start(f32[128,1024]{1,0:T(8,128)S(1)} %get-tuple-element.111), channel_id=1, source_target_pairs={{1,0},{2,1},{3,2},{4,3},{5,4},{6,5},{7,6},{8,7},{9,8},{10,9},{11,1... | collective-permute-start | bytes 1572872 | tf_op jit(solution)/shard_map/ppermute | solution.py:59
  34.5 36.5 %collective-permute-start.17 = (f32[128,1024]{1,0:T(8,128)S(1)}, f32[128,1024]{1,0:T(8,128)}, u32[]{:S(2)}, u32[]{:S(2)}) collective-permute-start(f32[128,1024]{1,0:T(8,128)S(1)} %get-tuple-element.112), channel_id=1, source_target_pairs={{0,1},{1,2},{2,3},{3,4},{4,5},{5,6},{6,7},{7,8},{8,9},{9,10},{10,1... | collective-permute-start | bytes 1572872 | tf_op jit(solution)/shard_map/ppermute | solution.py:59
  40.1 17.6 %collective-permute-start = (f32[8,64,128]{2,1,0:T(8,128)S(1)}, f32[8,64,128]{2,1,0:T(8,128)}, u32[]{:S(2)}, u32[]{:S(2)}) collective-permute-start(f32[8,64,128]{2,1,0:T(8,128)S(1)} %copy-done.32), channel_id=1, source_target_pairs={{0,8},{8,0},{1,9},{9,1},{2,10},{10,2},{3,11},{11,3},{4,12},{12,4},... | collective-permute-start | bytes 786440 | tf_op jit(solution)/shard_map/ppermute | solution.py:53
  46.0 31.4 %all-to-all-start = ((f32[128,2,1024]{2,1,0:T(2,128)}), f32[128,2,1024]{2,1,0:T(2,128)S(1)}, u32[]{:S(2)}, u32[]{:S(2)}) async-start(f32[128,2,1024]{2,1,0:T(2,128)} %shard_map.152), calls=%async_computation | async-start | bytes 2097152 | tf_op jit(solution)/shard_map/all_to_all | solution.py:298
  57.7 1.0 copy-start.30
  76.9 15.7 %collective-permute-start.19 = (f32[2,256,1024]{2,1,0:T(8,128)}, f32[2,256,1024]{2,1,0:T(8,128)S(1)}, u32[]{:S(2)}, u32[]{:S(2)}) collective-permute-start(f32[2,256,1024]{2,1,0:T(8,128)} %shard_map.151.is0), channel_id=1, source_target_pairs={{0,8},{8,0},{1,9},{9,1},{2,10},{10,2},{3,11},{11,3},{4,12},{12,4},... | collective-permute-start | bytes 6291464 | tf_op jit(solution)/shard_map/ppermute | solution.py:53
  77.4 1.0 copy-start.1
  81.5 5.2 %collective-permute-start.20 = (f32[256,1024]{1,0:T(8,128)}, f32[256,1024]{1,0:T(8,128)}, u32[]{:S(2)}, u32[]{:S(2)}) collective-permute-start(f32[256,1024]{1,0:T(8,128)} %shard_map.153.ic0), channel_id=1, source_target_pairs={{0,8},{8,0},{1,9},{9,1},{2,10},{10,2},{3,11},{11,3},{4,12},{12,4},... | collective-permute-start | bytes 3145736 | tf_op jit(solution)/shard_map/ppermute | solution.py:53
  81.6 5.1 %collective-permute-start.16 = (f32[8,64,256]{2,1,0:T(8,128)}, f32[8,64,256]{2,1,0:T(8,128)S(1)}, u32[]{:S(2)}, u32[]{:S(2)}) collective-permute-start(f32[8,64,256]{2,1,0:T(8,128)} %get-tuple-element.77), channel_id=1, source_target_pairs={{0,8},{8,0},{1,9},{9,1},{2,10},{10,2},{3,11},{11,3},{4,12},{12,4},... | collective-permute-start | bytes 1572872 | tf_op jit(solution)/shard_map/ppermute | solution.py:53
  82.0 24.6 %collective-permute-start.4 = (f32[2,2,32,1024]{3,2,1,0:T(8,128)}, f32[2,2,32,1024]{3,2,1,0:T(8,128)S(1)}, u32[]{:S(2)}, u32[]{:S(2)}) collective-permute-start(f32[2,2,32,1024]{3,2,1,0:T(8,128)} %get-tuple-element.62), channel_id=1, source_target_pairs={{0,16},{16,32},{32,48},{48,0},{1,17},{17,33},{33,49},{49,1},{2,18}... | collective-permute-start | bytes 1572872 | tf_op jit(solution)/shard_map/ppermute | solution.py:53
  83.9 27.0 %collective-permute-start.5 = (f32[2,2,32,1024]{3,2,1,0:T(8,128)}, f32[2,2,32,1024]{3,2,1,0:T(8,128)S(1)}, u32[]{:S(2)}, u32[]{:S(2)}) collective-permute-start(f32[2,2,32,1024]{3,2,1,0:T(8,128)} %get-tuple-element.63), channel_id=1, source_target_pairs={{0,32},{16,48},{32,0},{48,16},{1,33},{17,49},{33,1},{49,17},{2,34}... | collective-permute-start | bytes 1572872 | tf_op jit(solution)/shard_map/ppermute | solution.py:53
  92.7 1.4 copy-start.29
  101.5 33.3 %collective-permute-start.21 = (f32[3,2,32,1024]{3,2,1,0:T(8,128)}, f32[3,2,32,1024]{3,2,1,0:T(8,128)S(1)}, u32[]{:S(2)}, u32[]{:S(2)}) collective-permute-start(f32[3,2,32,1024]{3,2,1,0:T(8,128)} %get-tuple-element.87), channel_id=1, source_target_pairs={{0,16},{16,32},{32,48},{48,0},{1,17},{17,33},{33,49},{49,1},{2,18}... | collective-permute-start | bytes 2359304 | tf_op jit(solution)/shard_map/ppermute | solution.py:53
  102.2 14.1 %collective-permute-start.6 = (f32[2,2,32,1024]{3,2,1,0:T(8,128)}, f32[2,2,32,1024]{3,2,1,0:T(8,128)S(1)}, u32[]{:S(2)}, u32[]{:S(2)}) collective-permute-start(f32[2,2,32,1024]{3,2,1,0:T(8,128)} %get-tuple-element.64), channel_id=1, source_target_pairs={{0,48},{16,0},{32,16},{48,32},{1,49},{17,1},{33,17},{49,33},{2,50}... | collective-permute-start | bytes 1572872 | tf_op jit(solution)/shard_map/ppermute | solution.py:53
  105.0 16.5 %collective-permute-start.10 = (f32[2,8,32,256]{3,2,1,0:T(8,128)}, f32[2,8,32,256]{3,2,1,0:T(8,128)S(1)}, u32[]{:S(2)}, u32[]{:S(2)}) collective-permute-start(f32[2,8,32,256]{3,2,1,0:T(8,128)} %get-tuple-element.70), channel_id=1, source_target_pairs={{0,2},{2,4},{4,6},{6,0},{1,3},{3,5},{5,7},{7,1},{8,10},{10,12},{12... | collective-permute-start | bytes 1572872 | tf_op jit(solution)/shard_map/ppermute | solution.py:53
  106.6 27.7 %copy-start.7 = (f32[2,2,32,1024]{3,2,1,0:T(8,128)}, f32[2,2,32,1024]{3,2,1,0:T(8,128)S(1)}, u32[]{:S(2)}) copy-start(f32[2,2,32,1024]{3,2,1,0:T(8,128)S(1)} %collective-permute-done.4.a1) | copy-start | bytes 1572868
  106.6 27.7 %collective-permute-start.11 = (f32[2,8,32,256]{3,2,1,0:T(8,128)}, f32[2,8,32,256]{3,2,1,0:T(8,128)S(1)}, u32[]{:S(2)}, u32[]{:S(2)}) collective-permute-start(f32[2,8,32,256]{3,2,1,0:T(8,128)} %get-tuple-element.71), channel_id=1, source_target_pairs={{0,4},{2,6},{4,0},{6,2},{1,5},{3,7},{5,1},{7,3},{8,12},{10,14},{12... | collective-permute-start | bytes 1572872 | tf_op jit(solution)/shard_map/ppermute | solution.py:53
  110.9 23.3 %copy-start.8 = (f32[2,2,32,1024]{3,2,1,0:T(8,128)}, f32[2,2,32,1024]{3,2,1,0:T(8,128)S(1)}, u32[]{:S(2)}) copy-start(f32[2,2,32,1024]{3,2,1,0:T(8,128)S(1)} %collective-permute-done.5.a2) | copy-start | bytes 1572868
  110.9 23.4 %collective-permute-start.12 = (f32[2,8,32,256]{3,2,1,0:T(8,128)}, f32[2,8,32,256]{3,2,1,0:T(8,128)S(1)}, u32[]{:S(2)}, u32[]{:S(2)}) collective-permute-start(f32[2,8,32,256]{3,2,1,0:T(8,128)} %get-tuple-element.72), channel_id=1, source_target_pairs={{0,6},{2,0},{4,2},{6,4},{1,7},{3,1},{5,3},{7,5},{8,14},{10,8},{12,... | collective-permute-start | bytes 1572872 | tf_op jit(solution)/shard_map/ppermute | solution.py:53
  116.4 18.7 %copy-start.12 = (f32[2,2,32,1024]{3,2,1,0:T(8,128)}, f32[2,2,32,1024]{3,2,1,0:T(8,128)S(1)}, u32[]{:S(2)}) copy-start(f32[2,2,32,1024]{3,2,1,0:T(8,128)S(1)} %collective-permute-done.6.a3) | copy-start | bytes 1572868
  116.4 27.8 %collective-permute-start.22 = (f32[3,2,32,1024]{3,2,1,0:T(8,128)}, f32[3,2,32,1024]{3,2,1,0:T(8,128)S(1)}, u32[]{:S(2)}, u32[]{:S(2)}) collective-permute-start(f32[3,2,32,1024]{3,2,1,0:T(8,128)} %get-tuple-element.88), channel_id=1, source_target_pairs={{0,32},{16,48},{32,0},{48,16},{1,33},{17,49},{33,1},{49,17},{2,34}... | collective-permute-start | bytes 2359304 | tf_op jit(solution)/shard_map/ppermute | solution.py:53
  121.5 12.8 %copy-start.9 = (f32[2,8,32,256]{3,2,1,0:T(8,128)}, f32[2,8,32,256]{3,2,1,0:T(8,128)S(1)}, u32[]{:S(2)}) copy-start(f32[2,8,32,256]{3,2,1,0:T(8,128)S(1)} %collective-permute-done.10.a1) | copy-start | bytes 1572868
  121.5 32.7 %collective-permute-start.23 = (f32[3,2,32,1024]{3,2,1,0:T(8,128)}, f32[3,2,32,1024]{3,2,1,0:T(8,128)}, u32[]{:S(2)}, u32[]{:S(2)}) collective-permute-start(f32[3,2,32,1024]{3,2,1,0:T(8,128)} %get-tuple-element.89), channel_id=1, source_target_pairs={{0,48},{16,0},{32,16},{48,32},{1,49},{17,1},{33,17},{49,33},{2,50}... | collective-permute-start | bytes 2359304 | tf_op jit(solution)/shard_map/ppermute | solution.py:53
  134.3 47.9 %collective-permute-start.27 = (f32[3,8,32,256]{3,2,1,0:T(8,128)}, f32[3,8,32,256]{3,2,1,0:T(8,128)S(1)}, u32[]{:S(2)}, u32[]{:S(2)}) collective-permute-start(f32[3,8,32,256]{3,2,1,0:T(8,128)} %get-tuple-element.95), channel_id=1, source_target_pairs={{0,2},{2,4},{4,6},{6,0},{1,3},{3,5},{5,7},{7,1},{8,10},{10,12},{12... | collective-permute-start | bytes 2359304 | tf_op jit(solution)/shard_map/ppermute | solution.py:53
  134.4 48.0 %collective-permute-start.28 = (f32[3,8,32,256]{3,2,1,0:T(8,128)}, f32[3,8,32,256]{3,2,1,0:T(8,128)S(1)}, u32[]{:S(2)}, u32[]{:S(2)}) collective-permute-start(f32[3,8,32,256]{3,2,1,0:T(8,128)} %get-tuple-element.96), channel_id=1, source_target_pairs={{0,4},{2,6},{4,0},{6,2},{1,5},{3,7},{5,1},{7,3},{8,12},{10,14},{12... | collective-permute-start | bytes 2359304 | tf_op jit(solution)/shard_map/ppermute | solution.py:53
  135.1 22.4 %copy-start.4 = (f32[3,2,32,1024]{3,2,1,0:T(8,128)}, f32[3,2,32,1024]{3,2,1,0:T(8,128)S(1)}, u32[]{:S(2)}) copy-start(f32[3,2,32,1024]{3,2,1,0:T(8,128)S(1)} %collective-permute-done.21.a1) | copy-start | bytes 2359300
  135.3 49.2 %collective-permute-start.29 = (f32[3,8,32,256]{3,2,1,0:T(8,128)}, f32[3,8,32,256]{3,2,1,0:T(8,128)S(1)}, u32[]{:S(2)}, u32[]{:S(2)}) collective-permute-start(f32[3,8,32,256]{3,2,1,0:T(8,128)} %get-tuple-element.97), channel_id=1, source_target_pairs={{0,6},{2,0},{4,2},{6,4},{1,7},{3,1},{5,3},{7,5},{8,14},{10,8},{12,... | collective-permute-start | bytes 2359304 | tf_op jit(solution)/shard_map/ppermute | solution.py:53
  144.2 13.3 %copy-start.6 = (f32[3,2,32,1024]{3,2,1,0:T(8,128)}, f32[3,2,32,1024]{3,2,1,0:T(8,128)S(1)}, u32[]{:S(2)}) copy-start(f32[3,2,32,1024]{3,2,1,0:T(8,128)S(1)} %collective-permute-done.22.a2) | copy-start | bytes 2359300
  144.2 32.1 %collective-permute-start.7 = (f32[2,2,32,256]{3,2,1,0:T(8,128)}, f32[2,2,32,256]{3,2,1,0:T(8,128)S(1)}, u32[]{:S(2)}, u32[]{:S(2)}) collective-permute-start(f32[2,2,32,256]{3,2,1,0:T(8,128)} %get-tuple-element.66), channel_id=1, source_target_pairs={{0,2},{2,4},{4,6},{6,0},{1,3},{3,5},{5,7},{7,1},{8,10},{10,12},{12... | collective-permute-start | bytes 393224 | tf_op jit(solution)/shard_map/ppermute | solution.py:53
  154.2 24.7 %collective-permute-start.8 = (f32[2,2,32,256]{3,2,1,0:T(8,128)}, f32[2,2,32,256]{3,2,1,0:T(8,128)}, u32[]{:S(2)}, u32[]{:S(2)}) collective-permute-start(f32[2,2,32,256]{3,2,1,0:T(8,128)} %get-tuple-element.67), channel_id=1, source_target_pairs={{0,4},{2,6},{4,0},{6,2},{1,5},{3,7},{5,1},{7,3},{8,12},{10,14},{12... | collective-permute-start | bytes 393224 | tf_op jit(solution)/shard_map/ppermute | solution.py:53
  160.6 18.2 %copy-start.35 = (f32[2,2,32,256]{3,2,1,0:T(8,128)S(1)}, f32[2,2,32,256]{3,2,1,0:T(8,128)}, u32[]{:S(2)}) copy-start(f32[2,2,32,256]{3,2,1,0:T(8,128)} %get-tuple-element.68) | copy-start | bytes 393220
  176.3 13.3 %copy-start.24 = (f32[2,2,32,256]{3,2,1,0:T(8,128)}, f32[2,2,32,256]{3,2,1,0:T(8,128)S(1)}, u32[]{:S(2)}) copy-start(f32[2,2,32,256]{3,2,1,0:T(8,128)S(1)} %collective-permute-done.7.refs_1_) | copy-start | bytes 393220
  176.3 17.4 %collective-permute-start.24 = (f32[3,2,32,256]{3,2,1,0:T(8,128)}, f32[3,2,32,256]{3,2,1,0:T(8,128)S(1)}, u32[]{:S(2)}, u32[]{:S(2)}) collective-permute-start(f32[3,2,32,256]{3,2,1,0:T(8,128)} %get-tuple-element.91), channel_id=1, source_target_pairs={{0,2},{2,4},{4,6},{6,0},{1,3},{3,5},{5,7},{7,1},{8,10},{10,12},{12... | collective-permute-start | bytes 589832 | tf_op jit(solution)/shard_map/ppermute | solution.py:53
  178.8 10.8 %copy-start.34 = (f32[3,2,32,256]{3,2,1,0:T(8,128)S(1)}, f32[3,2,32,256]{3,2,1,0:T(8,128)}, u32[]{:S(2)}) copy-start(f32[3,2,32,256]{3,2,1,0:T(8,128)} %get-tuple-element.92) | copy-start | bytes 589828
  178.8 11.1 %copy-start.33 = (f32[3,2,32,256]{3,2,1,0:T(8,128)S(1)}, f32[3,2,32,256]{3,2,1,0:T(8,128)}, u32[]{:S(2)}) copy-start(f32[3,2,32,256]{3,2,1,0:T(8,128)} %get-tuple-element.93) | copy-start | bytes 589828
  178.9 10.8 %collective-permute-start.9 = (f32[2,2,32,256]{3,2,1,0:T(8,128)S(1)}, f32[2,2,32,256]{3,2,1,0:T(8,128)S(1)}, u32[]{:S(2)}, u32[]{:S(2)}) collective-permute-start(f32[2,2,32,256]{3,2,1,0:T(8,128)S(1)} %copy-done.35), channel_id=1, source_target_pairs={{0,6},{2,0},{4,2},{6,4},{1,7},{3,1},{5,3},{7,5},{8,14},{10,8},{12,... | collective-permute-start | bytes 393224 | tf_op jit(solution)/shard_map/ppermute | solution.py:53
  182.1 4.5 %copy-start.2 = (f32[3,8,32,256]{3,2,1,0:T(8,128)}, f32[3,8,32,256]{3,2,1,0:T(8,128)S(1)}, u32[]{:S(2)}) copy-start(f32[3,8,32,256]{3,2,1,0:T(8,128)S(1)} %collective-permute-done.27.a1) | copy-start | bytes 2359300
  182.1 7.8 %collective-permute-start.13 = (f32[2,2,32,256]{3,2,1,0:T(8,128)}, f32[2,2,32,256]{3,2,1,0:T(8,128)S(1)}, u32[]{:S(2)}, u32[]{:S(2)}) collective-permute-start(f32[2,2,32,256]{3,2,1,0:T(8,128)} %get-tuple-element.74), channel_id=1, source_target_pairs={{0,16},{16,32},{32,48},{48,0},{1,17},{17,33},{33,49},{49,1},{2,18}... | collective-permute-start | bytes 393224 | tf_op jit(solution)/shard_map/ppermute | solution.py:53
  182.4 4.2 %copy-start.3 = (f32[3,8,32,256]{3,2,1,0:T(8,128)}, f32[3,8,32,256]{3,2,1,0:T(8,128)S(1)}, u32[]{:S(2)}) copy-start(f32[3,8,32,256]{3,2,1,0:T(8,128)S(1)} %collective-permute-done.28.a2) | copy-start | bytes 2359300
  182.4 8.9 %collective-permute-start.14 = (f32[2,2,32,256]{3,2,1,0:T(8,128)}, f32[2,2,32,256]{3,2,1,0:T(8,128)S(1)}, u32[]{:S(2)}, u32[]{:S(2)}) collective-permute-start(f32[2,2,32,256]{3,2,1,0:T(8,128)} %get-tuple-element.75), channel_id=1, source_target_pairs={{0,32},{16,48},{32,0},{48,16},{1,33},{17,49},{33,1},{49,17},{2,34}... | collective-permute-start | bytes 393224 | tf_op jit(solution)/shard_map/ppermute | solution.py:53
  184.4 2.2 copy-start.5
  184.4 7.4 %collective-permute-start.15 = (f32[2,2,32,256]{3,2,1,0:T(8,128)}, f32[2,2,32,256]{3,2,1,0:T(8,128)S(1)}, u32[]{:S(2)}, u32[]{:S(2)}) collective-permute-start(f32[2,2,32,256]{3,2,1,0:T(8,128)} %get-tuple-element.76), channel_id=1, source_target_pairs={{0,48},{16,0},{32,16},{48,32},{1,49},{17,1},{33,17},{49,33},{2,50}... | collective-permute-start | bytes 393224 | tf_op jit(solution)/shard_map/ppermute | solution.py:53
  189.6 11.8 %copy-start.25 = (f32[2,2,32,256]{3,2,1,0:T(8,128)}, f32[2,2,32,256]{3,2,1,0:T(8,128)S(1)}, u32[]{:S(2)}) copy-start(f32[2,2,32,256]{3,2,1,0:T(8,128)S(1)} %collective-permute-done.9.refs_3_) | copy-start | bytes 393220
  189.7 7.3 %collective-permute-start.25 = (f32[3,2,32,256]{3,2,1,0:T(8,128)S(1)}, f32[3,2,32,256]{3,2,1,0:T(8,128)S(1)}, u32[]{:S(2)}, u32[]{:S(2)}) collective-permute-start(f32[3,2,32,256]{3,2,1,0:T(8,128)S(1)} %copy-done.34), channel_id=1, source_target_pairs={{0,4},{2,6},{4,0},{6,2},{1,5},{3,7},{5,1},{7,3},{8,12},{10,14},{12... | collective-permute-start | bytes 589832 | tf_op jit(solution)/shard_map/ppermute | solution.py:53
  189.9 11.5 %copy-start.26 = (f32[2,2,32,256]{3,2,1,0:T(8,128)}, f32[2,2,32,256]{3,2,1,0:T(8,128)S(1)}, u32[]{:S(2)}) copy-start(f32[2,2,32,256]{3,2,1,0:T(8,128)S(1)} %collective-permute-done.13.refs_5_) | copy-start | bytes 393220
  189.9 7.0 %collective-permute-start.26 = (f32[3,2,32,256]{3,2,1,0:T(8,128)S(1)}, f32[3,2,32,256]{3,2,1,0:T(8,128)S(1)}, u32[]{:S(2)}, u32[]{:S(2)}) collective-permute-start(f32[3,2,32,256]{3,2,1,0:T(8,128)S(1)} %copy-done.33), channel_id=1, source_target_pairs={{0,6},{2,0},{4,2},{6,4},{1,7},{3,1},{5,3},{7,5},{8,14},{10,8},{12,... | collective-permute-start | bytes 589832 | tf_op jit(solution)/shard_map/ppermute | solution.py:53
  191.3 10.1 %copy-start.27 = (f32[2,2,32,256]{3,2,1,0:T(8,128)}, f32[2,2,32,256]{3,2,1,0:T(8,128)S(1)}, u32[]{:S(2)}) copy-start(f32[2,2,32,256]{3,2,1,0:T(8,128)S(1)} %collective-permute-done.14.refs_6_) | copy-start | bytes 393220
  191.3 9.2 %collective-permute-start.30 = (f32[3,2,32,256]{3,2,1,0:T(8,128)}, f32[3,2,32,256]{3,2,1,0:T(8,128)S(1)}, u32[]{:S(2)}, u32[]{:S(2)}) collective-permute-start(f32[3,2,32,256]{3,2,1,0:T(8,128)} %get-tuple-element.99), channel_id=1, source_target_pairs={{0,16},{16,32},{32,48},{48,0},{1,17},{17,33},{33,49},{49,1},{2,18}... | collective-permute-start | bytes 589832 | tf_op jit(solution)/shard_map/ppermute | solution.py:53
  191.9 9.5 %copy-start.28 = (f32[2,2,32,256]{3,2,1,0:T(8,128)}, f32[2,2,32,256]{3,2,1,0:T(8,128)S(1)}, u32[]{:S(2)}) copy-start(f32[2,2,32,256]{3,2,1,0:T(8,128)S(1)} %collective-permute-done.15.refs_7_) | copy-start | bytes 393220
  191.9 8.7 %collective-permute-start.31 = (f32[3,2,32,256]{3,2,1,0:T(8,128)}, f32[3,2,32,256]{3,2,1,0:T(8,128)S(1)}, u32[]{:S(2)}, u32[]{:S(2)}) collective-permute-start(f32[3,2,32,256]{3,2,1,0:T(8,128)} %get-tuple-element.100), channel_id=1, source_target_pairs={{0,32},{16,48},{32,0},{48,16},{1,33},{17,49},{33,1},{49,17},{2,34}... | collective-permute-start | bytes 589832 | tf_op jit(solution)/shard_map/ppermute | solution.py:53
  193.7 7.7 %copy-start.15 = (f32[3,2,32,256]{3,2,1,0:T(8,128)}, f32[3,2,32,256]{3,2,1,0:T(8,128)S(1)}, u32[]{:S(2)}) copy-start(f32[3,2,32,256]{3,2,1,0:T(8,128)S(1)} %collective-permute-done.24.refs_9_) | copy-start | bytes 589828
  193.7 7.7 %collective-permute-start.32 = (f32[3,2,32,256]{3,2,1,0:T(8,128)}, f32[3,2,32,256]{3,2,1,0:T(8,128)S(1)}, u32[]{:S(2)}, u32[]{:S(2)}) collective-permute-start(f32[3,2,32,256]{3,2,1,0:T(8,128)} %get-tuple-element.101), channel_id=1, source_target_pairs={{0,48},{16,0},{32,16},{48,32},{1,49},{17,1},{33,17},{49,33},{2,50}... | collective-permute-start | bytes 589832 | tf_op jit(solution)/shard_map/ppermute | solution.py:53
  196.9 4.5 %copy-start.16 = (f32[3,2,32,256]{3,2,1,0:T(8,128)}, f32[3,2,32,256]{3,2,1,0:T(8,128)S(1)}, u32[]{:S(2)}) copy-start(f32[3,2,32,256]{3,2,1,0:T(8,128)S(1)} %collective-permute-done.25.refs_10_) | copy-start | bytes 589828
  196.9 4.5 %copy-start.17 = (f32[3,2,32,256]{3,2,1,0:T(8,128)}, f32[3,2,32,256]{3,2,1,0:T(8,128)S(1)}, u32[]{:S(2)}) copy-start(f32[3,2,32,256]{3,2,1,0:T(8,128)S(1)} %collective-permute-done.26.refs_11_) | copy-start | bytes 589828
  204.8 8.2 %collective-permute-start.33 = (f32[5,64,128]{2,1,0:T(8,128)}, f32[5,64,128]{2,1,0:T(8,128)S(1)}, u32[]{:S(2)}, u32[]{:S(2)}) collective-permute-start(f32[5,64,128]{2,1,0:T(8,128)} %get-tuple-element.103), channel_id=1, source_target_pairs={{0,1},{1,64},{64,65},{65,0},{2,3},{3,66},{66,67},{67,2},{4,5},{5,6... | collective-permute-start | bytes 491528 | tf_op jit(solution)/shard_map/ppermute | solution.py:53
  207.4 8.9 %collective-permute-start.34 = (f32[5,64,128]{2,1,0:T(8,128)}, f32[5,64,128]{2,1,0:T(8,128)S(1)}, u32[]{:S(2)}, u32[]{:S(2)}) collective-permute-start(f32[5,64,128]{2,1,0:T(8,128)} %get-tuple-element.104), channel_id=1, source_target_pairs={{0,64},{1,65},{64,0},{65,1},{2,66},{3,67},{66,2},{67,3},{4,68},{5,... | collective-permute-start | bytes 491528 | tf_op jit(solution)/shard_map/ppermute | solution.py:53
  211.0 5.5 %collective-permute-start.35 = (f32[5,64,128]{2,1,0:T(8,128)}, f32[5,64,128]{2,1,0:T(8,128)S(1)}, u32[]{:S(2)}, u32[]{:S(2)}) collective-permute-start(f32[5,64,128]{2,1,0:T(8,128)} %get-tuple-element.105), channel_id=1, source_target_pairs={{0,65},{1,0},{64,1},{65,64},{2,67},{3,2},{66,3},{67,66},{4,69},{5,... | collective-permute-start | bytes 491528 | tf_op jit(solution)/shard_map/ppermute | solution.py:53
  213.1 3.5 %copy-start.21 = (f32[5,64,128]{2,1,0:T(8,128)}, f32[5,64,128]{2,1,0:T(8,128)S(1)}, u32[]{:S(2)}) copy-start(f32[5,64,128]{2,1,0:T(8,128)S(1)} %collective-permute-done.33.a1) | copy-start | bytes 491524
  (9 other events, 7.1 us)

commit v4 on v3

--- a/solution.py
+++ b/solution.py
@@ -1,5 +1,3 @@
-import functools
-
 import jax
 import jax.numpy as jnp
 from jax import lax
@@ -141,63 +139,70 @@
     held[...] = product((left[0][...], left[1][...]), parts(right)).reshape(held.shape)
 
 
-def send_off(place, held, outs):
-    for o in range(4):
-        dx = lax.rem(place[0] + o, 4)
-        dy = lax.rem(place[1] + o, 4)
+def along_x(place, held, rows, outs):
+    for o, out in enumerate(outs):
+        d = lax.rem(place[0] + o, 4)
         for h in range(2):
-            outs[o][0, h] = held[h * 4 + dx, 0:HALF, :]
-        outs[4 + o][0] = held[:, HALF:, pl.ds(pl.multiple_of(dy * 256, 256), 256)]
-
-
-def fluid_product_kernel(place, lf0, lf1, if0, if1, *rest):
-    outs, (fh, fl, held) = rest[:8], rest[8:]
-
+            out[0, h] = held[h * 4 + d, rows, :]
+
+
+def along_y(place, held, rows, outs):
+    for o, out in enumerate(outs):
+        d = lax.rem(place[1] + o, 4)
+        out[0] = held[:, rows, pl.ds(pl.multiple_of(d * 256, 256), 256)]
+
+
+def fluid_product_kernel(place, lf0, lf1, if0, if1, o0, o1, o2, o3, fh, fl, held):
     @pl.when(pl.program_id(0) == 0)
     def _():
         fh[...], fl[...] = parts(joined(lf0, lf1))
 
     multiply(held, (fh, fl), if0[0], if1[0])
-    send_off(place, held, outs)
-
-
-def wet_product_kernel(place, ls0, ls1, ic0, ic1, *rest):
-    outs, (sh, sl, held) = rest[:8], rest[8:]
+    along_x(place, held, slice(0, 64), (o0, o1, o2, o3))
+
+
+def wet_product_kernel(place, ls0, ls1, ic0, ic1, o0, o1, o2, o3, sh, sl, held):
     sh[...], sl[...] = parts(joined(ls0, ls1))
     multiply(held, (sh, sl), ic0[...], ic1[...])
-    send_off(place, held, outs)
+    along_y(place, held, slice(0, 64), (o0, o1, o2, o3))
 
 
 def second_kernel(place, ls0, ls1, is0, is1, *rest):
-    outs, (sh, sl, held) = rest[8:16], rest[16:]
+    outs, (sh, sl, held) = rest[:8], rest[8:]
 
     @pl.when(pl.program_id(0) == 0)
     def _():
         sh[...], sl[...] = parts(joined(ls0, ls1))
 
     multiply(held, (sh, sl), is0[0], is1[0])
-    send_off(place, held, outs)
-
-
-def split_kernel(axis, place, a0, a1, a2, a3, o0, o1, o2, o3, held):
+    along_x(place, held, slice(0, HALF), outs[:4])
+    along_y(place, held, slice(HALF, 64), outs[4:])
+
+
+def to_y_kernel(place, a0, a1, a2, a3, o0, o1, o2, o3, held):
     held[...] = (a0[...] + a1[...]) + (a2[...] + a3[...])
     for o, out in enumerate((o0, o1, o2, o3)):
-        d = lax.rem(place[axis] + o, 4)
-        if axis == 1:
-            out[...] = held[..., pl.ds(pl.multiple_of(d * 256, 256), 256)]
-        else:
-            for h in range(2):
-                out[:, h] = held[:, h * 4 + d]
+        d = lax.rem(place[1] + o, 4)
+        out[...] = held[..., pl.ds(pl.multiple_of(d * 256, 256), 256)]
+
+
+def to_x_kernel(place, a0, a1, a2, a3, b0, b1, b2, b3, o0, o1, o2, o3, held):
+    held[0:2] = (a0[...] + a1[...]) + (a2[...] + a3[...])
+    for k in range(2):
+        rows = slice(k * HALF, (k + 1) * HALF)
+        held[2 + k] = (b0[0, :, rows] + b1[0, :, rows]) + (b2[0, :, rows] + b3[0, :, rows])
+    for o, out in enumerate((o0, o1, o2, o3)):
+        d = lax.rem(place[0] + o, 4)
+        for h in range(2):
+            out[:, h] = held[:, h * 4 + d]
 
 
 def spread_kernel(place, *refs):
-    ins, outs, held = refs[:16], refs[16:20], refs[20]
-    at = 0
-    for x, y in ((ins[0:4], ins[4:8]), (ins[8:12], ins[12:16])):
-        rows = slice(at, at + x[0].shape[0])
-        held[rows, :, 0:HALF] = (x[0][...] + x[1][...]) + (x[2][...] + x[3][...])
-        held[rows, :, HALF:] = (y[0][...] + y[1][...]) + (y[2][...] + y[3][...])
-        at = rows.stop
+    f, x, y, outs, held = refs[0:4], refs[4:8], refs[8:12], refs[12:16], refs[16]
+    held[0:2] = (f[0][...] + f[1][...]) + (f[2][...] + f[3][...])
+    held[2:4, :, 0:HALF] = (x[0][...] + x[1][...]) + (x[2][...] + x[3][...])
+    for m, k, at in ((2, 0, HALF), (3, 1, HALF), (4, 2, 0), (4, 3, HALF)):
+        held[m, :, at : at + HALF] = (y[0][k] + y[1][k]) + (y[2][k] + y[3][k])
     for o, out in enumerate(outs):
         d = lax.rem(place[2] + o, 4)
         lanes = pl.ds(pl.multiple_of(lax.rem(d, 2) * 128, 128), 128)
@@ -226,17 +231,10 @@
     return [slots[0]] + [shifted(slots[o], axis, o) for o in range(1, 4)]
 
 
-def split(place, arrived, axis):
-    count = arrived[0].shape[0]
-    size = arrived[0].size
+def split(kernel, place, arrived, out, held):
+    size = sum(a.size for a in arrived)
     return call(
-        functools.partial(split_kernel, axis),
-        [shape(count, 2, HALF, 256)] * 4,
-        5,
-        smem=1,
-        scratch=[pltpu.VMEM(arrived[0].shape, F32)],
-        flops=3 * size,
-        moved=20 * size,
+        kernel, [shape(*out)] * 4, 1 + len(arrived), smem=1, scratch=[pltpu.VMEM(held, F32)], flops=size, moved=5 * size
     )(place, *arrived)
 
 
@@ -244,7 +242,7 @@
     return call(
         spread_kernel,
         [shape(5, 64, 128)] * 4,
-        17,
+        13,
         smem=1,
         scratch=[pltpu.VMEM((5, 2, 64, 256), F32)],
         flops=2**20,
@@ -252,23 +250,22 @@
     )(place, *arrived)
 
 
-def partial_sums(kernel, steps, at, count, place, lefts, depth, operands, specs, carried=()):
+def partial_sums(kernel, steps, place, lefts, depth, operands, specs, x_rows, y_rows):
     left = pltpu.VMEM((512, depth), BF16)
+    outs = [(2, x_rows, R)] * 4 * (x_rows > 0) + [(8, y_rows, 256)] * 4 * (y_rows > 0)
     run = pl.pallas_call(
         kernel,
         grid=(steps,),
-        out_shape=[shape(count, 2, HALF, R)] * 4 + [shape(count, 8, HALF, 256)] * 4,
-        in_specs=[SMEM] + [VMEM] * len(lefts) + specs + [ANY] * len(carried),
-        out_specs=[pl.BlockSpec((1, 2, HALF, R), lambda m: (m + at, 0, 0, 0))] * 4
-        + [pl.BlockSpec((1, 8, HALF, 256), lambda m: (m + at, 0, 0, 0))] * 4,
+        out_shape=[shape(steps, *dims) for dims in outs],
+        in_specs=[SMEM] + [VMEM] * len(lefts) + specs,
+        out_specs=[pl.BlockSpec((1, *dims), lambda m: (m, 0, 0, 0)) for dims in outs],
         scratch_shapes=[left, left, pltpu.VMEM((8, 64, R), F32)],
-        input_output_aliases={1 + len(lefts) + len(specs) + i: i for i in range(len(carried))},
         compiler_params=PARAMS,
         cost_estimate=pl.CostEstimate(
             flops=6 * steps * 512 * depth * R, bytes_accessed=4 * steps * 2**20, transcendentals=0
         ),
     )
-    return run(place, *lefts, *operands, *carried)
+    return run(place, *lefts, *operands)
 
 
 def compute(
@@ -327,11 +324,10 @@
     def block(rows):
         return pl.BlockSpec((1, rows, R), lambda m: (m, 0, 0))
 
-    first = partial_sums(
-        fluid_product_kernel, 2, 0, 2, place, (own_f, left_f), 256, (image_f, other_f), [block(128)] * 2
-    )
-    first_x = exchanged(first[0:4], X)
-    first_y = exchanged(first[4:8], Y)
+    fluid = partial_sums(
+        fluid_product_kernel, 2, place, (own_f, left_f), 256, (image_f, other_f), [block(128)] * 2, 64, 0
+    )
+    fluid_x = exchanged(fluid, X)
 
     image_s = call(
         struct_kernel,
@@ -342,21 +338,21 @@
         scratch=[pltpu.VMEM((4, 512, TILE), F32)],
         flops=6 * 512 * 512 * R,
         moved=5 * 2**20,
-    )(struct_cols, stiff_tiles, mass_tiles, below_s, struct_basis, above_s, first[0])
+    )(struct_cols, stiff_tiles, mass_tiles, below_s, struct_basis, above_s, fluid[0])
     other_s = shifted(image_s, "core", 1)
 
-    wet = partial_sums(wet_product_kernel, 1, 2, 3, place, (own_s, left_s), 512, (image_c, other_c), [VMEM] * 2)
-    second = partial_sums(
-        second_kernel, 2, 0, 3, place, (own_s, left_s), 512, (image_s, other_s), [block(256)] * 2, wet
-    )
-    second_x = exchanged(second[0:4], X)
-    second_y = exchanged(second[4:8], Y)
-
-    first_xy = exchanged(split(place, first_x, 1), Y)
-    first_yx = exchanged(split(place, first_y, 0), X)
-    second_xy = exchanged(split(place, second_x, 1), Y)
-    second_yx = exchanged(split(place, second_y, 0), X)
-    summed = exchanged(spread(place, *first_xy, *first_yx, *second_xy, *second_yx), Z)
+    coupled = partial_sums(wet_product_kernel, 1, place, (own_s, left_s), 512, (image_c, other_c), [VMEM] * 2, 0, 64)
+    coupled_y = exchanged(coupled, Y)
+    struct = partial_sums(
+        second_kernel, 2, place, (own_s, left_s), 512, (image_s, other_s), [block(256)] * 2, HALF, HALF
+    )
+    struct_x = exchanged(struct[0:4], X)
+    struct_y = exchanged(struct[4:8], Y)
+
+    fluid_xy = exchanged(split(to_y_kernel, place, fluid_x, (2, 2, 64, 256), (2, 2, 64, R)), Y)
+    struct_xy = exchanged(split(to_y_kernel, place, struct_x, (2, 2, HALF, 256), (2, 2, HALF, R)), Y)
+    both_yx = exchanged(split(to_x_kernel, place, struct_y + coupled_y, (4, 2, HALF, 256), (4, 8, HALF, 256)), X)
+    summed = exchanged(spread(place, *fluid_xy, *struct_xy, *both_yx), Z)
     fstiff, fmass, stiff, mass, wet = call(last_kernel, [shape(64, 128)] * 5, 4, flops=2**18, moved=2**20)(*summed)
     return stiff, mass, fstiff, fmass, wet
 

time: 220 us -> 225 us (1.023)
  waiting for transfers between devices: 79 us -> 96.4 us
  starting transfers between devices: 79 us -> 68.6 us
    ppermute x4, waiting for transfers between devices: 25 us -> 37.6 us  [from_behind(): return lax.ppermute(value, AXES, pairs)]
    ppermute x32 -> x29, starting transfers between devices: 54.6 us -> 47 us  [shifted(): lax.ppermute(value, axis, [(i, (i + by) % size) for i in range(size)])]
    ppermute x32 -> x29, waiting for transfers between devices: 54.1 us -> 58.9 us  [shifted(): lax.ppermute(value, axis, [(i, (i + by) % size) for i in range(size)])]
    ppermute x4, starting transfers between devices: 12.8 us -> 9.57 us  [from_behind(): return lax.ppermute(value, AXES, pairs)]
    pallas_call x8 -> x7, Pallas kernels: 32 us -> 30.1 us  [the longest x3 17.8 us: partial_sums(): return run(place, *lefts, *operands)]
    unnamed x72 -> x60, local copies, waits for them, and re-layouts: 6.7 us -> 6.93 us
  transfers between devices with their start and end apart: 37 -> 34, of which waited for: 17 -> 18; matrix products, arithmetic and copies ran while one was open for 0% -> 0% of each run, Pallas kernels for 20% -> 19%
where the time goes in v4:
time: 225 us; the launch traced here: 224 us
  waiting for transfers between devices  96.4 us (43%)
  starting transfers between devices  68.6 us (30%)
  Pallas kernels  50.8 us (23%)
  local copies, waits for them, and re-layouts  7.01 us (3%)
    ppermute x29, waiting for transfers between devices, shifted(): lax.ppermute(value, axis, [(i, (i + by) % size) for i in range(size)])  58.9 us
    ppermute x29, starting transfers between devices, shifted(): lax.ppermute(value, axis, [(i, (i + by) % size) for i in range(size)])  47 us
    ppermute x4, waiting for transfers between devices, from_behind(): return lax.ppermute(value, AXES, pairs)  37.6 us
    pallas_call x3, Pallas kernels, partial_sums(): return run(place, *lefts, *operands)  17.8 us
    all_to_all x1, starting transfers between devices, compute(): lax.all_to_all(outgoing, AXES, split_axis=0, concat_axis=0, tiled=True)  12.1 us
    pallas_call x3, Pallas kernels, split(): call(kernel, [shape(*out)] * 4, 1 + len(arrived), smem=1, scratch=[pltpu....  9.61 us
    ppermute x4, starting transfers between devices, from_behind(): return lax.ppermute(value, AXES, pairs)  9.57 us
    unnamed x60, local copies, waits for them, and re-layouts  6.93 us
  transfers between devices with their start and end apart: 34, of which 18 were waited for; matrix products, arithmetic and copies ran while one was open for 0% of the time, Pallas kernels for 19%

profile of v4, /device:TPU:0, one launch (start us, length us, event | category | flops | bytes accessed | tf_op | source)
XLA Modules:
  0.0 224.3 jit_solution(12665120350815105257)
XLA Ops:
  0.6 4.0 %collective-permute-start.1 = (f32[128,1024]{1,0:T(8,128)}, f32[128,1024]{1,0:T(8,128)S(1)}, u32[]{:S(2)}, u32[]{:S(2)}) collective-permute-start(f32[128,1024]{1,0:T(8,128)} %fluid.3), channel_id=1, source_target_pairs={{0,1},{1,2},{2,3},{3,4},{4,5},{5,6},{6,7},{7,8},{8,9},{9,10},{10,1... | collective-permute-start | bytes 1572872 | tf_op jit(solution)/shard_map/ppermute | solution.py:57
  4.6 1.3 collective-permute-start.2
  5.9 0.6 pad_add_fusion.place
  6.5 2.9 %shard_map.146 = (f32[8,64,256]{2,1,0:T(8,128)}, f32[8,64,256]{2,1,0:T(8,128)}, f32[8,64,128]{2,1,0:T(8,128)}, f32[8,64,128]{2,1,0:T(8,128)}) custom-call(s32[4]{0:T(128)} %pad_add_fusion.place, f32[256,1024]{1,0:T(8,128)} %own.3, f32[128,1024]{1,0:T(8,128)} %fluid.3), custom_call_target="tpu_custom_call" | custom-call | flops 1048576 | bytes 3145728 | tf_op jit(solution)/shard_map/pallas_call | solution.py:297
  9.4 17.8 %collective-permute-done.1.lo = f32[128,1024]{1,0:T(8,128)S(1)} collective-permute-done((f32[128,1024]{1,0:T(8,128)}, f32[128,1024]{1,0:T(8,128)S(1)}, u32[]{:S(2)}, u32[]{:S(2)}) %collective-permute-start.1) | collective-permute-done | bytes 524320 | tf_op jit(solution)/shard_map/ppermute | solution.py:57
  27.3 0.8 copy-done.7
  28.3 4.0 %shard_map.147.if0 = f32[2,128,1024]{2,1,0:T(8,128)} custom-call(s32[1,4]{1,0:T(1,128)} %cols.2, f32[1,4,128,128]{3,2,1,0:T(8,128)} %stiff.2, f32[1,4,128,128]{3,2,1,0:T(8,128)} %mass.2, f32[128,1024]{1,0:T(8,128)} %copy-done.7, f32[128,1024]{1,0:T(8,128)} %fluid.3, f32[128,1024]{1,0:T(8,128)} %copy-done.8, f32[8,64,256]{2,1,0:T(8,128)} %get-tuple-element.48.after.ls0), custom_call_target="tpu_custom_call" | custom-call | flops 603979776 | bytes 3145728 | tf_op jit(solution)/shard_map/pallas_call | solution.py:312
  32.3 2.9 %shard_map.153 = f32[128,2,1024]{2,1,0:T(2,128)} custom-call(s32[1,128]{1,0:T(1,128)} %bitcast.6, s32[1,128]{1,0:T(1,128)} %bitcast.7, f32[128,1024]{1,0:T(8,128)} %fluid.3), custom_call_target="tpu_custom_call" | custom-call | flops 201326592 | bytes 2097152 | tf_op jit(solution)/shard_map/pallas_call | solution.py:292
  35.2 12.1 %all-to-all-start = ((f32[128,2,1024]{2,1,0:T(2,128)}), f32[128,2,1024]{2,1,0:T(2,128)S(1)}, u32[]{:S(2)}, u32[]{:S(2)}) async-start(f32[128,2,1024]{2,1,0:T(2,128)} %shard_map.153), calls=%async_computation | async-start | bytes 2097152 | tf_op jit(solution)/shard_map/all_to_all | solution.py:295
  47.4 3.0 %collective-permute-start.11 = (f32[128,1024]{1,0:T(8,128)S(1)}, f32[128,1024]{1,0:T(8,128)S(1)}, u32[]{:S(2)}, u32[]{:S(2)}) collective-permute-start(f32[128,1024]{1,0:T(8,128)S(1)} %get-tuple-element.88), channel_id=1, source_target_pairs={{0,1},{1,2},{2,3},{3,4},{4,5},{5,6},{6,7},{7,8},{8,9},{9,10},{10,1... | collective-permute-start | bytes 1572872 | tf_op jit(solution)/shard_map/ppermute | solution.py:57
  50.4 1.3 collective-permute-start.12
  51.7 3.1 %collective-permute-start = (f32[8,64,128]{2,1,0:T(8,128)S(1)}, f32[8,64,128]{2,1,0:T(8,128)S(1)}, u32[]{:S(2)}, u32[]{:S(2)}) collective-permute-start(f32[8,64,128]{2,1,0:T(8,128)S(1)} %copy-done.26), channel_id=1, source_target_pairs={{0,8},{8,0},{1,9},{9,1},{2,10},{10,2},{3,11},{11,3},{4,12},{12,4},... | collective-permute-start | bytes 786440 | tf_op jit(solution)/shard_map/ppermute | solution.py:51
  54.8 1.2 collective-permute-done.lf1
  56.0 0.7 copy-done.27
  56.7 5.2 %shard_map.148 = (f32[2,2,64,1024]{3,2,1,0:T(8,128)}, f32[2,2,64,1024]{3,2,1,0:T(8,128)}, f32[2,2,64,1024]{3,2,1,0:T(8,128)}, f32[2,2,64,1024]{3,2,1,0:T(8,128)}) custom-call(s32[4]{0:T(128)} %pad_add_fusion.place, f32[8,64,128]{2,1,0:T(8,128)} %get-tuple-element.46.lf0, f32[8,64,128]{2,1,0:T(8,128)} %copy-done.27, f32[2,128,1024]{2,1,0:T(8,128)} %shard_map.147.if0, ...), custom_call_target="tpu_custom_call" | custom-call | flops 1610612736 | bytes 8388608 | tf_op jit(solution)/shard_map/pallas_call | solution.py:268
  61.9 19.7 %collective-permute-done.11.lo = f32[128,1024]{1,0:T(8,128)S(1)} collective-permute-done((f32[128,1024]{1,0:T(8,128)S(1)}, f32[128,1024]{1,0:T(8,128)S(1)}, u32[]{:S(2)}, u32[]{:S(2)}) %collective-permute-start.11) | collective-permute-done | bytes 524320 | tf_op jit(solution)/shard_map/ppermute | solution.py:57
  81.6 0.8 copy-done.9
  82.6 5.9 %shard_map.150.is0 = f32[2,256,1024]{2,1,0:T(8,128)} custom-call(s32[2,4]{1,0:T(2,128)} %cols.3, f32[2,4,128,128]{3,2,1,0:T(8,128)} %stiff.3, f32[2,4,128,128]{3,2,1,0:T(8,128)} %mass.3, f32[128,1024]{1,0:T(8,128)} %copy-done.9, f32[256,1024]{1,0:T(8,128)} %own.3, f32[128,1024]{1,0:T(8,128)} %copy-done.10, f32[2,2,64,1024]{3,2,1,0:T(8,128)} %get-tuple-element.49.a0.after), custom_call_target="tpu_custom_call" | custom-call | flops 1610612736 | bytes 5242880 | tf_op jit(solution)/shard_map/pallas_call | solution.py:332
  88.6 1.0 copy-done.1
  89.6 3.1 %shard_map.154.ic0 = f32[256,1024]{1,0:T(8,128)} custom-call(f32[256,256]{1,0:T(8,128)} %coupling.1, f32[128,2,1024]{2,1,0:T(2,128)} %copy-done.1), custom_call_target="tpu_custom_call" | custom-call | flops 402653184 | bytes 2097152 | tf_op jit(solution)/shard_map/pallas_call | solution.py:309
  93.2 3.2 %collective-permute-done.10.ls1 = f32[8,64,256]{2,1,0:T(8,128)S(1)} collective-permute-done((f32[8,64,256]{2,1,0:T(8,128)S(1)}, f32[8,64,256]{2,1,0:T(8,128)S(1)}, u32[]{:S(2)}, u32[]{:S(2)}) %collective-permute-start.10) | collective-permute-done | bytes 524320 | tf_op jit(solution)/shard_map/ppermute | solution.py:51
  96.4 0.8 copy-done.25
  97.2 1.0 copy-done.23
  98.2 5.2 %shard_map.155 = (f32[1,8,64,256]{3,2,1,0:T(8,128)}, f32[1,8,64,256]{3,2,1,0:T(8,128)}, f32[1,8,64,256]{3,2,1,0:T(8,128)}, f32[1,8,64,256]{3,2,1,0:T(8,128)}) custom-call(s32[4]{0:T(128)} %pad_add_fusion.place, f32[8,64,256]{2,1,0:T(8,128)} %get-tuple-element.48.after.ls0, f32[8,64,256]{2,1,0:T(8,128)} %copy-done.25, f32[256,1024]{1,0:T(8,128)} %shard_map.154.ic0, ...), custom_call_target="tpu_custom_call" | custom-call | flops 1610612736 | bytes 4194304 | tf_op jit(solution)/shard_map/pallas_call | solution.py:268
  103.4 2.8 %collective-permute-start.24 = (f32[1,8,64,256]{3,2,1,0:T(8,128)}, f32[1,8,64,256]{3,2,1,0:T(8,128)S(1)}, u32[]{:S(2)}, u32[]{:S(2)}) collective-permute-start(f32[1,8,64,256]{3,2,1,0:T(8,128)} %get-tuple-element.71), channel_id=1, source_target_pairs={{0,2},{2,4},{4,6},{6,0},{1,3},{3,5},{5,7},{7,1},{8,10},{10,12},{12... | collective-permute-start | bytes 1572872 | tf_op jit(solution)/shard_map/ppermute | solution.py:51
  106.3 1.1 collective-permute-start.4
  107.4 2.7 %collective-permute-start.5 = (f32[2,2,64,1024]{3,2,1,0:T(8,128)}, f32[2,2,64,1024]{3,2,1,0:T(8,128)S(1)}, u32[]{:S(2)}, u32[]{:S(2)}) collective-permute-start(f32[2,2,64,1024]{3,2,1,0:T(8,128)} %get-tuple-element.51), channel_id=1, source_target_pairs={{0,32},{16,48},{32,0},{48,16},{1,33},{17,49},{33,1},{49,17},{2,34}... | collective-permute-start | bytes 3145736 | tf_op jit(solution)/shard_map/ppermute | solution.py:51
  110.1 1.5 collective-permute-start.6
  111.5 8.4 %collective-permute-done.24.b1 = f32[1,8,64,256]{3,2,1,0:T(8,128)S(1)} collective-permute-done((f32[1,8,64,256]{3,2,1,0:T(8,128)}, f32[1,8,64,256]{3,2,1,0:T(8,128)S(1)}, u32[]{:S(2)}, u32[]{:S(2)}) %collective-permute-start.24) | collective-permute-done | bytes 524320 | tf_op jit(solution)/shard_map/ppermute | solution.py:51
  120.0 1.9 collective-permute-start.25
  121.9 1.5 collective-permute-start.26
  123.4 7.4 %shard_map.151 = (f32[2,2,32,1024]{3,2,1,0:T(8,128)}, f32[2,2,32,1024]{3,2,1,0:T(8,128)}, f32[2,2,32,1024]{3,2,1,0:T(8,128)}, f32[2,2,32,1024]{3,2,1,0:T(8,128)}...) custom-call(s32[4]{0:T(128)} %pad_add_fusion.place, ...), custom_call_target="tpu_custom_call" | custom-call | flops 3221225472 | bytes 8388608 | tf_op jit(solution)/shard_map/pallas_call | solution.py:268
  130.8 4.7 %collective-permute-done.25.b2 = f32[1,8,64,256]{3,2,1,0:T(8,128)} collective-permute-done((f32[1,8,64,256]{3,2,1,0:T(8,128)}, f32[1,8,64,256]{3,2,1,0:T(8,128)}, u32[]{:S(2)}, u32[]{:S(2)}) %collective-permute-start.25) | collective-permute-done | bytes 524320 | tf_op jit(solution)/shard_map/ppermute | solution.py:51
  135.4 2.1 collective-permute-start.14
  137.5 8.0 %collective-permute-done.26.b3 = f32[1,8,64,256]{3,2,1,0:T(8,128)} collective-permute-done((f32[1,8,64,256]{3,2,1,0:T(8,128)}, f32[1,8,64,256]{3,2,1,0:T(8,128)}, u32[]{:S(2)}, u32[]{:S(2)}) %collective-permute-start.26) | collective-permute-done | bytes 524320 | tf_op jit(solution)/shard_map/ppermute | solution.py:51
  145.5 2.7 %collective-permute-start.15 = (f32[2,2,32,1024]{3,2,1,0:T(8,128)}, f32[2,2,32,1024]{3,2,1,0:T(8,128)}, u32[]{:S(2)}, u32[]{:S(2)}) collective-permute-start(f32[2,2,32,1024]{3,2,1,0:T(8,128)} %get-tuple-element.60), channel_id=1, source_target_pairs={{0,32},{16,48},{32,0},{48,16},{1,33},{17,49},{33,1},{49,17},{2,34}... | collective-permute-start | bytes 1572872 | tf_op jit(solution)/shard_map/ppermute | solution.py:51
  148.2 1.4 collective-permute-start.16
  149.6 7.3 %collective-permute-done.5.a2 = f32[2,2,64,1024]{3,2,1,0:T(8,128)S(1)} collective-permute-done((f32[2,2,64,1024]{3,2,1,0:T(8,128)}, f32[2,2,64,1024]{3,2,1,0:T(8,128)S(1)}, u32[]{:S(2)}, u32[]{:S(2)}) %collective-permute-start.5) | collective-permute-done | bytes 1048608 | tf_op jit(solution)/shard_map/ppermute | solution.py:51
  156.8 1.1 collective-permute-start.20
  157.9 2.6 %collective-permute-start.21 = (f32[2,8,32,256]{3,2,1,0:T(8,128)}, f32[2,8,32,256]{3,2,1,0:T(8,128)}, u32[]{:S(2)}, u32[]{:S(2)}) collective-permute-start(f32[2,8,32,256]{3,2,1,0:T(8,128)} %get-tuple-element.68), channel_id=1, source_target_pairs={{0,4},{2,6},{4,0},{6,2},{1,5},{3,7},{5,1},{7,3},{8,12},{10,14},{12... | collective-permute-start | bytes 1572872 | tf_op jit(solution)/shard_map/ppermute | solution.py:51
  160.5 7.6 %collective-permute-done.14.a1 = f32[2,2,32,1024]{3,2,1,0:T(8,128)} collective-permute-done((f32[2,2,32,1024]{3,2,1,0:T(8,128)}, f32[2,2,32,1024]{3,2,1,0:T(8,128)}, u32[]{:S(2)}, u32[]{:S(2)}) %collective-permute-start.14) | collective-permute-done | bytes 524320 | tf_op jit(solution)/shard_map/ppermute | solution.py:51
  168.1 2.2 collective-permute-start.22
  170.3 3.6 %shard_map.149 = (f32[2,2,64,256]{3,2,1,0:T(8,128)}, f32[2,2,64,256]{3,2,1,0:T(8,128)}, f32[2,2,64,256]{3,2,1,0:T(8,128)}, f32[2,2,64,256]{3,2,1,0:T(8,128)}) custom-call(s32[4]{0:T(128)} %pad_add_fusion.place, f32[2,2,64,1024]{3,2,1,0:T(8,128)} %get-tuple-element.49.a0.after, f32[2,2,64,1024]{3,2,1,0:T(8,128)} %copy-done.2, f32[2,2,64,1024]{3,2,1,0:T(8,128)} %copy-done.3, ...), custom_call_target="tpu_custom_call" | custom-call | flops 1048576 | bytes 5242880 | tf_op jit(solution)/shard_map/pallas_call | solution.py:236
  173.9 4.7 %collective-permute-done.15.a2 = f32[2,2,32,1024]{3,2,1,0:T(8,128)} collective-permute-done((f32[2,2,32,1024]{3,2,1,0:T(8,128)}, f32[2,2,32,1024]{3,2,1,0:T(8,128)}, u32[]{:S(2)}, u32[]{:S(2)}) %collective-permute-start.15) | collective-permute-done | bytes 524320 | tf_op jit(solution)/shard_map/ppermute | solution.py:51
  178.5 1.1 collective-permute-start.7
  179.6 2.6 %collective-permute-start.8 = (f32[2,2,64,256]{3,2,1,0:T(8,128)}, f32[2,2,64,256]{3,2,1,0:T(8,128)S(1)}, u32[]{:S(2)}, u32[]{:S(2)}) collective-permute-start(f32[2,2,64,256]{3,2,1,0:T(8,128)} %get-tuple-element.55), channel_id=1, source_target_pairs={{0,4},{2,6},{4,0},{6,2},{1,5},{3,7},{5,1},{7,3},{8,12},{10,14},{12... | collective-permute-start | bytes 786440 | tf_op jit(solution)/shard_map/ppermute | solution.py:51
  182.2 1.5 collective-permute-start.9
  183.7 2.5 %shard_map.152 = (f32[2,2,32,256]{3,2,1,0:T(8,128)}, f32[2,2,32,256]{3,2,1,0:T(8,128)}, f32[2,2,32,256]{3,2,1,0:T(8,128)}, f32[2,2,32,256]{3,2,1,0:T(8,128)}) custom-call(s32[4]{0:T(128)} %pad_add_fusion.place, f32[2,2,32,1024]{3,2,1,0:T(8,128)} %get-tuple-element.58.a0, f32[2,2,32,1024]{3,2,1,0:T(8,128)} %collective-permute-done.14.a1, ...), custom_call_target="tpu_custom_call" | custom-call | flops 524288 | bytes 2621440 | tf_op jit(solution)/shard_map/pallas_call | solution.py:236
  186.2 0.6 collective-permute-start.17
  186.8 3.5 %shard_map.156 = (f32[4,2,32,256]{3,2,1,0:T(8,128)}, f32[4,2,32,256]{3,2,1,0:T(8,128)}, f32[4,2,32,256]{3,2,1,0:T(8,128)}, f32[4,2,32,256]{3,2,1,0:T(8,128)}) custom-call(s32[4]{0:T(128)} %pad_add_fusion.place, f32[2,8,32,256]{3,2,1,0:T(8,128)} %get-tuple-element.66.a0, f32[2,8,32,256]{3,2,1,0:T(8,128)} %copy-done.6, ...), custom_call_target="tpu_custom_call" | custom-call | flops 1048576 | bytes 5242880 | tf_op jit(solution)/shard_map/pallas_call | solution.py:236
  190.3 0.5 collective-permute-start.27
  190.8 1.4 collective-permute-done.7.refs_1_
  192.2 1.1 collective-permute-start.28
  193.2 1.6 collective-permute-done.8.refs_2_
  194.9 1.2 collective-permute-start.18
  196.2 2.9 %collective-permute-start.19 = (f32[2,2,32,256]{3,2,1,0:T(8,128)S(1)}, f32[2,2,32,256]{3,2,1,0:T(8,128)S(1)}, u32[]{:S(2)}, u32[]{:S(2)}) collective-permute-start(f32[2,2,32,256]{3,2,1,0:T(8,128)S(1)} %copy-done.28), channel_id=1, source_target_pairs={{0,6},{2,0},{4,2},{6,4},{1,7},{3,1},{5,3},{7,5},{8,14},{10,8},{12,... | collective-permute-start | bytes 393224 | tf_op jit(solution)/shard_map/ppermute | solution.py:51
  199.0 2.5 %collective-permute-done.18.refs_6_ = f32[2,2,32,256]{3,2,1,0:T(8,128)S(1)} collective-permute-done((f32[2,2,32,256]{3,2,1,0:T(8,128)S(1)}, f32[2,2,32,256]{3,2,1,0:T(8,128)S(1)}, u32[]{:S(2)}, u32[]{:S(2)}) %collective-permute-start.18) | collective-permute-done | bytes 131104 | tf_op jit(solution)/shard_map/ppermute | solution.py:51
  201.5 2.7 %collective-permute-done.19.refs_7_ = f32[2,2,32,256]{3,2,1,0:T(8,128)S(1)} collective-permute-done((f32[2,2,32,256]{3,2,1,0:T(8,128)S(1)}, f32[2,2,32,256]{3,2,1,0:T(8,128)S(1)}, u32[]{:S(2)}, u32[]{:S(2)}) %collective-permute-start.19) | collective-permute-done | bytes 131104 | tf_op jit(solution)/shard_map/ppermute | solution.py:51
  205.2 2.7 %shard_map.157 = (f32[5,64,128]{2,1,0:T(8,128)}, f32[5,64,128]{2,1,0:T(8,128)}, f32[5,64,128]{2,1,0:T(8,128)}, f32[5,64,128]{2,1,0:T(8,128)}) custom-call(s32[4]{0:T(128)} %pad_add_fusion.place, f32[2,2,64,256]{3,2,1,0:T(8,128)} %get-tuple-element.53.refs_0_, f32[2,2,64,256]{3,2,1,0:T(8,128)} %copy-done.11, f32[2,2,64,256]{3,2,1,0:T(8,128)} %copy-done.12, ...), custom_call_target="tpu_custom_call" | custom-call | flops 1048576 | bytes 4194304 | tf_op jit(solution)/shard_map/pallas_call | solution.py:242
  207.9 4.9 %collective-permute-start.30 = (f32[5,64,128]{2,1,0:T(8,128)}, f32[5,64,128]{2,1,0:T(8,128)S(1)}, u32[]{:S(2)}, u32[]{:S(2)}) collective-permute-start(f32[5,64,128]{2,1,0:T(8,128)} %get-tuple-element.79), channel_id=1, source_target_pairs={{0,1},{1,64},{64,65},{65,0},{2,3},{3,66},{66,67},{67,2},{4,5},{5,6... | collective-permute-start | bytes 491528 | tf_op jit(solution)/shard_map/ppermute | solution.py:51
  212.8 3.4 %collective-permute-start.31 = (f32[5,64,128]{2,1,0:T(8,128)}, f32[5,64,128]{2,1,0:T(8,128)S(1)}, u32[]{:S(2)}, u32[]{:S(2)}) collective-permute-start(f32[5,64,128]{2,1,0:T(8,128)} %get-tuple-element.80), channel_id=1, source_target_pairs={{0,64},{1,65},{64,0},{65,1},{2,66},{3,67},{66,2},{67,3},{4,68},{5,... | collective-permute-start | bytes 491528 | tf_op jit(solution)/shard_map/ppermute | solution.py:51
  216.3 2.0 collective-permute-done.30.a1
  218.3 3.2 %collective-permute-done.31.a2 = f32[5,64,128]{2,1,0:T(8,128)S(1)} collective-permute-done((f32[5,64,128]{2,1,0:T(8,128)}, f32[5,64,128]{2,1,0:T(8,128)S(1)}, u32[]{:S(2)}, u32[]{:S(2)}) %collective-permute-start.31) | collective-permute-done | bytes 163872 | tf_op jit(solution)/shard_map/ppermute | solution.py:51
  222.5 1.8 shard_map.158
  (79 shorter events, 3.0 us)
Async XLA Ops:
  0.6 26.7 %collective-permute-start.1 = (f32[128,1024]{1,0:T(8,128)}, f32[128,1024]{1,0:T(8,128)S(1)}, u32[]{:S(2)}, u32[]{:S(2)}) collective-permute-start(f32[128,1024]{1,0:T(8,128)} %fluid.3), channel_id=1, source_target_pairs={{0,1},{1,2},{2,3},{3,4},{4,5},{5,6},{6,7},{7,8},{8,9},{9,10},{10,1... | collective-permute-start | bytes 1572872 | tf_op jit(solution)/shard_map/ppermute | solution.py:57
  4.6 22.7 %collective-permute-start.2 = (f32[128,1024]{1,0:T(8,128)}, f32[128,1024]{1,0:T(8,128)S(1)}, u32[]{:S(2)}, u32[]{:S(2)}) collective-permute-start(f32[128,1024]{1,0:T(8,128)} %fluid.3), channel_id=1, source_target_pairs={{1,0},{2,1},{3,2},{4,3},{5,4},{6,5},{7,6},{8,7},{9,8},{10,9},{11,1... | collective-permute-start | bytes 1572872 | tf_op jit(solution)/shard_map/ppermute | solution.py:57
  27.3 0.8 copy-start.7
  27.3 1.0 copy-start.8
  32.3 15.0 %copy-start = (f32[256,1024]{1,0:T(8,128)S(1)}, f32[256,1024]{1,0:T(8,128)}, u32[]{:S(2)}) copy-start(f32[256,1024]{1,0:T(8,128)} %own.3) | copy-start | bytes 3145732
  32.3 23.7 %collective-permute-start.3 = (f32[2,128,1024]{2,1,0:T(8,128)}, f32[2,128,1024]{2,1,0:T(8,128)}, u32[]{:S(2)}, u32[]{:S(2)}) collective-permute-start(f32[2,128,1024]{2,1,0:T(8,128)} %shard_map.147.if0), channel_id=1, source_target_pairs={{0,8},{8,0},{1,9},{9,1},{2,10},{10,2},{3,11},{11,3},{4,12},{12,4},... | collective-permute-start | bytes 3145736 | tf_op jit(solution)/shard_map/ppermute | solution.py:51
  35.2 16.5 %copy-start.26 = (f32[8,64,128]{2,1,0:T(8,128)S(1)}, f32[8,64,128]{2,1,0:T(8,128)}, u32[]{:S(2)}) copy-start(f32[8,64,128]{2,1,0:T(8,128)} %get-tuple-element.47) | copy-start | bytes 786436
  35.2 53.4 %all-to-all-start = ((f32[128,2,1024]{2,1,0:T(2,128)}), f32[128,2,1024]{2,1,0:T(2,128)S(1)}, u32[]{:S(2)}, u32[]{:S(2)}) async-start(f32[128,2,1024]{2,1,0:T(2,128)} %shard_map.153), calls=%async_computation | async-start | bytes 2097152 | tf_op jit(solution)/shard_map/all_to_all | solution.py:295
  47.4 34.2 %collective-permute-start.11 = (f32[128,1024]{1,0:T(8,128)S(1)}, f32[128,1024]{1,0:T(8,128)S(1)}, u32[]{:S(2)}, u32[]{:S(2)}) collective-permute-start(f32[128,1024]{1,0:T(8,128)S(1)} %get-tuple-element.88), channel_id=1, source_target_pairs={{0,1},{1,2},{2,3},{3,4},{4,5},{5,6},{6,7},{7,8},{8,9},{9,10},{10,1... | collective-permute-start | bytes 1572872 | tf_op jit(solution)/shard_map/ppermute | solution.py:57
  50.4 31.2 %collective-permute-start.12 = (f32[128,1024]{1,0:T(8,128)S(1)}, f32[128,1024]{1,0:T(8,128)S(1)}, u32[]{:S(2)}, u32[]{:S(2)}) collective-permute-start(f32[128,1024]{1,0:T(8,128)S(1)} %get-tuple-element.87), channel_id=1, source_target_pairs={{1,0},{2,1},{3,2},{4,3},{5,4},{6,5},{7,6},{8,7},{9,8},{10,9},{11,1... | collective-permute-start | bytes 1572872 | tf_op jit(solution)/shard_map/ppermute | solution.py:57
  51.7 4.3 %collective-permute-start = (f32[8,64,128]{2,1,0:T(8,128)S(1)}, f32[8,64,128]{2,1,0:T(8,128)S(1)}, u32[]{:S(2)}, u32[]{:S(2)}) collective-permute-start(f32[8,64,128]{2,1,0:T(8,128)S(1)} %copy-done.26), channel_id=1, source_target_pairs={{0,8},{8,0},{1,9},{9,1},{2,10},{10,2},{3,11},{11,3},{4,12},{12,4},... | collective-permute-start | bytes 786440 | tf_op jit(solution)/shard_map/ppermute | solution.py:51
  56.0 0.7 copy-start.27
  81.6 0.8 copy-start.9
  81.6 1.0 copy-start.10
  88.6 4.6 %copy-start.24 = (f32[8,64,256]{2,1,0:T(8,128)S(1)}, f32[8,64,256]{2,1,0:T(8,128)}, u32[]{:S(2)}) copy-start(f32[8,64,256]{2,1,0:T(8,128)} %get-tuple-element.57) | copy-start | bytes 1572868
  88.6 33.3 %collective-permute-start.13 = (f32[2,256,1024]{2,1,0:T(8,128)}, f32[2,256,1024]{2,1,0:T(8,128)}, u32[]{:S(2)}, u32[]{:S(2)}) collective-permute-start(f32[2,256,1024]{2,1,0:T(8,128)} %shard_map.150.is0), channel_id=1, source_target_pairs={{0,8},{8,0},{1,9},{9,1},{2,10},{10,2},{3,11},{11,3},{4,12},{12,4},... | collective-permute-start | bytes 6291464 | tf_op jit(solution)/shard_map/ppermute | solution.py:51
  88.6 1.0 copy-start.1
  92.7 3.7 %collective-permute-start.23 = (f32[256,1024]{1,0:T(8,128)}, f32[256,1024]{1,0:T(8,128)S(1)}, u32[]{:S(2)}, u32[]{:S(2)}) collective-permute-start(f32[256,1024]{1,0:T(8,128)} %shard_map.154.ic0), channel_id=1, source_target_pairs={{0,8},{8,0},{1,9},{9,1},{2,10},{10,2},{3,11},{11,3},{4,12},{12,4},... | collective-permute-start | bytes 3145736 | tf_op jit(solution)/shard_map/ppermute | solution.py:51
  93.2 3.2 %collective-permute-start.10 = (f32[8,64,256]{2,1,0:T(8,128)S(1)}, f32[8,64,256]{2,1,0:T(8,128)S(1)}, u32[]{:S(2)}, u32[]{:S(2)}) collective-permute-start(f32[8,64,256]{2,1,0:T(8,128)S(1)} %copy-done.24), channel_id=1, source_target_pairs={{0,8},{8,0},{1,9},{9,1},{2,10},{10,2},{3,11},{11,3},{4,12},{12,4},... | collective-permute-start | bytes 1572872 | tf_op jit(solution)/shard_map/ppermute | solution.py:51
  96.4 0.8 copy-start.25
  97.2 1.0 copy-start.23
  103.4 16.5 %collective-permute-start.24 = (f32[1,8,64,256]{3,2,1,0:T(8,128)}, f32[1,8,64,256]{3,2,1,0:T(8,128)S(1)}, u32[]{:S(2)}, u32[]{:S(2)}) collective-permute-start(f32[1,8,64,256]{3,2,1,0:T(8,128)} %get-tuple-element.71), channel_id=1, source_target_pairs={{0,2},{2,4},{4,6},{6,0},{1,3},{3,5},{5,7},{7,1},{8,10},{10,12},{12... | collective-permute-start | bytes 1572872 | tf_op jit(solution)/shard_map/ppermute | solution.py:51
  106.3 41.9 %collective-permute-start.4 = (f32[2,2,64,1024]{3,2,1,0:T(8,128)}, f32[2,2,64,1024]{3,2,1,0:T(8,128)S(1)}, u32[]{:S(2)}, u32[]{:S(2)}) collective-permute-start(f32[2,2,64,1024]{3,2,1,0:T(8,128)} %get-tuple-element.50), channel_id=1, source_target_pairs={{0,16},{16,32},{32,48},{48,0},{1,17},{17,33},{33,49},{49,1},{2,18}... | collective-permute-start | bytes 3145736 | tf_op jit(solution)/shard_map/ppermute | solution.py:51
  107.4 49.4 %collective-permute-start.5 = (f32[2,2,64,1024]{3,2,1,0:T(8,128)}, f32[2,2,64,1024]{3,2,1,0:T(8,128)S(1)}, u32[]{:S(2)}, u32[]{:S(2)}) collective-permute-start(f32[2,2,64,1024]{3,2,1,0:T(8,128)} %get-tuple-element.51), channel_id=1, source_target_pairs={{0,32},{16,48},{32,0},{48,16},{1,33},{17,49},{33,1},{49,17},{2,34}... | collective-permute-start | bytes 3145736 | tf_op jit(solution)/shard_map/ppermute | solution.py:51
  110.1 47.8 %collective-permute-start.6 = (f32[2,2,64,1024]{3,2,1,0:T(8,128)}, f32[2,2,64,1024]{3,2,1,0:T(8,128)S(1)}, u32[]{:S(2)}, u32[]{:S(2)}) collective-permute-start(f32[2,2,64,1024]{3,2,1,0:T(8,128)} %get-tuple-element.52), channel_id=1, source_target_pairs={{0,48},{16,0},{32,16},{48,32},{1,49},{17,1},{33,17},{49,33},{2,50}... | collective-permute-start | bytes 3145736 | tf_op jit(solution)/shard_map/ppermute | solution.py:51
  120.0 10.8 %copy-start.5 = (f32[1,8,64,256]{3,2,1,0:T(8,128)}, f32[1,8,64,256]{3,2,1,0:T(8,128)S(1)}, u32[]{:S(2)}) copy-start(f32[1,8,64,256]{3,2,1,0:T(8,128)S(1)} %collective-permute-done.24.b1) | copy-start | bytes 1572868
  120.0 15.4 %collective-permute-start.25 = (f32[1,8,64,256]{3,2,1,0:T(8,128)}, f32[1,8,64,256]{3,2,1,0:T(8,128)}, u32[]{:S(2)}, u32[]{:S(2)}) collective-permute-start(f32[1,8,64,256]{3,2,1,0:T(8,128)} %get-tuple-element.72), channel_id=1, source_target_pairs={{0,4},{2,6},{4,0},{6,2},{1,5},{3,7},{5,1},{7,3},{8,12},{10,14},{12... | collective-permute-start | bytes 1572872 | tf_op jit(solution)/shard_map/ppermute | solution.py:51
  121.9 23.6 %collective-permute-start.26 = (f32[1,8,64,256]{3,2,1,0:T(8,128)}, f32[1,8,64,256]{3,2,1,0:T(8,128)}, u32[]{:S(2)}, u32[]{:S(2)}) collective-permute-start(f32[1,8,64,256]{3,2,1,0:T(8,128)} %get-tuple-element.73), channel_id=1, source_target_pairs={{0,6},{2,0},{4,2},{6,4},{1,7},{3,1},{5,3},{7,5},{8,14},{10,8},{12,... | collective-permute-start | bytes 1572872 | tf_op jit(solution)/shard_map/ppermute | solution.py:51
  135.4 32.6 %collective-permute-start.14 = (f32[2,2,32,1024]{3,2,1,0:T(8,128)}, f32[2,2,32,1024]{3,2,1,0:T(8,128)}, u32[]{:S(2)}, u32[]{:S(2)}) collective-permute-start(f32[2,2,32,1024]{3,2,1,0:T(8,128)} %get-tuple-element.59), channel_id=1, source_target_pairs={{0,16},{16,32},{32,48},{48,0},{1,17},{17,33},{33,49},{49,1},{2,18}... | collective-permute-start | bytes 1572872 | tf_op jit(solution)/shard_map/ppermute | solution.py:51
  145.5 33.0 %collective-permute-start.15 = (f32[2,2,32,1024]{3,2,1,0:T(8,128)}, f32[2,2,32,1024]{3,2,1,0:T(8,128)}, u32[]{:S(2)}, u32[]{:S(2)}) collective-permute-start(f32[2,2,32,1024]{3,2,1,0:T(8,128)} %get-tuple-element.60), channel_id=1, source_target_pairs={{0,32},{16,48},{32,0},{48,16},{1,33},{17,49},{33,1},{49,17},{2,34}... | collective-permute-start | bytes 1572872 | tf_op jit(solution)/shard_map/ppermute | solution.py:51
  148.2 22.1 %copy-start.2 = (f32[2,2,64,1024]{3,2,1,0:T(8,128)}, f32[2,2,64,1024]{3,2,1,0:T(8,128)S(1)}, u32[]{:S(2)}) copy-start(f32[2,2,64,1024]{3,2,1,0:T(8,128)S(1)} %collective-permute-done.4.a1) | copy-start | bytes 3145732
  148.2 31.4 %collective-permute-start.16 = (f32[2,2,32,1024]{3,2,1,0:T(8,128)}, f32[2,2,32,1024]{3,2,1,0:T(8,128)}, u32[]{:S(2)}, u32[]{:S(2)}) collective-permute-start(f32[2,2,32,1024]{3,2,1,0:T(8,128)} %get-tuple-element.61), channel_id=1, source_target_pairs={{0,48},{16,0},{32,16},{48,32},{1,49},{17,1},{33,17},{49,33},{2,50}... | collective-permute-start | bytes 1572872 | tf_op jit(solution)/shard_map/ppermute | solution.py:51
  156.8 13.5 %copy-start.3 = (f32[2,2,64,1024]{3,2,1,0:T(8,128)}, f32[2,2,64,1024]{3,2,1,0:T(8,128)S(1)}, u32[]{:S(2)}) copy-start(f32[2,2,64,1024]{3,2,1,0:T(8,128)S(1)} %collective-permute-done.5.a2) | copy-start | bytes 3145732
  156.8 25.4 %collective-permute-start.20 = (f32[2,8,32,256]{3,2,1,0:T(8,128)}, f32[2,8,32,256]{3,2,1,0:T(8,128)S(1)}, u32[]{:S(2)}, u32[]{:S(2)}) collective-permute-start(f32[2,8,32,256]{3,2,1,0:T(8,128)} %get-tuple-element.67), channel_id=1, source_target_pairs={{0,2},{2,4},{4,6},{6,0},{1,3},{3,5},{5,7},{7,1},{8,10},{10,12},{12... | collective-permute-start | bytes 1572872 | tf_op jit(solution)/shard_map/ppermute | solution.py:51
  157.9 12.4 %copy-start.4 = (f32[2,2,64,1024]{3,2,1,0:T(8,128)}, f32[2,2,64,1024]{3,2,1,0:T(8,128)S(1)}, u32[]{:S(2)}) copy-start(f32[2,2,64,1024]{3,2,1,0:T(8,128)S(1)} %collective-permute-done.6.a3) | copy-start | bytes 3145732
  157.9 28.3 %collective-permute-start.21 = (f32[2,8,32,256]{3,2,1,0:T(8,128)}, f32[2,8,32,256]{3,2,1,0:T(8,128)}, u32[]{:S(2)}, u32[]{:S(2)}) collective-permute-start(f32[2,8,32,256]{3,2,1,0:T(8,128)} %get-tuple-element.68), channel_id=1, source_target_pairs={{0,4},{2,6},{4,0},{6,2},{1,5},{3,7},{5,1},{7,3},{8,12},{10,14},{12... | collective-permute-start | bytes 1572872 | tf_op jit(solution)/shard_map/ppermute | solution.py:51
  168.1 18.7 %collective-permute-start.22 = (f32[2,8,32,256]{3,2,1,0:T(8,128)}, f32[2,8,32,256]{3,2,1,0:T(8,128)}, u32[]{:S(2)}, u32[]{:S(2)}) collective-permute-start(f32[2,8,32,256]{3,2,1,0:T(8,128)} %get-tuple-element.69), channel_id=1, source_target_pairs={{0,6},{2,0},{4,2},{6,4},{1,7},{3,1},{5,3},{7,5},{8,14},{10,8},{12,... | collective-permute-start | bytes 1572872 | tf_op jit(solution)/shard_map/ppermute | solution.py:51
  178.5 13.7 %collective-permute-start.7 = (f32[2,2,64,256]{3,2,1,0:T(8,128)}, f32[2,2,64,256]{3,2,1,0:T(8,128)S(1)}, u32[]{:S(2)}, u32[]{:S(2)}) collective-permute-start(f32[2,2,64,256]{3,2,1,0:T(8,128)} %get-tuple-element.54), channel_id=1, source_target_pairs={{0,2},{2,4},{4,6},{6,0},{1,3},{3,5},{5,7},{7,1},{8,10},{10,12},{12... | collective-permute-start | bytes 786440 | tf_op jit(solution)/shard_map/ppermute | solution.py:51
  179.6 15.3 %collective-permute-start.8 = (f32[2,2,64,256]{3,2,1,0:T(8,128)}, f32[2,2,64,256]{3,2,1,0:T(8,128)S(1)}, u32[]{:S(2)}, u32[]{:S(2)}) collective-permute-start(f32[2,2,64,256]{3,2,1,0:T(8,128)} %get-tuple-element.55), channel_id=1, source_target_pairs={{0,4},{2,6},{4,0},{6,2},{1,5},{3,7},{5,1},{7,3},{8,12},{10,14},{12... | collective-permute-start | bytes 786440 | tf_op jit(solution)/shard_map/ppermute | solution.py:51
  182.2 4.6 %copy-start.6 = (f32[2,8,32,256]{3,2,1,0:T(8,128)}, f32[2,8,32,256]{3,2,1,0:T(8,128)S(1)}, u32[]{:S(2)}) copy-start(f32[2,8,32,256]{3,2,1,0:T(8,128)S(1)} %collective-permute-done.20.a1) | copy-start | bytes 1572868
  182.2 12.7 %collective-permute-start.9 = (f32[2,2,64,256]{3,2,1,0:T(8,128)}, f32[2,2,64,256]{3,2,1,0:T(8,128)S(1)}, u32[]{:S(2)}, u32[]{:S(2)}) collective-permute-start(f32[2,2,64,256]{3,2,1,0:T(8,128)} %get-tuple-element.56), channel_id=1, source_target_pairs={{0,6},{2,0},{4,2},{6,4},{1,7},{3,1},{5,3},{7,5},{8,14},{10,8},{12,... | collective-permute-start | bytes 786440 | tf_op jit(solution)/shard_map/ppermute | solution.py:51
  186.2 10.0 %collective-permute-start.17 = (f32[2,2,32,256]{3,2,1,0:T(8,128)}, f32[2,2,32,256]{3,2,1,0:T(8,128)S(1)}, u32[]{:S(2)}, u32[]{:S(2)}) collective-permute-start(f32[2,2,32,256]{3,2,1,0:T(8,128)} %get-tuple-element.63), channel_id=1, source_target_pairs={{0,2},{2,4},{4,6},{6,0},{1,3},{3,5},{5,7},{7,1},{8,10},{10,12},{12... | collective-permute-start | bytes 393224 | tf_op jit(solution)/shard_map/ppermute | solution.py:51
  186.8 8.1 %copy-start.29 = (f32[2,2,32,256]{3,2,1,0:T(8,128)S(1)}, f32[2,2,32,256]{3,2,1,0:T(8,128)}, u32[]{:S(2)}) copy-start(f32[2,2,32,256]{3,2,1,0:T(8,128)} %get-tuple-element.64) | copy-start | bytes 393220
  186.8 9.4 %copy-start.28 = (f32[2,2,32,256]{3,2,1,0:T(8,128)S(1)}, f32[2,2,32,256]{3,2,1,0:T(8,128)}, u32[]{:S(2)}) copy-start(f32[2,2,32,256]{3,2,1,0:T(8,128)} %get-tuple-element.65) | copy-start | bytes 393220
  190.3 13.9 %collective-permute-start.27 = (f32[4,2,32,256]{3,2,1,0:T(8,128)}, f32[4,2,32,256]{3,2,1,0:T(8,128)S(1)}, u32[]{:S(2)}, u32[]{:S(2)}) collective-permute-start(f32[4,2,32,256]{3,2,1,0:T(8,128)} %get-tuple-element.75), channel_id=1, source_target_pairs={{0,16},{16,32},{32,48},{48,0},{1,17},{17,33},{33,49},{49,1},{2,18}... | collective-permute-start | bytes 786440 | tf_op jit(solution)/shard_map/ppermute | solution.py:51
  192.2 12.2 %copy-start.11 = (f32[2,2,64,256]{3,2,1,0:T(8,128)}, f32[2,2,64,256]{3,2,1,0:T(8,128)S(1)}, u32[]{:S(2)}) copy-start(f32[2,2,64,256]{3,2,1,0:T(8,128)S(1)} %collective-permute-done.7.refs_1_) | copy-start | bytes 786436
  192.2 12.2 %collective-permute-start.28 = (f32[4,2,32,256]{3,2,1,0:T(8,128)}, f32[4,2,32,256]{3,2,1,0:T(8,128)S(1)}, u32[]{:S(2)}, u32[]{:S(2)}) collective-permute-start(f32[4,2,32,256]{3,2,1,0:T(8,128)} %get-tuple-element.76), channel_id=1, source_target_pairs={{0,32},{16,48},{32,0},{48,16},{1,33},{17,49},{33,1},{49,17},{2,34}... | collective-permute-start | bytes 786440 | tf_op jit(solution)/shard_map/ppermute | solution.py:51
  194.9 9.5 %copy-start.12 = (f32[2,2,64,256]{3,2,1,0:T(8,128)}, f32[2,2,64,256]{3,2,1,0:T(8,128)S(1)}, u32[]{:S(2)}) copy-start(f32[2,2,64,256]{3,2,1,0:T(8,128)S(1)} %collective-permute-done.8.refs_2_) | copy-start | bytes 786436
  194.9 9.5 %collective-permute-start.29 = (f32[4,2,32,256]{3,2,1,0:T(8,128)}, f32[4,2,32,256]{3,2,1,0:T(8,128)S(1)}, u32[]{:S(2)}, u32[]{:S(2)}) collective-permute-start(f32[4,2,32,256]{3,2,1,0:T(8,128)} %get-tuple-element.77), channel_id=1, source_target_pairs={{0,48},{16,0},{32,16},{48,32},{1,49},{17,1},{33,17},{49,33},{2,50}... | collective-permute-start | bytes 786440 | tf_op jit(solution)/shard_map/ppermute | solution.py:51
  194.9 9.5 %copy-start.13 = (f32[2,2,64,256]{3,2,1,0:T(8,128)}, f32[2,2,64,256]{3,2,1,0:T(8,128)S(1)}, u32[]{:S(2)}) copy-start(f32[2,2,64,256]{3,2,1,0:T(8,128)S(1)} %collective-permute-done.9.refs_3_) | copy-start | bytes 786436
  194.9 6.6 %collective-permute-start.18 = (f32[2,2,32,256]{3,2,1,0:T(8,128)S(1)}, f32[2,2,32,256]{3,2,1,0:T(8,128)S(1)}, u32[]{:S(2)}, u32[]{:S(2)}) collective-permute-start(f32[2,2,32,256]{3,2,1,0:T(8,128)S(1)} %copy-done.29), channel_id=1, source_target_pairs={{0,4},{2,6},{4,0},{6,2},{1,5},{3,7},{5,1},{7,3},{8,12},{10,14},{12... | collective-permute-start | bytes 393224 | tf_op jit(solution)/shard_map/ppermute | solution.py:51
  196.2 8.3 %copy-start.20 = (f32[2,2,32,256]{3,2,1,0:T(8,128)}, f32[2,2,32,256]{3,2,1,0:T(8,128)S(1)}, u32[]{:S(2)}) copy-start(f32[2,2,32,256]{3,2,1,0:T(8,128)S(1)} %collective-permute-done.17.refs_5_) | copy-start | bytes 393220
  196.2 8.0 %collective-permute-start.19 = (f32[2,2,32,256]{3,2,1,0:T(8,128)S(1)}, f32[2,2,32,256]{3,2,1,0:T(8,128)S(1)}, u32[]{:S(2)}, u32[]{:S(2)}) collective-permute-start(f32[2,2,32,256]{3,2,1,0:T(8,128)S(1)} %copy-done.28), channel_id=1, source_target_pairs={{0,6},{2,0},{4,2},{6,4},{1,7},{3,1},{5,3},{7,5},{8,14},{10,8},{12,... | collective-permute-start | bytes 393224 | tf_op jit(solution)/shard_map/ppermute | solution.py:51
  201.5 3.0 %copy-start.21 = (f32[2,2,32,256]{3,2,1,0:T(8,128)}, f32[2,2,32,256]{3,2,1,0:T(8,128)S(1)}, u32[]{:S(2)}) copy-start(f32[2,2,32,256]{3,2,1,0:T(8,128)S(1)} %collective-permute-done.18.refs_6_) | copy-start | bytes 393220
  204.2 0.6 copy-start.22
  204.2 0.7 copy-start.14
  204.4 0.7 copy-start.15
  204.4 0.8 copy-start.16
  207.9 10.4 %collective-permute-start.30 = (f32[5,64,128]{2,1,0:T(8,128)}, f32[5,64,128]{2,1,0:T(8,128)S(1)}, u32[]{:S(2)}, u32[]{:S(2)}) collective-permute-start(f32[5,64,128]{2,1,0:T(8,128)} %get-tuple-element.79), channel_id=1, source_target_pairs={{0,1},{1,64},{64,65},{65,0},{2,3},{3,66},{66,67},{67,2},{4,5},{5,6... | collective-permute-start | bytes 491528 | tf_op jit(solution)/shard_map/ppermute | solution.py:51
  212.8 8.7 %collective-permute-start.31 = (f32[5,64,128]{2,1,0:T(8,128)}, f32[5,64,128]{2,1,0:T(8,128)S(1)}, u32[]{:S(2)}, u32[]{:S(2)}) collective-permute-start(f32[5,64,128]{2,1,0:T(8,128)} %get-tuple-element.80), channel_id=1, source_target_pairs={{0,64},{1,65},{64,0},{65,1},{2,66},{3,67},{66,2},{67,3},{4,68},{5,... | collective-permute-start | bytes 491528 | tf_op jit(solution)/shard_map/ppermute | solution.py:51
  216.3 5.5 %collective-permute-start.32 = (f32[5,64,128]{2,1,0:T(8,128)}, f32[5,64,128]{2,1,0:T(8,128)S(1)}, u32[]{:S(2)}, u32[]{:S(2)}) collective-permute-start(f32[5,64,128]{2,1,0:T(8,128)} %get-tuple-element.81), channel_id=1, source_target_pairs={{0,65},{1,0},{64,1},{65,64},{2,67},{3,2},{66,3},{67,66},{4,69},{5,... | collective-permute-start | bytes 491528 | tf_op jit(solution)/shard_map/ppermute | solution.py:51
  218.3 3.5 %copy-start.17 = (f32[5,64,128]{2,1,0:T(8,128)}, f32[5,64,128]{2,1,0:T(8,128)S(1)}, u32[]{:S(2)}) copy-start(f32[5,64,128]{2,1,0:T(8,128)S(1)} %collective-permute-done.30.a1) | copy-start | bytes 491524
  221.5 0.7 copy-start.18
  221.8 0.7 copy-start.19

commit v5 on v4

--- a/solution.py
+++ b/solution.py
@@ -17,7 +17,8 @@
 ROW = ("zhi", "x", "core")
 COL = ("y", "zlo")
 X, Y, Z = "x", "y", ("zhi", "zlo")
-HALF = 32
+NX = 24
+NY = 40
 
 
 VMEM = pl.BlockSpec(memory_space=pltpu.VMEM)
@@ -152,6 +153,14 @@
         out[0] = held[:, rows, pl.ds(pl.multiple_of(d * 256, 256), 256)]
 
 
+def along_z(place, held, outs):
+    for o, out in enumerate(outs):
+        d = lax.rem(place[2] + o, 4)
+        for y in range(4):
+            lanes = pl.ds(pl.multiple_of(y * 256 + lax.rem(d, 2) * 128, 128), 128)
+            out[:, :, y * 128 : (y + 1) * 128] = held[pl.ds(d // 2 * 4, 4), :, lanes]
+
+
 def fluid_product_kernel(place, lf0, lf1, if0, if1, o0, o1, o2, o3, fh, fl, held):
     @pl.when(pl.program_id(0) == 0)
     def _():
@@ -164,7 +173,7 @@
 def wet_product_kernel(place, ls0, ls1, ic0, ic1, o0, o1, o2, o3, sh, sl, held):
     sh[...], sl[...] = parts(joined(ls0, ls1))
     multiply(held, (sh, sl), ic0[...], ic1[...])
-    along_y(place, held, slice(0, 64), (o0, o1, o2, o3))
+    along_z(place, held, (o0, o1, o2, o3))
 
 
 def second_kernel(place, ls0, ls1, is0, is1, *rest):
@@ -175,8 +184,8 @@
         sh[...], sl[...] = parts(joined(ls0, ls1))
 
     multiply(held, (sh, sl), is0[0], is1[0])
-    along_x(place, held, slice(0, HALF), outs[:4])
-    along_y(place, held, slice(HALF, 64), outs[4:])
+    along_x(place, held, slice(0, NX), outs[:4])
+    along_y(place, held, slice(NX, 64), outs[4:])
 
 
 def to_y_kernel(place, a0, a1, a2, a3, o0, o1, o2, o3, held):
@@ -186,32 +195,44 @@
         out[...] = held[..., pl.ds(pl.multiple_of(d * 256, 256), 256)]
 
 
-def to_x_kernel(place, a0, a1, a2, a3, b0, b1, b2, b3, o0, o1, o2, o3, held):
-    held[0:2] = (a0[...] + a1[...]) + (a2[...] + a3[...])
-    for k in range(2):
-        rows = slice(k * HALF, (k + 1) * HALF)
-        held[2 + k] = (b0[0, :, rows] + b1[0, :, rows]) + (b2[0, :, rows] + b3[0, :, rows])
+def to_x_kernel(place, a0, a1, a2, a3, b0, b1, b2, b3, o0, o1, o2, o3, held, wet):
+    held[...] = (a0[...] + a1[...]) + (a2[...] + a3[...])
+    wet[...] = (b0[...] + b1[...]) + (b2[...] + b3[...])
     for o, out in enumerate((o0, o1, o2, o3)):
         d = lax.rem(place[0] + o, 4)
+        for m in range(2):
+            for h in range(2):
+                at = (m * 2 + h) * NY
+                out[at : at + NY] = held[m, h * 4 + d]
+        for k in range(2):
+            at = 4 * NY + k * 64
+            out[at : at + 64] = wet[d, :, k * 256 : (k + 1) * 256]
+
+
+def spread_kernel(place, *refs):
+    f, x, y, outs, held, wet = refs[0:4], refs[4:8], refs[8:12], refs[12:20], refs[20], refs[21]
+    held[0:2] = (f[0][...] + f[1][...]) + (f[2][...] + f[3][...])
+    held[2:4, :, 0:NX] = (x[0][...] + x[1][...]) + (x[2][...] + x[3][...])
+    for m in range(2):
         for h in range(2):
-            out[:, h] = held[:, h * 4 + d]
-
-
-def spread_kernel(place, *refs):
-    f, x, y, outs, held = refs[0:4], refs[4:8], refs[8:12], refs[12:16], refs[16]
-    held[0:2] = (f[0][...] + f[1][...]) + (f[2][...] + f[3][...])
-    held[2:4, :, 0:HALF] = (x[0][...] + x[1][...]) + (x[2][...] + x[3][...])
-    for m, k, at in ((2, 0, HALF), (3, 1, HALF), (4, 2, 0), (4, 3, HALF)):
-        held[m, :, at : at + HALF] = (y[0][k] + y[1][k]) + (y[2][k] + y[3][k])
-    for o, out in enumerate(outs):
+            rows = slice((m * 2 + h) * NY, (m * 2 + h + 1) * NY)
+            held[2 + m, h, NX:] = (y[0][rows] + y[1][rows]) + (y[2][rows] + y[3][rows])
+    for k in range(2):
+        rows = slice(4 * NY + k * 64, 4 * NY + (k + 1) * 64)
+        wet[k] = (y[0][rows] + y[1][rows]) + (y[2][rows] + y[3][rows])
+    for o in range(4):
         d = lax.rem(place[2] + o, 4)
         lanes = pl.ds(pl.multiple_of(lax.rem(d, 2) * 128, 128), 128)
-        out[...] = held[:, d // 2, :, lanes]
-
-
-def last_kernel(a0, a1, a2, a3, *outs):
-    for m, out in enumerate(outs):
+        outs[o][...] = held[:, d // 2, :, lanes]
+        d = lax.rem(place[1] + o, 4)
+        lanes = pl.ds(pl.multiple_of(lax.rem(d, 2) * 128, 128), 128)
+        outs[4 + o][...] = wet[d // 2, :, lanes]
+
+
+def last_kernel(a0, a1, a2, a3, w0, w1, w2, w3, fstiff, fmass, stiff, mass, wet):
+    for m, out in enumerate((fstiff, fmass, stiff, mass)):
         out[...] = (a0[m] + a1[m]) + (a2[m] + a3[m])
+    wet[...] = (w0[...] + w1[...]) + (w2[...] + w3[...])
 
 
 def call(kernel, out, count, smem=0, anywhere=0, scratch=(), flops=0, moved=0):
@@ -231,20 +252,26 @@
     return [slots[0]] + [shifted(slots[o], axis, o) for o in range(1, 4)]
 
 
-def split(kernel, place, arrived, out, held):
+def split(kernel, place, arrived, out, *held):
     size = sum(a.size for a in arrived)
     return call(
-        kernel, [shape(*out)] * 4, 1 + len(arrived), smem=1, scratch=[pltpu.VMEM(held, F32)], flops=size, moved=5 * size
+        kernel,
+        [shape(*out)] * 4,
+        1 + len(arrived),
+        smem=1,
+        scratch=[pltpu.VMEM(dims, F32) for dims in held],
+        flops=size,
+        moved=5 * size,
     )(place, *arrived)
 
 
 def spread(place, *arrived):
     return call(
         spread_kernel,
-        [shape(5, 64, 128)] * 4,
+        [shape(4, 64, 128)] * 4 + [shape(64, 128)] * 4,
         13,
         smem=1,
-        scratch=[pltpu.VMEM((5, 2, 64, 256), F32)],
+        scratch=[pltpu.VMEM((4, 2, 64, 256), F32), pltpu.VMEM((2, 64, 256), F32)],
         flops=2**20,
         moved=2**22,
     )(place, *arrived)
@@ -341,19 +368,28 @@
     )(struct_cols, stiff_tiles, mass_tiles, below_s, struct_basis, above_s, fluid[0])
     other_s = shifted(image_s, "core", 1)
 
-    coupled = partial_sums(wet_product_kernel, 1, place, (own_s, left_s), 512, (image_c, other_c), [VMEM] * 2, 0, 64)
-    coupled_y = exchanged(coupled, Y)
-    struct = partial_sums(
-        second_kernel, 2, place, (own_s, left_s), 512, (image_s, other_s), [block(256)] * 2, HALF, HALF
-    )
+    coupled = call(
+        wet_product_kernel,
+        [shape(4, 64, 512)] * 4,
+        5,
+        smem=1,
+        scratch=[pltpu.VMEM((512, 512), BF16)] * 2 + [pltpu.VMEM((8, 64, R), F32)],
+        flops=6 * 512 * 512 * R,
+        moved=5 * 2**20,
+    )(place, own_s, left_s, image_c, other_c)
+    coupled_z = exchanged(coupled, Z)
+    struct = partial_sums(second_kernel, 2, place, (own_s, left_s), 512, (image_s, other_s), [block(256)] * 2, NX, NY)
     struct_x = exchanged(struct[0:4], X)
     struct_y = exchanged(struct[4:8], Y)
 
     fluid_xy = exchanged(split(to_y_kernel, place, fluid_x, (2, 2, 64, 256), (2, 2, 64, R)), Y)
-    struct_xy = exchanged(split(to_y_kernel, place, struct_x, (2, 2, HALF, 256), (2, 2, HALF, R)), Y)
-    both_yx = exchanged(split(to_x_kernel, place, struct_y + coupled_y, (4, 2, HALF, 256), (4, 8, HALF, 256)), X)
-    summed = exchanged(spread(place, *fluid_xy, *struct_xy, *both_yx), Z)
-    fstiff, fmass, stiff, mass, wet = call(last_kernel, [shape(64, 128)] * 5, 4, flops=2**18, moved=2**20)(*summed)
+    struct_xy = exchanged(split(to_y_kernel, place, struct_x, (2, 2, NX, 256), (2, 2, NX, R)), Y)
+    both_x = exchanged(
+        split(to_x_kernel, place, struct_y + coupled_z, (4 * NY + 128, 256), (2, 8, NY, 256), (4, 64, 512)), X
+    )
+    parted = spread(place, *fluid_xy, *struct_xy, *both_x)
+    summed = exchanged(parted[:4], Z) + exchanged(parted[4:], Y)
+    fstiff, fmass, stiff, mass, wet = call(last_kernel, [shape(64, 128)] * 5, 8, flops=2**18, moved=2**20)(*summed)
     return stiff, mass, fstiff, fmass, wet
 
 

time: 225 us -> 222 us (0.987)
  waiting for transfers between devices: 96.4 us -> 91.7 us
  starting transfers between devices: 68.6 us -> 71.3 us
    ppermute x4, waiting for transfers between devices: 37.6 us -> 27.4 us  [from_behind(): return lax.ppermute(value, AXES, pairs)]
    ppermute x29 -> x32, waiting for transfers between devices: 58.9 us -> 64.2 us  [shifted(): lax.ppermute(value, axis, [(i, (i + by) % size) for i in range(size)])]
    pallas_call x3 -> x2, Pallas kernels: 17.8 us -> 12.6 us  [partial_sums(): return run(place, *lefts, *operands)]
    pallas_call x2 -> x3, Pallas kernels: 4.5 us -> 9.51 us  [the longest x1 5.07 us: compute(): call(wet_product_kernel, [shape(4, 64, 512)] * 4, 5, smem=1, scratch=[plt...]
    ppermute x29 -> x32, starting transfers between devices: 47 us -> 48.7 us  [shifted(): lax.ppermute(value, axis, [(i, (i + by) % size) for i in range(size)])]
    unnamed x60 -> x64, local copies, waits for them, and re-layouts: 6.93 us -> 6.4 us
  transfers between devices with their start and end apart: 34 -> 37, of which waited for: 18 -> 12; matrix products, arithmetic and copies ran while one was open for 0% -> 0% of each run, Pallas kernels for 19% -> 19%
where the time goes in v5:
time: 222 us; the launch traced here: 221 us
  waiting for transfers between devices  91.7 us (41%)
  starting transfers between devices  71.3 us (32%)
  Pallas kernels  50.4 us (23%)
  local copies, waits for them, and re-layouts  6.47 us (3%)
    ppermute x32, waiting for transfers between devices, shifted(): lax.ppermute(value, axis, [(i, (i + by) % size) for i in range(size)])  64.2 us
    ppermute x32, starting transfers between devices, shifted(): lax.ppermute(value, axis, [(i, (i + by) % size) for i in range(size)])  48.7 us
    ppermute x4, waiting for transfers between devices, from_behind(): return lax.ppermute(value, AXES, pairs)  27.4 us
    pallas_call x2, Pallas kernels, partial_sums(): return run(place, *lefts, *operands)  12.6 us
    all_to_all x1, starting transfers between devices, compute(): lax.all_to_all(outgoing, AXES, split_axis=0, concat_axis=0, tiled=True)  11.7 us
    ppermute x4, starting transfers between devices, from_behind(): return lax.ppermute(value, AXES, pairs)  10.9 us
    pallas_call x3, Pallas kernels, split(): call(kernel, [shape(*out)] * 4, 1 + len(arrived), smem=1, scratch=[pltpu....  9.45 us
    unnamed x64, local copies, waits for them, and re-layouts  6.4 us
  transfers between devices with their start and end apart: 37, of which 12 were waited for; matrix products, arithmetic and copies ran while one was open for 0% of the time, Pallas kernels for 19%

profile of v5, /device:TPU:0, one launch (start us, length us, event | category | flops | bytes accessed | tf_op | source)
XLA Modules:
  0.0 221.4 jit_solution(10776947270052350146)
XLA Ops:
  0.6 4.0 %collective-permute-start.1 = (f32[128,1024]{1,0:T(8,128)}, f32[128,1024]{1,0:T(8,128)S(1)}, u32[]{:S(2)}, u32[]{:S(2)}) collective-permute-start(f32[128,1024]{1,0:T(8,128)} %fluid.3), channel_id=1, source_target_pairs={{0,1},{1,2},{2,3},{3,4},{4,5},{5,6},{6,7},{7,8},{8,9},{9,10},{10,1... | collective-permute-start | bytes 1572872 | tf_op jit(solution)/shard_map/ppermute | solution.py:58
  4.6 1.3 collective-permute-start.2
  5.9 0.6 pad_add_fusion.place
  6.5 3.0 %shard_map.146 = (f32[8,64,256]{2,1,0:T(8,128)}, f32[8,64,256]{2,1,0:T(8,128)}, f32[8,64,128]{2,1,0:T(8,128)}, f32[8,64,128]{2,1,0:T(8,128)}) custom-call(s32[4]{0:T(128)} %pad_add_fusion.place, f32[256,1024]{1,0:T(8,128)} %own.3, f32[128,1024]{1,0:T(8,128)} %fluid.3), custom_call_target="tpu_custom_call" | custom-call | flops 1048576 | bytes 3145728 | tf_op jit(solution)/shard_map/pallas_call | solution.py:324
  9.5 17.8 %collective-permute-done.1.lo = f32[128,1024]{1,0:T(8,128)S(1)} collective-permute-done((f32[128,1024]{1,0:T(8,128)}, f32[128,1024]{1,0:T(8,128)S(1)}, u32[]{:S(2)}, u32[]{:S(2)}) %collective-permute-start.1) | collective-permute-done | bytes 524320 | tf_op jit(solution)/shard_map/ppermute | solution.py:58
  27.3 0.8 copy-done.7
  28.1 0.2 copy-done.8
  28.3 4.0 %shard_map.147.if0 = f32[2,128,1024]{2,1,0:T(8,128)} custom-call(s32[1,4]{1,0:T(1,128)} %cols.2, f32[1,4,128,128]{3,2,1,0:T(8,128)} %stiff.2, f32[1,4,128,128]{3,2,1,0:T(8,128)} %mass.2, f32[128,1024]{1,0:T(8,128)} %copy-done.7, f32[128,1024]{1,0:T(8,128)} %fluid.3, f32[128,1024]{1,0:T(8,128)} %copy-done.8, f32[8,64,256]{2,1,0:T(8,128)} %get-tuple-element.52.after.ls0), custom_call_target="tpu_custom_call" | custom-call | flops 603979776 | bytes 3145728 | tf_op jit(solution)/shard_map/pallas_call | solution.py:339
  32.4 4.3 %collective-permute-start.11 = (f32[128,1024]{1,0:T(8,128)S(1)}, f32[128,1024]{1,0:T(8,128)S(1)}, u32[]{:S(2)}, u32[]{:S(2)}) collective-permute-start(f32[128,1024]{1,0:T(8,128)S(1)} %get-tuple-element.96), channel_id=1, source_target_pairs={{0,1},{1,2},{2,3},{3,4},{4,5},{5,6},{6,7},{7,8},{8,9},{9,10},{10,1... | collective-permute-start | bytes 1572872 | tf_op jit(solution)/shard_map/ppermute | solution.py:58
  36.7 1.3 collective-permute-start.12
  38.0 3.2 %collective-permute-start = (f32[8,64,128]{2,1,0:T(8,128)S(1)}, f32[8,64,128]{2,1,0:T(8,128)}, u32[]{:S(2)}, u32[]{:S(2)}) collective-permute-start(f32[8,64,128]{2,1,0:T(8,128)S(1)} %copy-done.31), channel_id=1, source_target_pairs={{0,8},{8,0},{1,9},{9,1},{2,10},{10,2},{3,11},{11,3},{4,12},{12,4},... | collective-permute-start | bytes 786440 | tf_op jit(solution)/shard_map/ppermute | solution.py:52
  41.2 2.8 %shard_map.153 = f32[128,2,1024]{2,1,0:T(2,128)} custom-call(s32[1,128]{1,0:T(1,128)} %bitcast.6, s32[1,128]{1,0:T(1,128)} %bitcast.7, f32[128,1024]{1,0:T(8,128)} %fluid.3), custom_call_target="tpu_custom_call" | custom-call | flops 201326592 | bytes 2097152 | tf_op jit(solution)/shard_map/pallas_call | solution.py:319
  44.1 11.7 %all-to-all-start = ((f32[128,2,1024]{2,1,0:T(2,128)}), f32[128,2,1024]{2,1,0:T(2,128)S(1)}, u32[]{:S(2)}, u32[]{:S(2)}) async-start(f32[128,2,1024]{2,1,0:T(2,128)} %shard_map.153), calls=%async_computation | async-start | bytes 2097152 | tf_op jit(solution)/shard_map/all_to_all | solution.py:322
  55.8 5.2 %shard_map.148 = (f32[2,2,64,1024]{3,2,1,0:T(8,128)}, f32[2,2,64,1024]{3,2,1,0:T(8,128)}, f32[2,2,64,1024]{3,2,1,0:T(8,128)}, f32[2,2,64,1024]{3,2,1,0:T(8,128)}) custom-call(s32[4]{0:T(128)} %pad_add_fusion.place, f32[8,64,128]{2,1,0:T(8,128)} %get-tuple-element.50.lf0, f32[8,64,128]{2,1,0:T(8,128)} %collective-permute-done.lf1, ...), custom_call_target="tpu_custom_call" | custom-call | flops 1610612736 | bytes 8388608 | tf_op jit(solution)/shard_map/pallas_call | solution.py:295
  61.0 9.6 %collective-permute-done.11.lo = f32[128,1024]{1,0:T(8,128)S(1)} collective-permute-done((f32[128,1024]{1,0:T(8,128)S(1)}, f32[128,1024]{1,0:T(8,128)S(1)}, u32[]{:S(2)}, u32[]{:S(2)}) %collective-permute-start.11) | collective-permute-done | bytes 524320 | tf_op jit(solution)/shard_map/ppermute | solution.py:58
  70.6 0.8 copy-done.9
  71.4 0.2 copy-done.10
  71.6 5.9 %shard_map.150.is0 = f32[2,256,1024]{2,1,0:T(8,128)} custom-call(s32[2,4]{1,0:T(2,128)} %cols.3, f32[2,4,128,128]{3,2,1,0:T(8,128)} %stiff.3, f32[2,4,128,128]{3,2,1,0:T(8,128)} %mass.3, f32[128,1024]{1,0:T(8,128)} %copy-done.9, f32[256,1024]{1,0:T(8,128)} %own.3, f32[128,1024]{1,0:T(8,128)} %copy-done.10, f32[2,2,64,1024]{3,2,1,0:T(8,128)} %get-tuple-element.53.a0.after), custom_call_target="tpu_custom_call" | custom-call | flops 1610612736 | bytes 5242880 | tf_op jit(solution)/shard_map/pallas_call | solution.py:359
  77.5 1.0 copy-done.1
  78.5 3.1 %shard_map.154.ic0 = f32[256,1024]{1,0:T(8,128)} custom-call(f32[256,256]{1,0:T(8,128)} %coupling.1, f32[128,2,1024]{2,1,0:T(2,128)} %copy-done.1), custom_call_target="tpu_custom_call" | custom-call | flops 402653184 | bytes 2097152 | tf_op jit(solution)/shard_map/pallas_call | solution.py:336
  81.6 0.5 collective-permute-start.23
  82.1 7.1 %collective-permute-start.4 = (f32[2,2,64,1024]{3,2,1,0:T(8,128)}, f32[2,2,64,1024]{3,2,1,0:T(8,128)S(1)}, u32[]{:S(2)}, u32[]{:S(2)}) collective-permute-start(f32[2,2,64,1024]{3,2,1,0:T(8,128)} %get-tuple-element.54), channel_id=1, source_target_pairs={{0,16},{16,32},{32,48},{48,0},{1,17},{17,33},{33,49},{49,1},{2,18}... | collective-permute-start | bytes 3145736 | tf_op jit(solution)/shard_map/ppermute | solution.py:52
  89.2 2.7 %collective-permute-start.5 = (f32[2,2,64,1024]{3,2,1,0:T(8,128)}, f32[2,2,64,1024]{3,2,1,0:T(8,128)S(1)}, u32[]{:S(2)}, u32[]{:S(2)}) collective-permute-start(f32[2,2,64,1024]{3,2,1,0:T(8,128)} %get-tuple-element.55), channel_id=1, source_target_pairs={{0,32},{16,48},{32,0},{48,16},{1,33},{17,49},{33,1},{49,17},{2,34}... | collective-permute-start | bytes 3145736 | tf_op jit(solution)/shard_map/ppermute | solution.py:52
  92.0 1.8 collective-permute-start.6
  93.8 5.1 %shard_map.155 = (f32[4,64,512]{2,1,0:T(8,128)}, f32[4,64,512]{2,1,0:T(8,128)}, f32[4,64,512]{2,1,0:T(8,128)}, f32[4,64,512]{2,1,0:T(8,128)}) custom-call(s32[4]{0:T(128)} %pad_add_fusion.place, f32[8,64,256]{2,1,0:T(8,128)} %get-tuple-element.52.after.ls0, f32[8,64,256]{2,1,0:T(8,128)} %copy-done.30, f32[256,1024]{1,0:T(8,128)} %shard_map.154.ic0, ...), custom_call_target="tpu_custom_call" | custom-call | flops 1610612736 | bytes 5242880 | tf_op jit(solution)/shard_map/pallas_call | solution.py:371
  98.8 3.8 %collective-permute-start.25 = (f32[4,64,512]{2,1,0:T(8,128)}, f32[4,64,512]{2,1,0:T(8,128)}, u32[]{:S(2)}, u32[]{:S(2)}) collective-permute-start(f32[4,64,512]{2,1,0:T(8,128)} %get-tuple-element.76), channel_id=1, source_target_pairs={{0,64},{1,65},{64,0},{65,1},{2,66},{3,67},{66,2},{67,3},{4,68},{5,... | collective-permute-start | bytes 1572872 | tf_op jit(solution)/shard_map/ppermute | solution.py:52
  102.7 7.4 %shard_map.151 = (f32[2,2,24,1024]{3,2,1,0:T(8,128)}, f32[2,2,24,1024]{3,2,1,0:T(8,128)}, f32[2,2,24,1024]{3,2,1,0:T(8,128)}, f32[2,2,24,1024]{3,2,1,0:T(8,128)}...) custom-call(s32[4]{0:T(128)} %pad_add_fusion.place, ...), custom_call_target="tpu_custom_call" | custom-call | flops 3221225472 | bytes 8388608 | tf_op jit(solution)/shard_map/pallas_call | solution.py:295
  110.1 4.1 %collective-permute-done.24.b1 = f32[4,64,512]{2,1,0:T(8,128)S(1)} collective-permute-done((f32[4,64,512]{2,1,0:T(8,128)}, f32[4,64,512]{2,1,0:T(8,128)S(1)}, u32[]{:S(2)}, u32[]{:S(2)}) %collective-permute-start.24) | collective-permute-done | bytes 524320 | tf_op jit(solution)/shard_map/ppermute | solution.py:52
  114.2 0.8 copy-done.6
  115.0 1.8 collective-permute-start.26
  116.9 21.3 %collective-permute-done.5.a2 = f32[2,2,64,1024]{3,2,1,0:T(8,128)S(1)} collective-permute-done((f32[2,2,64,1024]{3,2,1,0:T(8,128)}, f32[2,2,64,1024]{3,2,1,0:T(8,128)S(1)}, u32[]{:S(2)}, u32[]{:S(2)}) %collective-permute-start.5) | collective-permute-done | bytes 1048608 | tf_op jit(solution)/shard_map/ppermute | solution.py:52
  138.2 0.3 collective-permute-start.22
  138.5 0.6 copy-done.3
  139.2 0.3 copy-done.4
  139.5 3.5 %shard_map.149 = (f32[2,2,64,256]{3,2,1,0:T(8,128)}, f32[2,2,64,256]{3,2,1,0:T(8,128)}, f32[2,2,64,256]{3,2,1,0:T(8,128)}, f32[2,2,64,256]{3,2,1,0:T(8,128)}) custom-call(s32[4]{0:T(128)} %pad_add_fusion.place, f32[2,2,64,1024]{3,2,1,0:T(8,128)} %get-tuple-element.53.a0.after, f32[2,2,64,1024]{3,2,1,0:T(8,128)} %copy-done.2, f32[2,2,64,1024]{3,2,1,0:T(8,128)} %copy-done.3, ...), custom_call_target="tpu_custom_call" | custom-call | flops 1048576 | bytes 5242880 | tf_op jit(solution)/shard_map/pallas_call | solution.py:257
  143.1 0.8 collective-permute-start.7
  143.9 1.9 collective-permute-start.14
  145.8 16.0 %collective-permute-done.7.refs_1_ = f32[2,2,64,256]{3,2,1,0:T(8,128)S(1)} collective-permute-done((f32[2,2,64,256]{3,2,1,0:T(8,128)}, f32[2,2,64,256]{3,2,1,0:T(8,128)S(1)}, u32[]{:S(2)}, u32[]{:S(2)}) %collective-permute-start.7) | collective-permute-done | bytes 262176 | tf_op jit(solution)/shard_map/ppermute | solution.py:52
  161.8 0.8 collective-permute-start.15
  162.6 0.4 collective-permute-start.8
  163.0 5.2 %collective-permute-done.22.a3 = f32[2,8,40,256]{3,2,1,0:T(8,128)} collective-permute-done((f32[2,8,40,256]{3,2,1,0:T(8,128)}, f32[2,8,40,256]{3,2,1,0:T(8,128)}, u32[]{:S(2)}, u32[]{:S(2)}) %collective-permute-start.22) | collective-permute-done | bytes 655392 | tf_op jit(solution)/shard_map/ppermute | solution.py:52
  168.2 2.6 %collective-permute-start.9 = (f32[2,2,64,256]{3,2,1,0:T(8,128)}, f32[2,2,64,256]{3,2,1,0:T(8,128)S(1)}, u32[]{:S(2)}, u32[]{:S(2)}) collective-permute-start(f32[2,2,64,256]{3,2,1,0:T(8,128)} %get-tuple-element.60), channel_id=1, source_target_pairs={{0,6},{2,0},{4,2},{6,4},{1,7},{3,1},{5,3},{7,5},{8,14},{10,8},{12,... | collective-permute-start | bytes 786440 | tf_op jit(solution)/shard_map/ppermute | solution.py:52
  170.8 3.7 %shard_map.156 = (f32[288,256]{1,0:T(8,128)}, f32[288,256]{1,0:T(8,128)}, f32[288,256]{1,0:T(8,128)}, f32[288,256]{1,0:T(8,128)}) custom-call(s32[4]{0:T(128)} %pad_add_fusion.place, f32[2,8,40,256]{3,2,1,0:T(8,128)} %get-tuple-element.70.a0, f32[2,8,40,256]{3,2,1,0:T(8,128)} %copy-done.5, f32[2,8,40,256]{3,2,1,0:T(8,128)} %collective-permute-done.21.a2, ...), custom_call_target="tpu_custom_call" | custom-call | flops 1179648 | bytes 5898240 | tf_op jit(solution)/shard_map/pallas_call | solution.py:257
  174.4 0.1 collective-permute-start.27
  174.6 0.8 collective-permute-start.28
  175.4 2.5 %collective-permute-start.29 = (f32[288,256]{1,0:T(8,128)}, f32[288,256]{1,0:T(8,128)S(1)}, u32[]{:S(2)}, u32[]{:S(2)}) collective-permute-start(f32[288,256]{1,0:T(8,128)} %get-tuple-element.81), channel_id=1, source_target_pairs={{0,48},{16,0},{32,16},{48,32},{1,49},{17,1},{33,17},{49,33},{2,50}... | collective-permute-start | bytes 884744 | tf_op jit(solution)/shard_map/ppermute | solution.py:52
  177.8 2.3 %shard_map.152 = (f32[2,2,24,256]{3,2,1,0:T(8,128)}, f32[2,2,24,256]{3,2,1,0:T(8,128)}, f32[2,2,24,256]{3,2,1,0:T(8,128)}, f32[2,2,24,256]{3,2,1,0:T(8,128)}) custom-call(s32[4]{0:T(128)} %pad_add_fusion.place, f32[2,2,24,1024]{3,2,1,0:T(8,128)} %get-tuple-element.62.a0, f32[2,2,24,1024]{3,2,1,0:T(8,128)} %copy-done.11, f32[2,2,24,1024]{3,2,1,0:T(8,128)} %copy-done.12, ...), custom_call_target="tpu_custom_call" | custom-call | flops 393216 | bytes 1966080 | tf_op jit(solution)/shard_map/pallas_call | solution.py:257
  180.2 1.4 collective-permute-start.18
  181.6 5.9 %collective-permute-done.17.refs_5_ = f32[2,2,24,256]{3,2,1,0:T(8,128)S(1)} collective-permute-done((f32[2,2,24,256]{3,2,1,0:T(8,128)}, f32[2,2,24,256]{3,2,1,0:T(8,128)S(1)}, u32[]{:S(2)}, u32[]{:S(2)}) %collective-permute-start.17) | collective-permute-done | bytes 98336 | tf_op jit(solution)/shard_map/ppermute | solution.py:52
  187.6 4.8 %collective-permute-done.19.refs_7_ = f32[2,2,24,256]{3,2,1,0:T(8,128)S(1)} collective-permute-done((f32[2,2,24,256]{3,2,1,0:T(8,128)}, f32[2,2,24,256]{3,2,1,0:T(8,128)S(1)}, u32[]{:S(2)}, u32[]{:S(2)}) %collective-permute-start.19) | collective-permute-done | bytes 98336 | tf_op jit(solution)/shard_map/ppermute | solution.py:52
  192.5 0.6 copy-done.25
  193.0 0.1 copy-done.14
  193.1 0.1 copy-done.15
  193.3 0.1 copy-done.16
  193.4 2.7 %shard_map.157 = (f32[4,64,128]{2,1,0:T(8,128)}, f32[4,64,128]{2,1,0:T(8,128)}, f32[4,64,128]{2,1,0:T(8,128)}, f32[4,64,128]{2,1,0:T(8,128)}, f32[64,128]{1,0:T(...) custom-call(s32[4]{0:T(128)} %pad_add_fusion.place, ...), custom_call_target="tpu_custom_call" | custom-call | flops 1048576 | bytes 4194304 | tf_op jit(solution)/shard_map/pallas_call | solution.py:269
  196.0 9.2 %collective-permute-start.30 = (f32[4,64,128]{2,1,0:T(8,128)}, f32[4,64,128]{2,1,0:T(8,128)S(1)}, u32[]{:S(2)}, u32[]{:S(2)}) collective-permute-start(f32[4,64,128]{2,1,0:T(8,128)} %get-tuple-element.83), channel_id=1, source_target_pairs={{0,1},{1,64},{64,65},{65,0},{2,3},{3,66},{66,67},{67,2},{4,5},{5,6... | collective-permute-start | bytes 393224 | tf_op jit(solution)/shard_map/ppermute | solution.py:52
  205.2 1.6 collective-permute-start.31
  206.8 2.5 %collective-permute-start.32 = (f32[4,64,128]{2,1,0:T(8,128)}, f32[4,64,128]{2,1,0:T(8,128)S(1)}, u32[]{:S(2)}, u32[]{:S(2)}) collective-permute-start(f32[4,64,128]{2,1,0:T(8,128)} %get-tuple-element.85), channel_id=1, source_target_pairs={{0,65},{1,0},{64,1},{65,64},{2,67},{3,2},{66,3},{67,66},{4,69},{5,... | collective-permute-start | bytes 393224 | tf_op jit(solution)/shard_map/ppermute | solution.py:52
  209.4 2.7 %collective-permute-start.34 = (f32[64,128]{1,0:T(8,128)}, f32[64,128]{1,0:T(8,128)S(1)}, u32[]{:S(2)}, u32[]{:S(2)}) collective-permute-start(f32[64,128]{1,0:T(8,128)} %get-tuple-element.88), channel_id=1, source_target_pairs={{0,4},{2,6},{4,0},{6,2},{1,5},{3,7},{5,1},{7,3},{8,12},{10,14},{12... | collective-permute-start | bytes 98312 | tf_op jit(solution)/shard_map/ppermute | solution.py:52
  212.0 2.7 %collective-permute-done.33.w1 = f32[64,128]{1,0:T(8,128)S(1)} collective-permute-done((f32[64,128]{1,0:T(8,128)}, f32[64,128]{1,0:T(8,128)S(1)}, u32[]{:S(2)}, u32[]{:S(2)}) %collective-permute-start.33) | collective-permute-done | bytes 32800 | tf_op jit(solution)/shard_map/ppermute | solution.py:52
  214.7 0.3 collective-permute-done.34.w2
  215.1 3.8 %collective-permute-done.35.w3 = f32[64,128]{1,0:T(8,128)S(1)} collective-permute-done((f32[64,128]{1,0:T(8,128)}, f32[64,128]{1,0:T(8,128)S(1)}, u32[]{:S(2)}, u32[]{:S(2)}) %collective-permute-start.35) | collective-permute-done | bytes 32800 | tf_op jit(solution)/shard_map/ppermute | solution.py:52
  218.9 0.5 copy-done.28
  219.6 1.8 shard_map.158
  (89 shorter events, 0.6 us)
Async XLA Ops:
  0.6 26.7 %collective-permute-start.1 = (f32[128,1024]{1,0:T(8,128)}, f32[128,1024]{1,0:T(8,128)S(1)}, u32[]{:S(2)}, u32[]{:S(2)}) collective-permute-start(f32[128,1024]{1,0:T(8,128)} %fluid.3), channel_id=1, source_target_pairs={{0,1},{1,2},{2,3},{3,4},{4,5},{5,6},{6,7},{7,8},{8,9},{9,10},{10,1... | collective-permute-start | bytes 1572872 | tf_op jit(solution)/shard_map/ppermute | solution.py:58
  4.6 22.7 %collective-permute-start.2 = (f32[128,1024]{1,0:T(8,128)}, f32[128,1024]{1,0:T(8,128)S(1)}, u32[]{:S(2)}, u32[]{:S(2)}) collective-permute-start(f32[128,1024]{1,0:T(8,128)} %fluid.3), channel_id=1, source_target_pairs={{1,0},{2,1},{3,2},{4,3},{5,4},{6,5},{7,6},{8,7},{9,8},{10,9},{11,1... | collective-permute-start | bytes 1572872 | tf_op jit(solution)/shard_map/ppermute | solution.py:58
  9.5 22.8 %copy-start = (f32[256,1024]{1,0:T(8,128)S(1)}, f32[256,1024]{1,0:T(8,128)}, u32[]{:S(2)}) copy-start(f32[256,1024]{1,0:T(8,128)} %own.3) | copy-start | bytes 3145732
  27.3 0.8 copy-start.7
  27.3 1.0 copy-start.8
  28.3 9.7 %copy-start.31 = (f32[8,64,128]{2,1,0:T(8,128)S(1)}, f32[8,64,128]{2,1,0:T(8,128)}, u32[]{:S(2)}) copy-start(f32[8,64,128]{2,1,0:T(8,128)} %get-tuple-element.51) | copy-start | bytes 786436
  32.3 23.5 %collective-permute-start.3 = (f32[2,128,1024]{2,1,0:T(8,128)}, f32[2,128,1024]{2,1,0:T(8,128)}, u32[]{:S(2)}, u32[]{:S(2)}) collective-permute-start(f32[2,128,1024]{2,1,0:T(8,128)} %shard_map.147.if0), channel_id=1, source_target_pairs={{0,8},{8,0},{1,9},{9,1},{2,10},{10,2},{3,11},{11,3},{4,12},{12,4},... | collective-permute-start | bytes 3145736 | tf_op jit(solution)/shard_map/ppermute | solution.py:52
  32.4 38.2 %collective-permute-start.11 = (f32[128,1024]{1,0:T(8,128)S(1)}, f32[128,1024]{1,0:T(8,128)S(1)}, u32[]{:S(2)}, u32[]{:S(2)}) collective-permute-start(f32[128,1024]{1,0:T(8,128)S(1)} %get-tuple-element.96), channel_id=1, source_target_pairs={{0,1},{1,2},{2,3},{3,4},{4,5},{5,6},{6,7},{7,8},{8,9},{9,10},{10,1... | collective-permute-start | bytes 1572872 | tf_op jit(solution)/shard_map/ppermute | solution.py:58
  36.7 33.9 %collective-permute-start.12 = (f32[128,1024]{1,0:T(8,128)S(1)}, f32[128,1024]{1,0:T(8,128)S(1)}, u32[]{:S(2)}, u32[]{:S(2)}) collective-permute-start(f32[128,1024]{1,0:T(8,128)S(1)} %get-tuple-element.95), channel_id=1, source_target_pairs={{1,0},{2,1},{3,2},{4,3},{5,4},{6,5},{7,6},{8,7},{9,8},{10,9},{11,1... | collective-permute-start | bytes 1572872 | tf_op jit(solution)/shard_map/ppermute | solution.py:58
  38.0 17.8 %collective-permute-start = (f32[8,64,128]{2,1,0:T(8,128)S(1)}, f32[8,64,128]{2,1,0:T(8,128)}, u32[]{:S(2)}, u32[]{:S(2)}) collective-permute-start(f32[8,64,128]{2,1,0:T(8,128)S(1)} %copy-done.31), channel_id=1, source_target_pairs={{0,8},{8,0},{1,9},{9,1},{2,10},{10,2},{3,11},{11,3},{4,12},{12,4},... | collective-permute-start | bytes 786440 | tf_op jit(solution)/shard_map/ppermute | solution.py:52
  44.1 33.4 %all-to-all-start = ((f32[128,2,1024]{2,1,0:T(2,128)}), f32[128,2,1024]{2,1,0:T(2,128)S(1)}, u32[]{:S(2)}, u32[]{:S(2)}) async-start(f32[128,2,1024]{2,1,0:T(2,128)} %shard_map.153), calls=%async_computation | async-start | bytes 2097152 | tf_op jit(solution)/shard_map/all_to_all | solution.py:322
  70.6 0.8 copy-start.9
  70.6 1.0 copy-start.10
  77.5 4.6 %copy-start.29 = (f32[8,64,256]{2,1,0:T(8,128)S(1)}, f32[8,64,256]{2,1,0:T(8,128)}, u32[]{:S(2)}) copy-start(f32[8,64,256]{2,1,0:T(8,128)} %get-tuple-element.61) | copy-start | bytes 1572868
  77.5 21.4 %collective-permute-start.13 = (f32[2,256,1024]{2,1,0:T(8,128)}, f32[2,256,1024]{2,1,0:T(8,128)}, u32[]{:S(2)}, u32[]{:S(2)}) collective-permute-start(f32[2,256,1024]{2,1,0:T(8,128)} %shard_map.150.is0), channel_id=1, source_target_pairs={{0,8},{8,0},{1,9},{9,1},{2,10},{10,2},{3,11},{11,3},{4,12},{12,4},... | collective-permute-start | bytes 6291464 | tf_op jit(solution)/shard_map/ppermute | solution.py:52
  77.5 1.0 copy-start.1
  81.6 12.2 %collective-permute-start.23 = (f32[256,1024]{1,0:T(8,128)}, f32[256,1024]{1,0:T(8,128)}, u32[]{:S(2)}, u32[]{:S(2)}) collective-permute-start(f32[256,1024]{1,0:T(8,128)} %shard_map.154.ic0), channel_id=1, source_target_pairs={{0,8},{8,0},{1,9},{9,1},{2,10},{10,2},{3,11},{11,3},{4,12},{12,4},... | collective-permute-start | bytes 3145736 | tf_op jit(solution)/shard_map/ppermute | solution.py:52
  82.1 9.9 %collective-permute-start.10 = (f32[8,64,256]{2,1,0:T(8,128)S(1)}, f32[8,64,256]{2,1,0:T(8,128)S(1)}, u32[]{:S(2)}, u32[]{:S(2)}) collective-permute-start(f32[8,64,256]{2,1,0:T(8,128)S(1)} %copy-done.29), channel_id=1, source_target_pairs={{0,8},{8,0},{1,9},{9,1},{2,10},{10,2},{3,11},{11,3},{4,12},{12,4},... | collective-permute-start | bytes 1572872 | tf_op jit(solution)/shard_map/ppermute | solution.py:52
  82.1 32.9 %collective-permute-start.4 = (f32[2,2,64,1024]{3,2,1,0:T(8,128)}, f32[2,2,64,1024]{3,2,1,0:T(8,128)S(1)}, u32[]{:S(2)}, u32[]{:S(2)}) collective-permute-start(f32[2,2,64,1024]{3,2,1,0:T(8,128)} %get-tuple-element.54), channel_id=1, source_target_pairs={{0,16},{16,32},{32,48},{48,0},{1,17},{17,33},{33,49},{49,1},{2,18}... | collective-permute-start | bytes 3145736 | tf_op jit(solution)/shard_map/ppermute | solution.py:52
  89.2 49.0 %collective-permute-start.5 = (f32[2,2,64,1024]{3,2,1,0:T(8,128)}, f32[2,2,64,1024]{3,2,1,0:T(8,128)S(1)}, u32[]{:S(2)}, u32[]{:S(2)}) collective-permute-start(f32[2,2,64,1024]{3,2,1,0:T(8,128)} %get-tuple-element.55), channel_id=1, source_target_pairs={{0,32},{16,48},{32,0},{48,16},{1,33},{17,49},{33,1},{49,17},{2,34}... | collective-permute-start | bytes 3145736 | tf_op jit(solution)/shard_map/ppermute | solution.py:52
  92.0 1.8 copy-start.30
  92.0 46.2 %collective-permute-start.6 = (f32[2,2,64,1024]{3,2,1,0:T(8,128)}, f32[2,2,64,1024]{3,2,1,0:T(8,128)S(1)}, u32[]{:S(2)}, u32[]{:S(2)}) collective-permute-start(f32[2,2,64,1024]{3,2,1,0:T(8,128)} %get-tuple-element.56), channel_id=1, source_target_pairs={{0,48},{16,0},{32,16},{48,32},{1,49},{17,1},{33,17},{49,33},{2,50}... | collective-permute-start | bytes 3145736 | tf_op jit(solution)/shard_map/ppermute | solution.py:52
  98.8 15.3 %collective-permute-start.24 = (f32[4,64,512]{2,1,0:T(8,128)}, f32[4,64,512]{2,1,0:T(8,128)S(1)}, u32[]{:S(2)}, u32[]{:S(2)}) collective-permute-start(f32[4,64,512]{2,1,0:T(8,128)} %get-tuple-element.75), channel_id=1, source_target_pairs={{0,1},{1,64},{64,65},{65,0},{2,3},{3,66},{66,67},{67,2},{4,5},{5,6... | collective-permute-start | bytes 1572872 | tf_op jit(solution)/shard_map/ppermute | solution.py:52
  98.8 44.2 %collective-permute-start.25 = (f32[4,64,512]{2,1,0:T(8,128)}, f32[4,64,512]{2,1,0:T(8,128)}, u32[]{:S(2)}, u32[]{:S(2)}) collective-permute-start(f32[4,64,512]{2,1,0:T(8,128)} %get-tuple-element.76), channel_id=1, source_target_pairs={{0,64},{1,65},{64,0},{65,1},{2,66},{3,67},{66,2},{67,3},{4,68},{5,... | collective-permute-start | bytes 1572872 | tf_op jit(solution)/shard_map/ppermute | solution.py:52
  114.2 0.8 copy-start.6
  115.0 47.6 %collective-permute-start.20 = (f32[2,8,40,256]{3,2,1,0:T(8,128)}, f32[2,8,40,256]{3,2,1,0:T(8,128)S(1)}, u32[]{:S(2)}, u32[]{:S(2)}) collective-permute-start(f32[2,8,40,256]{3,2,1,0:T(8,128)} %get-tuple-element.71), channel_id=1, source_target_pairs={{0,2},{2,4},{4,6},{6,0},{1,3},{3,5},{5,7},{7,1},{8,10},{10,12},{12... | collective-permute-start | bytes 1966088 | tf_op jit(solution)/shard_map/ppermute | solution.py:52
  115.0 23.5 %copy-start.2 = (f32[2,2,64,1024]{3,2,1,0:T(8,128)}, f32[2,2,64,1024]{3,2,1,0:T(8,128)S(1)}, u32[]{:S(2)}) copy-start(f32[2,2,64,1024]{3,2,1,0:T(8,128)S(1)} %collective-permute-done.4.a1) | copy-start | bytes 3145732
  115.0 28.9 %collective-permute-start.26 = (f32[4,64,512]{2,1,0:T(8,128)}, f32[4,64,512]{2,1,0:T(8,128)}, u32[]{:S(2)}, u32[]{:S(2)}) collective-permute-start(f32[4,64,512]{2,1,0:T(8,128)} %get-tuple-element.77), channel_id=1, source_target_pairs={{0,65},{1,0},{64,1},{65,64},{2,67},{3,2},{66,3},{67,66},{4,69},{5,... | collective-permute-start | bytes 1572872 | tf_op jit(solution)/shard_map/ppermute | solution.py:52
  138.2 1.0 copy-start.3
  138.2 24.4 %collective-permute-start.21 = (f32[2,8,40,256]{3,2,1,0:T(8,128)}, f32[2,8,40,256]{3,2,1,0:T(8,128)}, u32[]{:S(2)}, u32[]{:S(2)}) collective-permute-start(f32[2,8,40,256]{3,2,1,0:T(8,128)} %get-tuple-element.72), channel_id=1, source_target_pairs={{0,4},{2,6},{4,0},{6,2},{1,5},{3,7},{5,1},{7,3},{8,12},{10,14},{12... | collective-permute-start | bytes 1966088 | tf_op jit(solution)/shard_map/ppermute | solution.py:52
  138.2 1.3 copy-start.4
  138.2 29.9 %collective-permute-start.22 = (f32[2,8,40,256]{3,2,1,0:T(8,128)}, f32[2,8,40,256]{3,2,1,0:T(8,128)}, u32[]{:S(2)}, u32[]{:S(2)}) collective-permute-start(f32[2,8,40,256]{3,2,1,0:T(8,128)} %get-tuple-element.73), channel_id=1, source_target_pairs={{0,6},{2,0},{4,2},{6,4},{1,7},{3,1},{5,3},{7,5},{8,14},{10,8},{12,... | collective-permute-start | bytes 1966088 | tf_op jit(solution)/shard_map/ppermute | solution.py:52
  143.1 18.8 %collective-permute-start.7 = (f32[2,2,64,256]{3,2,1,0:T(8,128)}, f32[2,2,64,256]{3,2,1,0:T(8,128)S(1)}, u32[]{:S(2)}, u32[]{:S(2)}) collective-permute-start(f32[2,2,64,256]{3,2,1,0:T(8,128)} %get-tuple-element.58), channel_id=1, source_target_pairs={{0,2},{2,4},{4,6},{6,0},{1,3},{3,5},{5,7},{7,1},{8,10},{10,12},{12... | collective-permute-start | bytes 786440 | tf_op jit(solution)/shard_map/ppermute | solution.py:52
  143.9 30.5 %collective-permute-start.14 = (f32[2,2,24,1024]{3,2,1,0:T(8,128)}, f32[2,2,24,1024]{3,2,1,0:T(8,128)S(1)}, u32[]{:S(2)}, u32[]{:S(2)}) collective-permute-start(f32[2,2,24,1024]{3,2,1,0:T(8,128)} %get-tuple-element.63), channel_id=1, source_target_pairs={{0,16},{16,32},{32,48},{48,0},{1,17},{17,33},{33,49},{49,1},{2,18}... | collective-permute-start | bytes 1179656 | tf_op jit(solution)/shard_map/ppermute | solution.py:52
  161.8 30.6 %copy-start.17 = (f32[2,2,64,256]{3,2,1,0:T(8,128)}, f32[2,2,64,256]{3,2,1,0:T(8,128)S(1)}, u32[]{:S(2)}) copy-start(f32[2,2,64,256]{3,2,1,0:T(8,128)S(1)} %collective-permute-done.7.refs_1_) | copy-start | bytes 786436
  161.8 12.8 %collective-permute-start.15 = (f32[2,2,24,1024]{3,2,1,0:T(8,128)}, f32[2,2,24,1024]{3,2,1,0:T(8,128)S(1)}, u32[]{:S(2)}, u32[]{:S(2)}) collective-permute-start(f32[2,2,24,1024]{3,2,1,0:T(8,128)} %get-tuple-element.64), channel_id=1, source_target_pairs={{0,32},{16,48},{32,0},{48,16},{1,33},{17,49},{33,1},{49,17},{2,34}... | collective-permute-start | bytes 1179656 | tf_op jit(solution)/shard_map/ppermute | solution.py:52
  162.6 8.1 %copy-start.5 = (f32[2,8,40,256]{3,2,1,0:T(8,128)}, f32[2,8,40,256]{3,2,1,0:T(8,128)S(1)}, u32[]{:S(2)}) copy-start(f32[2,8,40,256]{3,2,1,0:T(8,128)S(1)} %collective-permute-done.20.a1) | copy-start | bytes 1966084
  162.6 12.8 %collective-permute-start.16 = (f32[2,2,24,1024]{3,2,1,0:T(8,128)}, f32[2,2,24,1024]{3,2,1,0:T(8,128)S(1)}, u32[]{:S(2)}, u32[]{:S(2)}) collective-permute-start(f32[2,2,24,1024]{3,2,1,0:T(8,128)} %get-tuple-element.65), channel_id=1, source_target_pairs={{0,48},{16,0},{32,16},{48,32},{1,49},{17,1},{33,17},{49,33},{2,50}... | collective-permute-start | bytes 1179656 | tf_op jit(solution)/shard_map/ppermute | solution.py:52
  162.6 17.5 %collective-permute-start.8 = (f32[2,2,64,256]{3,2,1,0:T(8,128)}, f32[2,2,64,256]{3,2,1,0:T(8,128)S(1)}, u32[]{:S(2)}, u32[]{:S(2)}) collective-permute-start(f32[2,2,64,256]{3,2,1,0:T(8,128)} %get-tuple-element.59), channel_id=1, source_target_pairs={{0,4},{2,6},{4,0},{6,2},{1,5},{3,7},{5,1},{7,3},{8,12},{10,14},{12... | collective-permute-start | bytes 786440 | tf_op jit(solution)/shard_map/ppermute | solution.py:52
  168.2 12.0 %collective-permute-start.9 = (f32[2,2,64,256]{3,2,1,0:T(8,128)}, f32[2,2,64,256]{3,2,1,0:T(8,128)S(1)}, u32[]{:S(2)}, u32[]{:S(2)}) collective-permute-start(f32[2,2,64,256]{3,2,1,0:T(8,128)} %get-tuple-element.60), channel_id=1, source_target_pairs={{0,6},{2,0},{4,2},{6,4},{1,7},{3,1},{5,3},{7,5},{8,14},{10,8},{12,... | collective-permute-start | bytes 786440 | tf_op jit(solution)/shard_map/ppermute | solution.py:52
  174.4 3.4 %copy-start.11 = (f32[2,2,24,1024]{3,2,1,0:T(8,128)}, f32[2,2,24,1024]{3,2,1,0:T(8,128)S(1)}, u32[]{:S(2)}) copy-start(f32[2,2,24,1024]{3,2,1,0:T(8,128)S(1)} %collective-permute-done.14.a1) | copy-start | bytes 1179652
  174.4 18.0 %collective-permute-start.27 = (f32[288,256]{1,0:T(8,128)}, f32[288,256]{1,0:T(8,128)S(1)}, u32[]{:S(2)}, u32[]{:S(2)}) collective-permute-start(f32[288,256]{1,0:T(8,128)} %get-tuple-element.79), channel_id=1, source_target_pairs={{0,16},{16,32},{32,48},{48,0},{1,17},{17,33},{33,49},{49,1},{2,18}... | collective-permute-start | bytes 884744 | tf_op jit(solution)/shard_map/ppermute | solution.py:52
  174.6 3.3 %copy-start.12 = (f32[2,2,24,1024]{3,2,1,0:T(8,128)}, f32[2,2,24,1024]{3,2,1,0:T(8,128)S(1)}, u32[]{:S(2)}) copy-start(f32[2,2,24,1024]{3,2,1,0:T(8,128)S(1)} %collective-permute-done.15.a2) | copy-start | bytes 1179652
  174.6 17.8 %collective-permute-start.28 = (f32[288,256]{1,0:T(8,128)}, f32[288,256]{1,0:T(8,128)S(1)}, u32[]{:S(2)}, u32[]{:S(2)}) collective-permute-start(f32[288,256]{1,0:T(8,128)} %get-tuple-element.80), channel_id=1, source_target_pairs={{0,32},{16,48},{32,0},{48,16},{1,33},{17,49},{33,1},{49,17},{2,34}... | collective-permute-start | bytes 884744 | tf_op jit(solution)/shard_map/ppermute | solution.py:52
  175.4 2.5 %copy-start.13 = (f32[2,2,24,1024]{3,2,1,0:T(8,128)}, f32[2,2,24,1024]{3,2,1,0:T(8,128)S(1)}, u32[]{:S(2)}) copy-start(f32[2,2,24,1024]{3,2,1,0:T(8,128)S(1)} %collective-permute-done.16.a3) | copy-start | bytes 1179652
  175.4 17.0 %collective-permute-start.29 = (f32[288,256]{1,0:T(8,128)}, f32[288,256]{1,0:T(8,128)S(1)}, u32[]{:S(2)}, u32[]{:S(2)}) collective-permute-start(f32[288,256]{1,0:T(8,128)} %get-tuple-element.81), channel_id=1, source_target_pairs={{0,48},{16,0},{32,16},{48,32},{1,49},{17,1},{33,17},{49,33},{2,50}... | collective-permute-start | bytes 884744 | tf_op jit(solution)/shard_map/ppermute | solution.py:52
  180.1 12.4 %copy-start.18 = (f32[2,2,64,256]{3,2,1,0:T(8,128)}, f32[2,2,64,256]{3,2,1,0:T(8,128)S(1)}, u32[]{:S(2)}) copy-start(f32[2,2,64,256]{3,2,1,0:T(8,128)S(1)} %collective-permute-done.8.refs_2_) | copy-start | bytes 786436
  180.1 7.5 %collective-permute-start.17 = (f32[2,2,24,256]{3,2,1,0:T(8,128)}, f32[2,2,24,256]{3,2,1,0:T(8,128)S(1)}, u32[]{:S(2)}, u32[]{:S(2)}) collective-permute-start(f32[2,2,24,256]{3,2,1,0:T(8,128)} %get-tuple-element.67), channel_id=1, source_target_pairs={{0,2},{2,4},{4,6},{6,0},{1,3},{3,5},{5,7},{7,1},{8,10},{10,12},{12... | collective-permute-start | bytes 294920 | tf_op jit(solution)/shard_map/ppermute | solution.py:52
  180.2 12.3 %copy-start.19 = (f32[2,2,64,256]{3,2,1,0:T(8,128)}, f32[2,2,64,256]{3,2,1,0:T(8,128)S(1)}, u32[]{:S(2)}) copy-start(f32[2,2,64,256]{3,2,1,0:T(8,128)S(1)} %collective-permute-done.9.refs_3_) | copy-start | bytes 786436
  180.2 7.4 %collective-permute-start.18 = (f32[2,2,24,256]{3,2,1,0:T(8,128)}, f32[2,2,24,256]{3,2,1,0:T(8,128)S(1)}, u32[]{:S(2)}, u32[]{:S(2)}) collective-permute-start(f32[2,2,24,256]{3,2,1,0:T(8,128)} %get-tuple-element.68), channel_id=1, source_target_pairs={{0,4},{2,6},{4,0},{6,2},{1,5},{3,7},{5,1},{7,3},{8,12},{10,14},{12... | collective-permute-start | bytes 294920 | tf_op jit(solution)/shard_map/ppermute | solution.py:52
  187.6 4.9 %copy-start.23 = (f32[2,2,24,256]{3,2,1,0:T(8,128)}, f32[2,2,24,256]{3,2,1,0:T(8,128)S(1)}, u32[]{:S(2)}) copy-start(f32[2,2,24,256]{3,2,1,0:T(8,128)S(1)} %collective-permute-done.17.refs_5_) | copy-start | bytes 294916
  187.6 4.8 %collective-permute-start.19 = (f32[2,2,24,256]{3,2,1,0:T(8,128)}, f32[2,2,24,256]{3,2,1,0:T(8,128)S(1)}, u32[]{:S(2)}, u32[]{:S(2)}) collective-permute-start(f32[2,2,24,256]{3,2,1,0:T(8,128)} %get-tuple-element.69), channel_id=1, source_target_pairs={{0,6},{2,0},{4,2},{6,4},{1,7},{3,1},{5,3},{7,5},{8,14},{10,8},{12,... | collective-permute-start | bytes 294920 | tf_op jit(solution)/shard_map/ppermute | solution.py:52
  187.6 4.9 %copy-start.24 = (f32[2,2,24,256]{3,2,1,0:T(8,128)}, f32[2,2,24,256]{3,2,1,0:T(8,128)S(1)}, u32[]{:S(2)}) copy-start(f32[2,2,24,256]{3,2,1,0:T(8,128)S(1)} %collective-permute-done.18.refs_6_) | copy-start | bytes 294916
  192.4 0.7 copy-start.14
  192.4 0.8 copy-start.15
  192.4 1.0 copy-start.16
  196.0 22.8 %collective-permute-start.30 = (f32[4,64,128]{2,1,0:T(8,128)}, f32[4,64,128]{2,1,0:T(8,128)S(1)}, u32[]{:S(2)}, u32[]{:S(2)}) collective-permute-start(f32[4,64,128]{2,1,0:T(8,128)} %get-tuple-element.83), channel_id=1, source_target_pairs={{0,1},{1,64},{64,65},{65,0},{2,3},{3,66},{66,67},{67,2},{4,5},{5,6... | collective-permute-start | bytes 393224 | tf_op jit(solution)/shard_map/ppermute | solution.py:52
  205.2 13.6 %collective-permute-start.31 = (f32[4,64,128]{2,1,0:T(8,128)}, f32[4,64,128]{2,1,0:T(8,128)S(1)}, u32[]{:S(2)}, u32[]{:S(2)}) collective-permute-start(f32[4,64,128]{2,1,0:T(8,128)} %get-tuple-element.84), channel_id=1, source_target_pairs={{0,64},{1,65},{64,0},{65,1},{2,66},{3,67},{66,2},{67,3},{4,68},{5,... | collective-permute-start | bytes 393224 | tf_op jit(solution)/shard_map/ppermute | solution.py:52
  206.8 12.0 %collective-permute-start.32 = (f32[4,64,128]{2,1,0:T(8,128)}, f32[4,64,128]{2,1,0:T(8,128)S(1)}, u32[]{:S(2)}, u32[]{:S(2)}) collective-permute-start(f32[4,64,128]{2,1,0:T(8,128)} %get-tuple-element.85), channel_id=1, source_target_pairs={{0,65},{1,0},{64,1},{65,64},{2,67},{3,2},{66,3},{67,66},{4,69},{5,... | collective-permute-start | bytes 393224 | tf_op jit(solution)/shard_map/ppermute | solution.py:52
  209.4 5.3 %collective-permute-start.33 = (f32[64,128]{1,0:T(8,128)}, f32[64,128]{1,0:T(8,128)S(1)}, u32[]{:S(2)}, u32[]{:S(2)}) collective-permute-start(f32[64,128]{1,0:T(8,128)} %get-tuple-element.87), channel_id=1, source_target_pairs={{0,2},{2,4},{4,6},{6,0},{1,3},{3,5},{5,7},{7,1},{8,10},{10,12},{12... | collective-permute-start | bytes 98312 | tf_op jit(solution)/shard_map/ppermute | solution.py:52
  209.4 5.7 %collective-permute-start.34 = (f32[64,128]{1,0:T(8,128)}, f32[64,128]{1,0:T(8,128)S(1)}, u32[]{:S(2)}, u32[]{:S(2)}) collective-permute-start(f32[64,128]{1,0:T(8,128)} %get-tuple-element.88), channel_id=1, source_target_pairs={{0,4},{2,6},{4,0},{6,2},{1,5},{3,7},{5,1},{7,3},{8,12},{10,14},{12... | collective-permute-start | bytes 98312 | tf_op jit(solution)/shard_map/ppermute | solution.py:52
  214.7 4.2 %copy-start.26 = (f32[64,128]{1,0:T(8,128)}, f32[64,128]{1,0:T(8,128)S(1)}, u32[]{:S(2)}) copy-start(f32[64,128]{1,0:T(8,128)S(1)} %collective-permute-done.33.w1) | copy-start | bytes 98308
  214.7 4.1 %collective-permute-start.35 = (f32[64,128]{1,0:T(8,128)}, f32[64,128]{1,0:T(8,128)S(1)}, u32[]{:S(2)}, u32[]{:S(2)}) collective-permute-start(f32[64,128]{1,0:T(8,128)} %get-tuple-element.89), channel_id=1, source_target_pairs={{0,6},{2,0},{4,2},{6,4},{1,7},{3,1},{5,3},{7,5},{8,14},{10,8},{12,... | collective-permute-start | bytes 98312 | tf_op jit(solution)/shard_map/ppermute | solution.py:52
  215.1 3.8 %copy-start.27 = (f32[64,128]{1,0:T(8,128)}, f32[64,128]{1,0:T(8,128)S(1)}, u32[]{:S(2)}) copy-start(f32[64,128]{1,0:T(8,128)S(1)} %collective-permute-done.34.w2) | copy-start | bytes 98308
  (5 other events, 3.3 us)

commit v6 on v2

--- a/solution.py
+++ b/solution.py
@@ -19,6 +19,7 @@
 ROW = ("zhi", "x", "core")
 COL = ("y", "zlo")
 X, Y, Z = "x", "y", ("zhi", "zlo")
+YZ, XZ = ("y", "zhi", "zlo"), ("x", "zhi", "zlo")
 HALF = 32
 
 
@@ -59,10 +60,11 @@
     return lax.ppermute(value, AXES, pairs)
 
 
-def route_kernel(dest_col, dest_row, rows, fluid, out):
+def route_kernel(dest_row, rows, fluid, out):
     n = dest_row.shape[1]
+    dest = jnp.broadcast_to(dest_row[...].astype(F32), (n, n))
     earlier = lax.broadcasted_iota(jnp.int32, (n, n), 0) < lax.broadcasted_iota(jnp.int32, (n, n), 1)
-    same = (dest_col[...] == dest_row[...]) & earlier
+    same = (dest.T == dest) & earlier
     slot = jnp.sum(jnp.where(same, 1.0, 0.0), axis=0, keepdims=True).astype(jnp.int32)
     target = dest_row[...] * CAP + slot
     q = out.shape[0] * CAP
@@ -198,11 +200,35 @@
         out[...] = held[:, d // 2, :, lanes]
 
 
-def last_kernel(a0, a1, a2, a3, b0, b1, b2, b3, fstiff, fmass, wet, stiff, mass):
-    for m, out in enumerate((fstiff, fmass, wet)):
+def plane_x_kernel(a0, a1, a2, a3, out, held):
+    held[...] = (a0[...] + a1[...]) + (a2[...] + a3[...])
+    for y in range(4):
+        for h in range(2):
+            for l in range(2):
+                at = (y * 2 + l) * 128
+                out[y * 4 + h * 2 + l] = held[:, h, :, at : at + 128]
+
+
+def plane_y_kernel(a0, a1, a2, a3, out, held):
+    held[...] = (a0[...] + a1[...]) + (a2[...] + a3[...])
+    for x in range(4):
+        for h in range(2):
+            for l in range(2):
+                out[x * 4 + h * 2 + l] = held[:, h * 4 + x, :, l * 128 : (l + 1) * 128]
+
+
+def last_kernel(a0, a1, a2, a3, *outs):
+    for m, out in enumerate(outs):
         out[...] = (a0[m] + a1[m]) + (a2[m] + a3[m])
-    for m, out in enumerate((stiff, mass)):
-        out[...] = (b0[m] + b1[m]) + (b2[m] + b3[m])
+
+
+def last_plane_kernel(top, low, *outs):
+    for m, out in enumerate(outs):
+        for ref, at in ((top, 0), (low, HALF)):
+            terms = [ref[i, m] for i in range(ref.shape[0])]
+            while len(terms) > 1:
+                terms = [terms[i] + terms[i + 1] for i in range(0, len(terms), 2)]
+            out[at : at + HALF] = terms[0]
 
 
 def call(kernel, out, count, smem=0, anywhere=0, scratch=(), flops=0, moved=0):
@@ -234,6 +260,19 @@
         flops=3 * size,
         moved=20 * size,
     )(place, *arrived)
+
+
+def plane(kernel, arrived, axes):
+    size = arrived[0].size
+    slots = call(
+        kernel,
+        shape(16, arrived[0].shape[0], HALF, 128),
+        4,
+        scratch=[pltpu.VMEM(arrived[0].shape, F32)],
+        flops=3 * size,
+        moved=20 * size,
+    )(*arrived)
+    return lax.all_to_all(slots, axes, split_axis=0, concat_axis=0, tiled=True)
 
 
 def spread(place, x, y):
@@ -289,8 +328,8 @@
     below_f = from_behind(fluid_basis, 1)
     above_f = from_behind(fluid_basis, -1)
 
-    outgoing = call(route_kernel, shape(128, CAP, R), 4, flops=2 * 3 * 256 * 128 * R, moved=2**21)(
-        wet_dest, wet_dest.reshape(1, -1), wet_rows.reshape(1, -1), fluid_basis
+    outgoing = call(route_kernel, shape(128, CAP, R), 3, flops=2 * 3 * 256 * 128 * R, moved=2**21)(
+        wet_dest.reshape(1, -1), wet_rows.reshape(1, -1), fluid_basis
     )
     received = lax.all_to_all(outgoing, AXES, split_axis=0, concat_axis=0, tiled=True)
 
@@ -351,13 +390,11 @@
 
     first_xy = exchanged(split(place, first_x, 1), Y)
     first_yx = exchanged(split(place, first_y, 0), X)
-    second_xy = exchanged(split(place, second_x, 1), Y)
-    second_yx = exchanged(split(place, second_y, 0), X)
     first_z = exchanged(spread(place, first_xy, first_yx), Z)
-    second_z = exchanged(spread(place, second_xy, second_yx), Z)
-    fstiff, fmass, wet, stiff, mass = call(
-        last_kernel, [shape(64, 128)] * 5, 8, flops=2**18, moved=2**20
-    )(*first_z, *second_z)
+    second_top = plane(plane_x_kernel, second_x, YZ)
+    second_low = plane(plane_y_kernel, second_y, XZ)
+    fstiff, fmass, wet = call(last_kernel, [shape(64, 128)] * 3, 4, flops=2**17, moved=2**19)(*first_z)
+    stiff, mass = call(last_plane_kernel, [shape(64, 128)] * 2, 2, flops=2**18, moved=2**20)(second_top, second_low)
     return stiff, mass, fstiff, fmass, wet
 
 

time: 224 us -> 255 us (1.14)
  waiting for transfers between devices: 83.5 us -> 107 us
  starting transfers between devices: 74.3 us -> 85.2 us
  local copies, waits for them, and re-layouts: 9.89 us -> 7.21 us
    ppermute x35 -> x26, waiting for transfers between devices: 47.2 us -> 69.2 us  [shifted(): lax.ppermute(value, axis, [(i, (i + by) % size) for i in range(size)])]
    all_to_all x0 -> x2, starting transfers between devices: none -> 9.68 us  [plane(): return lax.all_to_all(slots, axes, split_axis=0, concat_axis=0, tiled=True)]
    pallas_call x2 -> x5, Pallas kernels: 4.64 us -> 11.4 us  [the longest x2 4.9 us: plane(): call(kernel, shape(16, arrived[0].shape[0], HALF, 128), 4, scratch=[pltpu...]
    pallas_call x4 -> x2, Pallas kernels: 11.1 us -> 6.08 us  [split(): call(functools.partial(split_kernel, axis), [shape(count, 2, HALF, 256)]...]
    unnamed x89 -> x58, local copies, waits for them, and re-layouts: 8.93 us -> 6.31 us
    ppermute x35 -> x26, starting transfers between devices: 53.1 us -> 54.3 us  [shifted(): lax.ppermute(value, axis, [(i, (i + by) % size) for i in range(size)])]
  transfers between devices with their start and end apart: 40 -> 33, of which waited for: 10 -> 12; matrix products, arithmetic and copies ran while one was open for 1% -> 1% of each run, Pallas kernels for 19% -> 17%
where the time goes in v6:
time: 255 us
  waiting for transfers between devices  107 us (42%)
  starting transfers between devices  85.2 us (33%)
  Pallas kernels  53.8 us (21%)
  local copies, waits for them, and re-layouts  7.21 us (3%)
    ppermute x26, waiting for transfers between devices, shifted(): lax.ppermute(value, axis, [(i, (i + by) % size) for i in range(size)])  69.2 us
    ppermute x26, starting transfers between devices, shifted(): lax.ppermute(value, axis, [(i, (i + by) % size) for i in range(size)])  54.3 us
    ppermute x4, waiting for transfers between devices, from_behind(): return lax.ppermute(value, AXES, pairs)  36.3 us
    pallas_call x3, Pallas kernels, partial_sums(): return run(place, *lefts, *operands, *carried)  17.9 us
    all_to_all x1, starting transfers between devices, compute(): lax.all_to_all(outgoing, AXES, split_axis=0, concat_axis=0, tiled=True)  11.2 us
    ppermute x4, starting transfers between devices, from_behind(): return lax.ppermute(value, AXES, pairs)  10 us
    all_to_all x2, starting transfers between devices, plane(): return lax.all_to_all(slots, axes, split_axis=0, concat_axis=0, tiled=True)  9.68 us
    unnamed x58, local copies, waits for them, and re-layouts  6.31 us
  transfers between devices with their start and end apart: 33, of which 12 were waited for; matrix products, arithmetic and copies ran while one was open for 1% of the time, Pallas kernels for 17%

profile of v6, /device:TPU:0, one launch (start us, length us, event | category | flops | bytes accessed | tf_op | source)
XLA Modules:
  0.0 254.7 jit_solution(4067175426722053595)
XLA Ops:
  0.6 2.9 %shard_map.147 = f32[128,2,1024]{2,1,0:T(2,128)} custom-call(s32[1,128]{1,0:T(1,128)} %bitcast.6, s32[1,128]{1,0:T(1,128)} %bitcast.7, f32[128,1024]{1,0:T(8,128)} %own.2), custom_call_target="tpu_custom_call" | custom-call | flops 201326592 | bytes 2097152 | tf_op jit(solution)/shard_map/pallas_call | solution.py:331
  3.6 11.2 %all-to-all-start = ((f32[128,2,1024]{2,1,0:T(2,128)}), f32[128,2,1024]{2,1,0:T(2,128)S(1)}, u32[]{:S(2)}, u32[]{:S(2)}) async-start(f32[128,2,1024]{2,1,0:T(2,128)} %shard_map.147), calls=%async_computation | async-start | bytes 2097152 | tf_op jit(solution)/shard_map/all_to_all | solution.py:334
  14.8 3.0 %collective-permute-start.5 = (f32[128,1024]{1,0:T(8,128)S(1)}, f32[128,1024]{1,0:T(8,128)S(1)}, u32[]{:S(2)}, u32[]{:S(2)}) collective-permute-start(f32[128,1024]{1,0:T(8,128)S(1)} %copy-done.1), channel_id=1, source_target_pairs={{0,1},{1,2},{2,3},{3,4},{4,5},{5,6},{6,7},{7,8},{8,9},{9,10},{10,1... | collective-permute-start | bytes 1572872 | tf_op jit(solution)/shard_map/ppermute | solution.py:60
  17.8 1.3 collective-permute-start.6
  19.1 0.6 pad_add_fusion.place
  19.7 3.0 %shard_map.146 = (f32[8,64,256]{2,1,0:T(8,128)}, f32[8,64,256]{2,1,0:T(8,128)}, f32[8,64,128]{2,1,0:T(8,128)}, f32[8,64,128]{2,1,0:T(8,128)}) custom-call(s32[4]{0:T(128)} %pad_add_fusion.place, f32[256,1024]{1,0:T(8,128)} %own.3, f32[128,1024]{1,0:T(8,128)} %own.2), custom_call_target="tpu_custom_call" | custom-call | flops 1048576 | bytes 3145728 | tf_op jit(solution)/shard_map/pallas_call | solution.py:336
  22.7 26.5 %collective-permute-done.5.lo = f32[128,1024]{1,0:T(8,128)S(1)} collective-permute-done((f32[128,1024]{1,0:T(8,128)S(1)}, f32[128,1024]{1,0:T(8,128)S(1)}, u32[]{:S(2)}, u32[]{:S(2)}) %collective-permute-start.5) | collective-permute-done | bytes 524320 | tf_op jit(solution)/shard_map/ppermute | solution.py:60
  49.1 0.8 copy-done.17
  50.1 4.0 %shard_map.149.if0 = f32[2,128,1024]{2,1,0:T(8,128)} custom-call(s32[1,4]{1,0:T(1,128)} %cols.2, f32[1,4,128,128]{3,2,1,0:T(8,128)} %stiff.2, f32[1,4,128,128]{3,2,1,0:T(8,128)} %mass.2, f32[128,1024]{1,0:T(8,128)} %copy-done.17, f32[128,1024]{1,0:T(8,128)} %own.2, f32[128,1024]{1,0:T(8,128)} %copy-done.18, f32[8,64,256]{2,1,0:T(8,128)} %get-tuple-element.50.after.ls0), custom_call_target="tpu_custom_call" | custom-call | flops 603979776 | bytes 3145728 | tf_op jit(solution)/shard_map/pallas_call | solution.py:351
  54.1 1.0 copy-done.2
  55.1 3.2 %shard_map.148.ic0 = f32[256,1024]{1,0:T(8,128)} custom-call(f32[256,256]{1,0:T(8,128)} %coupling.1, f32[128,2,1024]{2,1,0:T(2,128)} %copy-done.2), custom_call_target="tpu_custom_call" | custom-call | flops 402653184 | bytes 2097152 | tf_op jit(solution)/shard_map/pallas_call | solution.py:348
  58.2 0.5 collective-permute-start.3
  58.8 0.5 collective-permute-start
  59.2 0.9 fusion
  60.1 4.4 %collective-permute-start.1 = (f32[128,1024]{1,0:T(8,128)}, f32[128,1024]{1,0:T(8,128)S(1)}, u32[]{:S(2)}, u32[]{:S(2)}) collective-permute-start(f32[128,1024]{1,0:T(8,128)} %get-tuple-element.96), channel_id=1, source_target_pairs={{0,1},{1,2},{2,3},{3,4},{4,5},{5,6},{6,7},{7,8},{8,9},{9,10},{10,1... | collective-permute-start | bytes 1572872 | tf_op jit(solution)/shard_map/ppermute | solution.py:60
  64.6 1.3 collective-permute-start.2
  65.9 5.3 %shard_map.150 = (f32[3,2,32,1024]{3,2,1,0:T(8,128)}, f32[3,2,32,1024]{3,2,1,0:T(8,128)}, f32[3,2,32,1024]{3,2,1,0:T(8,128)}, f32[3,2,32,1024]{3,2,1,0:T(8,128)}...) custom-call(s32[4]{0:T(128)} %pad_add_fusion.place, ...), custom_call_target="tpu_custom_call" | custom-call | flops 1610612736 | bytes 8388608 | tf_op jit(solution)/shard_map/pallas_call | solution.py:307
  71.2 0.8 copy-done.10
  72.3 5.3 %shard_map.151 = (f32[3,2,32,1024]{3,2,1,0:T(8,128)}, f32[3,2,32,1024]{3,2,1,0:T(8,128)}, f32[3,2,32,1024]{3,2,1,0:T(8,128)}, f32[3,2,32,1024]{3,2,1,0:T(8,128)}...) custom-call(s32[4]{0:T(128)} %pad_add_fusion.place, ...), custom_call_target="tpu_custom_call", output_to_operand_aliasing={{0}: (5, {}), {1}: (6, {}), {2}: (7, {}), {3}: (8, {}), {4}... | custom-call | flops 1610612736 | bytes 4194304 | tf_op jit(solution)/shard_map/pallas_call | solution.py:307
  77.6 9.8 %collective-permute-done.1.lo = f32[128,1024]{1,0:T(8,128)S(1)} collective-permute-done((f32[128,1024]{1,0:T(8,128)}, f32[128,1024]{1,0:T(8,128)S(1)}, u32[]{:S(2)}, u32[]{:S(2)}) %collective-permute-start.1) | collective-permute-done | bytes 524320 | tf_op jit(solution)/shard_map/ppermute | solution.py:60
  87.4 0.8 copy-done.12
  88.4 6.0 %shard_map.152.is0 = f32[2,256,1024]{2,1,0:T(8,128)} custom-call(s32[2,4]{1,0:T(2,128)} %cols.3, f32[2,4,128,128]{3,2,1,0:T(8,128)} %stiff.3, f32[2,4,128,128]{3,2,1,0:T(8,128)} %mass.3, f32[128,1024]{1,0:T(8,128)} %copy-done.12, f32[256,1024]{1,0:T(8,128)} %own.3, f32[128,1024]{1,0:T(8,128)} %copy-done.15, f32[3,2,32,1024]{3,2,1,0:T(8,128)} %get-tuple-element.62.after.a0), custom_call_target="tpu_custom_call" | custom-call | flops 1610612736 | bytes 5242880 | tf_op jit(solution)/shard_map/pallas_call | solution.py:375
  94.4 3.6 %collective-permute-start.21 = (f32[3,8,32,256]{3,2,1,0:T(8,128)S(1)}, f32[3,8,32,256]{3,2,1,0:T(8,128)}, u32[]{:S(2)}, u32[]{:S(2)}) collective-permute-start(f32[3,8,32,256]{3,2,1,0:T(8,128)S(1)} %copy-done.9), channel_id=1, source_target_pairs={{0,2},{2,4},{4,6},{6,0},{1,3},{3,5},{5,7},{7,1},{8,10},{10,12},{12... | collective-permute-start | bytes 2359304 | tf_op jit(solution)/shard_map/ppermute | solution.py:54
  98.0 2.5 collective-permute-start.22
  100.5 1.3 collective-permute-start.23
  101.8 7.4 %shard_map.153 = (f32[2,2,32,1024]{3,2,1,0:T(8,128)}, f32[2,2,32,1024]{3,2,1,0:T(8,128)}, f32[2,2,32,1024]{3,2,1,0:T(8,128)}, f32[2,2,32,1024]{3,2,1,0:T(8,128)}...) custom-call(s32[4]{0:T(128)} %pad_add_fusion.place, ...), custom_call_target="tpu_custom_call" | custom-call | flops 3221225472 | bytes 8388608 | tf_op jit(solution)/shard_map/pallas_call | solution.py:307
  109.2 0.8 collective-permute-start.12
  110.0 2.4 collective-permute-start.13
  112.3 5.2 %collective-permute-done.21.a1 = f32[3,8,32,256]{3,2,1,0:T(8,128)} collective-permute-done((f32[3,8,32,256]{3,2,1,0:T(8,128)S(1)}, f32[3,8,32,256]{3,2,1,0:T(8,128)}, u32[]{:S(2)}, u32[]{:S(2)}) %collective-permute-start.21) | collective-permute-done | bytes 786464 | tf_op jit(solution)/shard_map/ppermute | solution.py:54
  117.5 2.0 collective-permute-start.14
  119.5 16.3 %collective-permute-done.22.a2 = f32[3,8,32,256]{3,2,1,0:T(8,128)} collective-permute-done((f32[3,8,32,256]{3,2,1,0:T(8,128)}, f32[3,8,32,256]{3,2,1,0:T(8,128)}, u32[]{:S(2)}, u32[]{:S(2)}) %collective-permute-start.22) | collective-permute-done | bytes 786464 | tf_op jit(solution)/shard_map/ppermute | solution.py:54
  135.9 3.6 %collective-permute-start.10 = (f32[2,2,32,1024]{3,2,1,0:T(8,128)}, f32[2,2,32,1024]{3,2,1,0:T(8,128)S(1)}, u32[]{:S(2)}, u32[]{:S(2)}) collective-permute-start(f32[2,2,32,1024]{3,2,1,0:T(8,128)} %get-tuple-element.65), channel_id=1, source_target_pairs={{0,32},{16,48},{32,0},{48,16},{1,33},{17,49},{33,1},{49,17},{2,34}... | collective-permute-start | bytes 1572872 | tf_op jit(solution)/shard_map/ppermute | solution.py:54
  139.9 5.3 %collective-permute-done.12.a1 = f32[2,8,32,256]{3,2,1,0:T(8,128)S(1)} collective-permute-done((f32[2,8,32,256]{3,2,1,0:T(8,128)}, f32[2,8,32,256]{3,2,1,0:T(8,128)S(1)}, u32[]{:S(2)}, u32[]{:S(2)}) %collective-permute-start.12) | collective-permute-done | bytes 524320 | tf_op jit(solution)/shard_map/ppermute | solution.py:54
  145.2 16.1 %collective-permute-start.16 = (f32[3,2,32,1024]{3,2,1,0:T(8,128)S(1)}, f32[3,2,32,1024]{3,2,1,0:T(8,128)}, u32[]{:S(2)}, u32[]{:S(2)}) collective-permute-start(f32[3,2,32,1024]{3,2,1,0:T(8,128)S(1)} %copy-done.7), channel_id=1, source_target_pairs={{0,32},{16,48},{32,0},{48,16},{1,33},{17,49},{33,1},{49,17},{2,34}... | collective-permute-start | bytes 2359304 | tf_op jit(solution)/shard_map/ppermute | solution.py:54
  161.3 1.4 collective-permute-start.17
  162.8 2.0 collective-permute-start.9
  164.8 2.5 shard_map.155
  167.2 5.7 %all-to-all-start.2 = ((f32[16,2,32,128]{3,2,1,0:T(8,128)}), f32[16,2,32,128]{3,2,1,0:T(8,128)S(1)}, u32[]{:S(2)}, u32[]{:S(2)}) async-start(f32[16,2,32,128]{3,2,1,0:T(8,128)} %shard_map.155), calls=%async_computation.2 | async-start | bytes 1048576 | tf_op jit(solution)/shard_map/all_to_all | solution.py:275
  173.0 3.0 %shard_map.158 = (f32[3,2,32,256]{3,2,1,0:T(8,128)}, f32[3,2,32,256]{3,2,1,0:T(8,128)}, f32[3,2,32,256]{3,2,1,0:T(8,128)}, f32[3,2,32,256]{3,2,1,0:T(8,128)}) custom-call(s32[4]{0:T(128)} %pad_add_fusion.place, f32[3,8,32,256]{3,2,1,0:T(8,128)} %get-tuple-element.80.a0, f32[3,8,32,256]{3,2,1,0:T(8,128)} %collective-permute-done.21.a1, ...), custom_call_target="tpu_custom_call" | custom-call | flops 589824 | bytes 3932160 | tf_op jit(solution)/shard_map/pallas_call | solution.py:254
  176.0 32.4 %collective-permute-done.11.a3 = f32[2,2,32,1024]{3,2,1,0:T(8,128)} collective-permute-done((f32[2,2,32,1024]{3,2,1,0:T(8,128)}, f32[2,2,32,1024]{3,2,1,0:T(8,128)}, u32[]{:S(2)}, u32[]{:S(2)}) %collective-permute-start.11) | collective-permute-done | bytes 524320 | tf_op jit(solution)/shard_map/ppermute | solution.py:54
  208.4 1.1 collective-permute-start.24
  209.5 2.4 shard_map.154
  211.9 1.5 all-to-all-done.2.low
  213.4 4.0 %all-to-all-start.1 = ((f32[16,2,32,128]{3,2,1,0:T(8,128)}), f32[16,2,32,128]{3,2,1,0:T(8,128)S(1)}, u32[]{:S(2)}, u32[]{:S(2)}) async-start(f32[16,2,32,128]{3,2,1,0:T(8,128)} %shard_map.154), calls=%async_computation.1 | async-start | bytes 1048576 | tf_op jit(solution)/shard_map/all_to_all | solution.py:275
  217.4 2.5 collective-permute-start.25
  219.9 2.0 collective-permute-start.26
  221.9 3.1 %shard_map.157 = (f32[3,2,32,256]{3,2,1,0:T(8,128)}, f32[3,2,32,256]{3,2,1,0:T(8,128)}, f32[3,2,32,256]{3,2,1,0:T(8,128)}, f32[3,2,32,256]{3,2,1,0:T(8,128)}) custom-call(s32[4]{0:T(128)} %pad_add_fusion.place, f32[3,2,32,1024]{3,2,1,0:T(8,128)} %get-tuple-element.62.after.a0, f32[3,2,32,1024]{3,2,1,0:T(8,128)} %collective-permute-done.15.a1, ...), custom_call_target="tpu_custom_call" | custom-call | flops 589824 | bytes 3932160 | tf_op jit(solution)/shard_map/pallas_call | solution.py:254
  225.0 1.8 collective-permute-start.18
  226.8 2.7 %collective-permute-start.19 = (f32[3,2,32,256]{3,2,1,0:T(8,128)}, f32[3,2,32,256]{3,2,1,0:T(8,128)S(1)}, u32[]{:S(2)}, u32[]{:S(2)}) collective-permute-start(f32[3,2,32,256]{3,2,1,0:T(8,128)} %get-tuple-element.78), channel_id=1, source_target_pairs={{0,4},{2,6},{4,0},{6,2},{1,5},{3,7},{5,1},{7,3},{8,12},{10,14},{12... | collective-permute-start | bytes 589832 | tf_op jit(solution)/shard_map/ppermute | solution.py:54
  229.5 1.5 collective-permute-start.20
  231.0 2.4 collective-permute-done.18.x1
  233.4 4.2 %collective-permute-done.19.x2 = f32[3,2,32,256]{3,2,1,0:T(8,128)S(1)} collective-permute-done((f32[3,2,32,256]{3,2,1,0:T(8,128)}, f32[3,2,32,256]{3,2,1,0:T(8,128)S(1)}, u32[]{:S(2)}, u32[]{:S(2)}) %collective-permute-start.19) | collective-permute-done | bytes 196640 | tf_op jit(solution)/shard_map/ppermute | solution.py:54
  237.6 0.7 copy-done.22
  238.4 2.3 shard_map.159
  240.7 1.5 collective-permute-start.27
  242.1 2.7 %collective-permute-start.28 = (f32[3,64,128]{2,1,0:T(8,128)}, f32[3,64,128]{2,1,0:T(8,128)S(1)}, u32[]{:S(2)}, u32[]{:S(2)}) collective-permute-start(f32[3,64,128]{2,1,0:T(8,128)} %get-tuple-element.90), channel_id=1, source_target_pairs={{0,64},{1,65},{64,0},{65,1},{2,66},{3,67},{66,2},{67,3},{4,68},{5,... | collective-permute-start | bytes 294920 | tf_op jit(solution)/shard_map/ppermute | solution.py:54
  244.8 1.5 collective-permute-start.29
  246.3 0.5 collective-permute-done.27.a1
  246.8 1.9 collective-permute-done.28.a2
  248.7 1.0 collective-permute-done.29.a3
  249.6 0.6 copy-done.26
  250.3 1.7 shard_map.160
  252.0 0.8 copy-done.4
  252.8 1.9 shard_map.156
  (77 shorter events, 1.5 us)
Async XLA Ops:
  0.6 14.1 %copy-start.1 = (f32[128,1024]{1,0:T(8,128)S(1)}, f32[128,1024]{1,0:T(8,128)}, u32[]{:S(2)}) copy-start(f32[128,1024]{1,0:T(8,128)} %own.2) | copy-start | bytes 1572868
  3.6 50.5 %all-to-all-start = ((f32[128,2,1024]{2,1,0:T(2,128)}), f32[128,2,1024]{2,1,0:T(2,128)S(1)}, u32[]{:S(2)}, u32[]{:S(2)}) async-start(f32[128,2,1024]{2,1,0:T(2,128)} %shard_map.147), calls=%async_computation | async-start | bytes 2097152 | tf_op jit(solution)/shard_map/all_to_all | solution.py:334
  14.8 34.3 %collective-permute-start.5 = (f32[128,1024]{1,0:T(8,128)S(1)}, f32[128,1024]{1,0:T(8,128)S(1)}, u32[]{:S(2)}, u32[]{:S(2)}) collective-permute-start(f32[128,1024]{1,0:T(8,128)S(1)} %copy-done.1), channel_id=1, source_target_pairs={{0,1},{1,2},{2,3},{3,4},{4,5},{5,6},{6,7},{7,8},{8,9},{9,10},{10,1... | collective-permute-start | bytes 1572872 | tf_op jit(solution)/shard_map/ppermute | solution.py:60
  17.8 31.3 %collective-permute-start.6 = (f32[128,1024]{1,0:T(8,128)S(1)}, f32[128,1024]{1,0:T(8,128)S(1)}, u32[]{:S(2)}, u32[]{:S(2)}) collective-permute-start(f32[128,1024]{1,0:T(8,128)S(1)} %copy-done.1), channel_id=1, source_target_pairs={{1,0},{2,1},{3,2},{4,3},{5,4},{6,5},{7,6},{8,7},{9,8},{10,9},{11,1... | collective-permute-start | bytes 1572872 | tf_op jit(solution)/shard_map/ppermute | solution.py:60
  49.1 0.8 copy-start.17
  49.1 1.0 copy-start.18
  54.1 4.6 %copy-start.27 = (f32[8,64,128]{2,1,0:T(8,128)S(1)}, f32[8,64,128]{2,1,0:T(8,128)}, u32[]{:S(2)}) copy-start(f32[8,64,128]{2,1,0:T(8,128)} %get-tuple-element.53) | copy-start | bytes 786436
  54.1 5.2 %copy-start = (f32[256,1024]{1,0:T(8,128)S(1)}, f32[256,1024]{1,0:T(8,128)}, u32[]{:S(2)}) copy-start(f32[256,1024]{1,0:T(8,128)} %own.3) | copy-start | bytes 3145732
  54.1 11.8 %collective-permute-start.7 = (f32[2,128,1024]{2,1,0:T(8,128)}, f32[2,128,1024]{2,1,0:T(8,128)}, u32[]{:S(2)}, u32[]{:S(2)}) collective-permute-start(f32[2,128,1024]{2,1,0:T(8,128)} %shard_map.149.if0), channel_id=1, source_target_pairs={{0,8},{8,0},{1,9},{9,1},{2,10},{10,2},{3,11},{11,3},{4,12},{12,4},... | collective-permute-start | bytes 3145736 | tf_op jit(solution)/shard_map/ppermute | solution.py:54
  54.1 1.0 copy-start.2
  58.2 13.0 %collective-permute-start.3 = (f32[256,1024]{1,0:T(8,128)}, f32[256,1024]{1,0:T(8,128)S(1)}, u32[]{:S(2)}, u32[]{:S(2)}) collective-permute-start(f32[256,1024]{1,0:T(8,128)} %shard_map.148.ic0), channel_id=1, source_target_pairs={{0,8},{8,0},{1,9},{9,1},{2,10},{10,2},{3,11},{11,3},{4,12},{12,4},... | collective-permute-start | bytes 3145736 | tf_op jit(solution)/shard_map/ppermute | solution.py:54
  58.7 5.8 %collective-permute-start.4 = (f32[8,64,128]{2,1,0:T(8,128)S(1)}, f32[8,64,128]{2,1,0:T(8,128)S(1)}, u32[]{:S(2)}, u32[]{:S(2)}) collective-permute-start(f32[8,64,128]{2,1,0:T(8,128)S(1)} %copy-done.27), channel_id=1, source_target_pairs={{0,8},{8,0},{1,9},{9,1},{2,10},{10,2},{3,11},{11,3},{4,12},{12,4},... | collective-permute-start | bytes 786440 | tf_op jit(solution)/shard_map/ppermute | solution.py:54
  58.8 12.4 %collective-permute-start = (f32[8,64,256]{2,1,0:T(8,128)}, f32[8,64,256]{2,1,0:T(8,128)S(1)}, u32[]{:S(2)}, u32[]{:S(2)}) collective-permute-start(f32[8,64,256]{2,1,0:T(8,128)} %get-tuple-element.51), channel_id=1, source_target_pairs={{0,8},{8,0},{1,9},{9,1},{2,10},{10,2},{3,11},{11,3},{4,12},{12,4},... | collective-permute-start | bytes 1572872 | tf_op jit(solution)/shard_map/ppermute | solution.py:54
  60.1 27.3 %collective-permute-start.1 = (f32[128,1024]{1,0:T(8,128)}, f32[128,1024]{1,0:T(8,128)S(1)}, u32[]{:S(2)}, u32[]{:S(2)}) collective-permute-start(f32[128,1024]{1,0:T(8,128)} %get-tuple-element.96), channel_id=1, source_target_pairs={{0,1},{1,2},{2,3},{3,4},{4,5},{5,6},{6,7},{7,8},{8,9},{9,10},{10,1... | collective-permute-start | bytes 1572872 | tf_op jit(solution)/shard_map/ppermute | solution.py:60
  64.6 1.3 copy-start.28
  64.6 22.9 %collective-permute-start.2 = (f32[128,1024]{1,0:T(8,128)S(1)}, f32[128,1024]{1,0:T(8,128)S(1)}, u32[]{:S(2)}, u32[]{:S(2)}) collective-permute-start(f32[128,1024]{1,0:T(8,128)S(1)} %get-tuple-element.95), channel_id=1, source_target_pairs={{1,0},{2,1},{3,2},{4,3},{5,4},{6,5},{7,6},{8,7},{9,8},{10,9},{11,1... | collective-permute-start | bytes 1572872 | tf_op jit(solution)/shard_map/ppermute | solution.py:60
  71.2 0.8 copy-start.10
  71.2 1.1 copy-start.5
  87.4 0.8 copy-start.12
  87.4 1.0 copy-start.15
  88.4 6.0 %copy-start.9 = (f32[3,8,32,256]{3,2,1,0:T(8,128)S(1)}, f32[3,8,32,256]{3,2,1,0:T(8,128)}, u32[]{:S(2)}) copy-start(f32[3,8,32,256]{3,2,1,0:T(8,128)} %get-tuple-element.81) | copy-start | bytes 2359300
  94.4 7.4 %collective-permute-start.8 = (f32[2,256,1024]{2,1,0:T(8,128)}, f32[2,256,1024]{2,1,0:T(8,128)}, u32[]{:S(2)}, u32[]{:S(2)}) collective-permute-start(f32[2,256,1024]{2,1,0:T(8,128)} %shard_map.152.is0), channel_id=1, source_target_pairs={{0,8},{8,0},{1,9},{9,1},{2,10},{10,2},{3,11},{11,3},{4,12},{12,4},... | collective-permute-start | bytes 6291464 | tf_op jit(solution)/shard_map/ppermute | solution.py:54
  94.4 23.1 %collective-permute-start.21 = (f32[3,8,32,256]{3,2,1,0:T(8,128)S(1)}, f32[3,8,32,256]{3,2,1,0:T(8,128)}, u32[]{:S(2)}, u32[]{:S(2)}) collective-permute-start(f32[3,8,32,256]{3,2,1,0:T(8,128)S(1)} %copy-done.9), channel_id=1, source_target_pairs={{0,2},{2,4},{4,6},{6,0},{1,3},{3,5},{5,7},{7,1},{8,10},{10,12},{12... | collective-permute-start | bytes 2359304 | tf_op jit(solution)/shard_map/ppermute | solution.py:54
  98.0 37.9 %collective-permute-start.22 = (f32[3,8,32,256]{3,2,1,0:T(8,128)}, f32[3,8,32,256]{3,2,1,0:T(8,128)}, u32[]{:S(2)}, u32[]{:S(2)}) collective-permute-start(f32[3,8,32,256]{3,2,1,0:T(8,128)} %get-tuple-element.82), channel_id=1, source_target_pairs={{0,4},{2,6},{4,0},{6,2},{1,5},{3,7},{5,1},{7,3},{8,12},{10,14},{12... | collective-permute-start | bytes 2359304 | tf_op jit(solution)/shard_map/ppermute | solution.py:54
  100.5 39.0 %copy-start.6 = (f32[3,2,32,1024]{3,2,1,0:T(8,128)S(1)}, f32[3,2,32,1024]{3,2,1,0:T(8,128)}, u32[]{:S(2)}) copy-start(f32[3,2,32,1024]{3,2,1,0:T(8,128)} %get-tuple-element.73) | copy-start | bytes 2359300
  100.5 44.7 %copy-start.7 = (f32[3,2,32,1024]{3,2,1,0:T(8,128)S(1)}, f32[3,2,32,1024]{3,2,1,0:T(8,128)}, u32[]{:S(2)}) copy-start(f32[3,2,32,1024]{3,2,1,0:T(8,128)} %get-tuple-element.74) | copy-start | bytes 2359300
  100.5 60.8 %copy-start.8 = (f32[3,2,32,1024]{3,2,1,0:T(8,128)S(1)}, f32[3,2,32,1024]{3,2,1,0:T(8,128)}, u32[]{:S(2)}) copy-start(f32[3,2,32,1024]{3,2,1,0:T(8,128)} %get-tuple-element.75) | copy-start | bytes 2359300
  100.5 39.0 %collective-permute-start.23 = (f32[3,8,32,256]{3,2,1,0:T(8,128)}, f32[3,8,32,256]{3,2,1,0:T(8,128)}, u32[]{:S(2)}, u32[]{:S(2)}) collective-permute-start(f32[3,8,32,256]{3,2,1,0:T(8,128)} %get-tuple-element.83), channel_id=1, source_target_pairs={{0,6},{2,0},{4,2},{6,4},{1,7},{3,1},{5,3},{7,5},{8,14},{10,8},{12,... | collective-permute-start | bytes 2359304 | tf_op jit(solution)/shard_map/ppermute | solution.py:54
  109.2 36.0 %collective-permute-start.12 = (f32[2,8,32,256]{3,2,1,0:T(8,128)}, f32[2,8,32,256]{3,2,1,0:T(8,128)S(1)}, u32[]{:S(2)}, u32[]{:S(2)}) collective-permute-start(f32[2,8,32,256]{3,2,1,0:T(8,128)} %get-tuple-element.68), channel_id=1, source_target_pairs={{0,2},{2,4},{4,6},{6,0},{1,3},{3,5},{5,7},{7,1},{8,10},{10,12},{12... | collective-permute-start | bytes 1572872 | tf_op jit(solution)/shard_map/ppermute | solution.py:54
  110.0 51.3 %collective-permute-start.13 = (f32[2,8,32,256]{3,2,1,0:T(8,128)}, f32[2,8,32,256]{3,2,1,0:T(8,128)S(1)}, u32[]{:S(2)}, u32[]{:S(2)}) collective-permute-start(f32[2,8,32,256]{3,2,1,0:T(8,128)} %get-tuple-element.69), channel_id=1, source_target_pairs={{0,4},{2,6},{4,0},{6,2},{1,5},{3,7},{5,1},{7,3},{8,12},{10,14},{12... | collective-permute-start | bytes 1572872 | tf_op jit(solution)/shard_map/ppermute | solution.py:54
  117.5 45.2 %collective-permute-start.14 = (f32[2,8,32,256]{3,2,1,0:T(8,128)}, f32[2,8,32,256]{3,2,1,0:T(8,128)S(1)}, u32[]{:S(2)}, u32[]{:S(2)}) collective-permute-start(f32[2,8,32,256]{3,2,1,0:T(8,128)} %get-tuple-element.70), channel_id=1, source_target_pairs={{0,6},{2,0},{4,2},{6,4},{1,7},{3,1},{5,3},{7,5},{8,14},{10,8},{12,... | collective-permute-start | bytes 1572872 | tf_op jit(solution)/shard_map/ppermute | solution.py:54
  135.9 26.9 %collective-permute-start.10 = (f32[2,2,32,1024]{3,2,1,0:T(8,128)}, f32[2,2,32,1024]{3,2,1,0:T(8,128)S(1)}, u32[]{:S(2)}, u32[]{:S(2)}) collective-permute-start(f32[2,2,32,1024]{3,2,1,0:T(8,128)} %get-tuple-element.65), channel_id=1, source_target_pairs={{0,32},{16,48},{32,0},{48,16},{1,33},{17,49},{33,1},{49,17},{2,34}... | collective-permute-start | bytes 1572872 | tf_op jit(solution)/shard_map/ppermute | solution.py:54
  139.5 80.5 %collective-permute-start.15 = (f32[3,2,32,1024]{3,2,1,0:T(8,128)S(1)}, f32[3,2,32,1024]{3,2,1,0:T(8,128)}, u32[]{:S(2)}, u32[]{:S(2)}) collective-permute-start(f32[3,2,32,1024]{3,2,1,0:T(8,128)S(1)} %copy-done.6), channel_id=1, source_target_pairs={{0,16},{16,32},{32,48},{48,0},{1,17},{17,33},{33,49},{49,1},{2,18}... | collective-permute-start | bytes 2359304 | tf_op jit(solution)/shard_map/ppermute | solution.py:54
  145.2 19.6 %copy-start.13 = (f32[2,8,32,256]{3,2,1,0:T(8,128)}, f32[2,8,32,256]{3,2,1,0:T(8,128)S(1)}, u32[]{:S(2)}) copy-start(f32[2,8,32,256]{3,2,1,0:T(8,128)S(1)} %collective-permute-done.12.a1) | copy-start | bytes 1572868
  145.2 76.7 %collective-permute-start.16 = (f32[3,2,32,1024]{3,2,1,0:T(8,128)S(1)}, f32[3,2,32,1024]{3,2,1,0:T(8,128)}, u32[]{:S(2)}, u32[]{:S(2)}) collective-permute-start(f32[3,2,32,1024]{3,2,1,0:T(8,128)S(1)} %copy-done.7), channel_id=1, source_target_pairs={{0,32},{16,48},{32,0},{48,16},{1,33},{17,49},{33,1},{49,17},{2,34}... | collective-permute-start | bytes 2359304 | tf_op jit(solution)/shard_map/ppermute | solution.py:54
  161.3 1.5 copy-start.14
  161.3 60.6 %collective-permute-start.17 = (f32[3,2,32,1024]{3,2,1,0:T(8,128)S(1)}, f32[3,2,32,1024]{3,2,1,0:T(8,128)}, u32[]{:S(2)}, u32[]{:S(2)}) collective-permute-start(f32[3,2,32,1024]{3,2,1,0:T(8,128)S(1)} %copy-done.8), channel_id=1, source_target_pairs={{0,48},{16,0},{32,16},{48,32},{1,49},{17,1},{33,17},{49,33},{2,50}... | collective-permute-start | bytes 2359304 | tf_op jit(solution)/shard_map/ppermute | solution.py:54
  162.7 2.1 copy-start.16
  162.7 45.7 %collective-permute-start.11 = (f32[2,2,32,1024]{3,2,1,0:T(8,128)}, f32[2,2,32,1024]{3,2,1,0:T(8,128)}, u32[]{:S(2)}, u32[]{:S(2)}) collective-permute-start(f32[2,2,32,1024]{3,2,1,0:T(8,128)} %get-tuple-element.66), channel_id=1, source_target_pairs={{0,48},{16,0},{32,16},{48,32},{1,49},{17,1},{33,17},{49,33},{2,50}... | collective-permute-start | bytes 1572872 | tf_op jit(solution)/shard_map/ppermute | solution.py:54
  162.8 13.2 %copy-start.11 = (f32[2,2,32,1024]{3,2,1,0:T(8,128)}, f32[2,2,32,1024]{3,2,1,0:T(8,128)S(1)}, u32[]{:S(2)}) copy-start(f32[2,2,32,1024]{3,2,1,0:T(8,128)S(1)} %collective-permute-done.10.a2) | copy-start | bytes 1572868
  162.8 46.7 %collective-permute-start.9 = (f32[2,2,32,1024]{3,2,1,0:T(8,128)}, f32[2,2,32,1024]{3,2,1,0:T(8,128)}, u32[]{:S(2)}, u32[]{:S(2)}) collective-permute-start(f32[2,2,32,1024]{3,2,1,0:T(8,128)} %get-tuple-element.64), channel_id=1, source_target_pairs={{0,16},{16,32},{32,48},{48,0},{1,17},{17,33},{33,49},{49,1},{2,18}... | collective-permute-start | bytes 1572872 | tf_op jit(solution)/shard_map/ppermute | solution.py:54
  167.2 46.2 %all-to-all-start.2 = ((f32[16,2,32,128]{3,2,1,0:T(8,128)}), f32[16,2,32,128]{3,2,1,0:T(8,128)S(1)}, u32[]{:S(2)}, u32[]{:S(2)}) async-start(f32[16,2,32,128]{3,2,1,0:T(8,128)} %shard_map.155), calls=%async_computation.2 | async-start | bytes 1048576 | tf_op jit(solution)/shard_map/all_to_all | solution.py:275
  208.4 21.1 %collective-permute-start.24 = (f32[3,2,32,256]{3,2,1,0:T(8,128)}, f32[3,2,32,256]{3,2,1,0:T(8,128)}, u32[]{:S(2)}, u32[]{:S(2)}) collective-permute-start(f32[3,2,32,256]{3,2,1,0:T(8,128)} %get-tuple-element.85), channel_id=1, source_target_pairs={{0,16},{16,32},{32,48},{48,0},{1,17},{17,33},{33,49},{49,1},{2,18}... | collective-permute-start | bytes 589832 | tf_op jit(solution)/shard_map/ppermute | solution.py:54
  213.4 11.5 %copy-start.3 = (f32[16,2,32,128]{3,2,1,0:T(8,128)}, f32[16,2,32,128]{3,2,1,0:T(8,128)S(1)}, u32[]{:S(2)}) copy-start(f32[16,2,32,128]{3,2,1,0:T(8,128)S(1)} %all-to-all-done.2.low) | copy-start | bytes 1572868
  213.4 38.5 %all-to-all-start.1 = ((f32[16,2,32,128]{3,2,1,0:T(8,128)}), f32[16,2,32,128]{3,2,1,0:T(8,128)S(1)}, u32[]{:S(2)}, u32[]{:S(2)}) async-start(f32[16,2,32,128]{3,2,1,0:T(8,128)} %shard_map.154), calls=%async_computation.1 | async-start | bytes 1048576 | tf_op jit(solution)/shard_map/all_to_all | solution.py:275
  217.4 13.6 %collective-permute-start.25 = (f32[3,2,32,256]{3,2,1,0:T(8,128)}, f32[3,2,32,256]{3,2,1,0:T(8,128)S(1)}, u32[]{:S(2)}, u32[]{:S(2)}) collective-permute-start(f32[3,2,32,256]{3,2,1,0:T(8,128)} %get-tuple-element.86), channel_id=1, source_target_pairs={{0,32},{16,48},{32,0},{48,16},{1,33},{17,49},{33,1},{49,17},{2,34}... | collective-permute-start | bytes 589832 | tf_op jit(solution)/shard_map/ppermute | solution.py:54
  219.9 11.0 %collective-permute-start.26 = (f32[3,2,32,256]{3,2,1,0:T(8,128)}, f32[3,2,32,256]{3,2,1,0:T(8,128)S(1)}, u32[]{:S(2)}, u32[]{:S(2)}) collective-permute-start(f32[3,2,32,256]{3,2,1,0:T(8,128)} %get-tuple-element.87), channel_id=1, source_target_pairs={{0,48},{16,0},{32,16},{48,32},{1,49},{17,1},{33,17},{49,33},{2,50}... | collective-permute-start | bytes 589832 | tf_op jit(solution)/shard_map/ppermute | solution.py:54
  225.0 8.5 %collective-permute-start.18 = (f32[3,2,32,256]{3,2,1,0:T(8,128)}, f32[3,2,32,256]{3,2,1,0:T(8,128)S(1)}, u32[]{:S(2)}, u32[]{:S(2)}) collective-permute-start(f32[3,2,32,256]{3,2,1,0:T(8,128)} %get-tuple-element.77), channel_id=1, source_target_pairs={{0,2},{2,4},{4,6},{6,0},{1,3},{3,5},{5,7},{7,1},{8,10},{10,12},{12... | collective-permute-start | bytes 589832 | tf_op jit(solution)/shard_map/ppermute | solution.py:54
  226.8 10.8 %collective-permute-start.19 = (f32[3,2,32,256]{3,2,1,0:T(8,128)}, f32[3,2,32,256]{3,2,1,0:T(8,128)S(1)}, u32[]{:S(2)}, u32[]{:S(2)}) collective-permute-start(f32[3,2,32,256]{3,2,1,0:T(8,128)} %get-tuple-element.78), channel_id=1, source_target_pairs={{0,4},{2,6},{4,0},{6,2},{1,5},{3,7},{5,1},{7,3},{8,12},{10,14},{12... | collective-permute-start | bytes 589832 | tf_op jit(solution)/shard_map/ppermute | solution.py:54
  229.5 8.1 %collective-permute-start.20 = (f32[3,2,32,256]{3,2,1,0:T(8,128)}, f32[3,2,32,256]{3,2,1,0:T(8,128)S(1)}, u32[]{:S(2)}, u32[]{:S(2)}) collective-permute-start(f32[3,2,32,256]{3,2,1,0:T(8,128)} %get-tuple-element.79), channel_id=1, source_target_pairs={{0,6},{2,0},{4,2},{6,4},{1,7},{3,1},{5,3},{7,5},{8,14},{10,8},{12,... | collective-permute-start | bytes 589832 | tf_op jit(solution)/shard_map/ppermute | solution.py:54
  231.0 6.6 %copy-start.19 = (f32[3,2,32,256]{3,2,1,0:T(8,128)}, f32[3,2,32,256]{3,2,1,0:T(8,128)S(1)}, u32[]{:S(2)}) copy-start(f32[3,2,32,256]{3,2,1,0:T(8,128)S(1)} %collective-permute-done.25.y2) | copy-start | bytes 589828
  231.0 6.6 %copy-start.20 = (f32[3,2,32,256]{3,2,1,0:T(8,128)}, f32[3,2,32,256]{3,2,1,0:T(8,128)S(1)}, u32[]{:S(2)}) copy-start(f32[3,2,32,256]{3,2,1,0:T(8,128)S(1)} %collective-permute-done.26.y3) | copy-start | bytes 589828
  233.4 4.2 %copy-start.21 = (f32[3,2,32,256]{3,2,1,0:T(8,128)}, f32[3,2,32,256]{3,2,1,0:T(8,128)S(1)}, u32[]{:S(2)}) copy-start(f32[3,2,32,256]{3,2,1,0:T(8,128)S(1)} %collective-permute-done.18.x1) | copy-start | bytes 589828
  237.6 0.7 copy-start.22
  237.6 0.8 copy-start.23
  240.7 6.1 %collective-permute-start.27 = (f32[3,64,128]{2,1,0:T(8,128)}, f32[3,64,128]{2,1,0:T(8,128)S(1)}, u32[]{:S(2)}, u32[]{:S(2)}) collective-permute-start(f32[3,64,128]{2,1,0:T(8,128)} %get-tuple-element.89), channel_id=1, source_target_pairs={{0,1},{1,64},{64,65},{65,0},{2,3},{3,66},{66,67},{67,2},{4,5},{5,6... | collective-permute-start | bytes 294920 | tf_op jit(solution)/shard_map/ppermute | solution.py:54
  242.1 6.5 %collective-permute-start.28 = (f32[3,64,128]{2,1,0:T(8,128)}, f32[3,64,128]{2,1,0:T(8,128)S(1)}, u32[]{:S(2)}, u32[]{:S(2)}) collective-permute-start(f32[3,64,128]{2,1,0:T(8,128)} %get-tuple-element.90), channel_id=1, source_target_pairs={{0,64},{1,65},{64,0},{65,1},{2,66},{3,67},{66,2},{67,3},{4,68},{5,... | collective-permute-start | bytes 294920 | tf_op jit(solution)/shard_map/ppermute | solution.py:54
  244.8 4.8 %collective-permute-start.29 = (f32[3,64,128]{2,1,0:T(8,128)}, f32[3,64,128]{2,1,0:T(8,128)S(1)}, u32[]{:S(2)}, u32[]{:S(2)}) collective-permute-start(f32[3,64,128]{2,1,0:T(8,128)} %get-tuple-element.91), channel_id=1, source_target_pairs={{0,65},{1,0},{64,1},{65,64},{2,67},{3,2},{66,3},{67,66},{4,69},{5,... | collective-permute-start | bytes 294920 | tf_op jit(solution)/shard_map/ppermute | solution.py:54
  246.8 2.9 %copy-start.24 = (f32[3,64,128]{2,1,0:T(8,128)}, f32[3,64,128]{2,1,0:T(8,128)S(1)}, u32[]{:S(2)}) copy-start(f32[3,64,128]{2,1,0:T(8,128)S(1)} %collective-permute-done.27.a1) | copy-start | bytes 294916
  248.7 1.0 copy-start.25
  249.6 0.6 copy-start.26
  252.0 0.8 copy-start.4

commit v7 on v3

--- a/solution.py
+++ b/solution.py
@@ -162,14 +162,14 @@
 
 
 def wet_product_kernel(place, ls0, ls1, ic0, ic1, *rest):
-    outs, (sh, sl, held) = rest[:8], rest[8:]
+    outs, (sh, sl, held) = rest[8:16], rest[16:]
     sh[...], sl[...] = parts(joined(ls0, ls1))
     multiply(held, (sh, sl), ic0[...], ic1[...])
     send_off(place, held, outs)
 
 
 def second_kernel(place, ls0, ls1, is0, is1, *rest):
-    outs, (sh, sl, held) = rest[8:16], rest[16:]
+    outs, (sh, sl, held) = rest[:8], rest[8:]
 
     @pl.when(pl.program_id(0) == 0)
     def _():
@@ -327,8 +327,11 @@
     def block(rows):
         return pl.BlockSpec((1, rows, R), lambda m: (m, 0, 0))
 
+    fluid = partial_sums(
+        fluid_product_kernel, 2, 0, 3, place, (own_f, left_f), 256, (image_f, other_f), [block(128)] * 2
+    )
     first = partial_sums(
-        fluid_product_kernel, 2, 0, 2, place, (own_f, left_f), 256, (image_f, other_f), [block(128)] * 2
+        wet_product_kernel, 1, 2, 3, place, (own_s, left_s), 512, (image_c, other_c), [VMEM] * 2, fluid
     )
     first_x = exchanged(first[0:4], X)
     first_y = exchanged(first[4:8], Y)
@@ -345,10 +348,7 @@
     )(struct_cols, stiff_tiles, mass_tiles, below_s, struct_basis, above_s, first[0])
     other_s = shifted(image_s, "core", 1)
 
-    wet = partial_sums(wet_product_kernel, 1, 2, 3, place, (own_s, left_s), 512, (image_c, other_c), [VMEM] * 2)
-    second = partial_sums(
-        second_kernel, 2, 0, 3, place, (own_s, left_s), 512, (image_s, other_s), [block(256)] * 2, wet
-    )
+    second = partial_sums(second_kernel, 2, 0, 2, place, (own_s, left_s), 512, (image_s, other_s), [block(256)] * 2)
     second_x = exchanged(second[0:4], X)
     second_y = exchanged(second[4:8], Y)
 
@@ -357,7 +357,7 @@
     second_xy = exchanged(split(place, second_x, 1), Y)
     second_yx = exchanged(split(place, second_y, 0), X)
     summed = exchanged(spread(place, *first_xy, *first_yx, *second_xy, *second_yx), Z)
-    fstiff, fmass, stiff, mass, wet = call(last_kernel, [shape(64, 128)] * 5, 4, flops=2**18, moved=2**20)(*summed)
+    fstiff, fmass, wet, stiff, mass = call(last_kernel, [shape(64, 128)] * 5, 4, flops=2**18, moved=2**20)(*summed)
     return stiff, mass, fstiff, fmass, wet
 
 

time: 220 us -> 220 us (level)
  starting transfers between devices: 79 us -> 61.2 us
  waiting for transfers between devices: 79 us -> 93.8 us
  local copies, waits for them, and re-layouts: 6.77 us -> 9.69 us
    ppermute x32, starting transfers between devices: 54.6 us -> 40 us  [shifted(): lax.ppermute(value, axis, [(i, (i + by) % size) for i in range(size)])]
    ppermute x4, waiting for transfers between devices: 25 us -> 36.3 us  [from_behind(): return lax.ppermute(value, AXES, pairs)]
    ppermute x32, waiting for transfers between devices: 54.1 us -> 57.5 us  [shifted(): lax.ppermute(value, axis, [(i, (i + by) % size) for i in range(size)])]
    ppermute x4, starting transfers between devices: 12.8 us -> 10 us  [from_behind(): return lax.ppermute(value, AXES, pairs)]
    unnamed x72 -> x84, local copies, waits for them, and re-layouts: 6.7 us -> 8.79 us
  transfers between devices with their start and end apart: 37 -> 37, of which waited for: 17 -> 16; matrix products, arithmetic and copies ran while one was open for 0% -> 1% of each run, Pallas kernels for 20% -> 18%
where the time goes in v7:
time: 220 us; the launch traced here: 219 us
  waiting for transfers between devices  93.8 us (43%)
  starting transfers between devices  61.2 us (28%)
  Pallas kernels  52.7 us (24%)
  local copies, waits for them, and re-layouts  9.69 us (4%)
    ppermute x32, waiting for transfers between devices, shifted(): lax.ppermute(value, axis, [(i, (i + by) % size) for i in range(size)])  57.5 us
    ppermute x32, starting transfers between devices, shifted(): lax.ppermute(value, axis, [(i, (i + by) % size) for i in range(size)])  40 us
    ppermute x4, waiting for transfers between devices, from_behind(): return lax.ppermute(value, AXES, pairs)  36.3 us
    pallas_call x3, Pallas kernels, partial_sums(): return run(place, *lefts, *operands, *carried)  17.9 us
    all_to_all x1, starting transfers between devices, compute(): lax.all_to_all(outgoing, AXES, split_axis=0, concat_axis=0, tiled=True)  11.2 us
    pallas_call x4, Pallas kernels, split(): call(functools.partial(split_kernel, axis), [shape(count, 2, HALF, 256)]...  11.2 us
    ppermute x4, starting transfers between devices, from_behind(): return lax.ppermute(value, AXES, pairs)  10 us
    unnamed x84, local copies, waits for them, and re-layouts  8.79 us
  transfers between devices with their start and end apart: 37, of which 16 were waited for; matrix products, arithmetic and copies ran while one was open for 1% of the time, Pallas kernels for 18%

profile of v7, /device:TPU:0, one launch (start us, length us, event | category | flops | bytes accessed | tf_op | source)
XLA Modules:
  0.0 219.0 jit_solution(13143004734027115096)
XLA Ops:
  0.6 2.9 %shard_map.147 = f32[128,2,1024]{2,1,0:T(2,128)} custom-call(s32[1,128]{1,0:T(1,128)} %bitcast.6, s32[1,128]{1,0:T(1,128)} %bitcast.7, f32[128,1024]{1,0:T(8,128)} %own.2), custom_call_target="tpu_custom_call" | custom-call | flops 201326592 | bytes 2097152 | tf_op jit(solution)/shard_map/pallas_call | solution.py:295
  3.6 11.2 %all-to-all-start = ((f32[128,2,1024]{2,1,0:T(2,128)}), f32[128,2,1024]{2,1,0:T(2,128)S(1)}, u32[]{:S(2)}, u32[]{:S(2)}) async-start(f32[128,2,1024]{2,1,0:T(2,128)} %shard_map.147), calls=%async_computation | async-start | bytes 2097152 | tf_op jit(solution)/shard_map/all_to_all | solution.py:298
  14.8 3.0 %collective-permute-start.3 = (f32[128,1024]{1,0:T(8,128)S(1)}, f32[128,1024]{1,0:T(8,128)S(1)}, u32[]{:S(2)}, u32[]{:S(2)}) collective-permute-start(f32[128,1024]{1,0:T(8,128)S(1)} %copy-done.1), channel_id=1, source_target_pairs={{0,1},{1,2},{2,3},{3,4},{4,5},{5,6},{6,7},{7,8},{8,9},{9,10},{10,1... | collective-permute-start | bytes 1572872 | tf_op jit(solution)/shard_map/ppermute | solution.py:59
  17.8 1.3 collective-permute-start.4
  19.1 0.6 pad_add_fusion.place
  19.7 2.9 %shard_map.146 = (f32[8,64,256]{2,1,0:T(8,128)}, f32[8,64,256]{2,1,0:T(8,128)}, f32[8,64,128]{2,1,0:T(8,128)}, f32[8,64,128]{2,1,0:T(8,128)}) custom-call(s32[4]{0:T(128)} %pad_add_fusion.place, f32[256,1024]{1,0:T(8,128)} %own.3, f32[128,1024]{1,0:T(8,128)} %own.2), custom_call_target="tpu_custom_call" | custom-call | flops 1048576 | bytes 3145728 | tf_op jit(solution)/shard_map/pallas_call | solution.py:300
  22.6 26.5 %collective-permute-done.3.lo = f32[128,1024]{1,0:T(8,128)S(1)} collective-permute-done((f32[128,1024]{1,0:T(8,128)S(1)}, f32[128,1024]{1,0:T(8,128)S(1)}, u32[]{:S(2)}, u32[]{:S(2)}) %collective-permute-start.3) | collective-permute-done | bytes 524320 | tf_op jit(solution)/shard_map/ppermute | solution.py:59
  49.1 0.8 copy-done.20
  50.1 4.0 %shard_map.149.if0 = f32[2,128,1024]{2,1,0:T(8,128)} custom-call(s32[1,4]{1,0:T(1,128)} %cols.2, f32[1,4,128,128]{3,2,1,0:T(8,128)} %stiff.2, f32[1,4,128,128]{3,2,1,0:T(8,128)} %mass.2, f32[128,1024]{1,0:T(8,128)} %copy-done.20, f32[128,1024]{1,0:T(8,128)} %own.2, f32[128,1024]{1,0:T(8,128)} %copy-done.21, f32[8,64,256]{2,1,0:T(8,128)} %get-tuple-element.58.after.ls0), custom_call_target="tpu_custom_call" | custom-call | flops 603979776 | bytes 3145728 | tf_op jit(solution)/shard_map/pallas_call | solution.py:315
  54.1 1.0 copy-done.2
  55.1 3.1 %shard_map.148.ic0 = f32[256,1024]{1,0:T(8,128)} custom-call(f32[256,256]{1,0:T(8,128)} %coupling.1, f32[128,2,1024]{2,1,0:T(2,128)} %copy-done.2), custom_call_target="tpu_custom_call" | custom-call | flops 402653184 | bytes 2097152 | tf_op jit(solution)/shard_map/pallas_call | solution.py:312
  59.2 0.9 fusion
  60.1 4.4 %collective-permute-start.18 = (f32[128,1024]{1,0:T(8,128)}, f32[128,1024]{1,0:T(8,128)S(1)}, u32[]{:S(2)}, u32[]{:S(2)}) collective-permute-start(f32[128,1024]{1,0:T(8,128)} %get-tuple-element.112), channel_id=1, source_target_pairs={{0,1},{1,2},{2,3},{3,4},{4,5},{5,6},{6,7},{7,8},{8,9},{9,10},{10,1... | collective-permute-start | bytes 1572872 | tf_op jit(solution)/shard_map/ppermute | solution.py:59
  64.5 1.3 collective-permute-start.19
  65.8 5.3 %shard_map.150 = (f32[3,2,32,1024]{3,2,1,0:T(8,128)}, f32[3,2,32,1024]{3,2,1,0:T(8,128)}, f32[3,2,32,1024]{3,2,1,0:T(8,128)}, f32[3,2,32,1024]{3,2,1,0:T(8,128)}...) custom-call(s32[4]{0:T(128)} %pad_add_fusion.place, ...), custom_call_target="tpu_custom_call" | custom-call | flops 1610612736 | bytes 8388608 | tf_op jit(solution)/shard_map/pallas_call | solution.py:271
  71.2 0.8 copy-done.11
  72.3 5.2 %shard_map.151 = (f32[3,2,32,1024]{3,2,1,0:T(8,128)}, f32[3,2,32,1024]{3,2,1,0:T(8,128)}, f32[3,2,32,1024]{3,2,1,0:T(8,128)}, f32[3,2,32,1024]{3,2,1,0:T(8,128)}...) custom-call(s32[4]{0:T(128)} %pad_add_fusion.place, ...), custom_call_target="tpu_custom_call", output_to_operand_aliasing={{0}: (5, {}), {1}: (6, {}), {2}: (7, {}), {3}: (8, {}), {4}... | custom-call | flops 1610612736 | bytes 4194304 | tf_op jit(solution)/shard_map/pallas_call | solution.py:271
  77.5 9.9 %collective-permute-done.18.lo = f32[128,1024]{1,0:T(8,128)S(1)} collective-permute-done((f32[128,1024]{1,0:T(8,128)}, f32[128,1024]{1,0:T(8,128)S(1)}, u32[]{:S(2)}, u32[]{:S(2)}) %collective-permute-start.18) | collective-permute-done | bytes 524320 | tf_op jit(solution)/shard_map/ppermute | solution.py:59
  87.4 0.8 copy-done.18
  88.2 0.8 copy-done.19
  89.0 6.1 %shard_map.154.is0 = f32[2,256,1024]{2,1,0:T(8,128)} custom-call(s32[2,4]{1,0:T(2,128)} %cols.3, f32[2,4,128,128]{3,2,1,0:T(8,128)} %stiff.3, f32[2,4,128,128]{3,2,1,0:T(8,128)} %mass.3, f32[128,1024]{1,0:T(8,128)} %copy-done.18, f32[256,1024]{1,0:T(8,128)} %own.3, f32[128,1024]{1,0:T(8,128)} %copy-done.19, f32[3,2,32,1024]{3,2,1,0:T(8,128)} %get-tuple-element.70.a0.after), custom_call_target="tpu_custom_call" | custom-call | flops 1610612736 | bytes 5242880 | tf_op jit(solution)/shard_map/pallas_call | solution.py:339
  95.1 4.8 %collective-permute-start.6 = (f32[3,2,32,1024]{3,2,1,0:T(8,128)S(1)}, f32[3,2,32,1024]{3,2,1,0:T(8,128)S(1)}, u32[]{:S(2)}, u32[]{:S(2)}) collective-permute-start(f32[3,2,32,1024]{3,2,1,0:T(8,128)S(1)} %copy-done.4), channel_id=1, source_target_pairs={{0,16},{16,32},{32,48},{48,0},{1,17},{17,33},{33,49},{49,1},{2,18}... | collective-permute-start | bytes 2359304 | tf_op jit(solution)/shard_map/ppermute | solution.py:53
  99.9 2.3 %collective-permute-start.7 = (f32[3,2,32,1024]{3,2,1,0:T(8,128)S(1)}, f32[3,2,32,1024]{3,2,1,0:T(8,128)}, u32[]{:S(2)}, u32[]{:S(2)}) collective-permute-start(f32[3,2,32,1024]{3,2,1,0:T(8,128)S(1)} %copy-done.5), channel_id=1, source_target_pairs={{0,32},{16,48},{32,0},{48,16},{1,33},{17,49},{33,1},{49,17},{2,34}... | collective-permute-start | bytes 2359304 | tf_op jit(solution)/shard_map/ppermute | solution.py:53
  102.2 1.8 collective-permute-start.8
  104.1 14.8 %collective-permute-done.6.a1 = f32[3,2,32,1024]{3,2,1,0:T(8,128)S(1)} collective-permute-done((f32[3,2,32,1024]{3,2,1,0:T(8,128)S(1)}, f32[3,2,32,1024]{3,2,1,0:T(8,128)S(1)}, u32[]{:S(2)}, u32[]{:S(2)}) %collective-permute-start.6) | collective-permute-done | bytes 786464 | tf_op jit(solution)/shard_map/ppermute | solution.py:53
  118.9 1.6 collective-permute-start.13
  120.5 1.3 copy-done.37
  121.8 1.5 collective-permute-start.14
  123.3 7.4 %shard_map.155 = (f32[2,2,32,1024]{3,2,1,0:T(8,128)}, f32[2,2,32,1024]{3,2,1,0:T(8,128)}, f32[2,2,32,1024]{3,2,1,0:T(8,128)}, f32[2,2,32,1024]{3,2,1,0:T(8,128)}...) custom-call(s32[4]{0:T(128)} %pad_add_fusion.place, ...), custom_call_target="tpu_custom_call" | custom-call | flops 3221225472 | bytes 8388608 | tf_op jit(solution)/shard_map/pallas_call | solution.py:271
  130.7 6.3 %collective-permute-done.7.a2 = f32[3,2,32,1024]{3,2,1,0:T(8,128)} collective-permute-done((f32[3,2,32,1024]{3,2,1,0:T(8,128)S(1)}, f32[3,2,32,1024]{3,2,1,0:T(8,128)}, u32[]{:S(2)}, u32[]{:S(2)}) %collective-permute-start.7) | collective-permute-done | bytes 786464 | tf_op jit(solution)/shard_map/ppermute | solution.py:53
  137.1 3.1 %shard_map.152 = (f32[3,2,32,256]{3,2,1,0:T(8,128)}, f32[3,2,32,256]{3,2,1,0:T(8,128)}, f32[3,2,32,256]{3,2,1,0:T(8,128)}, f32[3,2,32,256]{3,2,1,0:T(8,128)}) custom-call(s32[4]{0:T(128)} %pad_add_fusion.place, f32[3,2,32,1024]{3,2,1,0:T(8,128)} %get-tuple-element.70.a0.after, f32[3,2,32,1024]{3,2,1,0:T(8,128)} %copy-done.10, ...), custom_call_target="tpu_custom_call" | custom-call | flops 589824 | bytes 3932160 | tf_op jit(solution)/shard_map/pallas_call | solution.py:232
  140.1 1.2 collective-permute-done.12.a1
  141.3 1.0 collective-permute-start.10
  142.3 2.6 %collective-permute-start.22 = (f32[2,2,32,1024]{3,2,1,0:T(8,128)}, f32[2,2,32,1024]{3,2,1,0:T(8,128)S(1)}, u32[]{:S(2)}, u32[]{:S(2)}) collective-permute-start(f32[2,2,32,1024]{3,2,1,0:T(8,128)} %get-tuple-element.88), channel_id=1, source_target_pairs={{0,32},{16,48},{32,0},{48,16},{1,33},{17,49},{33,1},{49,17},{2,34}... | collective-permute-start | bytes 1572872 | tf_op jit(solution)/shard_map/ppermute | solution.py:53
  145.0 11.5 %collective-permute-done.14.a3 = f32[3,8,32,256]{3,2,1,0:T(8,128)} collective-permute-done((f32[3,8,32,256]{3,2,1,0:T(8,128)}, f32[3,8,32,256]{3,2,1,0:T(8,128)}, u32[]{:S(2)}, u32[]{:S(2)}) %collective-permute-start.14) | collective-permute-done | bytes 786464 | tf_op jit(solution)/shard_map/ppermute | solution.py:53
  156.4 1.7 collective-permute-start.23
  158.2 1.4 collective-permute-start.27
  159.6 0.7 copy-done.23
  160.3 2.7 %collective-permute-start.28 = (f32[2,8,32,256]{3,2,1,0:T(8,128)}, f32[2,8,32,256]{3,2,1,0:T(8,128)S(1)}, u32[]{:S(2)}, u32[]{:S(2)}) collective-permute-start(f32[2,8,32,256]{3,2,1,0:T(8,128)} %get-tuple-element.96), channel_id=1, source_target_pairs={{0,4},{2,6},{4,0},{6,2},{1,5},{3,7},{5,1},{7,3},{8,12},{10,14},{12... | collective-permute-start | bytes 1572872 | tf_op jit(solution)/shard_map/ppermute | solution.py:53
  163.1 1.1 collective-permute-start.29
  164.2 3.0 %shard_map.153 = (f32[3,2,32,256]{3,2,1,0:T(8,128)}, f32[3,2,32,256]{3,2,1,0:T(8,128)}, f32[3,2,32,256]{3,2,1,0:T(8,128)}, f32[3,2,32,256]{3,2,1,0:T(8,128)}) custom-call(s32[4]{0:T(128)} %pad_add_fusion.place, f32[3,8,32,256]{3,2,1,0:T(8,128)} %get-tuple-element.78.a0, f32[3,8,32,256]{3,2,1,0:T(8,128)} %collective-permute-done.12.a1, ...), custom_call_target="tpu_custom_call" | custom-call | flops 589824 | bytes 3932160 | tf_op jit(solution)/shard_map/pallas_call | solution.py:232
  167.5 1.3 collective-permute-done.23.a3
  168.8 1.1 collective-permute-start.15
  169.9 2.9 %collective-permute-done.27.a1 = f32[2,8,32,256]{3,2,1,0:T(8,128)S(1)} collective-permute-done((f32[2,8,32,256]{3,2,1,0:T(8,128)}, f32[2,8,32,256]{3,2,1,0:T(8,128)S(1)}, u32[]{:S(2)}, u32[]{:S(2)}) %collective-permute-start.27) | collective-permute-done | bytes 524320 | tf_op jit(solution)/shard_map/ppermute | solution.py:53
  172.9 1.0 collective-permute-start.16
  173.8 11.3 %collective-permute-done.28.a2 = f32[2,8,32,256]{3,2,1,0:T(8,128)S(1)} collective-permute-done((f32[2,8,32,256]{3,2,1,0:T(8,128)}, f32[2,8,32,256]{3,2,1,0:T(8,128)S(1)}, u32[]{:S(2)}, u32[]{:S(2)}) %collective-permute-start.28) | collective-permute-done | bytes 524320 | tf_op jit(solution)/shard_map/ppermute | solution.py:53
  185.1 0.7 collective-permute-start.17
  185.8 2.5 %shard_map.156 = (f32[2,2,32,256]{3,2,1,0:T(8,128)}, f32[2,2,32,256]{3,2,1,0:T(8,128)}, f32[2,2,32,256]{3,2,1,0:T(8,128)}, f32[2,2,32,256]{3,2,1,0:T(8,128)}) custom-call(s32[4]{0:T(128)} %pad_add_fusion.place, f32[2,2,32,1024]{3,2,1,0:T(8,128)} %get-tuple-element.86.a0, f32[2,2,32,1024]{3,2,1,0:T(8,128)} %copy-done.12, f32[2,2,32,1024]{3,2,1,0:T(8,128)} %copy-done.14, ...), custom_call_target="tpu_custom_call" | custom-call | flops 393216 | bytes 2621440 | tf_op jit(solution)/shard_map/pallas_call | solution.py:232
  188.5 0.7 copy-done.17
  189.2 2.5 %shard_map.157 = (f32[2,2,32,256]{3,2,1,0:T(8,128)}, f32[2,2,32,256]{3,2,1,0:T(8,128)}, f32[2,2,32,256]{3,2,1,0:T(8,128)}, f32[2,2,32,256]{3,2,1,0:T(8,128)}) custom-call(s32[4]{0:T(128)} %pad_add_fusion.place, f32[2,8,32,256]{3,2,1,0:T(8,128)} %get-tuple-element.94.a0, f32[2,8,32,256]{3,2,1,0:T(8,128)} %copy-done.13, f32[2,8,32,256]{3,2,1,0:T(8,128)} %copy-done.15, ...), custom_call_target="tpu_custom_call" | custom-call | flops 393216 | bytes 2621440 | tf_op jit(solution)/shard_map/pallas_call | solution.py:232
  191.8 1.4 collective-permute-start.25
  193.2 1.9 collective-permute-start.26
  195.1 0.9 collective-permute-start.30
  196.0 1.3 collective-permute-start.31
  197.3 2.0 collective-permute-start.32
  199.6 3.4 %collective-permute-done.30.refs_13_ = f32[2,2,32,256]{3,2,1,0:T(8,128)S(1)} collective-permute-done((f32[2,2,32,256]{3,2,1,0:T(8,128)}, f32[2,2,32,256]{3,2,1,0:T(8,128)S(1)}, u32[]{:S(2)}, u32[]{:S(2)}) %collective-permute-start.30) | collective-permute-done | bytes 131104 | tf_op jit(solution)/shard_map/ppermute | solution.py:53
  203.0 0.7 collective-permute-done.32.refs_15_
  203.8 0.6 copy-done.36
  204.4 2.8 %shard_map.158 = (f32[5,64,128]{2,1,0:T(8,128)}, f32[5,64,128]{2,1,0:T(8,128)}, f32[5,64,128]{2,1,0:T(8,128)}, f32[5,64,128]{2,1,0:T(8,128)}) custom-call(s32[4]{0:T(128)} %pad_add_fusion.place, f32[3,2,32,256]{3,2,1,0:T(8,128)} %get-tuple-element.74.refs_0_, f32[3,2,32,256]{3,2,1,0:T(8,128)} %copy-done.22, f32[3,2,32,256]{3,2,1,0:T(8,128)} %copy-done.23, ...), custom_call_target="tpu_custom_call" | custom-call | flops 1048576 | bytes 4194304 | tf_op jit(solution)/shard_map/pallas_call | solution.py:244
  207.5 3.4 %collective-permute-start.34 = (f32[5,64,128]{2,1,0:T(8,128)}, f32[5,64,128]{2,1,0:T(8,128)S(1)}, u32[]{:S(2)}, u32[]{:S(2)}) collective-permute-start(f32[5,64,128]{2,1,0:T(8,128)} %get-tuple-element.104), channel_id=1, source_target_pairs={{0,64},{1,65},{64,0},{65,1},{2,66},{3,67},{66,2},{67,3},{4,68},{5,... | collective-permute-start | bytes 491528 | tf_op jit(solution)/shard_map/ppermute | solution.py:53
  210.9 2.1 collective-permute-start.35
  213.0 0.9 collective-permute-done.33.a1
  213.9 2.2 %collective-permute-done.34.a2 = f32[5,64,128]{2,1,0:T(8,128)S(1)} collective-permute-done((f32[5,64,128]{2,1,0:T(8,128)}, f32[5,64,128]{2,1,0:T(8,128)S(1)}, u32[]{:S(2)}, u32[]{:S(2)}) %collective-permute-start.34) | collective-permute-done | bytes 163872 | tf_op jit(solution)/shard_map/ppermute | solution.py:53
  217.2 1.8 shard_map.159
  (110 shorter events, 4.0 us)
Async XLA Ops:
  0.6 14.1 %copy-start.1 = (f32[128,1024]{1,0:T(8,128)S(1)}, f32[128,1024]{1,0:T(8,128)}, u32[]{:S(2)}) copy-start(f32[128,1024]{1,0:T(8,128)} %own.2) | copy-start | bytes 1572868
  3.6 50.5 %all-to-all-start = ((f32[128,2,1024]{2,1,0:T(2,128)}), f32[128,2,1024]{2,1,0:T(2,128)S(1)}, u32[]{:S(2)}, u32[]{:S(2)}) async-start(f32[128,2,1024]{2,1,0:T(2,128)} %shard_map.147), calls=%async_computation | async-start | bytes 2097152 | tf_op jit(solution)/shard_map/all_to_all | solution.py:298
  14.8 34.3 %collective-permute-start.3 = (f32[128,1024]{1,0:T(8,128)S(1)}, f32[128,1024]{1,0:T(8,128)S(1)}, u32[]{:S(2)}, u32[]{:S(2)}) collective-permute-start(f32[128,1024]{1,0:T(8,128)S(1)} %copy-done.1), channel_id=1, source_target_pairs={{0,1},{1,2},{2,3},{3,4},{4,5},{5,6},{6,7},{7,8},{8,9},{9,10},{10,1... | collective-permute-start | bytes 1572872 | tf_op jit(solution)/shard_map/ppermute | solution.py:59
  17.8 31.3 %collective-permute-start.4 = (f32[128,1024]{1,0:T(8,128)S(1)}, f32[128,1024]{1,0:T(8,128)S(1)}, u32[]{:S(2)}, u32[]{:S(2)}) collective-permute-start(f32[128,1024]{1,0:T(8,128)S(1)} %copy-done.1), channel_id=1, source_target_pairs={{1,0},{2,1},{3,2},{4,3},{5,4},{6,5},{7,6},{8,7},{9,8},{10,9},{11,1... | collective-permute-start | bytes 1572872 | tf_op jit(solution)/shard_map/ppermute | solution.py:59
  54.0 4.7 %copy-start.38 = (f32[8,64,128]{2,1,0:T(8,128)S(1)}, f32[8,64,128]{2,1,0:T(8,128)}, u32[]{:S(2)}) copy-start(f32[8,64,128]{2,1,0:T(8,128)} %get-tuple-element.61) | copy-start | bytes 786436
  54.0 5.2 %copy-start = (f32[256,1024]{1,0:T(8,128)S(1)}, f32[256,1024]{1,0:T(8,128)}, u32[]{:S(2)}) copy-start(f32[256,1024]{1,0:T(8,128)} %own.3) | copy-start | bytes 3145732
  54.0 11.8 %collective-permute-start.5 = (f32[2,128,1024]{2,1,0:T(8,128)}, f32[2,128,1024]{2,1,0:T(8,128)}, u32[]{:S(2)}, u32[]{:S(2)}) collective-permute-start(f32[2,128,1024]{2,1,0:T(8,128)} %shard_map.149.if0), channel_id=1, source_target_pairs={{0,8},{8,0},{1,9},{9,1},{2,10},{10,2},{3,11},{11,3},{4,12},{12,4},... | collective-permute-start | bytes 3145736 | tf_op jit(solution)/shard_map/ppermute | solution.py:53
  58.2 12.9 %collective-permute-start.1 = (f32[256,1024]{1,0:T(8,128)}, f32[256,1024]{1,0:T(8,128)S(1)}, u32[]{:S(2)}, u32[]{:S(2)}) collective-permute-start(f32[256,1024]{1,0:T(8,128)} %shard_map.148.ic0), channel_id=1, source_target_pairs={{0,8},{8,0},{1,9},{9,1},{2,10},{10,2},{3,11},{11,3},{4,12},{12,4},... | collective-permute-start | bytes 3145736 | tf_op jit(solution)/shard_map/ppermute | solution.py:53
  58.7 12.5 %collective-permute-start = (f32[8,64,256]{2,1,0:T(8,128)}, f32[8,64,256]{2,1,0:T(8,128)S(1)}, u32[]{:S(2)}, u32[]{:S(2)}) collective-permute-start(f32[8,64,256]{2,1,0:T(8,128)} %get-tuple-element.59), channel_id=1, source_target_pairs={{0,8},{8,0},{1,9},{9,1},{2,10},{10,2},{3,11},{11,3},{4,12},{12,4},... | collective-permute-start | bytes 1572872 | tf_op jit(solution)/shard_map/ppermute | solution.py:53
  58.7 5.8 %collective-permute-start.2 = (f32[8,64,128]{2,1,0:T(8,128)S(1)}, f32[8,64,128]{2,1,0:T(8,128)S(1)}, u32[]{:S(2)}, u32[]{:S(2)}) collective-permute-start(f32[8,64,128]{2,1,0:T(8,128)S(1)} %copy-done.38), channel_id=1, source_target_pairs={{0,8},{8,0},{1,9},{9,1},{2,10},{10,2},{3,11},{11,3},{4,12},{12,4},... | collective-permute-start | bytes 786440 | tf_op jit(solution)/shard_map/ppermute | solution.py:53
  60.1 27.3 %collective-permute-start.18 = (f32[128,1024]{1,0:T(8,128)}, f32[128,1024]{1,0:T(8,128)S(1)}, u32[]{:S(2)}, u32[]{:S(2)}) collective-permute-start(f32[128,1024]{1,0:T(8,128)} %get-tuple-element.112), channel_id=1, source_target_pairs={{0,1},{1,2},{2,3},{3,4},{4,5},{5,6},{6,7},{7,8},{8,9},{9,10},{10,1... | collective-permute-start | bytes 1572872 | tf_op jit(solution)/shard_map/ppermute | solution.py:59
  64.5 1.3 copy-start.39
  64.5 22.9 %collective-permute-start.19 = (f32[128,1024]{1,0:T(8,128)S(1)}, f32[128,1024]{1,0:T(8,128)S(1)}, u32[]{:S(2)}, u32[]{:S(2)}) collective-permute-start(f32[128,1024]{1,0:T(8,128)S(1)} %get-tuple-element.111), channel_id=1, source_target_pairs={{1,0},{2,1},{3,2},{4,3},{5,4},{6,5},{7,6},{8,7},{9,8},{10,9},{11,1... | collective-permute-start | bytes 1572872 | tf_op jit(solution)/shard_map/ppermute | solution.py:59
  89.0 6.1 %copy-start.4 = (f32[3,2,32,1024]{3,2,1,0:T(8,128)S(1)}, f32[3,2,32,1024]{3,2,1,0:T(8,128)}, u32[]{:S(2)}) copy-start(f32[3,2,32,1024]{3,2,1,0:T(8,128)} %get-tuple-element.71) | copy-start | bytes 2359300
  89.0 10.9 %copy-start.5 = (f32[3,2,32,1024]{3,2,1,0:T(8,128)S(1)}, f32[3,2,32,1024]{3,2,1,0:T(8,128)}, u32[]{:S(2)}) copy-start(f32[3,2,32,1024]{3,2,1,0:T(8,128)} %get-tuple-element.72) | copy-start | bytes 2359300
  89.0 13.2 %copy-start.6 = (f32[3,2,32,1024]{3,2,1,0:T(8,128)S(1)}, f32[3,2,32,1024]{3,2,1,0:T(8,128)}, u32[]{:S(2)}) copy-start(f32[3,2,32,1024]{3,2,1,0:T(8,128)} %get-tuple-element.73) | copy-start | bytes 2359300
  89.0 15.1 %copy-start.7 = (f32[3,8,32,256]{3,2,1,0:T(8,128)S(1)}, f32[3,8,32,256]{3,2,1,0:T(8,128)}, u32[]{:S(2)}) copy-start(f32[3,8,32,256]{3,2,1,0:T(8,128)} %get-tuple-element.79) | copy-start | bytes 2359300
  89.0 29.9 %copy-start.8 = (f32[3,8,32,256]{3,2,1,0:T(8,128)S(1)}, f32[3,8,32,256]{3,2,1,0:T(8,128)}, u32[]{:S(2)}) copy-start(f32[3,8,32,256]{3,2,1,0:T(8,128)} %get-tuple-element.80) | copy-start | bytes 2359300
  95.1 25.4 %collective-permute-start.20 = (f32[2,256,1024]{2,1,0:T(8,128)}, f32[2,256,1024]{2,1,0:T(8,128)S(1)}, u32[]{:S(2)}, u32[]{:S(2)}) collective-permute-start(f32[2,256,1024]{2,1,0:T(8,128)} %shard_map.154.is0), channel_id=1, source_target_pairs={{0,8},{8,0},{1,9},{9,1},{2,10},{10,2},{3,11},{11,3},{4,12},{12,4},... | collective-permute-start | bytes 6291464 | tf_op jit(solution)/shard_map/ppermute | solution.py:53
  95.1 23.8 %collective-permute-start.6 = (f32[3,2,32,1024]{3,2,1,0:T(8,128)S(1)}, f32[3,2,32,1024]{3,2,1,0:T(8,128)S(1)}, u32[]{:S(2)}, u32[]{:S(2)}) collective-permute-start(f32[3,2,32,1024]{3,2,1,0:T(8,128)S(1)} %copy-done.4), channel_id=1, source_target_pairs={{0,16},{16,32},{32,48},{48,0},{1,17},{17,33},{33,49},{49,1},{2,18}... | collective-permute-start | bytes 2359304 | tf_op jit(solution)/shard_map/ppermute | solution.py:53
  99.9 37.1 %collective-permute-start.7 = (f32[3,2,32,1024]{3,2,1,0:T(8,128)S(1)}, f32[3,2,32,1024]{3,2,1,0:T(8,128)}, u32[]{:S(2)}, u32[]{:S(2)}) collective-permute-start(f32[3,2,32,1024]{3,2,1,0:T(8,128)S(1)} %copy-done.5), channel_id=1, source_target_pairs={{0,32},{16,48},{32,0},{48,16},{1,33},{17,49},{33,1},{49,17},{2,34}... | collective-permute-start | bytes 2359304 | tf_op jit(solution)/shard_map/ppermute | solution.py:53
  102.2 34.8 %collective-permute-start.8 = (f32[3,2,32,1024]{3,2,1,0:T(8,128)S(1)}, f32[3,2,32,1024]{3,2,1,0:T(8,128)}, u32[]{:S(2)}, u32[]{:S(2)}) collective-permute-start(f32[3,2,32,1024]{3,2,1,0:T(8,128)S(1)} %copy-done.6), channel_id=1, source_target_pairs={{0,48},{16,0},{32,16},{48,32},{1,49},{17,1},{33,17},{49,33},{2,50}... | collective-permute-start | bytes 2359304 | tf_op jit(solution)/shard_map/ppermute | solution.py:53
  104.1 37.2 %collective-permute-start.12 = (f32[3,8,32,256]{3,2,1,0:T(8,128)S(1)}, f32[3,8,32,256]{3,2,1,0:T(8,128)}, u32[]{:S(2)}, u32[]{:S(2)}) collective-permute-start(f32[3,8,32,256]{3,2,1,0:T(8,128)S(1)} %copy-done.7), channel_id=1, source_target_pairs={{0,2},{2,4},{4,6},{6,0},{1,3},{3,5},{5,7},{7,1},{8,10},{10,12},{12... | collective-permute-start | bytes 2359304 | tf_op jit(solution)/shard_map/ppermute | solution.py:53
  118.9 1.6 copy-start.10
  118.9 23.4 %collective-permute-start.13 = (f32[3,8,32,256]{3,2,1,0:T(8,128)S(1)}, f32[3,8,32,256]{3,2,1,0:T(8,128)S(1)}, u32[]{:S(2)}, u32[]{:S(2)}) collective-permute-start(f32[3,8,32,256]{3,2,1,0:T(8,128)S(1)} %copy-done.8), channel_id=1, source_target_pairs={{0,4},{2,6},{4,0},{6,2},{1,5},{3,7},{5,1},{7,3},{8,12},{10,14},{12... | collective-permute-start | bytes 2359304 | tf_op jit(solution)/shard_map/ppermute | solution.py:53
  121.8 34.6 %collective-permute-start.14 = (f32[3,8,32,256]{3,2,1,0:T(8,128)}, f32[3,8,32,256]{3,2,1,0:T(8,128)}, u32[]{:S(2)}, u32[]{:S(2)}) collective-permute-start(f32[3,8,32,256]{3,2,1,0:T(8,128)} %get-tuple-element.81), channel_id=1, source_target_pairs={{0,6},{2,0},{4,2},{6,4},{1,7},{3,1},{5,3},{7,5},{8,14},{10,8},{12,... | collective-permute-start | bytes 2359304 | tf_op jit(solution)/shard_map/ppermute | solution.py:53
  137.1 26.1 %collective-permute-start.21 = (f32[2,2,32,1024]{3,2,1,0:T(8,128)}, f32[2,2,32,1024]{3,2,1,0:T(8,128)S(1)}, u32[]{:S(2)}, u32[]{:S(2)}) collective-permute-start(f32[2,2,32,1024]{3,2,1,0:T(8,128)} %get-tuple-element.87), channel_id=1, source_target_pairs={{0,16},{16,32},{32,48},{48,0},{1,17},{17,33},{33,49},{49,1},{2,18}... | collective-permute-start | bytes 1572872 | tf_op jit(solution)/shard_map/ppermute | solution.py:53
  140.1 18.1 %collective-permute-start.9 = (f32[3,2,32,256]{3,2,1,0:T(8,128)}, f32[3,2,32,256]{3,2,1,0:T(8,128)S(1)}, u32[]{:S(2)}, u32[]{:S(2)}) collective-permute-start(f32[3,2,32,256]{3,2,1,0:T(8,128)} %get-tuple-element.75), channel_id=1, source_target_pairs={{0,2},{2,4},{4,6},{6,0},{1,3},{3,5},{5,7},{7,1},{8,10},{10,12},{12... | collective-permute-start | bytes 589832 | tf_op jit(solution)/shard_map/ppermute | solution.py:53
  141.3 18.3 %collective-permute-start.10 = (f32[3,2,32,256]{3,2,1,0:T(8,128)}, f32[3,2,32,256]{3,2,1,0:T(8,128)S(1)}, u32[]{:S(2)}, u32[]{:S(2)}) collective-permute-start(f32[3,2,32,256]{3,2,1,0:T(8,128)} %get-tuple-element.76), channel_id=1, source_target_pairs={{0,4},{2,6},{4,0},{6,2},{1,5},{3,7},{5,1},{7,3},{8,12},{10,14},{12... | collective-permute-start | bytes 589832 | tf_op jit(solution)/shard_map/ppermute | solution.py:53
  142.3 21.9 %copy-start.9 = (f32[3,8,32,256]{3,2,1,0:T(8,128)}, f32[3,8,32,256]{3,2,1,0:T(8,128)S(1)}, u32[]{:S(2)}) copy-start(f32[3,8,32,256]{3,2,1,0:T(8,128)S(1)} %collective-permute-done.13.a2) | copy-start | bytes 2359300
  142.3 24.9 %collective-permute-start.22 = (f32[2,2,32,1024]{3,2,1,0:T(8,128)}, f32[2,2,32,1024]{3,2,1,0:T(8,128)S(1)}, u32[]{:S(2)}, u32[]{:S(2)}) collective-permute-start(f32[2,2,32,1024]{3,2,1,0:T(8,128)} %get-tuple-element.88), channel_id=1, source_target_pairs={{0,32},{16,48},{32,0},{48,16},{1,33},{17,49},{33,1},{49,17},{2,34}... | collective-permute-start | bytes 1572872 | tf_op jit(solution)/shard_map/ppermute | solution.py:53
  156.4 12.4 %collective-permute-start.23 = (f32[2,2,32,1024]{3,2,1,0:T(8,128)}, f32[2,2,32,1024]{3,2,1,0:T(8,128)S(1)}, u32[]{:S(2)}, u32[]{:S(2)}) collective-permute-start(f32[2,2,32,1024]{3,2,1,0:T(8,128)} %get-tuple-element.89), channel_id=1, source_target_pairs={{0,48},{16,0},{32,16},{48,32},{1,49},{17,1},{33,17},{49,33},{2,50}... | collective-permute-start | bytes 1572872 | tf_op jit(solution)/shard_map/ppermute | solution.py:53
  158.2 30.2 %copy-start.22 = (f32[3,2,32,256]{3,2,1,0:T(8,128)}, f32[3,2,32,256]{3,2,1,0:T(8,128)S(1)}, u32[]{:S(2)}) copy-start(f32[3,2,32,256]{3,2,1,0:T(8,128)S(1)} %collective-permute-done.9.refs_1_) | copy-start | bytes 589828
  158.2 14.7 %collective-permute-start.27 = (f32[2,8,32,256]{3,2,1,0:T(8,128)}, f32[2,8,32,256]{3,2,1,0:T(8,128)S(1)}, u32[]{:S(2)}, u32[]{:S(2)}) collective-permute-start(f32[2,8,32,256]{3,2,1,0:T(8,128)} %get-tuple-element.95), channel_id=1, source_target_pairs={{0,2},{2,4},{4,6},{6,0},{1,3},{3,5},{5,7},{7,1},{8,10},{10,12},{12... | collective-permute-start | bytes 1572872 | tf_op jit(solution)/shard_map/ppermute | solution.py:53
  160.3 24.9 %collective-permute-start.28 = (f32[2,8,32,256]{3,2,1,0:T(8,128)}, f32[2,8,32,256]{3,2,1,0:T(8,128)S(1)}, u32[]{:S(2)}, u32[]{:S(2)}) collective-permute-start(f32[2,8,32,256]{3,2,1,0:T(8,128)} %get-tuple-element.96), channel_id=1, source_target_pairs={{0,4},{2,6},{4,0},{6,2},{1,5},{3,7},{5,1},{7,3},{8,12},{10,14},{12... | collective-permute-start | bytes 1572872 | tf_op jit(solution)/shard_map/ppermute | solution.py:53
  163.1 22.7 %copy-start.12 = (f32[2,2,32,1024]{3,2,1,0:T(8,128)}, f32[2,2,32,1024]{3,2,1,0:T(8,128)S(1)}, u32[]{:S(2)}) copy-start(f32[2,2,32,1024]{3,2,1,0:T(8,128)S(1)} %collective-permute-done.21.a1) | copy-start | bytes 1572868
  163.1 25.3 %collective-permute-start.29 = (f32[2,8,32,256]{3,2,1,0:T(8,128)}, f32[2,8,32,256]{3,2,1,0:T(8,128)S(1)}, u32[]{:S(2)}, u32[]{:S(2)}) collective-permute-start(f32[2,8,32,256]{3,2,1,0:T(8,128)} %get-tuple-element.97), channel_id=1, source_target_pairs={{0,6},{2,0},{4,2},{6,4},{1,7},{3,1},{5,3},{7,5},{8,14},{10,8},{12,... | collective-permute-start | bytes 1572872 | tf_op jit(solution)/shard_map/ppermute | solution.py:53
  167.3 18.6 %copy-start.14 = (f32[2,2,32,1024]{3,2,1,0:T(8,128)}, f32[2,2,32,1024]{3,2,1,0:T(8,128)S(1)}, u32[]{:S(2)}) copy-start(f32[2,2,32,1024]{3,2,1,0:T(8,128)S(1)} %collective-permute-done.22.a2) | copy-start | bytes 1572868
  167.3 24.5 %collective-permute-start.11 = (f32[3,2,32,256]{3,2,1,0:T(8,128)}, f32[3,2,32,256]{3,2,1,0:T(8,128)S(1)}, u32[]{:S(2)}, u32[]{:S(2)}) collective-permute-start(f32[3,2,32,256]{3,2,1,0:T(8,128)} %get-tuple-element.77), channel_id=1, source_target_pairs={{0,6},{2,0},{4,2},{6,4},{1,7},{3,1},{5,3},{7,5},{8,14},{10,8},{12,... | collective-permute-start | bytes 589832 | tf_op jit(solution)/shard_map/ppermute | solution.py:53
  168.8 17.0 %copy-start.16 = (f32[2,2,32,1024]{3,2,1,0:T(8,128)}, f32[2,2,32,1024]{3,2,1,0:T(8,128)S(1)}, u32[]{:S(2)}) copy-start(f32[2,2,32,1024]{3,2,1,0:T(8,128)S(1)} %collective-permute-done.23.a3) | copy-start | bytes 1572868
  168.8 24.4 %collective-permute-start.15 = (f32[3,2,32,256]{3,2,1,0:T(8,128)}, f32[3,2,32,256]{3,2,1,0:T(8,128)S(1)}, u32[]{:S(2)}, u32[]{:S(2)}) collective-permute-start(f32[3,2,32,256]{3,2,1,0:T(8,128)} %get-tuple-element.83), channel_id=1, source_target_pairs={{0,16},{16,32},{32,48},{48,0},{1,17},{17,33},{33,49},{49,1},{2,18}... | collective-permute-start | bytes 589832 | tf_op jit(solution)/shard_map/ppermute | solution.py:53
  172.9 15.6 %copy-start.13 = (f32[2,8,32,256]{3,2,1,0:T(8,128)}, f32[2,8,32,256]{3,2,1,0:T(8,128)S(1)}, u32[]{:S(2)}) copy-start(f32[2,8,32,256]{3,2,1,0:T(8,128)S(1)} %collective-permute-done.27.a1) | copy-start | bytes 1572868
  172.9 22.2 %collective-permute-start.16 = (f32[3,2,32,256]{3,2,1,0:T(8,128)}, f32[3,2,32,256]{3,2,1,0:T(8,128)S(1)}, u32[]{:S(2)}, u32[]{:S(2)}) collective-permute-start(f32[3,2,32,256]{3,2,1,0:T(8,128)} %get-tuple-element.84), channel_id=1, source_target_pairs={{0,32},{16,48},{32,0},{48,16},{1,33},{17,49},{33,1},{49,17},{2,34}... | collective-permute-start | bytes 589832 | tf_op jit(solution)/shard_map/ppermute | solution.py:53
  185.1 3.4 %copy-start.15 = (f32[2,8,32,256]{3,2,1,0:T(8,128)}, f32[2,8,32,256]{3,2,1,0:T(8,128)S(1)}, u32[]{:S(2)}) copy-start(f32[2,8,32,256]{3,2,1,0:T(8,128)S(1)} %collective-permute-done.28.a2) | copy-start | bytes 1572868
  185.1 10.9 %collective-permute-start.17 = (f32[3,2,32,256]{3,2,1,0:T(8,128)}, f32[3,2,32,256]{3,2,1,0:T(8,128)S(1)}, u32[]{:S(2)}, u32[]{:S(2)}) collective-permute-start(f32[3,2,32,256]{3,2,1,0:T(8,128)} %get-tuple-element.85), channel_id=1, source_target_pairs={{0,48},{16,0},{32,16},{48,32},{1,49},{17,1},{33,17},{49,33},{2,50}... | collective-permute-start | bytes 589832 | tf_op jit(solution)/shard_map/ppermute | solution.py:53
  188.4 3.4 %copy-start.41 = (f32[2,2,32,256]{3,2,1,0:T(8,128)S(1)}, f32[2,2,32,256]{3,2,1,0:T(8,128)}, u32[]{:S(2)}) copy-start(f32[2,2,32,256]{3,2,1,0:T(8,128)} %get-tuple-element.92) | copy-start | bytes 393220
  188.4 4.8 %copy-start.40 = (f32[2,2,32,256]{3,2,1,0:T(8,128)S(1)}, f32[2,2,32,256]{3,2,1,0:T(8,128)}, u32[]{:S(2)}) copy-start(f32[2,2,32,256]{3,2,1,0:T(8,128)} %get-tuple-element.93) | copy-start | bytes 393220
  188.4 8.9 %collective-permute-start.24 = (f32[2,2,32,256]{3,2,1,0:T(8,128)}, f32[2,2,32,256]{3,2,1,0:T(8,128)S(1)}, u32[]{:S(2)}, u32[]{:S(2)}) collective-permute-start(f32[2,2,32,256]{3,2,1,0:T(8,128)} %get-tuple-element.91), channel_id=1, source_target_pairs={{0,2},{2,4},{4,6},{6,0},{1,3},{3,5},{5,7},{7,1},{8,10},{10,12},{12... | collective-permute-start | bytes 393224 | tf_op jit(solution)/shard_map/ppermute | solution.py:53
  191.8 11.9 %copy-start.24 = (f32[3,2,32,256]{3,2,1,0:T(8,128)}, f32[3,2,32,256]{3,2,1,0:T(8,128)S(1)}, u32[]{:S(2)}) copy-start(f32[3,2,32,256]{3,2,1,0:T(8,128)S(1)} %collective-permute-done.11.refs_3_) | copy-start | bytes 589828
  191.8 7.5 %collective-permute-start.25 = (f32[2,2,32,256]{3,2,1,0:T(8,128)S(1)}, f32[2,2,32,256]{3,2,1,0:T(8,128)S(1)}, u32[]{:S(2)}, u32[]{:S(2)}) collective-permute-start(f32[2,2,32,256]{3,2,1,0:T(8,128)S(1)} %copy-done.41), channel_id=1, source_target_pairs={{0,4},{2,6},{4,0},{6,2},{1,5},{3,7},{5,1},{7,3},{8,12},{10,14},{12... | collective-permute-start | bytes 393224 | tf_op jit(solution)/shard_map/ppermute | solution.py:53
  193.2 10.5 %copy-start.25 = (f32[3,2,32,256]{3,2,1,0:T(8,128)}, f32[3,2,32,256]{3,2,1,0:T(8,128)S(1)}, u32[]{:S(2)}) copy-start(f32[3,2,32,256]{3,2,1,0:T(8,128)S(1)} %collective-permute-done.15.refs_5_) | copy-start | bytes 589828
  193.2 6.4 %collective-permute-start.26 = (f32[2,2,32,256]{3,2,1,0:T(8,128)S(1)}, f32[2,2,32,256]{3,2,1,0:T(8,128)S(1)}, u32[]{:S(2)}, u32[]{:S(2)}) collective-permute-start(f32[2,2,32,256]{3,2,1,0:T(8,128)S(1)} %copy-done.40), channel_id=1, source_target_pairs={{0,6},{2,0},{4,2},{6,4},{1,7},{3,1},{5,3},{7,5},{8,14},{10,8},{12,... | collective-permute-start | bytes 393224 | tf_op jit(solution)/shard_map/ppermute | solution.py:53
  195.0 8.7 %copy-start.26 = (f32[3,2,32,256]{3,2,1,0:T(8,128)}, f32[3,2,32,256]{3,2,1,0:T(8,128)S(1)}, u32[]{:S(2)}) copy-start(f32[3,2,32,256]{3,2,1,0:T(8,128)S(1)} %collective-permute-done.16.refs_6_) | copy-start | bytes 589828
  195.1 8.0 %collective-permute-start.30 = (f32[2,2,32,256]{3,2,1,0:T(8,128)}, f32[2,2,32,256]{3,2,1,0:T(8,128)S(1)}, u32[]{:S(2)}, u32[]{:S(2)}) collective-permute-start(f32[2,2,32,256]{3,2,1,0:T(8,128)} %get-tuple-element.99), channel_id=1, source_target_pairs={{0,16},{16,32},{32,48},{48,0},{1,17},{17,33},{33,49},{49,1},{2,18}... | collective-permute-start | bytes 393224 | tf_op jit(solution)/shard_map/ppermute | solution.py:53
  196.0 7.7 %copy-start.27 = (f32[3,2,32,256]{3,2,1,0:T(8,128)}, f32[3,2,32,256]{3,2,1,0:T(8,128)S(1)}, u32[]{:S(2)}) copy-start(f32[3,2,32,256]{3,2,1,0:T(8,128)S(1)} %collective-permute-done.17.refs_7_) | copy-start | bytes 589828
  196.0 7.0 %collective-permute-start.31 = (f32[2,2,32,256]{3,2,1,0:T(8,128)}, f32[2,2,32,256]{3,2,1,0:T(8,128)S(1)}, u32[]{:S(2)}, u32[]{:S(2)}) collective-permute-start(f32[2,2,32,256]{3,2,1,0:T(8,128)} %get-tuple-element.100), channel_id=1, source_target_pairs={{0,32},{16,48},{32,0},{48,16},{1,33},{17,49},{33,1},{49,17},{2,34}... | collective-permute-start | bytes 393224 | tf_op jit(solution)/shard_map/ppermute | solution.py:53
  197.3 6.4 %copy-start.31 = (f32[2,2,32,256]{3,2,1,0:T(8,128)}, f32[2,2,32,256]{3,2,1,0:T(8,128)S(1)}, u32[]{:S(2)}) copy-start(f32[2,2,32,256]{3,2,1,0:T(8,128)S(1)} %collective-permute-done.24.refs_9_) | copy-start | bytes 393220
  197.3 6.4 %collective-permute-start.32 = (f32[2,2,32,256]{3,2,1,0:T(8,128)}, f32[2,2,32,256]{3,2,1,0:T(8,128)S(1)}, u32[]{:S(2)}, u32[]{:S(2)}) collective-permute-start(f32[2,2,32,256]{3,2,1,0:T(8,128)} %get-tuple-element.101), channel_id=1, source_target_pairs={{0,48},{16,0},{32,16},{48,32},{1,49},{17,1},{33,17},{49,33},{2,50}... | collective-permute-start | bytes 393224 | tf_op jit(solution)/shard_map/ppermute | solution.py:53
  199.3 4.5 %copy-start.32 = (f32[2,2,32,256]{3,2,1,0:T(8,128)}, f32[2,2,32,256]{3,2,1,0:T(8,128)S(1)}, u32[]{:S(2)}) copy-start(f32[2,2,32,256]{3,2,1,0:T(8,128)S(1)} %collective-permute-done.25.refs_10_) | copy-start | bytes 393220
  199.6 4.1 %copy-start.33 = (f32[2,2,32,256]{3,2,1,0:T(8,128)}, f32[2,2,32,256]{3,2,1,0:T(8,128)S(1)}, u32[]{:S(2)}) copy-start(f32[2,2,32,256]{3,2,1,0:T(8,128)S(1)} %collective-permute-done.26.refs_11_) | copy-start | bytes 393220
  207.2 6.7 %collective-permute-start.33 = (f32[5,64,128]{2,1,0:T(8,128)}, f32[5,64,128]{2,1,0:T(8,128)S(1)}, u32[]{:S(2)}, u32[]{:S(2)}) collective-permute-start(f32[5,64,128]{2,1,0:T(8,128)} %get-tuple-element.103), channel_id=1, source_target_pairs={{0,1},{1,64},{64,65},{65,0},{2,3},{3,66},{66,67},{67,2},{4,5},{5,6... | collective-permute-start | bytes 491528 | tf_op jit(solution)/shard_map/ppermute | solution.py:53
  207.5 8.6 %collective-permute-start.34 = (f32[5,64,128]{2,1,0:T(8,128)}, f32[5,64,128]{2,1,0:T(8,128)S(1)}, u32[]{:S(2)}, u32[]{:S(2)}) collective-permute-start(f32[5,64,128]{2,1,0:T(8,128)} %get-tuple-element.104), channel_id=1, source_target_pairs={{0,64},{1,65},{64,0},{65,1},{2,66},{3,67},{66,2},{67,3},{4,68},{5,... | collective-permute-start | bytes 491528 | tf_op jit(solution)/shard_map/ppermute | solution.py:53
  210.9 5.6 %collective-permute-start.35 = (f32[5,64,128]{2,1,0:T(8,128)}, f32[5,64,128]{2,1,0:T(8,128)S(1)}, u32[]{:S(2)}, u32[]{:S(2)}) collective-permute-start(f32[5,64,128]{2,1,0:T(8,128)} %get-tuple-element.105), channel_id=1, source_target_pairs={{0,65},{1,0},{64,1},{65,64},{2,67},{3,2},{66,3},{67,66},{4,69},{5,... | collective-permute-start | bytes 491528 | tf_op jit(solution)/shard_map/ppermute | solution.py:53
  213.9 2.6 %copy-start.28 = (f32[5,64,128]{2,1,0:T(8,128)}, f32[5,64,128]{2,1,0:T(8,128)S(1)}, u32[]{:S(2)}) copy-start(f32[5,64,128]{2,1,0:T(8,128)S(1)} %collective-permute-done.33.a1) | copy-start | bytes 491524
  (15 other events, 12.7 us)

commit v8 on v7

--- a/solution.py
+++ b/solution.py
@@ -287,8 +287,9 @@
     place = jnp.stack([lax.axis_index(X), lax.axis_index(Y), lax.axis_index(Z), lax.axis_index("core")]).astype(
         jnp.int32
     )
-    below_s = from_behind(struct_basis[-TILE:], 1)
-    above_s = from_behind(struct_basis[:TILE], -1)
+    tail, head = lax.optimization_barrier((struct_basis[-TILE:], struct_basis[:TILE]))
+    below_s = from_behind(tail, 1)
+    above_s = from_behind(head, -1)
     below_f = from_behind(fluid_basis, 1)
     above_f = from_behind(fluid_basis, -1)
 

time: 220 us -> 220 us (level)
  no operation moved by 1% of the time
where the time goes in v8:
time: 220 us; the launch traced here: 219 us
  waiting for transfers between devices  93.8 us (43%)
  starting transfers between devices  61.2 us (28%)
  Pallas kernels  52.7 us (24%)
  local copies, waits for them, and re-layouts  9.69 us (4%)
    ppermute x32, waiting for transfers between devices, shifted(): lax.ppermute(value, axis, [(i, (i + by) % size) for i in range(size)])  57.5 us
    ppermute x32, starting transfers between devices, shifted(): lax.ppermute(value, axis, [(i, (i + by) % size) for i in range(size)])  40 us
    ppermute x4, waiting for transfers between devices, from_behind(): return lax.ppermute(value, AXES, pairs)  36.3 us
    pallas_call x3, Pallas kernels, partial_sums(): return run(place, *lefts, *operands, *carried)  17.9 us
    all_to_all x1, starting transfers between devices, compute(): lax.all_to_all(outgoing, AXES, split_axis=0, concat_axis=0, tiled=True)  11.2 us
    pallas_call x4, Pallas kernels, split(): call(functools.partial(split_kernel, axis), [shape(count, 2, HALF, 256)]...  11.2 us
    ppermute x4, starting transfers between devices, from_behind(): return lax.ppermute(value, AXES, pairs)  10 us
    unnamed x84, local copies, waits for them, and re-layouts  8.79 us
  transfers between devices with their start and end apart: 37, of which 16 were waited for; matrix products, arithmetic and copies ran while one was open for 1% of the time, Pallas kernels for 18%

profile of v8, /device:TPU:0, one launch (start us, length us, event | category | flops | bytes accessed | tf_op | source)
XLA Modules:
  0.0 219.0 jit_solution(13143004734027115096)
XLA Ops:
  0.6 2.9 %shard_map.147 = f32[128,2,1024]{2,1,0:T(2,128)} custom-call(s32[1,128]{1,0:T(1,128)} %bitcast.6, s32[1,128]{1,0:T(1,128)} %bitcast.7, f32[128,1024]{1,0:T(8,128)} %own.2), custom_call_target="tpu_custom_call" | custom-call | flops 201326592 | bytes 2097152 | tf_op jit(solution)/shard_map/pallas_call | solution.py:296
  3.6 11.2 %all-to-all-start = ((f32[128,2,1024]{2,1,0:T(2,128)}), f32[128,2,1024]{2,1,0:T(2,128)S(1)}, u32[]{:S(2)}, u32[]{:S(2)}) async-start(f32[128,2,1024]{2,1,0:T(2,128)} %shard_map.147), calls=%async_computation | async-start | bytes 2097152 | tf_op jit(solution)/shard_map/all_to_all | solution.py:299
  14.8 3.0 %collective-permute-start.3 = (f32[128,1024]{1,0:T(8,128)S(1)}, f32[128,1024]{1,0:T(8,128)S(1)}, u32[]{:S(2)}, u32[]{:S(2)}) collective-permute-start(f32[128,1024]{1,0:T(8,128)S(1)} %copy-done.1), channel_id=1, source_target_pairs={{0,1},{1,2},{2,3},{3,4},{4,5},{5,6},{6,7},{7,8},{8,9},{9,10},{10,1... | collective-permute-start | bytes 1572872 | tf_op jit(solution)/shard_map/ppermute | solution.py:59
  17.8 1.3 collective-permute-start.4
  19.1 0.6 pad_add_fusion.place
  19.7 2.9 %shard_map.146 = (f32[8,64,256]{2,1,0:T(8,128)}, f32[8,64,256]{2,1,0:T(8,128)}, f32[8,64,128]{2,1,0:T(8,128)}, f32[8,64,128]{2,1,0:T(8,128)}) custom-call(s32[4]{0:T(128)} %pad_add_fusion.place, f32[256,1024]{1,0:T(8,128)} %own.3, f32[128,1024]{1,0:T(8,128)} %own.2), custom_call_target="tpu_custom_call" | custom-call | flops 1048576 | bytes 3145728 | tf_op jit(solution)/shard_map/pallas_call | solution.py:301
  22.6 26.5 %collective-permute-done.3.lo = f32[128,1024]{1,0:T(8,128)S(1)} collective-permute-done((f32[128,1024]{1,0:T(8,128)S(1)}, f32[128,1024]{1,0:T(8,128)S(1)}, u32[]{:S(2)}, u32[]{:S(2)}) %collective-permute-start.3) | collective-permute-done | bytes 524320 | tf_op jit(solution)/shard_map/ppermute | solution.py:59
  49.1 0.8 copy-done.20
  50.1 4.0 %shard_map.149.if0 = f32[2,128,1024]{2,1,0:T(8,128)} custom-call(s32[1,4]{1,0:T(1,128)} %cols.2, f32[1,4,128,128]{3,2,1,0:T(8,128)} %stiff.2, f32[1,4,128,128]{3,2,1,0:T(8,128)} %mass.2, f32[128,1024]{1,0:T(8,128)} %copy-done.20, f32[128,1024]{1,0:T(8,128)} %own.2, f32[128,1024]{1,0:T(8,128)} %copy-done.21, f32[8,64,256]{2,1,0:T(8,128)} %get-tuple-element.60.after.ls0), custom_call_target="tpu_custom_call" | custom-call | flops 603979776 | bytes 3145728 | tf_op jit(solution)/shard_map/pallas_call | solution.py:316
  54.1 1.0 copy-done.2
  55.1 3.1 %shard_map.148.ic0 = f32[256,1024]{1,0:T(8,128)} custom-call(f32[256,256]{1,0:T(8,128)} %coupling.1, f32[128,2,1024]{2,1,0:T(2,128)} %copy-done.2), custom_call_target="tpu_custom_call" | custom-call | flops 402653184 | bytes 2097152 | tf_op jit(solution)/shard_map/pallas_call | solution.py:313
  59.2 0.9 fusion
  60.1 4.4 %collective-permute-start.18 = (f32[128,1024]{1,0:T(8,128)}, f32[128,1024]{1,0:T(8,128)S(1)}, u32[]{:S(2)}, u32[]{:S(2)}) collective-permute-start(f32[128,1024]{1,0:T(8,128)} %get-tuple-element.88), channel_id=1, source_target_pairs={{0,1},{1,2},{2,3},{3,4},{4,5},{5,6},{6,7},{7,8},{8,9},{9,10},{10,1... | collective-permute-start | bytes 1572872 | tf_op jit(solution)/shard_map/ppermute | solution.py:59
  64.5 1.3 collective-permute-start.19
  65.8 5.3 %shard_map.150 = (f32[3,2,32,1024]{3,2,1,0:T(8,128)}, f32[3,2,32,1024]{3,2,1,0:T(8,128)}, f32[3,2,32,1024]{3,2,1,0:T(8,128)}, f32[3,2,32,1024]{3,2,1,0:T(8,128)}...) custom-call(s32[4]{0:T(128)} %pad_add_fusion.place, ...), custom_call_target="tpu_custom_call" | custom-call | flops 1610612736 | bytes 8388608 | tf_op jit(solution)/shard_map/pallas_call | solution.py:271
  71.2 0.8 copy-done.11
  72.3 5.2 %shard_map.151 = (f32[3,2,32,1024]{3,2,1,0:T(8,128)}, f32[3,2,32,1024]{3,2,1,0:T(8,128)}, f32[3,2,32,1024]{3,2,1,0:T(8,128)}, f32[3,2,32,1024]{3,2,1,0:T(8,128)}...) custom-call(s32[4]{0:T(128)} %pad_add_fusion.place, ...), custom_call_target="tpu_custom_call", output_to_operand_aliasing={{0}: (5, {}), {1}: (6, {}), {2}: (7, {}), {3}: (8, {}), {4}... | custom-call | flops 1610612736 | bytes 4194304 | tf_op jit(solution)/shard_map/pallas_call | solution.py:271
  77.5 9.9 %collective-permute-done.18.lo = f32[128,1024]{1,0:T(8,128)S(1)} collective-permute-done((f32[128,1024]{1,0:T(8,128)}, f32[128,1024]{1,0:T(8,128)S(1)}, u32[]{:S(2)}, u32[]{:S(2)}) %collective-permute-start.18) | collective-permute-done | bytes 524320 | tf_op jit(solution)/shard_map/ppermute | solution.py:59
  87.4 0.8 copy-done.18
  88.2 0.8 copy-done.19
  89.0 6.1 %shard_map.154.is0 = f32[2,256,1024]{2,1,0:T(8,128)} custom-call(s32[2,4]{1,0:T(2,128)} %cols.3, f32[2,4,128,128]{3,2,1,0:T(8,128)} %stiff.3, f32[2,4,128,128]{3,2,1,0:T(8,128)} %mass.3, f32[128,1024]{1,0:T(8,128)} %copy-done.18, f32[256,1024]{1,0:T(8,128)} %own.3, f32[128,1024]{1,0:T(8,128)} %copy-done.19, f32[3,2,32,1024]{3,2,1,0:T(8,128)} %get-tuple-element.72.a0.after), custom_call_target="tpu_custom_call" | custom-call | flops 1610612736 | bytes 5242880 | tf_op jit(solution)/shard_map/pallas_call | solution.py:340
  95.1 4.8 %collective-permute-start.6 = (f32[3,2,32,1024]{3,2,1,0:T(8,128)S(1)}, f32[3,2,32,1024]{3,2,1,0:T(8,128)S(1)}, u32[]{:S(2)}, u32[]{:S(2)}) collective-permute-start(f32[3,2,32,1024]{3,2,1,0:T(8,128)S(1)} %copy-done.4), channel_id=1, source_target_pairs={{0,16},{16,32},{32,48},{48,0},{1,17},{17,33},{33,49},{49,1},{2,18}... | collective-permute-start | bytes 2359304 | tf_op jit(solution)/shard_map/ppermute | solution.py:53
  99.9 2.3 %collective-permute-start.7 = (f32[3,2,32,1024]{3,2,1,0:T(8,128)S(1)}, f32[3,2,32,1024]{3,2,1,0:T(8,128)}, u32[]{:S(2)}, u32[]{:S(2)}) collective-permute-start(f32[3,2,32,1024]{3,2,1,0:T(8,128)S(1)} %copy-done.5), channel_id=1, source_target_pairs={{0,32},{16,48},{32,0},{48,16},{1,33},{17,49},{33,1},{49,17},{2,34}... | collective-permute-start | bytes 2359304 | tf_op jit(solution)/shard_map/ppermute | solution.py:53
  102.2 1.8 collective-permute-start.8
  104.1 14.8 %collective-permute-done.6.a1 = f32[3,2,32,1024]{3,2,1,0:T(8,128)S(1)} collective-permute-done((f32[3,2,32,1024]{3,2,1,0:T(8,128)S(1)}, f32[3,2,32,1024]{3,2,1,0:T(8,128)S(1)}, u32[]{:S(2)}, u32[]{:S(2)}) %collective-permute-start.6) | collective-permute-done | bytes 786464 | tf_op jit(solution)/shard_map/ppermute | solution.py:53
  118.9 1.6 collective-permute-start.13
  120.5 1.3 copy-done.37
  121.8 1.5 collective-permute-start.14
  123.3 7.4 %shard_map.155 = (f32[2,2,32,1024]{3,2,1,0:T(8,128)}, f32[2,2,32,1024]{3,2,1,0:T(8,128)}, f32[2,2,32,1024]{3,2,1,0:T(8,128)}, f32[2,2,32,1024]{3,2,1,0:T(8,128)}...) custom-call(s32[4]{0:T(128)} %pad_add_fusion.place, ...), custom_call_target="tpu_custom_call" | custom-call | flops 3221225472 | bytes 8388608 | tf_op jit(solution)/shard_map/pallas_call | solution.py:271
  130.7 6.3 %collective-permute-done.7.a2 = f32[3,2,32,1024]{3,2,1,0:T(8,128)} collective-permute-done((f32[3,2,32,1024]{3,2,1,0:T(8,128)S(1)}, f32[3,2,32,1024]{3,2,1,0:T(8,128)}, u32[]{:S(2)}, u32[]{:S(2)}) %collective-permute-start.7) | collective-permute-done | bytes 786464 | tf_op jit(solution)/shard_map/ppermute | solution.py:53
  137.1 3.1 %shard_map.152 = (f32[3,2,32,256]{3,2,1,0:T(8,128)}, f32[3,2,32,256]{3,2,1,0:T(8,128)}, f32[3,2,32,256]{3,2,1,0:T(8,128)}, f32[3,2,32,256]{3,2,1,0:T(8,128)}) custom-call(s32[4]{0:T(128)} %pad_add_fusion.place, f32[3,2,32,1024]{3,2,1,0:T(8,128)} %get-tuple-element.72.a0.after, f32[3,2,32,1024]{3,2,1,0:T(8,128)} %copy-done.10, ...), custom_call_target="tpu_custom_call" | custom-call | flops 589824 | bytes 3932160 | tf_op jit(solution)/shard_map/pallas_call | solution.py:232
  140.1 1.2 collective-permute-done.12.a1
  141.3 1.0 collective-permute-start.10
  142.3 2.6 %collective-permute-start.22 = (f32[2,2,32,1024]{3,2,1,0:T(8,128)}, f32[2,2,32,1024]{3,2,1,0:T(8,128)S(1)}, u32[]{:S(2)}, u32[]{:S(2)}) collective-permute-start(f32[2,2,32,1024]{3,2,1,0:T(8,128)} %get-tuple-element.92), channel_id=1, source_target_pairs={{0,32},{16,48},{32,0},{48,16},{1,33},{17,49},{33,1},{49,17},{2,34}... | collective-permute-start | bytes 1572872 | tf_op jit(solution)/shard_map/ppermute | solution.py:53
  145.0 11.5 %collective-permute-done.14.a3 = f32[3,8,32,256]{3,2,1,0:T(8,128)} collective-permute-done((f32[3,8,32,256]{3,2,1,0:T(8,128)}, f32[3,8,32,256]{3,2,1,0:T(8,128)}, u32[]{:S(2)}, u32[]{:S(2)}) %collective-permute-start.14) | collective-permute-done | bytes 786464 | tf_op jit(solution)/shard_map/ppermute | solution.py:53
  156.4 1.7 collective-permute-start.23
  158.2 1.4 collective-permute-start.27
  159.6 0.7 copy-done.23
  160.3 2.7 %collective-permute-start.28 = (f32[2,8,32,256]{3,2,1,0:T(8,128)}, f32[2,8,32,256]{3,2,1,0:T(8,128)S(1)}, u32[]{:S(2)}, u32[]{:S(2)}) collective-permute-start(f32[2,8,32,256]{3,2,1,0:T(8,128)} %get-tuple-element.100), channel_id=1, source_target_pairs={{0,4},{2,6},{4,0},{6,2},{1,5},{3,7},{5,1},{7,3},{8,12},{10,14},{12... | collective-permute-start | bytes 1572872 | tf_op jit(solution)/shard_map/ppermute | solution.py:53
  163.1 1.1 collective-permute-start.29
  164.2 3.0 %shard_map.153 = (f32[3,2,32,256]{3,2,1,0:T(8,128)}, f32[3,2,32,256]{3,2,1,0:T(8,128)}, f32[3,2,32,256]{3,2,1,0:T(8,128)}, f32[3,2,32,256]{3,2,1,0:T(8,128)}) custom-call(s32[4]{0:T(128)} %pad_add_fusion.place, f32[3,8,32,256]{3,2,1,0:T(8,128)} %get-tuple-element.80.a0, f32[3,8,32,256]{3,2,1,0:T(8,128)} %collective-permute-done.12.a1, ...), custom_call_target="tpu_custom_call" | custom-call | flops 589824 | bytes 3932160 | tf_op jit(solution)/shard_map/pallas_call | solution.py:232
  167.5 1.3 collective-permute-done.23.a3
  168.8 1.1 collective-permute-start.15
  169.9 2.9 %collective-permute-done.27.a1 = f32[2,8,32,256]{3,2,1,0:T(8,128)S(1)} collective-permute-done((f32[2,8,32,256]{3,2,1,0:T(8,128)}, f32[2,8,32,256]{3,2,1,0:T(8,128)S(1)}, u32[]{:S(2)}, u32[]{:S(2)}) %collective-permute-start.27) | collective-permute-done | bytes 524320 | tf_op jit(solution)/shard_map/ppermute | solution.py:53
  172.9 1.0 collective-permute-start.16
  173.8 11.3 %collective-permute-done.28.a2 = f32[2,8,32,256]{3,2,1,0:T(8,128)S(1)} collective-permute-done((f32[2,8,32,256]{3,2,1,0:T(8,128)}, f32[2,8,32,256]{3,2,1,0:T(8,128)S(1)}, u32[]{:S(2)}, u32[]{:S(2)}) %collective-permute-start.28) | collective-permute-done | bytes 524320 | tf_op jit(solution)/shard_map/ppermute | solution.py:53
  185.1 0.7 collective-permute-start.17
  185.8 2.5 %shard_map.156 = (f32[2,2,32,256]{3,2,1,0:T(8,128)}, f32[2,2,32,256]{3,2,1,0:T(8,128)}, f32[2,2,32,256]{3,2,1,0:T(8,128)}, f32[2,2,32,256]{3,2,1,0:T(8,128)}) custom-call(s32[4]{0:T(128)} %pad_add_fusion.place, f32[2,2,32,1024]{3,2,1,0:T(8,128)} %get-tuple-element.90.a0, f32[2,2,32,1024]{3,2,1,0:T(8,128)} %copy-done.12, f32[2,2,32,1024]{3,2,1,0:T(8,128)} %copy-done.14, ...), custom_call_target="tpu_custom_call" | custom-call | flops 393216 | bytes 2621440 | tf_op jit(solution)/shard_map/pallas_call | solution.py:232
  188.5 0.7 copy-done.17
  189.2 2.5 %shard_map.157 = (f32[2,2,32,256]{3,2,1,0:T(8,128)}, f32[2,2,32,256]{3,2,1,0:T(8,128)}, f32[2,2,32,256]{3,2,1,0:T(8,128)}, f32[2,2,32,256]{3,2,1,0:T(8,128)}) custom-call(s32[4]{0:T(128)} %pad_add_fusion.place, f32[2,8,32,256]{3,2,1,0:T(8,128)} %get-tuple-element.98.a0, f32[2,8,32,256]{3,2,1,0:T(8,128)} %copy-done.13, f32[2,8,32,256]{3,2,1,0:T(8,128)} %copy-done.15, ...), custom_call_target="tpu_custom_call" | custom-call | flops 393216 | bytes 2621440 | tf_op jit(solution)/shard_map/pallas_call | solution.py:232
  191.8 1.4 collective-permute-start.25
  193.2 1.9 collective-permute-start.26
  195.1 0.9 collective-permute-start.30
  196.0 1.3 collective-permute-start.31
  197.3 2.0 collective-permute-start.32
  199.6 3.4 %collective-permute-done.30.refs_13_ = f32[2,2,32,256]{3,2,1,0:T(8,128)S(1)} collective-permute-done((f32[2,2,32,256]{3,2,1,0:T(8,128)}, f32[2,2,32,256]{3,2,1,0:T(8,128)S(1)}, u32[]{:S(2)}, u32[]{:S(2)}) %collective-permute-start.30) | collective-permute-done | bytes 131104 | tf_op jit(solution)/shard_map/ppermute | solution.py:53
  203.0 0.7 collective-permute-done.32.refs_15_
  203.8 0.6 copy-done.36
  204.4 2.8 %shard_map.158 = (f32[5,64,128]{2,1,0:T(8,128)}, f32[5,64,128]{2,1,0:T(8,128)}, f32[5,64,128]{2,1,0:T(8,128)}, f32[5,64,128]{2,1,0:T(8,128)}) custom-call(s32[4]{0:T(128)} %pad_add_fusion.place, f32[3,2,32,256]{3,2,1,0:T(8,128)} %get-tuple-element.76.refs_0_, f32[3,2,32,256]{3,2,1,0:T(8,128)} %copy-done.22, f32[3,2,32,256]{3,2,1,0:T(8,128)} %copy-done.23, ...), custom_call_target="tpu_custom_call" | custom-call | flops 1048576 | bytes 4194304 | tf_op jit(solution)/shard_map/pallas_call | solution.py:244
  207.5 3.4 %collective-permute-start.34 = (f32[5,64,128]{2,1,0:T(8,128)}, f32[5,64,128]{2,1,0:T(8,128)S(1)}, u32[]{:S(2)}, u32[]{:S(2)}) collective-permute-start(f32[5,64,128]{2,1,0:T(8,128)} %get-tuple-element.108), channel_id=1, source_target_pairs={{0,64},{1,65},{64,0},{65,1},{2,66},{3,67},{66,2},{67,3},{4,68},{5,... | collective-permute-start | bytes 491528 | tf_op jit(solution)/shard_map/ppermute | solution.py:53
  210.9 2.1 collective-permute-start.35
  213.0 0.9 collective-permute-done.33.a1
  213.9 2.2 %collective-permute-done.34.a2 = f32[5,64,128]{2,1,0:T(8,128)S(1)} collective-permute-done((f32[5,64,128]{2,1,0:T(8,128)}, f32[5,64,128]{2,1,0:T(8,128)S(1)}, u32[]{:S(2)}, u32[]{:S(2)}) %collective-permute-start.34) | collective-permute-done | bytes 163872 | tf_op jit(solution)/shard_map/ppermute | solution.py:53
  217.2 1.8 shard_map.159
  (110 shorter events, 4.0 us)
Async XLA Ops:
  0.6 14.1 %copy-start.1 = (f32[128,1024]{1,0:T(8,128)S(1)}, f32[128,1024]{1,0:T(8,128)}, u32[]{:S(2)}) copy-start(f32[128,1024]{1,0:T(8,128)} %own.2) | copy-start | bytes 1572868
  3.6 50.5 %all-to-all-start = ((f32[128,2,1024]{2,1,0:T(2,128)}), f32[128,2,1024]{2,1,0:T(2,128)S(1)}, u32[]{:S(2)}, u32[]{:S(2)}) async-start(f32[128,2,1024]{2,1,0:T(2,128)} %shard_map.147), calls=%async_computation | async-start | bytes 2097152 | tf_op jit(solution)/shard_map/all_to_all | solution.py:299
  14.8 34.3 %collective-permute-start.3 = (f32[128,1024]{1,0:T(8,128)S(1)}, f32[128,1024]{1,0:T(8,128)S(1)}, u32[]{:S(2)}, u32[]{:S(2)}) collective-permute-start(f32[128,1024]{1,0:T(8,128)S(1)} %copy-done.1), channel_id=1, source_target_pairs={{0,1},{1,2},{2,3},{3,4},{4,5},{5,6},{6,7},{7,8},{8,9},{9,10},{10,1... | collective-permute-start | bytes 1572872 | tf_op jit(solution)/shard_map/ppermute | solution.py:59
  17.8 31.3 %collective-permute-start.4 = (f32[128,1024]{1,0:T(8,128)S(1)}, f32[128,1024]{1,0:T(8,128)S(1)}, u32[]{:S(2)}, u32[]{:S(2)}) collective-permute-start(f32[128,1024]{1,0:T(8,128)S(1)} %copy-done.1), channel_id=1, source_target_pairs={{1,0},{2,1},{3,2},{4,3},{5,4},{6,5},{7,6},{8,7},{9,8},{10,9},{11,1... | collective-permute-start | bytes 1572872 | tf_op jit(solution)/shard_map/ppermute | solution.py:59
  54.0 4.7 %copy-start.38 = (f32[8,64,128]{2,1,0:T(8,128)S(1)}, f32[8,64,128]{2,1,0:T(8,128)}, u32[]{:S(2)}) copy-start(f32[8,64,128]{2,1,0:T(8,128)} %get-tuple-element.63) | copy-start | bytes 786436
  54.0 5.2 %copy-start = (f32[256,1024]{1,0:T(8,128)S(1)}, f32[256,1024]{1,0:T(8,128)}, u32[]{:S(2)}) copy-start(f32[256,1024]{1,0:T(8,128)} %own.3) | copy-start | bytes 3145732
  54.0 11.8 %collective-permute-start.5 = (f32[2,128,1024]{2,1,0:T(8,128)}, f32[2,128,1024]{2,1,0:T(8,128)}, u32[]{:S(2)}, u32[]{:S(2)}) collective-permute-start(f32[2,128,1024]{2,1,0:T(8,128)} %shard_map.149.if0), channel_id=1, source_target_pairs={{0,8},{8,0},{1,9},{9,1},{2,10},{10,2},{3,11},{11,3},{4,12},{12,4},... | collective-permute-start | bytes 3145736 | tf_op jit(solution)/shard_map/ppermute | solution.py:53
  58.2 12.9 %collective-permute-start.1 = (f32[256,1024]{1,0:T(8,128)}, f32[256,1024]{1,0:T(8,128)S(1)}, u32[]{:S(2)}, u32[]{:S(2)}) collective-permute-start(f32[256,1024]{1,0:T(8,128)} %shard_map.148.ic0), channel_id=1, source_target_pairs={{0,8},{8,0},{1,9},{9,1},{2,10},{10,2},{3,11},{11,3},{4,12},{12,4},... | collective-permute-start | bytes 3145736 | tf_op jit(solution)/shard_map/ppermute | solution.py:53
  58.7 12.5 %collective-permute-start = (f32[8,64,256]{2,1,0:T(8,128)}, f32[8,64,256]{2,1,0:T(8,128)S(1)}, u32[]{:S(2)}, u32[]{:S(2)}) collective-permute-start(f32[8,64,256]{2,1,0:T(8,128)} %get-tuple-element.61), channel_id=1, source_target_pairs={{0,8},{8,0},{1,9},{9,1},{2,10},{10,2},{3,11},{11,3},{4,12},{12,4},... | collective-permute-start | bytes 1572872 | tf_op jit(solution)/shard_map/ppermute | solution.py:53
  58.7 5.8 %collective-permute-start.2 = (f32[8,64,128]{2,1,0:T(8,128)S(1)}, f32[8,64,128]{2,1,0:T(8,128)S(1)}, u32[]{:S(2)}, u32[]{:S(2)}) collective-permute-start(f32[8,64,128]{2,1,0:T(8,128)S(1)} %copy-done.38), channel_id=1, source_target_pairs={{0,8},{8,0},{1,9},{9,1},{2,10},{10,2},{3,11},{11,3},{4,12},{12,4},... | collective-permute-start | bytes 786440 | tf_op jit(solution)/shard_map/ppermute | solution.py:53
  60.1 27.3 %collective-permute-start.18 = (f32[128,1024]{1,0:T(8,128)}, f32[128,1024]{1,0:T(8,128)S(1)}, u32[]{:S(2)}, u32[]{:S(2)}) collective-permute-start(f32[128,1024]{1,0:T(8,128)} %get-tuple-element.88), channel_id=1, source_target_pairs={{0,1},{1,2},{2,3},{3,4},{4,5},{5,6},{6,7},{7,8},{8,9},{9,10},{10,1... | collective-permute-start | bytes 1572872 | tf_op jit(solution)/shard_map/ppermute | solution.py:59
  64.5 1.3 copy-start.39
  64.5 22.9 %collective-permute-start.19 = (f32[128,1024]{1,0:T(8,128)S(1)}, f32[128,1024]{1,0:T(8,128)S(1)}, u32[]{:S(2)}, u32[]{:S(2)}) collective-permute-start(f32[128,1024]{1,0:T(8,128)S(1)} %get-tuple-element.89), channel_id=1, source_target_pairs={{1,0},{2,1},{3,2},{4,3},{5,4},{6,5},{7,6},{8,7},{9,8},{10,9},{11,1... | collective-permute-start | bytes 1572872 | tf_op jit(solution)/shard_map/ppermute | solution.py:59
  89.0 6.1 %copy-start.4 = (f32[3,2,32,1024]{3,2,1,0:T(8,128)S(1)}, f32[3,2,32,1024]{3,2,1,0:T(8,128)}, u32[]{:S(2)}) copy-start(f32[3,2,32,1024]{3,2,1,0:T(8,128)} %get-tuple-element.73) | copy-start | bytes 2359300
  89.0 10.9 %copy-start.5 = (f32[3,2,32,1024]{3,2,1,0:T(8,128)S(1)}, f32[3,2,32,1024]{3,2,1,0:T(8,128)}, u32[]{:S(2)}) copy-start(f32[3,2,32,1024]{3,2,1,0:T(8,128)} %get-tuple-element.74) | copy-start | bytes 2359300
  89.0 13.2 %copy-start.6 = (f32[3,2,32,1024]{3,2,1,0:T(8,128)S(1)}, f32[3,2,32,1024]{3,2,1,0:T(8,128)}, u32[]{:S(2)}) copy-start(f32[3,2,32,1024]{3,2,1,0:T(8,128)} %get-tuple-element.75) | copy-start | bytes 2359300
  89.0 15.1 %copy-start.7 = (f32[3,8,32,256]{3,2,1,0:T(8,128)S(1)}, f32[3,8,32,256]{3,2,1,0:T(8,128)}, u32[]{:S(2)}) copy-start(f32[3,8,32,256]{3,2,1,0:T(8,128)} %get-tuple-element.81) | copy-start | bytes 2359300
  89.0 29.9 %copy-start.8 = (f32[3,8,32,256]{3,2,1,0:T(8,128)S(1)}, f32[3,8,32,256]{3,2,1,0:T(8,128)}, u32[]{:S(2)}) copy-start(f32[3,8,32,256]{3,2,1,0:T(8,128)} %get-tuple-element.82) | copy-start | bytes 2359300
  95.1 25.4 %collective-permute-start.20 = (f32[2,256,1024]{2,1,0:T(8,128)}, f32[2,256,1024]{2,1,0:T(8,128)S(1)}, u32[]{:S(2)}, u32[]{:S(2)}) collective-permute-start(f32[2,256,1024]{2,1,0:T(8,128)} %shard_map.154.is0), channel_id=1, source_target_pairs={{0,8},{8,0},{1,9},{9,1},{2,10},{10,2},{3,11},{11,3},{4,12},{12,4},... | collective-permute-start | bytes 6291464 | tf_op jit(solution)/shard_map/ppermute | solution.py:53
  95.1 23.8 %collective-permute-start.6 = (f32[3,2,32,1024]{3,2,1,0:T(8,128)S(1)}, f32[3,2,32,1024]{3,2,1,0:T(8,128)S(1)}, u32[]{:S(2)}, u32[]{:S(2)}) collective-permute-start(f32[3,2,32,1024]{3,2,1,0:T(8,128)S(1)} %copy-done.4), channel_id=1, source_target_pairs={{0,16},{16,32},{32,48},{48,0},{1,17},{17,33},{33,49},{49,1},{2,18}... | collective-permute-start | bytes 2359304 | tf_op jit(solution)/shard_map/ppermute | solution.py:53
  99.9 37.1 %collective-permute-start.7 = (f32[3,2,32,1024]{3,2,1,0:T(8,128)S(1)}, f32[3,2,32,1024]{3,2,1,0:T(8,128)}, u32[]{:S(2)}, u32[]{:S(2)}) collective-permute-start(f32[3,2,32,1024]{3,2,1,0:T(8,128)S(1)} %copy-done.5), channel_id=1, source_target_pairs={{0,32},{16,48},{32,0},{48,16},{1,33},{17,49},{33,1},{49,17},{2,34}... | collective-permute-start | bytes 2359304 | tf_op jit(solution)/shard_map/ppermute | solution.py:53
  102.2 34.8 %collective-permute-start.8 = (f32[3,2,32,1024]{3,2,1,0:T(8,128)S(1)}, f32[3,2,32,1024]{3,2,1,0:T(8,128)}, u32[]{:S(2)}, u32[]{:S(2)}) collective-permute-start(f32[3,2,32,1024]{3,2,1,0:T(8,128)S(1)} %copy-done.6), channel_id=1, source_target_pairs={{0,48},{16,0},{32,16},{48,32},{1,49},{17,1},{33,17},{49,33},{2,50}... | collective-permute-start | bytes 2359304 | tf_op jit(solution)/shard_map/ppermute | solution.py:53
  104.1 37.2 %collective-permute-start.12 = (f32[3,8,32,256]{3,2,1,0:T(8,128)S(1)}, f32[3,8,32,256]{3,2,1,0:T(8,128)}, u32[]{:S(2)}, u32[]{:S(2)}) collective-permute-start(f32[3,8,32,256]{3,2,1,0:T(8,128)S(1)} %copy-done.7), channel_id=1, source_target_pairs={{0,2},{2,4},{4,6},{6,0},{1,3},{3,5},{5,7},{7,1},{8,10},{10,12},{12... | collective-permute-start | bytes 2359304 | tf_op jit(solution)/shard_map/ppermute | solution.py:53
  118.9 1.6 copy-start.10
  118.9 23.4 %collective-permute-start.13 = (f32[3,8,32,256]{3,2,1,0:T(8,128)S(1)}, f32[3,8,32,256]{3,2,1,0:T(8,128)S(1)}, u32[]{:S(2)}, u32[]{:S(2)}) collective-permute-start(f32[3,8,32,256]{3,2,1,0:T(8,128)S(1)} %copy-done.8), channel_id=1, source_target_pairs={{0,4},{2,6},{4,0},{6,2},{1,5},{3,7},{5,1},{7,3},{8,12},{10,14},{12... | collective-permute-start | bytes 2359304 | tf_op jit(solution)/shard_map/ppermute | solution.py:53
  121.8 34.6 %collective-permute-start.14 = (f32[3,8,32,256]{3,2,1,0:T(8,128)}, f32[3,8,32,256]{3,2,1,0:T(8,128)}, u32[]{:S(2)}, u32[]{:S(2)}) collective-permute-start(f32[3,8,32,256]{3,2,1,0:T(8,128)} %get-tuple-element.83), channel_id=1, source_target_pairs={{0,6},{2,0},{4,2},{6,4},{1,7},{3,1},{5,3},{7,5},{8,14},{10,8},{12,... | collective-permute-start | bytes 2359304 | tf_op jit(solution)/shard_map/ppermute | solution.py:53
  137.1 26.1 %collective-permute-start.21 = (f32[2,2,32,1024]{3,2,1,0:T(8,128)}, f32[2,2,32,1024]{3,2,1,0:T(8,128)S(1)}, u32[]{:S(2)}, u32[]{:S(2)}) collective-permute-start(f32[2,2,32,1024]{3,2,1,0:T(8,128)} %get-tuple-element.91), channel_id=1, source_target_pairs={{0,16},{16,32},{32,48},{48,0},{1,17},{17,33},{33,49},{49,1},{2,18}... | collective-permute-start | bytes 1572872 | tf_op jit(solution)/shard_map/ppermute | solution.py:53
  140.1 18.1 %collective-permute-start.9 = (f32[3,2,32,256]{3,2,1,0:T(8,128)}, f32[3,2,32,256]{3,2,1,0:T(8,128)S(1)}, u32[]{:S(2)}, u32[]{:S(2)}) collective-permute-start(f32[3,2,32,256]{3,2,1,0:T(8,128)} %get-tuple-element.77), channel_id=1, source_target_pairs={{0,2},{2,4},{4,6},{6,0},{1,3},{3,5},{5,7},{7,1},{8,10},{10,12},{12... | collective-permute-start | bytes 589832 | tf_op jit(solution)/shard_map/ppermute | solution.py:53
  141.3 18.3 %collective-permute-start.10 = (f32[3,2,32,256]{3,2,1,0:T(8,128)}, f32[3,2,32,256]{3,2,1,0:T(8,128)S(1)}, u32[]{:S(2)}, u32[]{:S(2)}) collective-permute-start(f32[3,2,32,256]{3,2,1,0:T(8,128)} %get-tuple-element.78), channel_id=1, source_target_pairs={{0,4},{2,6},{4,0},{6,2},{1,5},{3,7},{5,1},{7,3},{8,12},{10,14},{12... | collective-permute-start | bytes 589832 | tf_op jit(solution)/shard_map/ppermute | solution.py:53
  142.3 21.9 %copy-start.9 = (f32[3,8,32,256]{3,2,1,0:T(8,128)}, f32[3,8,32,256]{3,2,1,0:T(8,128)S(1)}, u32[]{:S(2)}) copy-start(f32[3,8,32,256]{3,2,1,0:T(8,128)S(1)} %collective-permute-done.13.a2) | copy-start | bytes 2359300
  142.3 24.9 %collective-permute-start.22 = (f32[2,2,32,1024]{3,2,1,0:T(8,128)}, f32[2,2,32,1024]{3,2,1,0:T(8,128)S(1)}, u32[]{:S(2)}, u32[]{:S(2)}) collective-permute-start(f32[2,2,32,1024]{3,2,1,0:T(8,128)} %get-tuple-element.92), channel_id=1, source_target_pairs={{0,32},{16,48},{32,0},{48,16},{1,33},{17,49},{33,1},{49,17},{2,34}... | collective-permute-start | bytes 1572872 | tf_op jit(solution)/shard_map/ppermute | solution.py:53
  156.4 12.4 %collective-permute-start.23 = (f32[2,2,32,1024]{3,2,1,0:T(8,128)}, f32[2,2,32,1024]{3,2,1,0:T(8,128)S(1)}, u32[]{:S(2)}, u32[]{:S(2)}) collective-permute-start(f32[2,2,32,1024]{3,2,1,0:T(8,128)} %get-tuple-element.93), channel_id=1, source_target_pairs={{0,48},{16,0},{32,16},{48,32},{1,49},{17,1},{33,17},{49,33},{2,50}... | collective-permute-start | bytes 1572872 | tf_op jit(solution)/shard_map/ppermute | solution.py:53
  158.2 30.2 %copy-start.22 = (f32[3,2,32,256]{3,2,1,0:T(8,128)}, f32[3,2,32,256]{3,2,1,0:T(8,128)S(1)}, u32[]{:S(2)}) copy-start(f32[3,2,32,256]{3,2,1,0:T(8,128)S(1)} %collective-permute-done.9.refs_1_) | copy-start | bytes 589828
  158.2 14.7 %collective-permute-start.27 = (f32[2,8,32,256]{3,2,1,0:T(8,128)}, f32[2,8,32,256]{3,2,1,0:T(8,128)S(1)}, u32[]{:S(2)}, u32[]{:S(2)}) collective-permute-start(f32[2,8,32,256]{3,2,1,0:T(8,128)} %get-tuple-element.99), channel_id=1, source_target_pairs={{0,2},{2,4},{4,6},{6,0},{1,3},{3,5},{5,7},{7,1},{8,10},{10,12},{12... | collective-permute-start | bytes 1572872 | tf_op jit(solution)/shard_map/ppermute | solution.py:53
  160.3 24.9 %collective-permute-start.28 = (f32[2,8,32,256]{3,2,1,0:T(8,128)}, f32[2,8,32,256]{3,2,1,0:T(8,128)S(1)}, u32[]{:S(2)}, u32[]{:S(2)}) collective-permute-start(f32[2,8,32,256]{3,2,1,0:T(8,128)} %get-tuple-element.100), channel_id=1, source_target_pairs={{0,4},{2,6},{4,0},{6,2},{1,5},{3,7},{5,1},{7,3},{8,12},{10,14},{12... | collective-permute-start | bytes 1572872 | tf_op jit(solution)/shard_map/ppermute | solution.py:53
  163.1 22.7 %copy-start.12 = (f32[2,2,32,1024]{3,2,1,0:T(8,128)}, f32[2,2,32,1024]{3,2,1,0:T(8,128)S(1)}, u32[]{:S(2)}) copy-start(f32[2,2,32,1024]{3,2,1,0:T(8,128)S(1)} %collective-permute-done.21.a1) | copy-start | bytes 1572868
  163.1 25.3 %collective-permute-start.29 = (f32[2,8,32,256]{3,2,1,0:T(8,128)}, f32[2,8,32,256]{3,2,1,0:T(8,128)S(1)}, u32[]{:S(2)}, u32[]{:S(2)}) collective-permute-start(f32[2,8,32,256]{3,2,1,0:T(8,128)} %get-tuple-element.101), channel_id=1, source_target_pairs={{0,6},{2,0},{4,2},{6,4},{1,7},{3,1},{5,3},{7,5},{8,14},{10,8},{12,... | collective-permute-start | bytes 1572872 | tf_op jit(solution)/shard_map/ppermute | solution.py:53
  167.3 18.6 %copy-start.14 = (f32[2,2,32,1024]{3,2,1,0:T(8,128)}, f32[2,2,32,1024]{3,2,1,0:T(8,128)S(1)}, u32[]{:S(2)}) copy-start(f32[2,2,32,1024]{3,2,1,0:T(8,128)S(1)} %collective-permute-done.22.a2) | copy-start | bytes 1572868
  167.3 24.5 %collective-permute-start.11 = (f32[3,2,32,256]{3,2,1,0:T(8,128)}, f32[3,2,32,256]{3,2,1,0:T(8,128)S(1)}, u32[]{:S(2)}, u32[]{:S(2)}) collective-permute-start(f32[3,2,32,256]{3,2,1,0:T(8,128)} %get-tuple-element.79), channel_id=1, source_target_pairs={{0,6},{2,0},{4,2},{6,4},{1,7},{3,1},{5,3},{7,5},{8,14},{10,8},{12,... | collective-permute-start | bytes 589832 | tf_op jit(solution)/shard_map/ppermute | solution.py:53
  168.8 17.0 %copy-start.16 = (f32[2,2,32,1024]{3,2,1,0:T(8,128)}, f32[2,2,32,1024]{3,2,1,0:T(8,128)S(1)}, u32[]{:S(2)}) copy-start(f32[2,2,32,1024]{3,2,1,0:T(8,128)S(1)} %collective-permute-done.23.a3) | copy-start | bytes 1572868
  168.8 24.4 %collective-permute-start.15 = (f32[3,2,32,256]{3,2,1,0:T(8,128)}, f32[3,2,32,256]{3,2,1,0:T(8,128)S(1)}, u32[]{:S(2)}, u32[]{:S(2)}) collective-permute-start(f32[3,2,32,256]{3,2,1,0:T(8,128)} %get-tuple-element.85), channel_id=1, source_target_pairs={{0,16},{16,32},{32,48},{48,0},{1,17},{17,33},{33,49},{49,1},{2,18}... | collective-permute-start | bytes 589832 | tf_op jit(solution)/shard_map/ppermute | solution.py:53
  172.9 15.6 %copy-start.13 = (f32[2,8,32,256]{3,2,1,0:T(8,128)}, f32[2,8,32,256]{3,2,1,0:T(8,128)S(1)}, u32[]{:S(2)}) copy-start(f32[2,8,32,256]{3,2,1,0:T(8,128)S(1)} %collective-permute-done.27.a1) | copy-start | bytes 1572868
  172.9 22.2 %collective-permute-start.16 = (f32[3,2,32,256]{3,2,1,0:T(8,128)}, f32[3,2,32,256]{3,2,1,0:T(8,128)S(1)}, u32[]{:S(2)}, u32[]{:S(2)}) collective-permute-start(f32[3,2,32,256]{3,2,1,0:T(8,128)} %get-tuple-element.86), channel_id=1, source_target_pairs={{0,32},{16,48},{32,0},{48,16},{1,33},{17,49},{33,1},{49,17},{2,34}... | collective-permute-start | bytes 589832 | tf_op jit(solution)/shard_map/ppermute | solution.py:53
  185.1 3.4 %copy-start.15 = (f32[2,8,32,256]{3,2,1,0:T(8,128)}, f32[2,8,32,256]{3,2,1,0:T(8,128)S(1)}, u32[]{:S(2)}) copy-start(f32[2,8,32,256]{3,2,1,0:T(8,128)S(1)} %collective-permute-done.28.a2) | copy-start | bytes 1572868
  185.1 10.9 %collective-permute-start.17 = (f32[3,2,32,256]{3,2,1,0:T(8,128)}, f32[3,2,32,256]{3,2,1,0:T(8,128)S(1)}, u32[]{:S(2)}, u32[]{:S(2)}) collective-permute-start(f32[3,2,32,256]{3,2,1,0:T(8,128)} %get-tuple-element.87), channel_id=1, source_target_pairs={{0,48},{16,0},{32,16},{48,32},{1,49},{17,1},{33,17},{49,33},{2,50}... | collective-permute-start | bytes 589832 | tf_op jit(solution)/shard_map/ppermute | solution.py:53
  188.4 3.4 %copy-start.41 = (f32[2,2,32,256]{3,2,1,0:T(8,128)S(1)}, f32[2,2,32,256]{3,2,1,0:T(8,128)}, u32[]{:S(2)}) copy-start(f32[2,2,32,256]{3,2,1,0:T(8,128)} %get-tuple-element.96) | copy-start | bytes 393220
  188.4 4.8 %copy-start.40 = (f32[2,2,32,256]{3,2,1,0:T(8,128)S(1)}, f32[2,2,32,256]{3,2,1,0:T(8,128)}, u32[]{:S(2)}) copy-start(f32[2,2,32,256]{3,2,1,0:T(8,128)} %get-tuple-element.97) | copy-start | bytes 393220
  188.4 8.9 %collective-permute-start.24 = (f32[2,2,32,256]{3,2,1,0:T(8,128)}, f32[2,2,32,256]{3,2,1,0:T(8,128)S(1)}, u32[]{:S(2)}, u32[]{:S(2)}) collective-permute-start(f32[2,2,32,256]{3,2,1,0:T(8,128)} %get-tuple-element.95), channel_id=1, source_target_pairs={{0,2},{2,4},{4,6},{6,0},{1,3},{3,5},{5,7},{7,1},{8,10},{10,12},{12... | collective-permute-start | bytes 393224 | tf_op jit(solution)/shard_map/ppermute | solution.py:53
  191.8 11.9 %copy-start.24 = (f32[3,2,32,256]{3,2,1,0:T(8,128)}, f32[3,2,32,256]{3,2,1,0:T(8,128)S(1)}, u32[]{:S(2)}) copy-start(f32[3,2,32,256]{3,2,1,0:T(8,128)S(1)} %collective-permute-done.11.refs_3_) | copy-start | bytes 589828
  191.8 7.5 %collective-permute-start.25 = (f32[2,2,32,256]{3,2,1,0:T(8,128)S(1)}, f32[2,2,32,256]{3,2,1,0:T(8,128)S(1)}, u32[]{:S(2)}, u32[]{:S(2)}) collective-permute-start(f32[2,2,32,256]{3,2,1,0:T(8,128)S(1)} %copy-done.41), channel_id=1, source_target_pairs={{0,4},{2,6},{4,0},{6,2},{1,5},{3,7},{5,1},{7,3},{8,12},{10,14},{12... | collective-permute-start | bytes 393224 | tf_op jit(solution)/shard_map/ppermute | solution.py:53
  193.2 10.5 %copy-start.25 = (f32[3,2,32,256]{3,2,1,0:T(8,128)}, f32[3,2,32,256]{3,2,1,0:T(8,128)S(1)}, u32[]{:S(2)}) copy-start(f32[3,2,32,256]{3,2,1,0:T(8,128)S(1)} %collective-permute-done.15.refs_5_) | copy-start | bytes 589828
  193.2 6.4 %collective-permute-start.26 = (f32[2,2,32,256]{3,2,1,0:T(8,128)S(1)}, f32[2,2,32,256]{3,2,1,0:T(8,128)S(1)}, u32[]{:S(2)}, u32[]{:S(2)}) collective-permute-start(f32[2,2,32,256]{3,2,1,0:T(8,128)S(1)} %copy-done.40), channel_id=1, source_target_pairs={{0,6},{2,0},{4,2},{6,4},{1,7},{3,1},{5,3},{7,5},{8,14},{10,8},{12,... | collective-permute-start | bytes 393224 | tf_op jit(solution)/shard_map/ppermute | solution.py:53
  195.0 8.7 %copy-start.26 = (f32[3,2,32,256]{3,2,1,0:T(8,128)}, f32[3,2,32,256]{3,2,1,0:T(8,128)S(1)}, u32[]{:S(2)}) copy-start(f32[3,2,32,256]{3,2,1,0:T(8,128)S(1)} %collective-permute-done.16.refs_6_) | copy-start | bytes 589828
  195.1 8.0 %collective-permute-start.30 = (f32[2,2,32,256]{3,2,1,0:T(8,128)}, f32[2,2,32,256]{3,2,1,0:T(8,128)S(1)}, u32[]{:S(2)}, u32[]{:S(2)}) collective-permute-start(f32[2,2,32,256]{3,2,1,0:T(8,128)} %get-tuple-element.103), channel_id=1, source_target_pairs={{0,16},{16,32},{32,48},{48,0},{1,17},{17,33},{33,49},{49,1},{2,18}... | collective-permute-start | bytes 393224 | tf_op jit(solution)/shard_map/ppermute | solution.py:53
  196.0 7.7 %copy-start.27 = (f32[3,2,32,256]{3,2,1,0:T(8,128)}, f32[3,2,32,256]{3,2,1,0:T(8,128)S(1)}, u32[]{:S(2)}) copy-start(f32[3,2,32,256]{3,2,1,0:T(8,128)S(1)} %collective-permute-done.17.refs_7_) | copy-start | bytes 589828
  196.0 7.0 %collective-permute-start.31 = (f32[2,2,32,256]{3,2,1,0:T(8,128)}, f32[2,2,32,256]{3,2,1,0:T(8,128)S(1)}, u32[]{:S(2)}, u32[]{:S(2)}) collective-permute-start(f32[2,2,32,256]{3,2,1,0:T(8,128)} %get-tuple-element.104), channel_id=1, source_target_pairs={{0,32},{16,48},{32,0},{48,16},{1,33},{17,49},{33,1},{49,17},{2,34}... | collective-permute-start | bytes 393224 | tf_op jit(solution)/shard_map/ppermute | solution.py:53
  197.3 6.4 %copy-start.31 = (f32[2,2,32,256]{3,2,1,0:T(8,128)}, f32[2,2,32,256]{3,2,1,0:T(8,128)S(1)}, u32[]{:S(2)}) copy-start(f32[2,2,32,256]{3,2,1,0:T(8,128)S(1)} %collective-permute-done.24.refs_9_) | copy-start | bytes 393220
  197.3 6.4 %collective-permute-start.32 = (f32[2,2,32,256]{3,2,1,0:T(8,128)}, f32[2,2,32,256]{3,2,1,0:T(8,128)S(1)}, u32[]{:S(2)}, u32[]{:S(2)}) collective-permute-start(f32[2,2,32,256]{3,2,1,0:T(8,128)} %get-tuple-element.105), channel_id=1, source_target_pairs={{0,48},{16,0},{32,16},{48,32},{1,49},{17,1},{33,17},{49,33},{2,50}... | collective-permute-start | bytes 393224 | tf_op jit(solution)/shard_map/ppermute | solution.py:53
  199.3 4.5 %copy-start.32 = (f32[2,2,32,256]{3,2,1,0:T(8,128)}, f32[2,2,32,256]{3,2,1,0:T(8,128)S(1)}, u32[]{:S(2)}) copy-start(f32[2,2,32,256]{3,2,1,0:T(8,128)S(1)} %collective-permute-done.25.refs_10_) | copy-start | bytes 393220
  199.6 4.1 %copy-start.33 = (f32[2,2,32,256]{3,2,1,0:T(8,128)}, f32[2,2,32,256]{3,2,1,0:T(8,128)S(1)}, u32[]{:S(2)}) copy-start(f32[2,2,32,256]{3,2,1,0:T(8,128)S(1)} %collective-permute-done.26.refs_11_) | copy-start | bytes 393220
  207.2 6.7 %collective-permute-start.33 = (f32[5,64,128]{2,1,0:T(8,128)}, f32[5,64,128]{2,1,0:T(8,128)S(1)}, u32[]{:S(2)}, u32[]{:S(2)}) collective-permute-start(f32[5,64,128]{2,1,0:T(8,128)} %get-tuple-element.107), channel_id=1, source_target_pairs={{0,1},{1,64},{64,65},{65,0},{2,3},{3,66},{66,67},{67,2},{4,5},{5,6... | collective-permute-start | bytes 491528 | tf_op jit(solution)/shard_map/ppermute | solution.py:53
  207.5 8.6 %collective-permute-start.34 = (f32[5,64,128]{2,1,0:T(8,128)}, f32[5,64,128]{2,1,0:T(8,128)S(1)}, u32[]{:S(2)}, u32[]{:S(2)}) collective-permute-start(f32[5,64,128]{2,1,0:T(8,128)} %get-tuple-element.108), channel_id=1, source_target_pairs={{0,64},{1,65},{64,0},{65,1},{2,66},{3,67},{66,2},{67,3},{4,68},{5,... | collective-permute-start | bytes 491528 | tf_op jit(solution)/shard_map/ppermute | solution.py:53
  210.9 5.6 %collective-permute-start.35 = (f32[5,64,128]{2,1,0:T(8,128)}, f32[5,64,128]{2,1,0:T(8,128)S(1)}, u32[]{:S(2)}, u32[]{:S(2)}) collective-permute-start(f32[5,64,128]{2,1,0:T(8,128)} %get-tuple-element.109), channel_id=1, source_target_pairs={{0,65},{1,0},{64,1},{65,64},{2,67},{3,2},{66,3},{67,66},{4,69},{5,... | collective-permute-start | bytes 491528 | tf_op jit(solution)/shard_map/ppermute | solution.py:53
  213.9 2.6 %copy-start.28 = (f32[5,64,128]{2,1,0:T(8,128)}, f32[5,64,128]{2,1,0:T(8,128)S(1)}, u32[]{:S(2)}) copy-start(f32[5,64,128]{2,1,0:T(8,128)S(1)} %collective-permute-done.33.a1) | copy-start | bytes 491524
  (15 other events, 12.7 us)
